TPU v7x, 256 devices: a whole 4x4x8 slice. The times are simulated.
256 devices in a mesh: mp: 16 (over y, x_hi, core), shard: 16 (over z, x_lo).
Axes of the slice: x: 4 (x_hi: 2, x_lo: 2; x = x_hi * 2 + x_lo), y: 4, z: 8, core: 2. Of those that a mesh axis runs over, the one named last changes fastest.
Arguments:
- bank: bfloat16 [4096, 8192], P('shard'), may hold values from -6 to 6
- calib_ids: int32 [16, 1024], P('mp', 'shard'), may hold values from 0 to 4095, as said below
- norm_gains: float32 [16, 8192], P('mp'), may hold values from 0.5 to 1.5
- proj_slabs: bfloat16 [16, 8192, 512], P('mp', 'shard'), may hold values from -0.0625 to 0.0625
Outputs:
- merged_gram: float32 [8192, 8192], P('mp', 'shard')
- numer: float32 [8192, 512], P('shard')
Inputs may be any that keep to these rules, and one draw needn't show every extreme that they name: `calib_ids`: token t of every model names a bank row in block t // 64, rows (t // 64) * 256 to (t // 64) * 256 + 255.
All inputs are finite; a program needn't handle non-finite values.
Results may differ from a plain program's by a relative error of at most 0.0048.
Values may be sent and summed in bfloat16 or wider, within the bound.
No kernel may reach another device: no remote copies, remote signals or barrier semaphores. Data moves between devices by JAX's collectives and lax.ppermute only.
A program may use at most 128 MiB of HBM per device.

v0:
```python
import jax
import jax.numpy as jnp
from jax import lax
from jax.experimental import pallas as pl
from jax.experimental.pallas import tpu as pltpu
from jax.sharding import PartitionSpec as P

ALPHA = 0.9
EPSILON = 1e-05
BF = jnp.bfloat16
F4 = jnp.float32
AXES = ("mp", "shard")
Z_GROUPS = [[z * 2 + xl for z in range(8)] for xl in range(2)]
CORE_GROUPS = [[q * 2 + c for q in range(8)] for c in range(2)]


def shift(x, y=0, xh=0, c=0, z=0, xl=0):
    pairs = []
    for p in range(16):
        for s in range(16):
            py, pxh, pc = p // 4, p // 2 % 2, p % 2
            sz, sxl = s // 2, s % 2
            tp = (py + y) % 4 * 4 + (pxh ^ xh) * 2 + (pc ^ c)
            ts = (sz + z) % 8 * 2 + (sxl ^ xl)
            pairs.append((p * 16 + s, tp * 16 + ts))
    return lax.ppermute(x, AXES, pairs)


def swap_z(x):
    return lax.all_to_all(x, "shard", 0, 0, tiled=True, axis_index_groups=Z_GROUPS)


def dot(a, b):
    return jnp.dot(a, b, preferred_element_type=F4)


def contract_rows(a, b):
    return lax.dot_general(a, b, (((0,), (0,)), ((), ())), preferred_element_type=F4)


def gather_mp(x):
    half = x.shape[0] // 2
    h = shift(x, xh=1)
    u = shift(x, y=1)
    d = shift(x, y=-1)
    hu = shift(h, y=1)
    hd = shift(h, y=-1)
    t = jnp.concatenate([shift(u[:half], y=1), shift(d[half:], y=-1)], 0)
    ht = shift(t, xh=1)
    own = jnp.stack([x, h, d, hd, t, ht, u, hu], 0)
    return own, shift(own, c=1)


def gather_z(x):
    u, d = [x], [x]
    for _ in range(3):
        u.append(shift(u[-1], z=1))
        d.append(shift(d[-1], z=-1))
    far = [shift(u[3][:128], z=1), shift(d[3][128:], z=-1)]
    return [x, d[1], d[2], d[3]] + far + [u[3], u[2], u[1]]


def prepare_kernel(info, bank, ids, gains, calib_out, piece_out, rows):
    p, xl = info[0], info[1]
    pick = (ids[...] == lax.broadcasted_iota(jnp.int32, (64, 256), 1)).astype(BF)

    def take(b, total):
        at = pl.multiple_of(b * 512, 512)
        got = dot(pick, bank[:, pl.ds(at, 512)])
        rows[b] = got
        return total + jnp.sum(got * got, axis=1, keepdims=True)

    total = lax.fori_loop(0, 16, take, jnp.zeros((64, 1), F4))
    scale = lax.rsqrt(total / 8192 + EPSILON)
    hi = scale.astype(BF).astype(F4)
    mid = (scale - hi).astype(BF).astype(F4)
    low = scale - hi - mid
    lane = lax.broadcasted_iota(jnp.int32, (16, 128), 1)
    extra = jnp.zeros((16, 128), F4)
    for q in range(4):
        part = slice(q * 16, q * 16 + 16)
        for j, v in enumerate((ids[...].astype(F4), hi, mid, low)):
            extra = jnp.where(lane == q * 32 + j, v[part], extra)
    extra = extra.astype(BF)
    own_row = pl.multiple_of(p * 16, 16)

    def emit(zz, carry):
        for j in range(2):
            b = zz * 2 + (xl ^ j)
            g = gains[pl.ds(b, 1), :]
            calib_out[zz, :, j * 512 : j * 512 + 512] = (rows[b] * scale * g).astype(BF)
            piece_out[zz, :, j * 512 : j * 512 + 512] = bank[
                pl.ds(own_row, 16), pl.ds(pl.multiple_of(b * 512, 512), 512)
            ]
        piece_out[zz, :, 1024:] = extra
        return carry

    lax.fori_loop(0, 8, emit, 0)


def prepare(info, bank, ids, gains):
    return pl.pallas_call(
        prepare_kernel,
        in_specs=[
            pl.BlockSpec(memory_space=pltpu.SMEM),
            pl.BlockSpec(memory_space=pltpu.VMEM),
            pl.BlockSpec(memory_space=pltpu.VMEM),
            pl.BlockSpec(memory_space=pltpu.VMEM),
        ],
        out_specs=[pl.BlockSpec(memory_space=pltpu.VMEM)] * 2,
        out_shape=[
            jax.ShapeDtypeStruct((8, 64, 1024), BF),
            jax.ShapeDtypeStruct((8, 16, 1152), BF),
        ],
        scratch_shapes=[pltpu.VMEM((16, 64, 512), F4)],
        compiler_params=pltpu.CompilerParams(vmem_limit_bytes=32 * 2**20),
        cost_estimate=pl.CostEstimate(flops=2**28, bytes_accessed=6 * 2**20, transcendentals=64),
        name="prepare",
    )(info, bank, ids, gains)


def gram_kernel(
    info, b0, b1, b2, b3, b4a, b4b, b5, b6, b7, own_s, other_s, gains, near, far, acc, table, pick, scale, calib
):
    k = pl.program_id(0)
    y, xh, c = info[2], info[3], info[4]

    @pl.when(k == 0)
    def _():
        acc[...] = jnp.zeros_like(acc)

    for i, b in enumerate((b0, b1, b2, b3, None, b5, b6, b7)):

        @pl.when(k == i)
        def _(b=b):
            if b is None:
                table[0:128, 0:512] = b4a[...]
                table[128:256, 0:512] = b4b[...]
            else:
                table[:, 0:512] = b[...]

    lane = lax.broadcasted_iota(jnp.int32, (16, 256), 1).astype(F4)
    models = []
    for core in range(2):
        src = own_s if core == 0 else other_s
        for slot in range(8):
            dy, dxh = slot // 2, slot % 2
            q = lax.rem(y + dy, 4) * 4 + (xh ^ dxh) * 2 + (c ^ core)
            models.append(q)
            table[pl.ds(pl.multiple_of(q * 16, 16), 16), 512:1536] = src[slot, 0, :, 0:1024]
            extra = src[slot, 0, :, 1024:1152].astype(F4)
            for t in range(4):
                row = (core * 8 + slot) * 64 + t * 16
                at = t * 32
                hit = extra[:, at : at + 1] == lane
                pick[row : row + 16, :] = jnp.where(hit, 1.0, 0.0).astype(BF)
                value = extra[:, at + 1 : at + 2] + extra[:, at + 2 : at + 3] + extra[:, at + 3 : at + 4]
                scale[row : row + 16, :] = jnp.broadcast_to(value, (16, 128))

    for n in range(6):
        cols = slice(n * 256, n * 256 + 256)
        got = dot(pick[...], table[:, cols])
        for m in range(16):
            part = slice(m * 64, m * 64 + 64)
            r = scale[part, :]
            r = jnp.concatenate([r, r], 1)
            g = gains[pl.ds(models[m], 1), cols]
            calib[part, cols] = (got[part] * r * g).astype(BF)
    for n in range(4):
        cols = slice(n * 256, n * 256 + 256)
        rhs = calib[:, 512 + n * 256 : 512 + n * 256 + 256]
        acc[:, cols] += contract_rows(calib[:, 0:512], rhs)

    @pl.when(k == 7)
    def _():
        near[...] = acc[:, 0:512]
        far[...] = acc[:, 512:1024].astype(BF)


def gram_call(info, blocks, own_s, other_s, gains):
    whole = lambda shape: pl.BlockSpec(shape, lambda k, info: (0,) * len(shape))
    by_z = pl.BlockSpec((8, 1, 16, 1152), lambda k, info: (0, (info[5] + k) % 8, 0, 0))
    return pl.pallas_call(
        gram_kernel,
        grid_spec=pltpu.PrefetchScalarGridSpec(
            num_scalar_prefetch=1,
            grid=(8,),
            in_specs=[whole(b.shape) for b in blocks] + [by_z, by_z, whole((16, 1536))],
            out_specs=[whole((512, 512)), whole((512, 512))],
            scratch_shapes=[
                pltpu.VMEM((512, 1024), F4),
                pltpu.VMEM((256, 1536), BF),
                pltpu.VMEM((1024, 256), BF),
                pltpu.VMEM((1024, 128), F4),
                pltpu.VMEM((1024, 1536), BF),
            ],
        ),
        out_shape=[
            jax.ShapeDtypeStruct((512, 512), F4),
            jax.ShapeDtypeStruct((512, 512), BF),
        ],
        compiler_params=pltpu.CompilerParams(
            dimension_semantics=("arbitrary",), vmem_limit_bytes=44 * 2**20
        ),
        cost_estimate=pl.CostEstimate(flops=15 * 2**30, bytes_accessed=9 * 2**20, transcendentals=0),
        name="gram",
    )(info, *blocks, own_s, other_s, gains)


def local(bank, calib_ids, norm_gains, proj_slabs):
    p = lax.axis_index("mp")
    s = lax.axis_index("shard")
    y, xh, c = p // 4, p // 2 % 2, p % 2
    z, xl = s // 2, s % 2
    info = jnp.stack([p, xl, y, xh, c, z]).astype(jnp.int32)
    weights = proj_slabs[0]
    ids = (calib_ids[0] - s * 256).reshape(64, 1)
    gain_blocks = norm_gains.reshape(16, 512)

    mine = lax.dynamic_slice_in_dim(gain_blocks, z * 2, 2, 0)
    mine = jnp.where(xl == 0, mine, mine[::-1]).reshape(1, 1024)
    sent = jnp.concatenate([gain_blocks, jnp.broadcast_to(mine, (16, 1024))], 1)
    gains_all = lax.all_to_all(sent.reshape(16, 12, 128), "mp", 0, 0, tiled=True).reshape(16, 1536)

    calib_own, piece = prepare(info, bank, ids, gain_blocks)
    piece = swap_z(piece)
    cols = swap_z(calib_own).reshape(512, 1024)

    blocks = gather_z(lax.dynamic_slice_in_dim(bank, p * 512, 512, 1))
    own_s, other_s = gather_mp(piece)
    near, far = gram_call(info, blocks, own_s, other_s, gains_all)
    gram = near + shift(far, xl=1).astype(F4)
    on_diag = (p == s) & (
        lax.broadcasted_iota(jnp.int32, (512, 512), 0) == lax.broadcasted_iota(jnp.int32, (512, 512), 1)
    )
    merged_gram = gram * jnp.where(on_diag, 1.0 / 1024, ALPHA / 1024)

    both = jnp.concatenate([weights, shift(weights, xl=1)], 0)
    partial_out = swap_z(dot(cols, both).astype(BF).reshape(8, 64, 512))
    model_out = jnp.sum(partial_out.astype(F4), 0).astype(BF)
    model_out = swap_z(jnp.broadcast_to(model_out[None], (8, 64, 512))).reshape(512, 512)

    cols_f = cols.astype(F4)
    diag = jnp.sum(cols_f * cols_f, 0)
    numer = contract_rows(cols, model_out) * (ALPHA / 1024)
    numer = numer + ((1.0 - ALPHA) / 1024 * diag)[:, None] * both.astype(F4)
    numer = numer[:512] + shift(numer[512:].astype(BF), xl=1).astype(F4)
    numer = lax.all_to_all(numer.astype(BF).reshape(16, 32, 512), "mp", 0, 0, tiled=True)
    numer = jnp.sum(numer.astype(F4), 0)
    mine = lax.all_to_all(
        jnp.broadcast_to(numer[None], (8, 32, 512)), "mp", 0, 0, tiled=True, axis_index_groups=CORE_GROUPS
    )
    theirs = shift(mine, c=1)
    numer = jnp.where(c == 0, jnp.stack([mine, theirs], 1), jnp.stack([theirs, mine], 1)).reshape(512, 512)
    return (merged_gram, numer)


def solution(mesh):
    placed = (P("shard", None), P("mp", "shard"), P("mp", None), P("mp", "shard", None))
    return jax.shard_map(
        local,
        mesh=mesh,
        in_specs=placed,
        out_specs=(P("mp", "shard"), P("shard", None)),
        check_vma=False,
    )
```

profile of v0, /device:TPU:1, one launch (start us, length us, event | category | flops | bytes accessed | tf_op | source)
XLA Modules:
  0.0 199.9 jit_solution(16106838497492070426)
XLA Ops:
  5.8 6.0 %prepare.1 = (bf16[8,64,1024]{2,1,0:T(8,128)(2,1)}, bf16[8,16,1152]{2,1,0:T(8,128)(2,1)}) custom-call(s32[6]{0:T(128)S(1)} %stack.68.info, bf16[256,8192]{1,0:T(8,128)(2,1)S(1)} %copy-done, s32[64,1]{1,0:T(8,128)S(1)} %copy.7.ids, f32[16,512]{1,0:T(8,128)S(1)} %reshape.48.gains), custom_call_target="tpu_custom_call" | custom-call | flops 268435456 | bytes 6291456 | tf_op jit(solution)/shard_map/prepare/pallas_call | solution.py:102
  11.8 9.1 %all-to-all-start = ((bf16[8,16,1152]{2,1,0:T(8,128)(2,1)}), bf16[8,16,1152]{2,1,0:T(8,128)(2,1)S(1)}, u32[]{:S(2)}, u32[]{:S(2)}) async-start(bf16[8,16,1152]{2,1,0:T(8,128)(2,1)} %get-tuple-element.6), calls=%async_computation | async-start | bytes 589824 | tf_op jit(solution)/shard_map/all_to_all | solution.py:30
  24.7 7.5 %all-to-all-done = bf16[8,16,1152]{2,1,0:T(8,128)(2,1)S(1)} async-done(((bf16[8,16,1152]{2,1,0:T(8,128)(2,1)}), bf16[8,16,1152]{2,1,0:T(8,128)(2,1)S(1)}, u32[]{:S(2)}, u32[]{:S(2)}) %all-to-all-start) | async-done | bytes 294944 | tf_op jit(solution)/shard_map/all_to_all | solution.py:30
  32.2 4.2 %all-to-all-start.2 = ((bf16[8,64,1024]{2,1,0:T(8,128)(2,1)}), bf16[8,64,1024]{2,1,0:T(8,128)(2,1)}, u32[]{:S(2)}, u32[]{:S(2)}) async-start(bf16[8,64,1024]{2,1,0:T(8,128)(2,1)} %get-tuple-element.9), calls=%async_computation.2 | async-start | bytes 2097152 | tf_op jit(solution)/shard_map/all_to_all | solution.py:30
  36.5 2.8 %collective-permute-start.8 = (bf16[8,16,1152]{2,1,0:T(8,128)(2,1)S(1)}, bf16[8,16,1152]{2,1,0:T(8,128)(2,1)S(1)}, u32[]{:S(2)}, u32[]{:S(2)}) collective-permute-start(bf16[8,16,1152]{2,1,0:T(8,128)(2,1)S(1)} %all-to-all-done), channel_id=1, source_target_pairs={{0,32},{1,33},{2,34},{3,35},{4,36},{5,37},{6,38},{7,39},{8,40},{9,... | collective-permute-start | bytes 884744 | tf_op jit(solution)/shard_map/ppermute | solution.py:26
  39.3 2.7 %collective-permute-start.9 = (bf16[8,16,1152]{2,1,0:T(8,128)(2,1)S(1)}, bf16[8,16,1152]{2,1,0:T(8,128)(2,1)S(1)}, u32[]{:S(2)}, u32[]{:S(2)}) collective-permute-start(bf16[8,16,1152]{2,1,0:T(8,128)(2,1)S(1)} %all-to-all-done), channel_id=1, source_target_pairs={{0,192},{1,193},{2,194},{3,195},{4,196},{5,197},{6,198},{7,199},{8... | collective-permute-start | bytes 884744 | tf_op jit(solution)/shard_map/ppermute | solution.py:26
  42.8 6.4 %collective-permute-done.11 = bf16[8,16,1152]{2,1,0:T(8,128)(2,1)S(1)} collective-permute-done((bf16[8,16,1152]{2,1,0:T(8,128)(2,1)S(1)}, bf16[8,16,1152]{2,1,0:T(8,128)(2,1)S(1)}, u32[]{:S(2)}, u32[]{:S(2)}) %collective-permute-start.11) | collective-permute-done | bytes 294944 | tf_op jit(solution)/shard_map/ppermute | solution.py:26
  49.7 2.7 %collective-permute-start.13 = (bf16[4,16,1152]{2,1,0:T(8,128)(2,1)S(1)}, bf16[4,16,1152]{2,1,0:T(8,128)(2,1)S(1)}, u32[]{:S(2)}, u32[]{:S(2)}) collective-permute-start(bf16[4,16,1152]{2,1,0:T(8,128)(2,1)S(1)} %slice.28), channel_id=1, source_target_pairs={{0,192},{1,193},{2,194},{3,195},{4,196},{5,197},{6,198},{7,199},{8... | collective-permute-start | bytes 442376 | tf_op jit(solution)/shard_map/ppermute | solution.py:26
  56.8 5.4 %collective-permute-done.10 = bf16[8,16,1152]{2,1,0:T(8,128)(2,1)S(1)} collective-permute-done((bf16[8,16,1152]{2,1,0:T(8,128)(2,1)S(1)}, bf16[8,16,1152]{2,1,0:T(8,128)(2,1)S(1)}, u32[]{:S(2)}, u32[]{:S(2)}) %collective-permute-start.10) | collective-permute-done | bytes 294944 | tf_op jit(solution)/shard_map/ppermute | solution.py:26
  65.2 2.9 %convolution_convert_fusion = bf16[512,512]{1,0:T(8,128)(2,1)} fusion(bf16[512,1024]{1,0:T(8,128)(2,1)} %bitcast.15, bf16[512,512]{1,0:T(8,128)(2,1)S(1)} %collective-permute-done.18, bf16[512,512]{1,0:T(8,128)(2,1)S(1)} %bitcast.52), kind=kOutput, calls=%fused_computation.3 | convolution fusion | flops 539230208 | bytes 2621440 | tf_op jit(solution)/shard_map/dot_general | solution.py:34
  68.1 6.7 %all-to-all-start.3 = ((bf16[8,64,512]{2,1,0:T(8,128)(2,1)}), bf16[8,64,512]{2,1,0:T(8,128)(2,1)S(1)}, u32[]{:S(2)}, u32[]{:S(2)}) async-start(bf16[8,64,512]{2,1,0:T(8,128)(2,1)} %bitcast.17), calls=%async_computation.3 | async-start | bytes 1048576 | tf_op jit(solution)/shard_map/all_to_all | solution.py:30
  76.3 10.8 %all-to-all-done.3 = bf16[8,64,512]{2,1,0:T(8,128)(2,1)S(1)} async-done(((bf16[8,64,512]{2,1,0:T(8,128)(2,1)}), bf16[8,64,512]{2,1,0:T(8,128)(2,1)S(1)}, u32[]{:S(2)}, u32[]{:S(2)}) %all-to-all-start.3) | async-done | bytes 524320 | tf_op jit(solution)/shard_map/all_to_all | solution.py:30
  87.9 4.1 %all-to-all-start.4 = ((bf16[8,64,512]{2,1,0:T(8,128)(2,1)}), bf16[8,64,512]{2,1,0:T(8,128)(2,1)}, u32[]{:S(2)}, u32[]{:S(2)}) async-start(bf16[8,64,512]{2,1,0:T(8,128)(2,1)} %broadcast_in_dim.32), calls=%async_computation.4 | async-start | bytes 1048576 | tf_op jit(solution)/shard_map/all_to_all | solution.py:30
  92.8 8.2 %collective-permute-start.16 = (bf16[8,8,16,1152]{3,2,1,0:T(8,128)(2,1)}, bf16[8,8,16,1152]{3,2,1,0:T(8,128)(2,1)}, u32[]{:S(2)}, u32[]{:S(2)}) collective-permute-start(bf16[8,8,16,1152]{3,2,1,0:T(8,128)(2,1)} %bitcast_dynamic-update-slice_fusion.own_s), channel_id=1, source_target_pairs={{0,16},{1,17},{2,18},{3,19},{4,20},{5,21},{6,22},{7,23},{8,24},{9,... | collective-permute-start | bytes 7077896 | tf_op jit(solution)/shard_map/ppermute | solution.py:26
  104.2 2.4 %fusion = f32[1024,512]{1,0:T(8,128)S(1)} fusion(bf16[8,64,1024]{2,1,0:T(8,128)(2,1)} %all-to-all-done.2, bf16[8,64,512]{2,1,0:T(8,128)(2,1)} %all-to-all-done.4, f32[1024]{0:T(1024)S(1)} %broadcast_multiply_fusion, bf16[512,512]{1,0:T(8,128)(2,1)} %copy-done.6, bf16[512,512]{1,0:T(8,128)(2,1)} %bitcast.50), kind=kOutput, calls=%fused_computation.1 | convolution fusion | flops 540540928 | bytes 4722688 | tf_op jit(solution)/shard_map/dot_general | solution.py:38
  108.2 14.8 %all-to-all-start.1 = ((f32[16,12,128]{2,1,0:T(8,128)}), f32[16,12,128]{2,1,0:T(8,128)S(1)}, u32[]{:S(2)}, u32[]{:S(2)}) async-start(f32[16,12,128]{2,1,0:T(8,128)} %reshape.49), calls=%async_computation.1 | async-start | bytes 262144 | tf_op jit(solution)/shard_map/all_to_all | solution.py:223
  127.9 2.8 %all-to-all-done.1 = f32[16,12,128]{2,1,0:T(8,128)S(1)} async-done(((f32[16,12,128]{2,1,0:T(8,128)}), f32[16,12,128]{2,1,0:T(8,128)S(1)}, u32[]{:S(2)}, u32[]{:S(2)}) %all-to-all-start.1) | async-done | bytes 98336 | tf_op jit(solution)/shard_map/all_to_all | solution.py:223
  130.7 4.9 %all-to-all-start.5 = ((bf16[16,32,512]{2,1,0:T(8,128)(2,1)}), bf16[16,32,512]{2,1,0:T(8,128)(2,1)S(1)}, u32[]{:S(2)}, u32[]{:S(2)}) async-start(bf16[16,32,512]{2,1,0:T(8,128)(2,1)} %bitcast.19), calls=%async_computation.5 | async-start | bytes 1048576 | tf_op jit(solution)/shard_map/all_to_all | solution.py:248
  135.8 2.7 %collective-permute-start.2 = (bf16[256,512]{1,0:T(8,128)(2,1)S(1)}, bf16[256,512]{1,0:T(8,128)(2,1)S(1)}, u32[]{:S(2)}, u32[]{:S(2)}) collective-permute-start(bf16[256,512]{1,0:T(8,128)(2,1)S(1)} %collective-permute-done.1.b2), channel_id=1, source_target_pairs={{0,14},{1,15},{2,0},{3,1},{4,2},{5,3},{6,4},{7,5},{8,6},{9,7},{10,... | collective-permute-start | bytes 786440 | tf_op jit(solution)/shard_map/ppermute | solution.py:26
  138.5 6.3 %collective-permute-done.5.b5 = bf16[256,512]{1,0:T(8,128)(2,1)S(1)} collective-permute-done((bf16[256,512]{1,0:T(8,128)(2,1)S(1)}, bf16[256,512]{1,0:T(8,128)(2,1)S(1)}, u32[]{:S(2)}, u32[]{:S(2)}) %collective-permute-start.5) | collective-permute-done | bytes 262176 | tf_op jit(solution)/shard_map/ppermute | solution.py:26
  145.0 2.7 %collective-permute-start.7 = (bf16[128,512]{1,0:T(8,128)(2,1)S(1)}, bf16[128,512]{1,0:T(8,128)(2,1)S(1)}, u32[]{:S(2)}, u32[]{:S(2)}) collective-permute-start(bf16[128,512]{1,0:T(8,128)(2,1)S(1)} %slice.26), channel_id=1, source_target_pairs={{0,14},{1,15},{2,0},{3,1},{4,2},{5,3},{6,4},{7,5},{8,6},{9,7},{10,... | collective-permute-start | bytes 393224 | tf_op jit(solution)/shard_map/ppermute | solution.py:26
  148.6 6.2 %all-to-all-start.6 = ((f32[8,32,512]{2,1,0:T(8,128)}), f32[8,32,512]{2,1,0:T(8,128)}, u32[]{:S(2)}, u32[]{:S(2)}) async-start(f32[8,32,512]{2,1,0:T(8,128)} %broadcast_in_dim.33), calls=%async_computation.6 | async-start | bytes 1048576 | tf_op jit(solution)/shard_map/all_to_all | solution.py:250
  158.0 26.9 %gram.1 = (f32[512,512]{1,0:T(8,128)S(1)}, bf16[512,512]{1,0:T(8,128)(2,1)S(1)}) custom-call(s32[6]{0:T(128)S(1)} %stack.68.info, bf16[256,512]{1,0:T(8,128)(2,1)S(1)} %constant_dynamic-slice_fusion.1.b0, bf16[256,512]{1,0:T(8,128)(2,1)S(1)} %collective-permute-done.b1, bf16[256,512]{1,0:T(8,128)(2,1)S(1)} %collective-permute-done.1.b2, ...), custom_call_target="tpu_custom_call" | custom-call | flops 16106127360 | bytes 9437184 | tf_op jit(solution)/shard_map/gram/pallas_call | solution.py:183
  187.1 9.2 %collective-permute-done.17 = bf16[512,512]{1,0:T(8,128)(2,1)S(1)} collective-permute-done((bf16[512,512]{1,0:T(8,128)(2,1)S(1)}, bf16[512,512]{1,0:T(8,128)(2,1)S(1)}, u32[]{:S(2)}, u32[]{:S(2)}) %collective-permute-start.17) | collective-permute-done | bytes 524320 | tf_op jit(solution)/shard_map/ppermute | solution.py:26
  (89 shorter events, 40.1 us)
Async XLA Ops:
  11.8 20.4 %all-to-all-start = ((bf16[8,16,1152]{2,1,0:T(8,128)(2,1)}), bf16[8,16,1152]{2,1,0:T(8,128)(2,1)S(1)}, u32[]{:S(2)}, u32[]{:S(2)}) async-start(bf16[8,16,1152]{2,1,0:T(8,128)(2,1)} %get-tuple-element.6), calls=%async_computation | async-start | bytes 589824 | tf_op jit(solution)/shard_map/all_to_all | solution.py:30
  21.9 101.2 %collective-permute-start.3 = (bf16[256,512]{1,0:T(8,128)(2,1)S(1)}, bf16[256,512]{1,0:T(8,128)(2,1)S(1)}, u32[]{:S(2)}, u32[]{:S(2)}) collective-permute-start(bf16[256,512]{1,0:T(8,128)(2,1)S(1)} %constant_dynamic-slice_fusion.1.b0), channel_id=1, source_target_pairs={{0,2},{1,3},{2,4},{3,5},{4,6},{5,7},{6,8},{7,9},{8,10},{9,11},{10,... | collective-permute-start | bytes 786440 | tf_op jit(solution)/shard_map/ppermute | solution.py:26
  23.4 100.0 %collective-permute-start = (bf16[256,512]{1,0:T(8,128)(2,1)S(1)}, bf16[256,512]{1,0:T(8,128)(2,1)S(1)}, u32[]{:S(2)}, u32[]{:S(2)}) collective-permute-start(bf16[256,512]{1,0:T(8,128)(2,1)S(1)} %constant_dynamic-slice_fusion.1.b0), channel_id=1, source_target_pairs={{0,14},{1,15},{2,0},{3,1},{4,2},{5,3},{6,4},{7,5},{8,6},{9,7},{10,... | collective-permute-start | bytes 786440 | tf_op jit(solution)/shard_map/ppermute | solution.py:26
  32.2 33.0 %all-to-all-start.2 = ((bf16[8,64,1024]{2,1,0:T(8,128)(2,1)}), bf16[8,64,1024]{2,1,0:T(8,128)(2,1)}, u32[]{:S(2)}, u32[]{:S(2)}) async-start(bf16[8,64,1024]{2,1,0:T(8,128)(2,1)} %get-tuple-element.9), calls=%async_computation.2 | async-start | bytes 2097152 | tf_op jit(solution)/shard_map/all_to_all | solution.py:30
  36.5 13.2 %collective-permute-start.8 = (bf16[8,16,1152]{2,1,0:T(8,128)(2,1)S(1)}, bf16[8,16,1152]{2,1,0:T(8,128)(2,1)S(1)}, u32[]{:S(2)}, u32[]{:S(2)}) collective-permute-start(bf16[8,16,1152]{2,1,0:T(8,128)(2,1)S(1)} %all-to-all-done), channel_id=1, source_target_pairs={{0,32},{1,33},{2,34},{3,35},{4,36},{5,37},{6,38},{7,39},{8,40},{9,... | collective-permute-start | bytes 884744 | tf_op jit(solution)/shard_map/ppermute | solution.py:26
  39.3 10.2 %collective-permute-start.9 = (bf16[8,16,1152]{2,1,0:T(8,128)(2,1)S(1)}, bf16[8,16,1152]{2,1,0:T(8,128)(2,1)S(1)}, u32[]{:S(2)}, u32[]{:S(2)}) collective-permute-start(bf16[8,16,1152]{2,1,0:T(8,128)(2,1)S(1)} %all-to-all-done), channel_id=1, source_target_pairs={{0,192},{1,193},{2,194},{3,195},{4,196},{5,197},{6,198},{7,199},{8... | collective-permute-start | bytes 884744 | tf_op jit(solution)/shard_map/ppermute | solution.py:26
  49.2 16.0 %collective-permute-start.18 = (bf16[512,512]{1,0:T(8,128)(2,1)S(1)}, bf16[512,512]{1,0:T(8,128)(2,1)S(1)}, u32[]{:S(2)}, u32[]{:S(2)}) collective-permute-start(bf16[512,512]{1,0:T(8,128)(2,1)S(1)} %bitcast.51), channel_id=1, source_target_pairs={{0,1},{1,0},{2,3},{3,2},{4,5},{5,4},{6,7},{7,6},{8,9},{9,8},{10,11... | collective-permute-start | bytes 1572872 | tf_op jit(solution)/shard_map/ppermute | solution.py:26
  55.3 36.8 %collective-permute-start.15 = (bf16[8,16,1152]{2,1,0:T(8,128)(2,1)S(1)}, bf16[8,16,1152]{2,1,0:T(8,128)(2,1)S(1)}, u32[]{:S(2)}, u32[]{:S(2)}) collective-permute-start(bf16[8,16,1152]{2,1,0:T(8,128)(2,1)S(1)} %collective-permute-done.8), channel_id=1, source_target_pairs={{0,64},{1,65},{2,66},{3,67},{4,68},{5,69},{6,70},{7,71},{8,72},{9,... | collective-permute-start | bytes 884744 | tf_op jit(solution)/shard_map/ppermute | solution.py:26
  62.2 12.6 %collective-permute-start.14 = (bf16[8,16,1152]{2,1,0:T(8,128)(2,1)S(1)}, bf16[8,16,1152]{2,1,0:T(8,128)(2,1)S(1)}, u32[]{:S(2)}, u32[]{:S(2)}) collective-permute-start(bf16[8,16,1152]{2,1,0:T(8,128)(2,1)S(1)} %constant_dynamic-update-slice_fusion), channel_id=1, source_target_pairs={{0,32},{1,33},{2,34},{3,35},{4,36},{5,37},{6,38},{7,39},{8,40},{9,... | collective-permute-start | bytes 884744 | tf_op jit(solution)/shard_map/ppermute | solution.py:26
  68.1 18.9 %all-to-all-start.3 = ((bf16[8,64,512]{2,1,0:T(8,128)(2,1)}), bf16[8,64,512]{2,1,0:T(8,128)(2,1)S(1)}, u32[]{:S(2)}, u32[]{:S(2)}) async-start(bf16[8,64,512]{2,1,0:T(8,128)(2,1)} %bitcast.17), calls=%async_computation.3 | async-start | bytes 1048576 | tf_op jit(solution)/shard_map/all_to_all | solution.py:30
  87.9 16.3 %all-to-all-start.4 = ((bf16[8,64,512]{2,1,0:T(8,128)(2,1)}), bf16[8,64,512]{2,1,0:T(8,128)(2,1)}, u32[]{:S(2)}, u32[]{:S(2)}) async-start(bf16[8,64,512]{2,1,0:T(8,128)(2,1)} %broadcast_in_dim.32), calls=%async_computation.4 | async-start | bytes 1048576 | tf_op jit(solution)/shard_map/all_to_all | solution.py:30
  92.8 63.3 %collective-permute-start.16 = (bf16[8,8,16,1152]{3,2,1,0:T(8,128)(2,1)}, bf16[8,8,16,1152]{3,2,1,0:T(8,128)(2,1)}, u32[]{:S(2)}, u32[]{:S(2)}) collective-permute-start(bf16[8,8,16,1152]{3,2,1,0:T(8,128)(2,1)} %bitcast_dynamic-update-slice_fusion.own_s), channel_id=1, source_target_pairs={{0,16},{1,17},{2,18},{3,19},{4,20},{5,21},{6,22},{7,23},{8,24},{9,... | collective-permute-start | bytes 7077896 | tf_op jit(solution)/shard_map/ppermute | solution.py:26
  107.5 18.3 %collective-permute-start.19 = (bf16[512,512]{1,0:T(8,128)(2,1)}, bf16[512,512]{1,0:T(8,128)(2,1)}, u32[]{:S(2)}, u32[]{:S(2)}) collective-permute-start(bf16[512,512]{1,0:T(8,128)(2,1)} %slice.35), channel_id=1, source_target_pairs={{0,1},{1,0},{2,3},{3,2},{4,5},{5,4},{6,7},{7,6},{8,9},{9,8},{10,11... | collective-permute-start | bytes 1572872 | tf_op jit(solution)/shard_map/ppermute | solution.py:26
  108.2 22.5 %all-to-all-start.1 = ((f32[16,12,128]{2,1,0:T(8,128)}), f32[16,12,128]{2,1,0:T(8,128)S(1)}, u32[]{:S(2)}, u32[]{:S(2)}) async-start(f32[16,12,128]{2,1,0:T(8,128)} %reshape.49), calls=%async_computation.1 | async-start | bytes 262144 | tf_op jit(solution)/shard_map/all_to_all | solution.py:223
  123.1 12.6 %collective-permute-start.4 = (bf16[256,512]{1,0:T(8,128)(2,1)S(1)}, bf16[256,512]{1,0:T(8,128)(2,1)S(1)}, u32[]{:S(2)}, u32[]{:S(2)}) collective-permute-start(bf16[256,512]{1,0:T(8,128)(2,1)S(1)} %collective-permute-done.3.b7), channel_id=1, source_target_pairs={{0,2},{1,3},{2,4},{3,5},{4,6},{5,7},{6,8},{7,9},{8,10},{9,11},{10,... | collective-permute-start | bytes 786440 | tf_op jit(solution)/shard_map/ppermute | solution.py:26
  123.5 12.3 %collective-permute-start.1 = (bf16[256,512]{1,0:T(8,128)(2,1)S(1)}, bf16[256,512]{1,0:T(8,128)(2,1)S(1)}, u32[]{:S(2)}, u32[]{:S(2)}) collective-permute-start(bf16[256,512]{1,0:T(8,128)(2,1)S(1)} %collective-permute-done.b1), channel_id=1, source_target_pairs={{0,14},{1,15},{2,0},{3,1},{4,2},{5,3},{6,4},{7,5},{8,6},{9,7},{10,... | collective-permute-start | bytes 786440 | tf_op jit(solution)/shard_map/ppermute | solution.py:26
  130.7 17.0 %all-to-all-start.5 = ((bf16[16,32,512]{2,1,0:T(8,128)(2,1)}), bf16[16,32,512]{2,1,0:T(8,128)(2,1)S(1)}, u32[]{:S(2)}, u32[]{:S(2)}) async-start(bf16[16,32,512]{2,1,0:T(8,128)(2,1)} %bitcast.19), calls=%async_computation.5 | async-start | bytes 1048576 | tf_op jit(solution)/shard_map/all_to_all | solution.py:248
  135.7 9.2 %collective-permute-start.5 = (bf16[256,512]{1,0:T(8,128)(2,1)S(1)}, bf16[256,512]{1,0:T(8,128)(2,1)S(1)}, u32[]{:S(2)}, u32[]{:S(2)}) collective-permute-start(bf16[256,512]{1,0:T(8,128)(2,1)S(1)} %collective-permute-done.4.b6), channel_id=1, source_target_pairs={{0,2},{1,3},{2,4},{3,5},{4,6},{5,7},{6,8},{7,9},{8,10},{9,11},{10,... | collective-permute-start | bytes 786440 | tf_op jit(solution)/shard_map/ppermute | solution.py:26
  135.8 9.2 %collective-permute-start.2 = (bf16[256,512]{1,0:T(8,128)(2,1)S(1)}, bf16[256,512]{1,0:T(8,128)(2,1)S(1)}, u32[]{:S(2)}, u32[]{:S(2)}) collective-permute-start(bf16[256,512]{1,0:T(8,128)(2,1)S(1)} %collective-permute-done.1.b2), channel_id=1, source_target_pairs={{0,14},{1,15},{2,0},{3,1},{4,2},{5,3},{6,4},{7,5},{8,6},{9,7},{10,... | collective-permute-start | bytes 786440 | tf_op jit(solution)/shard_map/ppermute | solution.py:26
  144.8 10.0 %collective-permute-start.6 = (bf16[128,512]{1,0:T(8,128)(2,1)S(1)}, bf16[128,512]{1,0:T(8,128)(2,1)S(1)}, u32[]{:S(2)}, u32[]{:S(2)}) collective-permute-start(bf16[128,512]{1,0:T(8,128)(2,1)S(1)} %slice.25), channel_id=1, source_target_pairs={{0,2},{1,3},{2,4},{3,5},{4,6},{5,7},{6,8},{7,9},{8,10},{9,11},{10,... | collective-permute-start | bytes 393224 | tf_op jit(solution)/shard_map/ppermute | solution.py:26
  145.0 10.6 %collective-permute-start.7 = (bf16[128,512]{1,0:T(8,128)(2,1)S(1)}, bf16[128,512]{1,0:T(8,128)(2,1)S(1)}, u32[]{:S(2)}, u32[]{:S(2)}) collective-permute-start(bf16[128,512]{1,0:T(8,128)(2,1)S(1)} %slice.26), channel_id=1, source_target_pairs={{0,14},{1,15},{2,0},{3,1},{4,2},{5,3},{6,4},{7,5},{8,6},{9,7},{10,... | collective-permute-start | bytes 393224 | tf_op jit(solution)/shard_map/ppermute | solution.py:26
  148.6 36.4 %all-to-all-start.6 = ((f32[8,32,512]{2,1,0:T(8,128)}), f32[8,32,512]{2,1,0:T(8,128)}, u32[]{:S(2)}, u32[]{:S(2)}) async-start(f32[8,32,512]{2,1,0:T(8,128)} %broadcast_in_dim.33), calls=%async_computation.6 | async-start | bytes 1048576 | tf_op jit(solution)/shard_map/all_to_all | solution.py:250
  184.9 11.5 %collective-permute-start.17 = (bf16[512,512]{1,0:T(8,128)(2,1)S(1)}, bf16[512,512]{1,0:T(8,128)(2,1)S(1)}, u32[]{:S(2)}, u32[]{:S(2)}) collective-permute-start(bf16[512,512]{1,0:T(8,128)(2,1)S(1)} %get-tuple-element.8), channel_id=1, source_target_pairs={{0,1},{1,0},{2,3},{3,2},{4,5},{5,4},{6,7},{7,6},{8,9},{9,8},{10,11... | collective-permute-start | bytes 1572872 | tf_op jit(solution)/shard_map/ppermute | solution.py:26
  185.0 12.5 %collective-permute-start.20 = (f32[8,32,512]{2,1,0:T(8,128)}, f32[8,32,512]{2,1,0:T(8,128)S(1)}, u32[]{:S(2)}, u32[]{:S(2)}) collective-permute-start(f32[8,32,512]{2,1,0:T(8,128)} %all-to-all-done.6), channel_id=1, source_target_pairs={{0,16},{1,17},{2,18},{3,19},{4,20},{5,21},{6,22},{7,23},{8,24},{9,... | collective-permute-start | bytes 1572872 | tf_op jit(solution)/shard_map/ppermute | solution.py:26
  (11 other events, 71.1 us)
where the time goes:
time: 203 us; the launch traced here: 200 us
  starting transfers between devices  83.7 us (41%)
  waiting for transfers between devices  51.3 us (25%)
  Pallas kernels  32.9 us (16%)
  local copies, waits for them, and re-layouts  16.3 us (8%)
  other arithmetic  9.37 us (5%)
  matrix products  5.34 us (3%)
    ppermute x21, starting transfers between devices, shift(): return lax.ppermute(x, AXES, pairs)  33.5 us
    ppermute x21, waiting for transfers between devices, shift(): return lax.ppermute(x, AXES, pairs)  28.8 us
    pallas_call x1, Pallas kernels, gram_call(): pl.pallas_call(gram_kernel, grid_spec=pltpu.PrefetchScalarGridSpec(num_sc...  26.9 us
    all_to_all x4, starting transfers between devices, swap_z(): lax.all_to_all(x, 'shard', 0, 0, tiled=True, axis_index_groups=Z_GROUPS)  24.2 us
    all_to_all x4, waiting for transfers between devices, swap_z(): lax.all_to_all(x, 'shard', 0, 0, tiled=True, axis_index_groups=Z_GROUPS)  19.8 us
    all_to_all x1, starting transfers between devices, local(): lax.all_to_all(sent.reshape(16, 12, 128), 'mp', 0, 0, tiled=True)  14.8 us
    unnamed x25, local copies, waits for them, and re-layouts  11 us
    all_to_all x1, starting transfers between devices, local(): lax.all_to_all(jnp.broadcast_to(numer[None], (8, 32, 512)), 'mp', 0, 0, t...  6.23 us
  transfers between devices with their start and end apart: 28, of which 9 were waited for; matrix products, arithmetic and copies ran while one was open for 10% of the time, Pallas kernels for 13%

commit v1 on v0

v1 whole, which is shorter than its diff:
```python
import jax
import jax.numpy as jnp
from jax import lax
from jax.experimental import pallas as pl
from jax.experimental.pallas import tpu as pltpu
from jax.sharding import PartitionSpec as P

ALPHA = 0.9
EPSILON = 1e-05
BF = jnp.bfloat16
F4 = jnp.float32
AXES = ("mp", "shard")
Z_GROUPS = [[z * 2 + xl for z in range(8)] for xl in range(2)]
CORE_GROUPS = [[q * 2 + c for q in range(8)] for c in range(2)]


def shift(x, y=0, xh=0, c=0, z=0, xl=0):
    pairs = []
    for p in range(16):
        for s in range(16):
            py, pxh, pc = p // 4, p // 2 % 2, p % 2
            sz, sxl = s // 2, s % 2
            tp = (py + y) % 4 * 4 + (pxh ^ xh) * 2 + (pc ^ c)
            ts = (sz + z) % 8 * 2 + (sxl ^ xl)
            pairs.append((p * 16 + s, tp * 16 + ts))
    return lax.ppermute(x, AXES, pairs)


def swap_z(x):
    return lax.all_to_all(x, "shard", 0, 0, tiled=True, axis_index_groups=Z_GROUPS)


def dot(a, b):
    return jnp.dot(a, b, preferred_element_type=F4)


def contract_rows(a, b):
    return lax.dot_general(a, b, (((0,), (0,)), ((), ())), preferred_element_type=F4)


def gather_mp(x):
    half = x.shape[0] // 2
    h = shift(x, xh=1)
    u = shift(x, y=1)
    d = shift(x, y=-1)
    hu = shift(h, y=1)
    hd = shift(h, y=-1)
    t = jnp.concatenate([shift(u[:half], y=1), shift(d[half:], y=-1)], 0)
    ht = shift(t, xh=1)
    own = jnp.stack([x, h, d, hd, t, ht, u, hu], 0)
    return own, shift(own, c=1)


def gather_z(x):
    u, d = [x], [x]
    for _ in range(3):
        u.append(shift(u[-1], z=1))
        d.append(shift(d[-1], z=-1))
    far = [shift(u[3][:128], z=1), shift(d[3][128:], z=-1)]
    return [x, d[1], d[2], d[3]] + far + [u[3], u[2], u[1]]


def prepare_kernel(info, bank, ids, gains, calib_out, piece_out, cols_out, rows, total):
    zz = pl.program_id(0)
    p, s, xl = info[0], info[1], info[2]
    i0 = lax.broadcasted_iota(jnp.int32, (64, 64), 0)
    i1 = lax.broadcasted_iota(jnp.int32, (64, 64), 1)
    row_ids = (ids[...] - s * 256).astype(F4)
    row_ids = jnp.sum(jnp.where(i0 == i1, row_ids, 0.0), axis=1, keepdims=True)
    pick = jnp.where(row_ids == lax.broadcasted_iota(jnp.int32, (64, 256), 1).astype(F4), 1.0, 0.0).astype(BF)

    @pl.when(zz == 0)
    def _():
        total[...] = jnp.zeros_like(total)

    got = dot(pick, bank[...])
    total[...] += jnp.sum(got * got, axis=1, keepdims=True)
    own_row = pl.multiple_of(p * 16, 16)
    for j in range(2):
        at = pl.multiple_of((xl ^ j) * 512, 512)
        piece_out[zz, :, j * 512 : j * 512 + 512] = bank[pl.ds(own_row, 16), pl.ds(at, 512)]
        rows[zz, j] = got[:, j * 512 : j * 512 + 512]

    @pl.when(zz == p // 2)
    def _():
        cols_out[...] = bank[:, pl.ds(pl.multiple_of(p % 2 * 512, 512), 512)]

    @pl.when(zz == 7)
    def _():
        scale = lax.rsqrt(total[:, 0:1] / 8192 + EPSILON)
        hi = scale.astype(BF).astype(F4)
        mid = (scale - hi).astype(BF).astype(F4)
        low = scale - hi - mid
        lane = lax.broadcasted_iota(jnp.int32, (16, 128), 1)
        extra = jnp.zeros((16, 128), F4)
        for q in range(4):
            part = slice(q * 16, q * 16 + 16)
            for j, v in enumerate((row_ids, hi, mid, low)):
                extra = jnp.where(lane == q * 32 + j, v[part], extra)
        extra = extra.astype(BF)
        own = [gains[pl.ds(s // 2 * 2 + i, 1), :] for i in range(2)]
        own = jnp.concatenate([g[:, i * 128 : i * 128 + 128] for g in own for i in range(4)], 0)
        own_hi = own.astype(BF).astype(F4)
        own = jnp.concatenate([own_hi, own - own_hi], 0).astype(BF)
        for to in range(8):
            piece_out[to, :, 1024:1152] = extra
            piece_out[to, :, 1152:1280] = own
            for j in range(2):
                g = gains[pl.ds(to * 2 + (xl ^ j), 1), :]
                calib_out[to, :, j * 512 : j * 512 + 512] = (rows[to, xl ^ j] * scale * g).astype(BF)


def prepare(info, bank, ids, gains):
    whole = lambda shape: pl.BlockSpec(shape, lambda i, info: (0,) * len(shape))
    return pl.pallas_call(
        prepare_kernel,
        grid_spec=pltpu.PrefetchScalarGridSpec(
            num_scalar_prefetch=1,
            grid=(8,),
            in_specs=[pl.BlockSpec((256, 1024), lambda i, info: (0, i)), whole((1, 64)), whole((16, 512))],
            out_specs=[whole((8, 64, 1024)), whole((8, 16, 1280)), whole((256, 512))],
            scratch_shapes=[pltpu.VMEM((8, 2, 64, 512), F4), pltpu.VMEM((64, 128), F4)],
        ),
        out_shape=[
            jax.ShapeDtypeStruct((8, 64, 1024), BF),
            jax.ShapeDtypeStruct((8, 16, 1280), BF),
            jax.ShapeDtypeStruct((256, 512), BF),
        ],
        compiler_params=pltpu.CompilerParams(
            dimension_semantics=("arbitrary",), vmem_limit_bytes=24 * 2**20
        ),
        cost_estimate=pl.CostEstimate(flops=2**28, bytes_accessed=6 * 2**20, transcendentals=64),
        name="prepare",
    )(info, bank, ids, gains)


ORDER = (0, 7, 1, 6, 2, 5, 3, 4)


def slot_model(info, core, slot):
    y, xh, c = info[3], info[4], info[5]
    return lax.rem(y + slot // 2, 4) * 4 + (xh ^ (slot % 2)) * 2 + (c ^ core)


def gram_kernel(first, last, info, *refs):
    refs = list(refs)
    blocks = [refs.pop(0) for _ in range(3 if last else 2)]
    own_s, other_s = refs.pop(0), refs.pop(0)
    if first:
        own_g, other_g = refs.pop(0), refs.pop(0)
    else:
        gains, before = refs.pop(0), refs.pop(0)
    if last:
        near, far = refs.pop(0), refs.pop(0)
    else:
        acc = refs.pop(0)
    if first:
        gains = refs.pop(0)
    if last:
        acc = refs.pop(0)
    table, pick, scale, calib = refs
    step = pl.program_id(0)
    p, xl, z = info[0], info[2], info[6]

    @pl.when(step == 0)
    def _():
        if not first:
            acc[...] = before[...]
        else:
            acc[...] = jnp.zeros_like(acc)
            for core in range(2):
                src = own_g if core == 0 else other_g
                for slot in range(8):
                    m = slot_model(info, core, slot)
                    row = []
                    for b in (p, z * 2 + xl, z * 2 + (1 - xl)):
                        tile = src[slot, b // 2].astype(F4)
                        tile = tile[0:8] + tile[8:16]
                        tile = jnp.where(b % 2 == 0, tile[0:4], tile[4:8])
                        row += [tile[i : i + 1] for i in range(4)]
                    gains[pl.ds(m, 1), :] = jnp.concatenate(row, 1)
        table[:, 0:512] = blocks[0][...]

    @pl.when(step == 1)
    def _():
        if last:
            table[0:128, 0:512] = blocks[1][...]
            table[128:256, 0:512] = blocks[2][...]
        else:
            table[:, 0:512] = blocks[1][...]

    lane = lax.broadcasted_iota(jnp.int32, (16, 256), 1).astype(F4)
    models = []
    for core in range(2):
        src = own_s if core == 0 else other_s
        for slot in range(8):
            m = slot_model(info, core, slot)
            models.append(m)
            table[pl.ds(pl.multiple_of(m * 16, 16), 16), 512:1536] = src[slot, 0, :, 0:1024]
            extra = src[slot, 0, :, 1024:1152].astype(F4)
            for t in range(4):
                row = (core * 8 + slot) * 64 + t * 16
                at = t * 32
                hit = extra[:, at : at + 1] == lane
                pick[row : row + 16, :] = jnp.where(hit, 1.0, 0.0).astype(BF)
                value = extra[:, at + 1 : at + 2] + extra[:, at + 2 : at + 3] + extra[:, at + 3 : at + 4]
                scale[row : row + 16, :] = jnp.broadcast_to(value, (16, 128))

    for n in range(6):
        cols = slice(n * 256, n * 256 + 256)
        got = dot(pick[...], table[:, cols])
        for m in range(16):
            part = slice(m * 64, m * 64 + 64)
            r = scale[part, :]
            r = jnp.concatenate([r, r], 1)
            g = gains[pl.ds(models[m], 1), cols]
            calib[part, cols] = (got[part] * r * g).astype(BF)
    acc[...] += contract_rows(calib[:, 0:512], calib[:, 512:1536])

    if last:

        @pl.when(step == 1)
        def _():
            near[...] = acc[:, 0:512]
            far[...] = acc[:, 512:1024].astype(BF)


def gram_call(i, info, blocks, own_s, other_s, gains, before):
    first, last = i == 0, i == 3
    k0, k1 = ORDER[2 * i], ORDER[2 * i + 1]
    whole = lambda shape: pl.BlockSpec(shape, lambda j, info: (0,) * len(shape))
    by_z = pl.BlockSpec((8, 1, 16, 1280), lambda j, info: (0, (info[6] + k0 + j * (k1 - k0) + 8) % 8, 0, 0))
    gain_view = pl.BlockSpec((8, 8, 16, 128), lambda j, info: (0, 0, 0, 9))
    shapes = [jax.ShapeDtypeStruct((512, 1024), F4)]
    if last:
        shapes = [jax.ShapeDtypeStruct((512, 512), F4), jax.ShapeDtypeStruct((512, 512), BF)]
    if first:
        shapes.append(jax.ShapeDtypeStruct((16, 1536), F4))
    extra = [own_s, other_s] if first else [gains, before]
    extra_specs = [gain_view, gain_view] if first else [whole((16, 1536)), whole((512, 1024))]
    operands = [info, *blocks, own_s, other_s, *extra]
    return pl.pallas_call(
        lambda *refs: gram_kernel(first, last, *refs),
        grid_spec=pltpu.PrefetchScalarGridSpec(
            num_scalar_prefetch=1,
            grid=(2,),
            in_specs=[whole(b.shape) for b in blocks] + [by_z, by_z] + extra_specs,
            out_specs=[whole(o.shape) for o in shapes],
            scratch_shapes=([pltpu.VMEM((512, 1024), F4)] if last else [])
            + [
                pltpu.VMEM((256, 1536), BF),
                pltpu.VMEM((1024, 256), BF),
                pltpu.VMEM((1024, 128), F4),
                pltpu.VMEM((1024, 1536), BF),
            ],
        ),
        out_shape=shapes,
        input_output_aliases={} if first or last else {len(operands) - 1: 0},
        compiler_params=pltpu.CompilerParams(
            dimension_semantics=("arbitrary",), vmem_limit_bytes=44 * 2**20
        ),
        cost_estimate=pl.CostEstimate(flops=4 * 2**30, bytes_accessed=6 * 2**20, transcendentals=0),
        name="gram" + str(i),
    )(*operands)


def local(bank, calib_ids, norm_gains, proj_slabs):
    p = lax.axis_index("mp")
    s = lax.axis_index("shard")
    y, xh, c = p // 4, p // 2 % 2, p % 2
    z, xl = s // 2, s % 2
    info = jnp.stack([p, s, xl, y, xh, c, z]).astype(jnp.int32)
    weights = proj_slabs[0]

    calib_own, piece, bank_cols = prepare(info, bank, calib_ids, norm_gains.reshape(16, 512))
    piece = swap_z(piece)
    cols = swap_z(calib_own).reshape(512, 1024)

    b = gather_z(bank_cols)
    own_s, other_s = gather_mp(piece)
    both = jnp.concatenate([weights, shift(weights, xl=1)], 0)
    cols, b[1], b[8] = lax.optimization_barrier((cols, b[1], b[8]))
    partial_out = swap_z(dot(cols, both).astype(BF).reshape(8, 64, 512))
    partial_out, b[2], b[7] = lax.optimization_barrier((partial_out, b[2], b[7]))
    model_out = jnp.sum(partial_out.astype(F4), 0).astype(BF)
    model_out = swap_z(jnp.broadcast_to(model_out[None], (8, 64, 512))).reshape(512, 512)

    cols_f = cols.astype(F4)
    diag = jnp.sum(cols_f * cols_f, 0)
    numer = contract_rows(cols, model_out) * (ALPHA / 1024)
    numer = numer + ((1.0 - ALPHA) / 1024 * diag)[:, None] * both.astype(F4)
    numer = numer[:512] + shift(numer[512:].astype(BF), xl=1).astype(F4)
    numer = lax.all_to_all(numer.astype(BF).reshape(16, 32, 512), "mp", 0, 0, tiled=True)
    numer = jnp.sum(numer.astype(F4), 0)
    mine = lax.all_to_all(
        jnp.broadcast_to(numer[None], (8, 32, 512)), "mp", 0, 0, tiled=True, axis_index_groups=CORE_GROUPS
    )
    theirs = shift(mine, c=1)
    numer = jnp.where(c == 0, jnp.stack([mine, theirs], 1), jnp.stack([theirs, mine], 1)).reshape(512, 512)
    acc, gains = gram_call(0, info, [b[0], b[8]], own_s, other_s, None, None)
    (acc,) = gram_call(1, info, [b[1], b[7]], own_s, other_s, gains, acc)
    (acc,) = gram_call(2, info, [b[2], b[6]], own_s, other_s, gains, acc)
    near, far = gram_call(3, info, [b[3], b[4], b[5]], own_s, other_s, gains, acc)
    gram = near + shift(far, xl=1).astype(F4)
    on_diag = (p == s) & (
        lax.broadcasted_iota(jnp.int32, (512, 512), 0) == lax.broadcasted_iota(jnp.int32, (512, 512), 1)
    )
    merged_gram = gram * jnp.where(on_diag, 1.0 / 1024, ALPHA / 1024)

    return (merged_gram, numer)


def solution(mesh):
    placed = (P("shard", None), P("mp", "shard"), P("mp", None), P("mp", "shard", None))
    return jax.shard_map(
        local,
        mesh=mesh,
        in_specs=placed,
        out_specs=(P("mp", "shard"), P("shard", None)),
        check_vma=False,
    )
```

time: 203 us -> 203 us (level)
  waiting for transfers between devices: 51.3 us -> 71.2 us
  starting transfers between devices: 83.7 us -> 70 us
  other arithmetic: 9.37 us -> 6.13 us
    ppermute x21, waiting for transfers between devices: 28.8 us -> 44.9 us  [shift(): return lax.ppermute(x, AXES, pairs)]
    all_to_all x1 -> x0, starting transfers between devices: 14.8 us -> none  [local(): lax.all_to_all(sent.reshape(16, 12, 128), 'mp', 0, 0, tiled=True)]
    all_to_all x4, waiting for transfers between devices: 19.8 us -> 24.5 us  [swap_z(): lax.all_to_all(x, 'shard', 0, 0, tiled=True, axis_index_groups=Z_GROUPS)]
    unnamed x25 -> x23, local copies, waits for them, and re-layouts: 11 us -> 14.4 us
    all_to_all x1 -> x0, waiting for transfers between devices: 2.82 us -> none  [local(): lax.all_to_all(sent.reshape(16, 12, 128), 'mp', 0, 0, tiled=True)]
    pallas_call x2 -> x5, Pallas kernels: 32.9 us -> 32 us  [the longest x4 26.6 us: gram_call(): pl.pallas_call(lambda *refs: gram_kernel(first, last, *refs), grid_spec=p...]
  transfers between devices with their start and end apart: 28 -> 27, of which waited for: 9 -> 11; matrix products, arithmetic and copies ran while one was open for 10% -> 8% of each run, Pallas kernels for 13% -> 13%
where the time goes in v1:
time: 203 us; the launch traced here: 202 us
  waiting for transfers between devices  71.2 us (35%)
  starting transfers between devices  70 us (34%)
  Pallas kernels  32 us (16%)
  local copies, waits for them, and re-layouts  17.1 us (8%)
  other arithmetic  6.13 us (3%)
  matrix products  4.49 us (2%)
    ppermute x21, waiting for transfers between devices, shift(): return lax.ppermute(x, AXES, pairs)  44.9 us
    ppermute x21, starting transfers between devices, shift(): return lax.ppermute(x, AXES, pairs)  33.2 us
    pallas_call x4, Pallas kernels, gram_call(): pl.pallas_call(lambda *refs: gram_kernel(first, last, *refs), grid_spec=p...  26.6 us
    all_to_all x4, starting transfers between devices, swap_z(): lax.all_to_all(x, 'shard', 0, 0, tiled=True, axis_index_groups=Z_GROUPS)  24.7 us
    all_to_all x4, waiting for transfers between devices, swap_z(): lax.all_to_all(x, 'shard', 0, 0, tiled=True, axis_index_groups=Z_GROUPS)  24.5 us
    unnamed x23, local copies, waits for them, and re-layouts  14.4 us
    all_to_all x1, starting transfers between devices, local(): lax.all_to_all(jnp.broadcast_to(numer[None], (8, 32, 512)), 'mp', 0, 0, t...  6.59 us
    all_to_all x1, starting transfers between devices, local(): lax.all_to_all(numer.astype(BF).reshape(16, 32, 512), 'mp', 0, 0, tiled=T...  5.5 us
  transfers between devices with their start and end apart: 27, of which 11 were waited for; matrix products, arithmetic and copies ran while one was open for 8% of the time, Pallas kernels for 13%

profile of v1, /device:TPU:1, one launch (start us, length us, event | category | flops | bytes accessed | tf_op | source)
XLA Modules:
  0.0 201.8 jit_solution(5830927056615091560)
XLA Ops:
  5.7 5.4 %prepare.1 = (bf16[8,64,1024]{2,1,0:T(8,128)(2,1)}, bf16[8,16,1280]{2,1,0:T(8,128)(2,1)}, bf16[256,512]{1,0:T(8,128)(2,1)S(1)}) custom-call(s32[7]{0:T(128)S(1)} %stack.72.info.refs_0_, bf16[256,8192]{1,0:T(8,128)(2,1)S(1)} %copy-done, s32[1,64]{1,0:T(1,128)S(1)} %copy-done.1, f32[16,512]{1,0:T(8,128)S(1)} %reshape.29.gains), custom_call_target="tpu_custom_call" | custom-call | flops 268435456 | bytes 6291456 | tf_op jit(solution)/shard_map/prepare/pallas_call | solution.py:115
  11.1 9.1 %all-to-all-start = ((bf16[8,16,1280]{2,1,0:T(8,128)(2,1)}), bf16[8,16,1280]{2,1,0:T(8,128)(2,1)S(1)}, u32[]{:S(2)}, u32[]{:S(2)}) async-start(bf16[8,16,1280]{2,1,0:T(8,128)(2,1)} %get-tuple-element.16), calls=%async_computation | async-start | bytes 655360 | tf_op jit(solution)/shard_map/all_to_all | solution.py:30
  20.2 2.7 %collective-permute-start = (bf16[256,512]{1,0:T(8,128)(2,1)S(1)}, bf16[256,512]{1,0:T(8,128)(2,1)S(1)}, u32[]{:S(2)}, u32[]{:S(2)}) collective-permute-start(bf16[256,512]{1,0:T(8,128)(2,1)S(1)} %get-tuple-element.15.refs_1_), channel_id=1, source_target_pairs={{0,14},{1,15},{2,0},{3,1},{4,2},{5,3},{6,4},{7,5},{8,6},{9,7},{10,... | collective-permute-start | bytes 786440 | tf_op jit(solution)/shard_map/ppermute | solution.py:26
  22.9 9.8 %all-to-all-done = bf16[8,16,1280]{2,1,0:T(8,128)(2,1)S(1)} async-done(((bf16[8,16,1280]{2,1,0:T(8,128)(2,1)}), bf16[8,16,1280]{2,1,0:T(8,128)(2,1)S(1)}, u32[]{:S(2)}, u32[]{:S(2)}) %all-to-all-start) | async-done | bytes 327712 | tf_op jit(solution)/shard_map/all_to_all | solution.py:30
  32.7 3.6 %all-to-all-start.1 = ((bf16[8,64,1024]{2,1,0:T(8,128)(2,1)}), bf16[8,64,1024]{2,1,0:T(8,128)(2,1)S(1)}, u32[]{:S(2)}, u32[]{:S(2)}) async-start(bf16[8,64,1024]{2,1,0:T(8,128)(2,1)} %get-tuple-element.17), calls=%async_computation.1 | async-start | bytes 2097152 | tf_op jit(solution)/shard_map/all_to_all | solution.py:30
  36.3 2.8 %collective-permute-start.8 = (bf16[8,16,1280]{2,1,0:T(8,128)(2,1)S(1)}, bf16[8,16,1280]{2,1,0:T(8,128)(2,1)S(1)}, u32[]{:S(2)}, u32[]{:S(2)}) collective-permute-start(bf16[8,16,1280]{2,1,0:T(8,128)(2,1)S(1)} %all-to-all-done), channel_id=1, source_target_pairs={{0,32},{1,33},{2,34},{3,35},{4,36},{5,37},{6,38},{7,39},{8,40},{9,... | collective-permute-start | bytes 983048 | tf_op jit(solution)/shard_map/ppermute | solution.py:26
  39.1 2.7 %collective-permute-start.9 = (bf16[8,16,1280]{2,1,0:T(8,128)(2,1)S(1)}, bf16[8,16,1280]{2,1,0:T(8,128)(2,1)S(1)}, u32[]{:S(2)}, u32[]{:S(2)}) collective-permute-start(bf16[8,16,1280]{2,1,0:T(8,128)(2,1)S(1)} %all-to-all-done), channel_id=1, source_target_pairs={{0,192},{1,193},{2,194},{3,195},{4,196},{5,197},{6,198},{7,199},{8... | collective-permute-start | bytes 983048 | tf_op jit(solution)/shard_map/ppermute | solution.py:26
  42.6 6.7 %collective-permute-done.11 = bf16[8,16,1280]{2,1,0:T(8,128)(2,1)S(1)} collective-permute-done((bf16[8,16,1280]{2,1,0:T(8,128)(2,1)S(1)}, bf16[8,16,1280]{2,1,0:T(8,128)(2,1)S(1)}, u32[]{:S(2)}, u32[]{:S(2)}) %collective-permute-start.11) | collective-permute-done | bytes 327712 | tf_op jit(solution)/shard_map/ppermute | solution.py:26
  49.8 2.7 %collective-permute-start.13 = (bf16[4,16,1280]{2,1,0:T(8,128)(2,1)S(1)}, bf16[4,16,1280]{2,1,0:T(8,128)(2,1)S(1)}, u32[]{:S(2)}, u32[]{:S(2)}) collective-permute-start(bf16[4,16,1280]{2,1,0:T(8,128)(2,1)S(1)} %slice.28), channel_id=1, source_target_pairs={{0,192},{1,193},{2,194},{3,195},{4,196},{5,197},{6,198},{7,199},{8... | collective-permute-start | bytes 491528 | tf_op jit(solution)/shard_map/ppermute | solution.py:26
  57.0 5.5 %collective-permute-done.10 = bf16[8,16,1280]{2,1,0:T(8,128)(2,1)S(1)} collective-permute-done((bf16[8,16,1280]{2,1,0:T(8,128)(2,1)S(1)}, bf16[8,16,1280]{2,1,0:T(8,128)(2,1)S(1)}, u32[]{:S(2)}, u32[]{:S(2)}) %collective-permute-start.10) | collective-permute-done | bytes 327712 | tf_op jit(solution)/shard_map/ppermute | solution.py:26
  65.6 4.3 %collective-permute-done.14 = bf16[8,16,1280]{2,1,0:T(8,128)(2,1)S(1)} collective-permute-done((bf16[8,16,1280]{2,1,0:T(8,128)(2,1)S(1)}, bf16[8,16,1280]{2,1,0:T(8,128)(2,1)S(1)}, u32[]{:S(2)}, u32[]{:S(2)}) %collective-permute-start.14) | collective-permute-done | bytes 327712 | tf_op jit(solution)/shard_map/ppermute | solution.py:26
  72.2 6.6 %collective-permute-start.16 = (bf16[8,8,16,1280]{3,2,1,0:T(8,128)(2,1)}, bf16[8,8,16,1280]{3,2,1,0:T(8,128)(2,1)}, u32[]{:S(2)}, u32[]{:S(2)}) collective-permute-start(bf16[8,8,16,1280]{3,2,1,0:T(8,128)(2,1)} %bitcast_dynamic-update-slice_fusion.refs_3_.refs_5_.refs_4_), channel_id=1, source_target_pairs={{0,16},{1,17},{2,18},{3,19},{4,20},{5,21},{6,22},{7,23},{8,24},{9,... | collective-permute-start | bytes 7864328 | tf_op jit(solution)/shard_map/ppermute | solution.py:26
  81.4 7.0 %all-to-all-start.2 = ((bf16[8,64,512]{2,1,0:T(8,128)(2,1)}), bf16[8,64,512]{2,1,0:T(8,128)(2,1)S(1)}, u32[]{:S(2)}, u32[]{:S(2)}) async-start(bf16[8,64,512]{2,1,0:T(8,128)(2,1)} %bitcast.17), calls=%async_computation.2 | async-start | bytes 1048576 | tf_op jit(solution)/shard_map/all_to_all | solution.py:30
  91.1 16.4 %collective-permute-done.1.refs_1_ = bf16[256,512]{1,0:T(8,128)(2,1)S(1)} collective-permute-done((bf16[256,512]{1,0:T(8,128)(2,1)S(1)}, bf16[256,512]{1,0:T(8,128)(2,1)S(1)}, u32[]{:S(2)}, u32[]{:S(2)}) %collective-permute-start.1) | collective-permute-done | bytes 262176 | tf_op jit(solution)/shard_map/ppermute | solution.py:26
  109.6 4.9 %all-to-all-start.3 = ((bf16[8,64,512]{2,1,0:T(8,128)(2,1)}), bf16[8,64,512]{2,1,0:T(8,128)(2,1)S(1)}, u32[]{:S(2)}, u32[]{:S(2)}) async-start(bf16[8,64,512]{2,1,0:T(8,128)(2,1)} %broadcast_in_dim.23), calls=%async_computation.3 | async-start | bytes 1048576 | tf_op jit(solution)/shard_map/all_to_all | solution.py:30
  117.6 14.7 %all-to-all-done.3 = bf16[8,64,512]{2,1,0:T(8,128)(2,1)S(1)} async-done(((bf16[8,64,512]{2,1,0:T(8,128)(2,1)}), bf16[8,64,512]{2,1,0:T(8,128)(2,1)S(1)}, u32[]{:S(2)}, u32[]{:S(2)}) %all-to-all-start.3) | async-done | bytes 524320 | tf_op jit(solution)/shard_map/all_to_all | solution.py:30
  135.7 2.7 %collective-permute-start.7 = (bf16[128,512]{1,0:T(8,128)(2,1)S(1)}, bf16[128,512]{1,0:T(8,128)(2,1)S(1)}, u32[]{:S(2)}, u32[]{:S(2)}) collective-permute-start(bf16[128,512]{1,0:T(8,128)(2,1)S(1)} %slice.26), channel_id=1, source_target_pairs={{0,14},{1,15},{2,0},{3,1},{4,2},{5,3},{6,4},{7,5},{8,6},{9,7},{10,... | collective-permute-start | bytes 393224 | tf_op jit(solution)/shard_map/ppermute | solution.py:26
  138.4 6.8 %gram0.1 = (f32[512,1024]{1,0:T(8,128)S(1)}, f32[16,1536]{1,0:T(8,128)S(1)}) custom-call(s32[7]{0:T(128)S(1)} %stack.72.info.refs_0_, bf16[256,512]{1,0:T(8,128)(2,1)S(1)} %get-tuple-element.15.refs_1_, bf16[256,512]{1,0:T(8,128)(2,1)S(1)} %collective-permute-done.3.refs_2_, ...), custom_call_target="tpu_custom_call" | custom-call | flops 4294967296 | bytes 6291456 | tf_op jit(solution)/shard_map/gram0/pallas_call | solution.py:242
  148.0 5.5 %all-to-all-start.4 = ((bf16[16,32,512]{2,1,0:T(8,128)(2,1)}), bf16[16,32,512]{2,1,0:T(8,128)(2,1)S(1)}, u32[]{:S(2)}, u32[]{:S(2)}) async-start(bf16[16,32,512]{2,1,0:T(8,128)(2,1)} %bitcast.19), calls=%async_computation.4 | async-start | bytes 1048576 | tf_op jit(solution)/shard_map/all_to_all | solution.py:293
  155.1 6.6 %gram1.1.refs_6_ = f32[512,1024]{1,0:T(8,128)S(1)} custom-call(s32[7]{0:T(128)S(1)} %stack.72.info.refs_0_, bf16[256,512]{1,0:T(8,128)(2,1)S(1)} %collective-permute-done.refs_1_, bf16[256,512]{1,0:T(8,128)(2,1)S(1)} %collective-permute-done.4.refs_2_, ...), custom_call_target="tpu_custom_call", output_to_operand_aliasing={{}: (6, {})} | custom-call | flops 4294967296 | bytes 6291456 | tf_op jit(solution)/shard_map/gram1/pallas_call | solution.py:242
  161.8 6.6 %gram2.1.refs_7_ = f32[512,1024]{1,0:T(8,128)S(1)} custom-call(s32[7]{0:T(128)S(1)} %stack.72.info.refs_0_, bf16[256,512]{1,0:T(8,128)(2,1)S(1)} %collective-permute-done.1.refs_1_, bf16[256,512]{1,0:T(8,128)(2,1)S(1)} %collective-permute-done.5.refs_2_, ...), custom_call_target="tpu_custom_call", output_to_operand_aliasing={{}: (6, {})} | custom-call | flops 4294967296 | bytes 6291456 | tf_op jit(solution)/shard_map/gram2/pallas_call | solution.py:242
  170.7 6.6 %all-to-all-start.5 = ((f32[8,32,512]{2,1,0:T(8,128)}), f32[8,32,512]{2,1,0:T(8,128)S(1)}, u32[]{:S(2)}, u32[]{:S(2)}) async-start(f32[8,32,512]{2,1,0:T(8,128)} %broadcast_in_dim.24), calls=%async_computation.5 | async-start | bytes 1048576 | tf_op jit(solution)/shard_map/all_to_all | solution.py:295
  178.9 6.6 %gram3.1 = (f32[512,512]{1,0:T(8,128)S(1)}, bf16[512,512]{1,0:T(8,128)(2,1)S(1)}) custom-call(s32[7]{0:T(128)S(1)} %stack.72.info.refs_0_, bf16[256,512]{1,0:T(8,128)(2,1)S(1)} %collective-permute-done.2.refs_1_, bf16[128,512]{1,0:T(8,128)(2,1)S(1)} %collective-permute-done.6.refs_2_, bf16[128,512]{1,0:T(8,128)(2,1)S(1)} %collective-permute-done.7.refs_3_, ...), custom_call_target="tpu_custom_call" | custom-call | flops 4294967296 | bytes 6291456 | tf_op jit(solution)/shard_map/gram3/pallas_call | solution.py:242
  189.8 8.7 %collective-permute-done.18 = bf16[512,512]{1,0:T(8,128)(2,1)} collective-permute-done((bf16[512,512]{1,0:T(8,128)(2,1)S(1)}, bf16[512,512]{1,0:T(8,128)(2,1)}, u32[]{:S(2)}, u32[]{:S(2)}) %collective-permute-start.18) | collective-permute-done | bytes 524320 | tf_op jit(solution)/shard_map/ppermute | solution.py:26
  (79 shorter events, 45.5 us)
Async XLA Ops:
  11.1 21.6 %all-to-all-start = ((bf16[8,16,1280]{2,1,0:T(8,128)(2,1)}), bf16[8,16,1280]{2,1,0:T(8,128)(2,1)S(1)}, u32[]{:S(2)}, u32[]{:S(2)}) async-start(bf16[8,16,1280]{2,1,0:T(8,128)(2,1)} %get-tuple-element.16), calls=%async_computation | async-start | bytes 655360 | tf_op jit(solution)/shard_map/all_to_all | solution.py:30
  20.2 58.6 %collective-permute-start = (bf16[256,512]{1,0:T(8,128)(2,1)S(1)}, bf16[256,512]{1,0:T(8,128)(2,1)S(1)}, u32[]{:S(2)}, u32[]{:S(2)}) collective-permute-start(bf16[256,512]{1,0:T(8,128)(2,1)S(1)} %get-tuple-element.15.refs_1_), channel_id=1, source_target_pairs={{0,14},{1,15},{2,0},{3,1},{4,2},{5,3},{6,4},{7,5},{8,6},{9,7},{10,... | collective-permute-start | bytes 786440 | tf_op jit(solution)/shard_map/ppermute | solution.py:26
  22.9 55.9 %collective-permute-start.3 = (bf16[256,512]{1,0:T(8,128)(2,1)S(1)}, bf16[256,512]{1,0:T(8,128)(2,1)S(1)}, u32[]{:S(2)}, u32[]{:S(2)}) collective-permute-start(bf16[256,512]{1,0:T(8,128)(2,1)S(1)} %get-tuple-element.15.refs_1_), channel_id=1, source_target_pairs={{0,2},{1,3},{2,4},{3,5},{4,6},{5,7},{6,8},{7,9},{8,10},{9,11},{10,... | collective-permute-start | bytes 786440 | tf_op jit(solution)/shard_map/ppermute | solution.py:26
  32.7 46.1 %all-to-all-start.1 = ((bf16[8,64,1024]{2,1,0:T(8,128)(2,1)}), bf16[8,64,1024]{2,1,0:T(8,128)(2,1)S(1)}, u32[]{:S(2)}, u32[]{:S(2)}) async-start(bf16[8,64,1024]{2,1,0:T(8,128)(2,1)} %get-tuple-element.17), calls=%async_computation.1 | async-start | bytes 2097152 | tf_op jit(solution)/shard_map/all_to_all | solution.py:30
  36.3 13.5 %collective-permute-start.8 = (bf16[8,16,1280]{2,1,0:T(8,128)(2,1)S(1)}, bf16[8,16,1280]{2,1,0:T(8,128)(2,1)S(1)}, u32[]{:S(2)}, u32[]{:S(2)}) collective-permute-start(bf16[8,16,1280]{2,1,0:T(8,128)(2,1)S(1)} %all-to-all-done), channel_id=1, source_target_pairs={{0,32},{1,33},{2,34},{3,35},{4,36},{5,37},{6,38},{7,39},{8,40},{9,... | collective-permute-start | bytes 983048 | tf_op jit(solution)/shard_map/ppermute | solution.py:26
  39.1 10.6 %collective-permute-start.9 = (bf16[8,16,1280]{2,1,0:T(8,128)(2,1)S(1)}, bf16[8,16,1280]{2,1,0:T(8,128)(2,1)S(1)}, u32[]{:S(2)}, u32[]{:S(2)}) collective-permute-start(bf16[8,16,1280]{2,1,0:T(8,128)(2,1)S(1)} %all-to-all-done), channel_id=1, source_target_pairs={{0,192},{1,193},{2,194},{3,195},{4,196},{5,197},{6,198},{7,199},{8... | collective-permute-start | bytes 983048 | tf_op jit(solution)/shard_map/ppermute | solution.py:26
  41.8 7.5 %collective-permute-start.11 = (bf16[8,16,1280]{2,1,0:T(8,128)(2,1)S(1)}, bf16[8,16,1280]{2,1,0:T(8,128)(2,1)S(1)}, u32[]{:S(2)}, u32[]{:S(2)}) collective-permute-start(bf16[8,16,1280]{2,1,0:T(8,128)(2,1)S(1)} %all-to-all-done), channel_id=1, source_target_pairs={{0,64},{1,65},{2,66},{3,67},{4,68},{5,69},{6,70},{7,71},{8,72},{9,... | collective-permute-start | bytes 983048 | tf_op jit(solution)/shard_map/ppermute | solution.py:26
  49.3 29.5 %collective-permute-start.17 = (bf16[512,512]{1,0:T(8,128)(2,1)S(1)}, bf16[512,512]{1,0:T(8,128)(2,1)}, u32[]{:S(2)}, u32[]{:S(2)}) collective-permute-start(bf16[512,512]{1,0:T(8,128)(2,1)S(1)} %bitcast.42), channel_id=1, source_target_pairs={{0,1},{1,0},{2,3},{3,2},{4,5},{5,4},{6,7},{7,6},{8,9},{9,8},{10,11... | collective-permute-start | bytes 1572872 | tf_op jit(solution)/shard_map/ppermute | solution.py:26
  55.5 16.0 %collective-permute-start.15 = (bf16[8,16,1280]{2,1,0:T(8,128)(2,1)S(1)}, bf16[8,16,1280]{2,1,0:T(8,128)(2,1)S(1)}, u32[]{:S(2)}, u32[]{:S(2)}) collective-permute-start(bf16[8,16,1280]{2,1,0:T(8,128)(2,1)S(1)} %collective-permute-done.8), channel_id=1, source_target_pairs={{0,64},{1,65},{2,66},{3,67},{4,68},{5,69},{6,70},{7,71},{8,72},{9,... | collective-permute-start | bytes 983048 | tf_op jit(solution)/shard_map/ppermute | solution.py:26
  62.5 7.4 %collective-permute-start.14 = (bf16[8,16,1280]{2,1,0:T(8,128)(2,1)S(1)}, bf16[8,16,1280]{2,1,0:T(8,128)(2,1)S(1)}, u32[]{:S(2)}, u32[]{:S(2)}) collective-permute-start(bf16[8,16,1280]{2,1,0:T(8,128)(2,1)S(1)} %constant_dynamic-update-slice_fusion), channel_id=1, source_target_pairs={{0,32},{1,33},{2,34},{3,35},{4,36},{5,37},{6,38},{7,39},{8,40},{9,... | collective-permute-start | bytes 983048 | tf_op jit(solution)/shard_map/ppermute | solution.py:26
  72.2 66.2 %collective-permute-start.16 = (bf16[8,8,16,1280]{3,2,1,0:T(8,128)(2,1)}, bf16[8,8,16,1280]{3,2,1,0:T(8,128)(2,1)}, u32[]{:S(2)}, u32[]{:S(2)}) collective-permute-start(bf16[8,8,16,1280]{3,2,1,0:T(8,128)(2,1)} %bitcast_dynamic-update-slice_fusion.refs_3_.refs_5_.refs_4_), channel_id=1, source_target_pairs={{0,16},{1,17},{2,18},{3,19},{4,20},{5,21},{6,22},{7,23},{8,24},{9,... | collective-permute-start | bytes 7864328 | tf_op jit(solution)/shard_map/ppermute | solution.py:26
  81.4 27.3 %all-to-all-start.2 = ((bf16[8,64,512]{2,1,0:T(8,128)(2,1)}), bf16[8,64,512]{2,1,0:T(8,128)(2,1)S(1)}, u32[]{:S(2)}, u32[]{:S(2)}) async-start(bf16[8,64,512]{2,1,0:T(8,128)(2,1)} %bitcast.17), calls=%async_computation.2 | async-start | bytes 1048576 | tf_op jit(solution)/shard_map/all_to_all | solution.py:30
  88.5 19.1 %collective-permute-start.1 = (bf16[256,512]{1,0:T(8,128)(2,1)S(1)}, bf16[256,512]{1,0:T(8,128)(2,1)S(1)}, u32[]{:S(2)}, u32[]{:S(2)}) collective-permute-start(bf16[256,512]{1,0:T(8,128)(2,1)S(1)} %collective-permute-done.refs_1_), channel_id=1, source_target_pairs={{0,14},{1,15},{2,0},{3,1},{4,2},{5,3},{6,4},{7,5},{8,6},{9,7},{10,... | collective-permute-start | bytes 786440 | tf_op jit(solution)/shard_map/ppermute | solution.py:26
  91.1 17.6 %collective-permute-start.4 = (bf16[256,512]{1,0:T(8,128)(2,1)S(1)}, bf16[256,512]{1,0:T(8,128)(2,1)S(1)}, u32[]{:S(2)}, u32[]{:S(2)}) collective-permute-start(bf16[256,512]{1,0:T(8,128)(2,1)S(1)} %collective-permute-done.3.refs_2_), channel_id=1, source_target_pairs={{0,2},{1,3},{2,4},{3,5},{4,6},{5,7},{6,8},{7,9},{8,10},{9,11},{10,... | collective-permute-start | bytes 786440 | tf_op jit(solution)/shard_map/ppermute | solution.py:26
  109.6 22.6 %all-to-all-start.3 = ((bf16[8,64,512]{2,1,0:T(8,128)(2,1)}), bf16[8,64,512]{2,1,0:T(8,128)(2,1)S(1)}, u32[]{:S(2)}, u32[]{:S(2)}) async-start(bf16[8,64,512]{2,1,0:T(8,128)(2,1)} %broadcast_in_dim.23), calls=%async_computation.3 | async-start | bytes 1048576 | tf_op jit(solution)/shard_map/all_to_all | solution.py:30
  114.6 21.0 %collective-permute-start.5 = (bf16[256,512]{1,0:T(8,128)(2,1)S(1)}, bf16[256,512]{1,0:T(8,128)(2,1)S(1)}, u32[]{:S(2)}, u32[]{:S(2)}) collective-permute-start(bf16[256,512]{1,0:T(8,128)(2,1)S(1)} %collective-permute-done.4.refs_2_), channel_id=1, source_target_pairs={{0,2},{1,3},{2,4},{3,5},{4,6},{5,7},{6,8},{7,9},{8,10},{9,11},{10,... | collective-permute-start | bytes 786440 | tf_op jit(solution)/shard_map/ppermute | solution.py:26
  116.1 19.6 %collective-permute-start.2 = (bf16[256,512]{1,0:T(8,128)(2,1)S(1)}, bf16[256,512]{1,0:T(8,128)(2,1)S(1)}, u32[]{:S(2)}, u32[]{:S(2)}) collective-permute-start(bf16[256,512]{1,0:T(8,128)(2,1)S(1)} %collective-permute-done.1.refs_1_), channel_id=1, source_target_pairs={{0,14},{1,15},{2,0},{3,1},{4,2},{5,3},{6,4},{7,5},{8,6},{9,7},{10,... | collective-permute-start | bytes 786440 | tf_op jit(solution)/shard_map/ppermute | solution.py:26
  134.3 12.8 %collective-permute-start.19 = (bf16[512,512]{1,0:T(8,128)(2,1)S(1)}, bf16[512,512]{1,0:T(8,128)(2,1)S(1)}, u32[]{:S(2)}, u32[]{:S(2)}) collective-permute-start(bf16[512,512]{1,0:T(8,128)(2,1)S(1)} %slice.35), channel_id=1, source_target_pairs={{0,1},{1,0},{2,3},{3,2},{4,5},{5,4},{6,7},{7,6},{8,9},{9,8},{10,11... | collective-permute-start | bytes 1572872 | tf_op jit(solution)/shard_map/ppermute | solution.py:26
  135.6 41.7 %collective-permute-start.6 = (bf16[128,512]{1,0:T(8,128)(2,1)S(1)}, bf16[128,512]{1,0:T(8,128)(2,1)S(1)}, u32[]{:S(2)}, u32[]{:S(2)}) collective-permute-start(bf16[128,512]{1,0:T(8,128)(2,1)S(1)} %slice.25), channel_id=1, source_target_pairs={{0,2},{1,3},{2,4},{3,5},{4,6},{5,7},{6,8},{7,9},{8,10},{9,11},{10,... | collective-permute-start | bytes 393224 | tf_op jit(solution)/shard_map/ppermute | solution.py:26
  135.7 41.6 %collective-permute-start.7 = (bf16[128,512]{1,0:T(8,128)(2,1)S(1)}, bf16[128,512]{1,0:T(8,128)(2,1)S(1)}, u32[]{:S(2)}, u32[]{:S(2)}) collective-permute-start(bf16[128,512]{1,0:T(8,128)(2,1)S(1)} %slice.26), channel_id=1, source_target_pairs={{0,14},{1,15},{2,0},{3,1},{4,2},{5,3},{6,4},{7,5},{8,6},{9,7},{10,... | collective-permute-start | bytes 393224 | tf_op jit(solution)/shard_map/ppermute | solution.py:26
  148.0 21.7 %all-to-all-start.4 = ((bf16[16,32,512]{2,1,0:T(8,128)(2,1)}), bf16[16,32,512]{2,1,0:T(8,128)(2,1)S(1)}, u32[]{:S(2)}, u32[]{:S(2)}) async-start(bf16[16,32,512]{2,1,0:T(8,128)(2,1)} %bitcast.19), calls=%async_computation.4 | async-start | bytes 1048576 | tf_op jit(solution)/shard_map/all_to_all | solution.py:293
  170.7 17.3 %all-to-all-start.5 = ((f32[8,32,512]{2,1,0:T(8,128)}), f32[8,32,512]{2,1,0:T(8,128)S(1)}, u32[]{:S(2)}, u32[]{:S(2)}) async-start(f32[8,32,512]{2,1,0:T(8,128)} %broadcast_in_dim.24), calls=%async_computation.5 | async-start | bytes 1048576 | tf_op jit(solution)/shard_map/all_to_all | solution.py:295
  185.5 13.1 %collective-permute-start.18 = (bf16[512,512]{1,0:T(8,128)(2,1)S(1)}, bf16[512,512]{1,0:T(8,128)(2,1)}, u32[]{:S(2)}, u32[]{:S(2)}) collective-permute-start(bf16[512,512]{1,0:T(8,128)(2,1)S(1)} %get-tuple-element.26), channel_id=1, source_target_pairs={{0,1},{1,0},{2,3},{3,2},{4,5},{5,4},{6,7},{7,6},{8,9},{9,8},{10,11... | collective-permute-start | bytes 1572872 | tf_op jit(solution)/shard_map/ppermute | solution.py:26
  188.0 12.7 %collective-permute-start.20 = (f32[8,32,512]{2,1,0:T(8,128)S(1)}, f32[8,32,512]{2,1,0:T(8,128)S(1)}, u32[]{:S(2)}, u32[]{:S(2)}) collective-permute-start(f32[8,32,512]{2,1,0:T(8,128)S(1)} %all-to-all-done.5), channel_id=1, source_target_pairs={{0,16},{1,17},{2,18},{3,19},{4,20},{5,21},{6,22},{7,23},{8,24},{9,... | collective-permute-start | bytes 1572872 | tf_op jit(solution)/shard_map/ppermute | solution.py:26
  (10 other events, 65.4 us)

commit v2 on v1

--- a/solution.py
+++ b/solution.py
@@ -9,6 +9,7 @@
 EPSILON = 1e-05
 BF = jnp.bfloat16
 F4 = jnp.float32
+VMEM = 60 * 2**20
 AXES = ("mp", "shard")
 Z_GROUPS = [[z * 2 + xl for z in range(8)] for xl in range(2)]
 CORE_GROUPS = [[q * 2 + c for q in range(8)] for c in range(2)]
@@ -38,29 +39,31 @@
     return lax.dot_general(a, b, (((0,), (0,)), ((), ())), preferred_element_type=F4)
 
 
-def gather_mp(x):
-    half = x.shape[0] // 2
-    h = shift(x, xh=1)
-    u = shift(x, y=1)
-    d = shift(x, y=-1)
-    hu = shift(h, y=1)
-    hd = shift(h, y=-1)
-    t = jnp.concatenate([shift(u[:half], y=1), shift(d[half:], y=-1)], 0)
+def gather_both(piece, x, w):
+    tie = lax.optimization_barrier
+    z = [x]
+    zu, zd = shift(x, z=1), shift(x, z=-1)
+    piece, zu, zd, w = tie((swap_z(piece), zu, zd, shift(w, xl=1)))
+    z += [zu, zd]
+    h, u, d = shift(piece, xh=1), shift(piece, y=1), shift(piece, y=-1)
+    zu, zd = shift(zu, z=1), shift(zd, z=-1)
+    h, u, d, zu, zd = tie((h, u, d, zu, zd))
+    z += [zu, zd]
+    half = piece.shape[0] // 2
+    t0, t1 = shift(u[:half], y=1), shift(d[half:], y=-1)
+    hu, hd = shift(h, y=1), shift(h, y=-1)
+    zu, zd = shift(zu, z=1), shift(zd, z=-1)
+    hu, hd, t0, t1, zu, zd = tie((hu, hd, t0, t1, zu, zd))
+    z += [zu, zd]
+    t = jnp.concatenate([t0, t1], 0)
     ht = shift(t, xh=1)
-    own = jnp.stack([x, h, d, hd, t, ht, u, hu], 0)
-    return own, shift(own, c=1)
-
-
-def gather_z(x):
-    u, d = [x], [x]
-    for _ in range(3):
-        u.append(shift(u[-1], z=1))
-        d.append(shift(d[-1], z=-1))
-    far = [shift(u[3][:128], z=1), shift(d[3][128:], z=-1)]
-    return [x, d[1], d[2], d[3]] + far + [u[3], u[2], u[1]]
-
-
-def prepare_kernel(info, bank, ids, gains, calib_out, piece_out, cols_out, rows, total):
+    zu, zd = shift(zu[:128], z=1), shift(zd[128:], z=-1)
+    ht, zu, zd = tie((ht, zu, zd))
+    own = jnp.stack([piece, h, d, hd, t, ht, u, hu], 0)
+    return own, shift(own, c=1), w, [x, z[2], z[4], z[6], zu, zd, z[5], z[3], z[1]]
+
+
+def prepare_kernel(info, bank, ids, gains, piece_out, cols_out, total):
     zz = pl.program_id(0)
     p, s, xl = info[0], info[1], info[2]
     i0 = lax.broadcasted_iota(jnp.int32, (64, 64), 0)
@@ -79,7 +82,6 @@
     for j in range(2):
         at = pl.multiple_of((xl ^ j) * 512, 512)
         piece_out[zz, :, j * 512 : j * 512 + 512] = bank[pl.ds(own_row, 16), pl.ds(at, 512)]
-        rows[zz, j] = got[:, j * 512 : j * 512 + 512]
 
     @pl.when(zz == p // 2)
     def _():
@@ -98,16 +100,13 @@
             for j, v in enumerate((row_ids, hi, mid, low)):
                 extra = jnp.where(lane == q * 32 + j, v[part], extra)
         extra = extra.astype(BF)
-        own = [gains[pl.ds(s // 2 * 2 + i, 1), :] for i in range(2)]
-        own = jnp.concatenate([g[:, i * 128 : i * 128 + 128] for g in own for i in range(4)], 0)
+        own = gains[:, pl.ds(pl.multiple_of(s // 2 * 1024, 1024), 1024)]
+        own = jnp.concatenate([own[:, i * 128 : i * 128 + 128] for i in range(8)], 0)
         own_hi = own.astype(BF).astype(F4)
         own = jnp.concatenate([own_hi, own - own_hi], 0).astype(BF)
         for to in range(8):
             piece_out[to, :, 1024:1152] = extra
             piece_out[to, :, 1152:1280] = own
-            for j in range(2):
-                g = gains[pl.ds(to * 2 + (xl ^ j), 1), :]
-                calib_out[to, :, j * 512 : j * 512 + 512] = (rows[to, xl ^ j] * scale * g).astype(BF)
 
 
 def prepare(info, bank, ids, gains):
@@ -117,21 +116,97 @@
         grid_spec=pltpu.PrefetchScalarGridSpec(
             num_scalar_prefetch=1,
             grid=(8,),
-            in_specs=[pl.BlockSpec((256, 1024), lambda i, info: (0, i)), whole((1, 64)), whole((16, 512))],
-            out_specs=[whole((8, 64, 1024)), whole((8, 16, 1280)), whole((256, 512))],
-            scratch_shapes=[pltpu.VMEM((8, 2, 64, 512), F4), pltpu.VMEM((64, 128), F4)],
+            in_specs=[pl.BlockSpec((256, 1024), lambda i, info: (0, i)), whole((1, 64)), whole((1, 8192))],
+            out_specs=[whole((8, 16, 1280)), whole((256, 512))],
+            scratch_shapes=[pltpu.VMEM((64, 128), F4)],
+        ),
+        out_shape=[jax.ShapeDtypeStruct((8, 16, 1280), BF), jax.ShapeDtypeStruct((256, 512), BF)],
+        compiler_params=pltpu.CompilerParams(dimension_semantics=("arbitrary",), vmem_limit_bytes=VMEM),
+        cost_estimate=pl.CostEstimate(flops=2**28, bytes_accessed=5 * 2**20, transcendentals=64),
+        name="prepare",
+    )(info, bank, ids, gains)
+
+
+def project_kernel(info, own_s, other_s, gains, weights, part_out, calib_out, diag_out, table, calib):
+    zz = pl.program_id(0)
+    xl, z = info[2], info[6]
+    for core in range(2):
+        src = own_s if core == 0 else other_s
+        for slot in range(8):
+            m = slot_model(info, core, slot)
+            table[pl.ds(pl.multiple_of(m * 16, 16), 16), :] = src[slot, 0, :, 0:1024]
+    extra = own_s[0, 0, :, 1024:1152].astype(F4)
+    lane = lax.broadcasted_iota(jnp.int32, (16, 256), 1).astype(F4)
+    pick, scale = [], []
+    for t in range(4):
+        at = t * 32
+        pick.append(jnp.where(extra[:, at : at + 1] == lane, 1.0, 0.0))
+        scale.append(extra[:, at + 1 : at + 2] + extra[:, at + 2 : at + 3] + extra[:, at + 3 : at + 4])
+    pick = jnp.concatenate(pick, 0).astype(BF)
+    scale = jnp.concatenate(scale, 0)
+    rows = pl.ds(pl.multiple_of(zz * 64, 64), 64)
+    for j in range(2):
+        cols = slice(j * 512, j * 512 + 512)
+        g = gains[:, pl.ds(pl.multiple_of((z * 2 + (xl ^ j)) * 512, 512), 512)]
+        calib[rows, cols] = (dot(pick, table[:, cols]) * scale * g).astype(BF)
+
+    @pl.when(zz == 7)
+    def _():
+        calib_out[...] = calib[...]
+        part = dot(calib[...], weights[...]).astype(BF)
+        for to in range(8):
+            part_out[to] = part[to * 64 : to * 64 + 64]
+        whole = calib[...].astype(F4)
+        diag_out[...] = jnp.sum(whole * whole, axis=0, keepdims=True)
+
+
+def project(info, own_s, other_s, gains, weights):
+    whole = lambda shape: pl.BlockSpec(shape, lambda i, info: (0,) * len(shape))
+    by_z = pl.BlockSpec((8, 1, 16, 1280), lambda i, info: (0, i, 0, 0))
+    return pl.pallas_call(
+        project_kernel,
+        grid_spec=pltpu.PrefetchScalarGridSpec(
+            num_scalar_prefetch=1,
+            grid=(8,),
+            in_specs=[by_z, by_z, whole((1, 8192)), whole((1024, 512))],
+            out_specs=[whole((8, 64, 512)), whole((512, 1024)), whole((1, 1024))],
+            scratch_shapes=[pltpu.VMEM((256, 1024), BF), pltpu.VMEM((512, 1024), BF)],
         ),
         out_shape=[
-            jax.ShapeDtypeStruct((8, 64, 1024), BF),
-            jax.ShapeDtypeStruct((8, 16, 1280), BF),
-            jax.ShapeDtypeStruct((256, 512), BF),
+            jax.ShapeDtypeStruct((8, 64, 512), BF),
+            jax.ShapeDtypeStruct((512, 1024), BF),
+            jax.ShapeDtypeStruct((1, 1024), F4),
         ],
-        compiler_params=pltpu.CompilerParams(
-            dimension_semantics=("arbitrary",), vmem_limit_bytes=24 * 2**20
-        ),
-        cost_estimate=pl.CostEstimate(flops=2**28, bytes_accessed=6 * 2**20, transcendentals=64),
-        name="prepare",
-    )(info, bank, ids, gains)
+        compiler_params=pltpu.CompilerParams(dimension_semantics=("arbitrary",), vmem_limit_bytes=VMEM),
+        cost_estimate=pl.CostEstimate(flops=2**30, bytes_accessed=8 * 2**20, transcendentals=0),
+        name="project",
+    )(info, own_s, other_s, gains, weights)
+
+
+def numer_kernel(calib, model_out, diag, weights, near, far):
+    ratio = lax.broadcasted_iota(jnp.int32, (512, 512), 0) == lax.broadcasted_iota(jnp.int32, (512, 512), 1)
+    for j in range(2):
+        cols = slice(j * 512, j * 512 + 512)
+        d = diag[:, cols] * ((1.0 - ALPHA) / 1024)
+        d = jnp.sum(jnp.where(ratio, d, 0.0), axis=1, keepdims=True)
+        got = contract_rows(calib[:, cols], model_out[...]) * (ALPHA / 1024)
+        got = got + d * weights[cols, :].astype(F4)
+        if j == 0:
+            near[...] = got
+        else:
+            far[...] = got.astype(BF)
+
+
+def numer_call(calib, model_out, diag, weights):
+    return pl.pallas_call(
+        numer_kernel,
+        in_specs=[pl.BlockSpec(memory_space=pltpu.VMEM)] * 4,
+        out_specs=[pl.BlockSpec(memory_space=pltpu.VMEM)] * 2,
+        out_shape=[jax.ShapeDtypeStruct((512, 512), F4), jax.ShapeDtypeStruct((512, 512), BF)],
+        compiler_params=pltpu.CompilerParams(vmem_limit_bytes=VMEM),
+        cost_estimate=pl.CostEstimate(flops=2**29, bytes_accessed=4 * 2**20, transcendentals=0),
+        name="numer",
+    )(calib, model_out, diag, weights)
 
 
 ORDER = (0, 7, 1, 6, 2, 5, 3, 4)
@@ -256,9 +331,7 @@
         ),
         out_shape=shapes,
         input_output_aliases={} if first or last else {len(operands) - 1: 0},
-        compiler_params=pltpu.CompilerParams(
-            dimension_semantics=("arbitrary",), vmem_limit_bytes=44 * 2**20
-        ),
+        compiler_params=pltpu.CompilerParams(dimension_semantics=("arbitrary",), vmem_limit_bytes=VMEM),
         cost_estimate=pl.CostEstimate(flops=4 * 2**30, bytes_accessed=6 * 2**20, transcendentals=0),
         name="gram" + str(i),
     )(*operands)
@@ -272,35 +345,35 @@
     info = jnp.stack([p, s, xl, y, xh, c, z]).astype(jnp.int32)
     weights = proj_slabs[0]
 
-    calib_own, piece, bank_cols = prepare(info, bank, calib_ids, norm_gains.reshape(16, 512))
-    piece = swap_z(piece)
-    cols = swap_z(calib_own).reshape(512, 1024)
-
-    b = gather_z(bank_cols)
-    own_s, other_s = gather_mp(piece)
-    both = jnp.concatenate([weights, shift(weights, xl=1)], 0)
-    cols, b[1], b[8] = lax.optimization_barrier((cols, b[1], b[8]))
-    partial_out = swap_z(dot(cols, both).astype(BF).reshape(8, 64, 512))
-    partial_out, b[2], b[7] = lax.optimization_barrier((partial_out, b[2], b[7]))
+    piece, bank_cols = prepare(info, bank, calib_ids, norm_gains)
+    own_s, other_s, weights_other, b = gather_both(piece, bank_cols, weights)
+    both = jnp.concatenate([weights, weights_other], 0)
+
+    partial_out, calib, diag = project(info, own_s, other_s, norm_gains, both)
+    tie = lax.optimization_barrier
+    partial_out, info = tie((partial_out, info))
+    acc, gains = gram_call(0, info, [b[0], b[8]], own_s, other_s, None, None)
+    partial_out, gains = tie((swap_z(partial_out), gains))
     model_out = jnp.sum(partial_out.astype(F4), 0).astype(BF)
-    model_out = swap_z(jnp.broadcast_to(model_out[None], (8, 64, 512))).reshape(512, 512)
-
-    cols_f = cols.astype(F4)
-    diag = jnp.sum(cols_f * cols_f, 0)
-    numer = contract_rows(cols, model_out) * (ALPHA / 1024)
-    numer = numer + ((1.0 - ALPHA) / 1024 * diag)[:, None] * both.astype(F4)
-    numer = numer[:512] + shift(numer[512:].astype(BF), xl=1).astype(F4)
-    numer = lax.all_to_all(numer.astype(BF).reshape(16, 32, 512), "mp", 0, 0, tiled=True)
+    model_out, info = tie((jnp.broadcast_to(model_out[None], (8, 64, 512)), info))
+    (acc,) = gram_call(1, info, [b[1], b[7]], own_s, other_s, gains, acc)
+    model_out, acc = tie((swap_z(model_out), acc))
+
+    near, far = numer_call(calib, model_out.reshape(512, 512), diag, both)
+    far, info = tie((far, info))
+    (acc,) = gram_call(2, info, [b[2], b[6]], own_s, other_s, gains, acc)
+    far, acc = tie((shift(far, xl=1), acc))
+    numer = (near + far.astype(F4)).astype(BF).reshape(16, 32, 512)
+    numer, info = tie((numer, info))
+    near, far = gram_call(3, info, [b[3], b[4], b[5]], own_s, other_s, gains, acc)
+    numer, far = tie((lax.all_to_all(numer, "mp", 0, 0, tiled=True), far))
     numer = jnp.sum(numer.astype(F4), 0)
     mine = lax.all_to_all(
         jnp.broadcast_to(numer[None], (8, 32, 512)), "mp", 0, 0, tiled=True, axis_index_groups=CORE_GROUPS
     )
     theirs = shift(mine, c=1)
     numer = jnp.where(c == 0, jnp.stack([mine, theirs], 1), jnp.stack([theirs, mine], 1)).reshape(512, 512)
-    acc, gains = gram_call(0, info, [b[0], b[8]], own_s, other_s, None, None)
-    (acc,) = gram_call(1, info, [b[1], b[7]], own_s, other_s, gains, acc)
-    (acc,) = gram_call(2, info, [b[2], b[6]], own_s, other_s, gains, acc)
-    near, far = gram_call(3, info, [b[3], b[4], b[5]], own_s, other_s, gains, acc)
+
     gram = near + shift(far, xl=1).astype(F4)
     on_diag = (p == s) & (
         lax.broadcasted_iota(jnp.int32, (512, 512), 0) == lax.broadcasted_iota(jnp.int32, (512, 512), 1)

time: 203 us -> 205 us (level)
  Pallas kernels: 32 us -> 54.9 us
  local copies, waits for them, and re-layouts: 17.1 us -> 3.47 us
  starting transfers between devices: 70 us -> 60.5 us
  waiting for transfers between devices: 71.2 us -> 79.4 us
  matrix products: 4.49 us -> 0 us
    unnamed x23 -> x30, local copies, waits for them, and re-layouts: 14.4 us -> 1.01 us
    pallas_call x0 -> x2, Pallas kernels: none -> 12.4 us  [the longest x1 8.92 us: project(): pl.pallas_call(project_kernel, grid_spec=pltpu.PrefetchScalarGridSpec(num...]
    all_to_all x1, waiting for transfers between devices: 1.73 us -> 10.4 us  [local(): lax.all_to_all(jnp.broadcast_to(numer[None], (8, 32, 512)), 'mp', 0, 0, t...]
    pallas_call x4, Pallas kernels: 26.6 us -> 34.6 us  [gram_call(): pl.pallas_call(lambda *refs: gram_kernel(first, last, *refs), grid_spec=p...]
    all_to_all x4 -> x3, starting transfers between devices: 24.7 us -> 17.4 us  [swap_z(): lax.all_to_all(x, 'shard', 0, 0, tiled=True, axis_index_groups=Z_GROUPS)]
    all_to_all x4 -> x3, waiting for transfers between devices: 24.5 us -> 18.8 us  [swap_z(): lax.all_to_all(x, 'shard', 0, 0, tiled=True, axis_index_groups=Z_GROUPS)]
    dot_general x2 -> x0, matrix products: 4.49 us -> none  [the longest x1 2.55 us: dot(): return jnp.dot(a, b, preferred_element_type=F4)]
    all_to_all x1, waiting for transfers between devices: 0.01 us -> 2.64 us  [local(): numer, far = tie((lax.all_to_all(numer, 'mp', 0, 0, tiled=True), far))]
  transfers between devices with their start and end apart: 27 -> 26, of which waited for: 11 -> 15; matrix products, arithmetic and copies ran while one was open for 8% -> 1% of each run, Pallas kernels for 13% -> 17%
where the time goes in v2:
time: 205 us; the launch traced here: 204 us
  waiting for transfers between devices  79.4 us (39%)
  starting transfers between devices  60.5 us (30%)
  Pallas kernels  54.9 us (27%)
  other arithmetic  4.48 us (2%)
  local copies, waits for them, and re-layouts  3.47 us (2%)
    ppermute x21, waiting for transfers between devices, shift(): return lax.ppermute(x, AXES, pairs)  47.5 us
    pallas_call x4, Pallas kernels, gram_call(): pl.pallas_call(lambda *refs: gram_kernel(first, last, *refs), grid_spec=p...  34.6 us
    ppermute x21, starting transfers between devices, shift(): return lax.ppermute(x, AXES, pairs)  34.4 us
    all_to_all x3, waiting for transfers between devices, swap_z(): lax.all_to_all(x, 'shard', 0, 0, tiled=True, axis_index_groups=Z_GROUPS)  18.8 us
    all_to_all x3, starting transfers between devices, swap_z(): lax.all_to_all(x, 'shard', 0, 0, tiled=True, axis_index_groups=Z_GROUPS)  17.4 us
    all_to_all x1, waiting for transfers between devices, local(): lax.all_to_all(jnp.broadcast_to(numer[None], (8, 32, 512)), 'mp', 0, 0, t...  10.4 us
    pallas_call x1, Pallas kernels, project(): pl.pallas_call(project_kernel, grid_spec=pltpu.PrefetchScalarGridSpec(num...  8.92 us
    pallas_call x1, Pallas kernels, prepare(): pl.pallas_call(prepare_kernel, grid_spec=pltpu.PrefetchScalarGridSpec(num...  7.89 us
  transfers between devices with their start and end apart: 26, of which 15 were waited for; matrix products, arithmetic and copies ran while one was open for 1% of the time, Pallas kernels for 17%

profile of v2, /device:TPU:1, one launch (start us, length us, event | category | flops | bytes accessed | tf_op | source)
XLA Modules:
  0.0 203.7 jit_solution(10277914709624329942)
XLA Ops:
  1.4 7.9 %prepare.1 = (bf16[8,16,1280]{2,1,0:T(8,128)(2,1)}, bf16[256,512]{1,0:T(8,128)(2,1)}) custom-call(s32[7]{0:T(128)} %stack.72.info.refs_0_, bf16[256,8192]{1,0:T(8,128)(2,1)} %bank.1, s32[1,64]{1,0:T(1,128)} %ids.1, f32[1,8192]{1,0:T(1,128)} %gains.3), custom_call_target="tpu_custom_call" | custom-call | flops 268435456 | bytes 5242880 | tf_op jit(solution)/shard_map/prepare/pallas_call | solution.py:114
  9.2 9.0 %all-to-all-start = ((bf16[8,16,1280]{2,1,0:T(8,128)(2,1)}), bf16[8,16,1280]{2,1,0:T(8,128)(2,1)S(1)}, u32[]{:S(2)}, u32[]{:S(2)}) async-start(bf16[8,16,1280]{2,1,0:T(8,128)(2,1)} %get-tuple-element.47), calls=%async_computation | async-start | bytes 655360 | tf_op jit(solution)/shard_map/all_to_all | solution.py:31
  22.1 10.3 %collective-permute-done.1.refs_1_ = bf16[256,512]{1,0:T(8,128)(2,1)} collective-permute-done((bf16[256,512]{1,0:T(8,128)(2,1)}, bf16[256,512]{1,0:T(8,128)(2,1)}, u32[]{:S(2)}, u32[]{:S(2)}) %collective-permute-start.1) | collective-permute-done | bytes 262176 | tf_op jit(solution)/shard_map/ppermute | solution.py:27
  42.8 5.0 %collective-permute-done.6.refs_2_ = bf16[256,512]{1,0:T(8,128)(2,1)S(1)} collective-permute-done((bf16[256,512]{1,0:T(8,128)(2,1)}, bf16[256,512]{1,0:T(8,128)(2,1)S(1)}, u32[]{:S(2)}, u32[]{:S(2)}) %collective-permute-start.6) | collective-permute-done | bytes 262176 | tf_op jit(solution)/shard_map/ppermute | solution.py:27
  53.4 7.9 %collective-permute-done.10 = bf16[4,16,1280]{2,1,0:T(8,128)(2,1)S(1)} collective-permute-done((bf16[4,16,1280]{2,1,0:T(8,128)(2,1)S(1)}, bf16[4,16,1280]{2,1,0:T(8,128)(2,1)S(1)}, u32[]{:S(2)}, u32[]{:S(2)}) %collective-permute-start.10) | collective-permute-done | bytes 163872 | tf_op jit(solution)/shard_map/ppermute | solution.py:27
  63.4 3.3 %collective-permute-done.13.refs_1_ = bf16[256,512]{1,0:T(8,128)(2,1)S(1)} collective-permute-done((bf16[256,512]{1,0:T(8,128)(2,1)S(1)}, bf16[256,512]{1,0:T(8,128)(2,1)S(1)}, u32[]{:S(2)}, u32[]{:S(2)}) %collective-permute-start.13) | collective-permute-done | bytes 262176 | tf_op jit(solution)/shard_map/ppermute | solution.py:27
  66.7 3.2 %collective-permute-start.16 = (bf16[128,512]{1,0:T(8,128)(2,1)S(1)}, bf16[128,512]{1,0:T(8,128)(2,1)S(1)}, u32[]{:S(2)}, u32[]{:S(2)}) collective-permute-start(bf16[128,512]{1,0:T(8,128)(2,1)S(1)} %slice.15), channel_id=1, source_target_pairs={{0,14},{1,15},{2,0},{3,1},{4,2},{5,3},{6,4},{7,5},{8,6},{9,7},{10,... | collective-permute-start | bytes 393224 | tf_op jit(solution)/shard_map/ppermute | solution.py:27
  77.6 7.7 %collective-permute-start.17 = (bf16[8,8,16,1280]{3,2,1,0:T(8,128)(2,1)S(1)}, bf16[8,8,16,1280]{3,2,1,0:T(8,128)(2,1)}, u32[]{:S(2)}, u32[]{:S(2)}) collective-permute-start(bf16[8,8,16,1280]{3,2,1,0:T(8,128)(2,1)S(1)} %bitcast_dynamic-update-slice_fusion.own_s.refs_3_.refs_5_.refs_4_), channel_id=1, source_target_pairs={{0,16},{1,17},{2,18},{3,19},{4,20},{5,21},{6,22},{7,23},{8,24},{9,... | collective-permute-start | bytes 7864328 | tf_op jit(solution)/shard_map/ppermute | solution.py:27
  86.3 3.6 %collective-permute-done.17.other_s.refs_4_.refs_6_.refs_5_ = bf16[8,8,16,1280]{3,2,1,0:T(8,128)(2,1)} collective-permute-done((bf16[8,8,16,1280]{3,2,1,0:T(8,128)(2,1)S(1)}, bf16[8,8,16,1280]{3,2,1,0:T(8,128)(2,1)}, u32[]{:S(2)}, u32[]{:S(2)}) %collective-permute-start.17) | collective-permute-done | bytes 2621472 | tf_op jit(solution)/shard_map/ppermute | solution.py:27
  89.9 8.9 %project.1 = (bf16[8,64,512]{2,1,0:T(8,128)(2,1)}, bf16[512,1024]{1,0:T(8,128)(2,1)}, f32[1,1024]{1,0:T(1,128)}) custom-call(s32[7]{0:T(128)} %stack.72.info.refs_0_, bf16[8,8,16,1280]{3,2,1,0:T(8,128)(2,1)} %copy-done, bf16[8,8,16,1280]{3,2,1,0:T(8,128)(2,1)} %collective-permute-done.17.other_s.refs_4_.refs_6_.refs_5_, f32[1,8192]{1,0:T(1,128)} %gains.3, ...), custom_call_target="tpu_custom_call" | custom-call | flops 1073741824 | bytes 8388608 | tf_op jit(solution)/shard_map/project/pallas_call | solution.py:166
  98.9 4.9 %all-to-all-start.1 = ((bf16[8,64,512]{2,1,0:T(8,128)(2,1)}), bf16[8,64,512]{2,1,0:T(8,128)(2,1)S(1)}, u32[]{:S(2)}, u32[]{:S(2)}) async-start(bf16[8,64,512]{2,1,0:T(8,128)(2,1)} %get-tuple-element.67), calls=%async_computation.1 | async-start | bytes 1048576 | tf_op jit(solution)/shard_map/all_to_all | solution.py:31
  103.8 8.3 %gram0.1 = (f32[512,1024]{1,0:T(8,128)}, f32[16,1536]{1,0:T(8,128)}) custom-call(s32[7]{0:T(128)} %stack.72.info.refs_0_, bf16[256,512]{1,0:T(8,128)(2,1)} %get-tuple-element.48.refs_1_, bf16[256,512]{1,0:T(8,128)(2,1)} %collective-permute-done.refs_2_, bf16[8,8,16,1280]{3,2,1,0:T(8,128)(2,1)} %copy-done, ...), custom_call_target="tpu_custom_call" | custom-call | flops 4294967296 | bytes 6291456 | tf_op jit(solution)/shard_map/gram0/pallas_call | solution.py:317
  112.0 9.7 %all-to-all-done.1 = bf16[8,64,512]{2,1,0:T(8,128)(2,1)S(1)} async-done(((bf16[8,64,512]{2,1,0:T(8,128)(2,1)}), bf16[8,64,512]{2,1,0:T(8,128)(2,1)S(1)}, u32[]{:S(2)}, u32[]{:S(2)}) %all-to-all-start.1) | async-done | bytes 524320 | tf_op jit(solution)/shard_map/all_to_all | solution.py:31
  122.7 3.5 %all-to-all-start.2 = ((bf16[8,64,512]{2,1,0:T(8,128)(2,1)}), bf16[8,64,512]{2,1,0:T(8,128)(2,1)S(1)}, u32[]{:S(2)}, u32[]{:S(2)}) async-start(bf16[8,64,512]{2,1,0:T(8,128)(2,1)} %broadcast_in_dim.20), calls=%async_computation.2 | async-start | bytes 1048576 | tf_op jit(solution)/shard_map/all_to_all | solution.py:31
  126.2 8.8 %gram1.1.refs_6_ = f32[512,1024]{1,0:T(8,128)} custom-call(s32[7]{0:T(128)} %stack.72.info.refs_0_, bf16[256,512]{1,0:T(8,128)(2,1)} %collective-permute-done.1.refs_1_, bf16[256,512]{1,0:T(8,128)(2,1)} %copy-done.8, bf16[8,8,16,1280]{3,2,1,0:T(8,128)(2,1)} %copy-done, ...), custom_call_target="tpu_custom_call", output_to_operand_aliasing={{}: (6, {})} | custom-call | flops 4294967296 | bytes 6291456 | tf_op jit(solution)/shard_map/gram1/pallas_call | solution.py:317
  135.0 9.1 %all-to-all-done.2 = bf16[8,64,512]{2,1,0:T(8,128)(2,1)S(1)} async-done(((bf16[8,64,512]{2,1,0:T(8,128)(2,1)}), bf16[8,64,512]{2,1,0:T(8,128)(2,1)S(1)}, u32[]{:S(2)}, u32[]{:S(2)}) %all-to-all-start.2) | async-done | bytes 524320 | tf_op jit(solution)/shard_map/all_to_all | solution.py:31
  144.9 3.5 %numer.1 = (f32[512,512]{1,0:T(8,128)}, bf16[512,512]{1,0:T(8,128)(2,1)}) custom-call(bf16[512,1024]{1,0:T(8,128)(2,1)} %get-tuple-element.65.calib, bf16[512,512]{1,0:T(8,128)(2,1)} %bitcast.30, f32[1,1024]{1,0:T(1,128)} %get-tuple-element.76.diag, bf16[1024,512]{1,0:T(8,128)(2,1)} %pad_maximum_fusion.weights), custom_call_target="tpu_custom_call" | custom-call | flops 536870912 | bytes 4194304 | tf_op jit(solution)/shard_map/numer/pallas_call | solution.py:201
  148.7 8.8 %gram2.1.refs_7_ = f32[512,1024]{1,0:T(8,128)} custom-call(s32[7]{0:T(128)} %stack.72.info.refs_0_, bf16[256,512]{1,0:T(8,128)(2,1)} %copy-done.7, bf16[256,512]{1,0:T(8,128)(2,1)} %copy-done.6, bf16[8,8,16,1280]{3,2,1,0:T(8,128)(2,1)} %copy-done, ...), custom_call_target="tpu_custom_call", output_to_operand_aliasing={{}: (6, {})} | custom-call | flops 4294967296 | bytes 6291456 | tf_op jit(solution)/shard_map/gram2/pallas_call | solution.py:317
  157.5 4.1 %collective-permute-done.18 = bf16[512,512]{1,0:T(8,128)(2,1)S(1)} collective-permute-done((bf16[512,512]{1,0:T(8,128)(2,1)}, bf16[512,512]{1,0:T(8,128)(2,1)S(1)}, u32[]{:S(2)}, u32[]{:S(2)}) %collective-permute-start.18) | collective-permute-done | bytes 524320 | tf_op jit(solution)/shard_map/ppermute | solution.py:27
  162.6 4.7 %all-to-all-start.3 = ((bf16[16,32,512]{2,1,0:T(8,128)(2,1)}), bf16[16,32,512]{2,1,0:T(8,128)(2,1)S(1)}, u32[]{:S(2)}, u32[]{:S(2)}) async-start(bf16[16,32,512]{2,1,0:T(8,128)(2,1)} %bitcast.17), calls=%async_computation.3 | async-start | bytes 1048576 | tf_op jit(solution)/shard_map/all_to_all | solution.py:369
  167.3 8.7 %gram3.1 = (f32[512,512]{1,0:T(8,128)}, bf16[512,512]{1,0:T(8,128)(2,1)}) custom-call(s32[7]{0:T(128)} %stack.72.info.refs_0_, bf16[256,512]{1,0:T(8,128)(2,1)} %copy-done.5, bf16[128,512]{1,0:T(8,128)(2,1)} %copy-done.10, bf16[128,512]{1,0:T(8,128)(2,1)} %copy-done.9, bf16[8,8,16,1280]{3,2,1,0:T(8,128)(2,1)} %copy-done, ...), custom_call_target="tpu_custom_call" | custom-call | flops 4294967296 | bytes 6291456 | tf_op jit(solution)/shard_map/gram3/pallas_call | solution.py:317
  179.6 4.0 %all-to-all-start.4 = ((f32[8,32,512]{2,1,0:T(8,128)}), f32[8,32,512]{2,1,0:T(8,128)S(1)}, u32[]{:S(2)}, u32[]{:S(2)}) async-start(f32[8,32,512]{2,1,0:T(8,128)} %broadcast_in_dim.23), calls=%async_computation.4 | async-start | bytes 1048576 | tf_op jit(solution)/shard_map/all_to_all | solution.py:371
  183.9 10.4 %all-to-all-done.4 = f32[8,32,512]{2,1,0:T(8,128)S(1)} async-done(((f32[8,32,512]{2,1,0:T(8,128)}), f32[8,32,512]{2,1,0:T(8,128)S(1)}, u32[]{:S(2)}, u32[]{:S(2)}) %all-to-all-start.4) | async-done | bytes 524320 | tf_op jit(solution)/shard_map/all_to_all | solution.py:371
  197.2 4.2 %collective-permute-done.19 = bf16[512,512]{1,0:T(8,128)(2,1)S(1)} collective-permute-done((bf16[512,512]{1,0:T(8,128)(2,1)}, bf16[512,512]{1,0:T(8,128)(2,1)S(1)}, u32[]{:S(2)}, u32[]{:S(2)}) %collective-permute-start.19) | collective-permute-done | bytes 524320 | tf_op jit(solution)/shard_map/ppermute | solution.py:27
  (80 shorter events, 43.4 us)
Async XLA Ops:
  9.2 25.4 %all-to-all-start = ((bf16[8,16,1280]{2,1,0:T(8,128)(2,1)}), bf16[8,16,1280]{2,1,0:T(8,128)(2,1)S(1)}, u32[]{:S(2)}, u32[]{:S(2)}) async-start(bf16[8,16,1280]{2,1,0:T(8,128)(2,1)} %get-tuple-element.47), calls=%async_computation | async-start | bytes 655360 | tf_op jit(solution)/shard_map/all_to_all | solution.py:31
  18.3 16.4 %collective-permute-start.2 = (bf16[512,512]{1,0:T(8,128)(2,1)S(1)}, bf16[512,512]{1,0:T(8,128)(2,1)S(1)}, u32[]{:S(2)}, u32[]{:S(2)}) collective-permute-start(bf16[512,512]{1,0:T(8,128)(2,1)S(1)} %bitcast.33), channel_id=1, source_target_pairs={{0,1},{1,0},{2,3},{3,2},{4,5},{5,4},{6,7},{7,6},{8,9},{9,8},{10,11... | collective-permute-start | bytes 1572872 | tf_op jit(solution)/shard_map/ppermute | solution.py:27
  19.6 12.9 %collective-permute-start.1 = (bf16[256,512]{1,0:T(8,128)(2,1)}, bf16[256,512]{1,0:T(8,128)(2,1)}, u32[]{:S(2)}, u32[]{:S(2)}) collective-permute-start(bf16[256,512]{1,0:T(8,128)(2,1)} %get-tuple-element.48.refs_1_), channel_id=1, source_target_pairs={{0,14},{1,15},{2,0},{3,1},{4,2},{5,3},{6,4},{7,5},{8,6},{9,7},{10,... | collective-permute-start | bytes 786440 | tf_op jit(solution)/shard_map/ppermute | solution.py:27
  22.1 12.5 %collective-permute-start = (bf16[256,512]{1,0:T(8,128)(2,1)}, bf16[256,512]{1,0:T(8,128)(2,1)}, u32[]{:S(2)}, u32[]{:S(2)}) collective-permute-start(bf16[256,512]{1,0:T(8,128)(2,1)} %get-tuple-element.48.refs_1_), channel_id=1, source_target_pairs={{0,2},{1,3},{2,4},{3,5},{4,6},{5,7},{6,8},{7,9},{8,10},{9,11},{10,... | collective-permute-start | bytes 786440 | tf_op jit(solution)/shard_map/ppermute | solution.py:27
  34.6 13.2 %collective-permute-start.5 = (bf16[8,16,1280]{2,1,0:T(8,128)(2,1)S(1)}, bf16[8,16,1280]{2,1,0:T(8,128)(2,1)S(1)}, u32[]{:S(2)}, u32[]{:S(2)}) collective-permute-start(bf16[8,16,1280]{2,1,0:T(8,128)(2,1)S(1)} %all-to-all-done), channel_id=1, source_target_pairs={{0,192},{1,193},{2,194},{3,195},{4,196},{5,197},{6,198},{7,199},{8... | collective-permute-start | bytes 983048 | tf_op jit(solution)/shard_map/ppermute | solution.py:27
  37.3 10.4 %collective-permute-start.4 = (bf16[8,16,1280]{2,1,0:T(8,128)(2,1)S(1)}, bf16[8,16,1280]{2,1,0:T(8,128)(2,1)S(1)}, u32[]{:S(2)}, u32[]{:S(2)}) collective-permute-start(bf16[8,16,1280]{2,1,0:T(8,128)(2,1)S(1)} %all-to-all-done), channel_id=1, source_target_pairs={{0,64},{1,65},{2,66},{3,67},{4,68},{5,69},{6,70},{7,71},{8,72},{9,... | collective-permute-start | bytes 983048 | tf_op jit(solution)/shard_map/ppermute | solution.py:27
  37.3 10.5 %collective-permute-start.3 = (bf16[8,16,1280]{2,1,0:T(8,128)(2,1)S(1)}, bf16[8,16,1280]{2,1,0:T(8,128)(2,1)S(1)}, u32[]{:S(2)}, u32[]{:S(2)}) collective-permute-start(bf16[8,16,1280]{2,1,0:T(8,128)(2,1)S(1)} %all-to-all-done), channel_id=1, source_target_pairs={{0,32},{1,33},{2,34},{3,35},{4,36},{5,37},{6,38},{7,39},{8,40},{9,... | collective-permute-start | bytes 983048 | tf_op jit(solution)/shard_map/ppermute | solution.py:27
  40.1 7.7 %collective-permute-start.6 = (bf16[256,512]{1,0:T(8,128)(2,1)}, bf16[256,512]{1,0:T(8,128)(2,1)S(1)}, u32[]{:S(2)}, u32[]{:S(2)}) collective-permute-start(bf16[256,512]{1,0:T(8,128)(2,1)} %collective-permute-done.refs_2_), channel_id=1, source_target_pairs={{0,2},{1,3},{2,4},{3,5},{4,6},{5,7},{6,8},{7,9},{8,10},{9,11},{10,... | collective-permute-start | bytes 786440 | tf_op jit(solution)/shard_map/ppermute | solution.py:27
  40.1 7.7 %collective-permute-start.7 = (bf16[256,512]{1,0:T(8,128)(2,1)}, bf16[256,512]{1,0:T(8,128)(2,1)S(1)}, u32[]{:S(2)}, u32[]{:S(2)}) collective-permute-start(bf16[256,512]{1,0:T(8,128)(2,1)} %collective-permute-done.1.refs_1_), channel_id=1, source_target_pairs={{0,14},{1,15},{2,0},{3,1},{4,2},{5,3},{6,4},{7,5},{8,6},{9,7},{10,... | collective-permute-start | bytes 786440 | tf_op jit(solution)/shard_map/ppermute | solution.py:27
  47.8 18.8 %collective-permute-start.9 = (bf16[8,16,1280]{2,1,0:T(8,128)(2,1)S(1)}, bf16[8,16,1280]{2,1,0:T(8,128)(2,1)S(1)}, u32[]{:S(2)}, u32[]{:S(2)}) collective-permute-start(bf16[8,16,1280]{2,1,0:T(8,128)(2,1)S(1)} %collective-permute-done.3), channel_id=1, source_target_pairs={{0,192},{1,193},{2,194},{3,195},{4,196},{5,197},{6,198},{7,199},{8... | collective-permute-start | bytes 983048 | tf_op jit(solution)/shard_map/ppermute | solution.py:27
  50.3 16.4 %collective-permute-start.8 = (bf16[8,16,1280]{2,1,0:T(8,128)(2,1)S(1)}, bf16[8,16,1280]{2,1,0:T(8,128)(2,1)S(1)}, u32[]{:S(2)}, u32[]{:S(2)}) collective-permute-start(bf16[8,16,1280]{2,1,0:T(8,128)(2,1)S(1)} %collective-permute-done.3), channel_id=1, source_target_pairs={{0,64},{1,65},{2,66},{3,67},{4,68},{5,69},{6,70},{7,71},{8,72},{9,... | collective-permute-start | bytes 983048 | tf_op jit(solution)/shard_map/ppermute | solution.py:27
  50.3 10.9 %collective-permute-start.10 = (bf16[4,16,1280]{2,1,0:T(8,128)(2,1)S(1)}, bf16[4,16,1280]{2,1,0:T(8,128)(2,1)S(1)}, u32[]{:S(2)}, u32[]{:S(2)}) collective-permute-start(bf16[4,16,1280]{2,1,0:T(8,128)(2,1)S(1)} %slice.12), channel_id=1, source_target_pairs={{0,64},{1,65},{2,66},{3,67},{4,68},{5,69},{6,70},{7,71},{8,72},{9,... | collective-permute-start | bytes 491528 | tf_op jit(solution)/shard_map/ppermute | solution.py:27
  50.4 12.9 %collective-permute-start.11 = (bf16[4,16,1280]{2,1,0:T(8,128)(2,1)S(1)}, bf16[4,16,1280]{2,1,0:T(8,128)(2,1)S(1)}, u32[]{:S(2)}, u32[]{:S(2)}) collective-permute-start(bf16[4,16,1280]{2,1,0:T(8,128)(2,1)S(1)} %slice.13), channel_id=1, source_target_pairs={{0,192},{1,193},{2,194},{3,195},{4,196},{5,197},{6,198},{7,199},{8... | collective-permute-start | bytes 491528 | tf_op jit(solution)/shard_map/ppermute | solution.py:27
  53.2 10.2 %collective-permute-start.12 = (bf16[256,512]{1,0:T(8,128)(2,1)S(1)}, bf16[256,512]{1,0:T(8,128)(2,1)S(1)}, u32[]{:S(2)}, u32[]{:S(2)}) collective-permute-start(bf16[256,512]{1,0:T(8,128)(2,1)S(1)} %collective-permute-done.6.refs_2_), channel_id=1, source_target_pairs={{0,2},{1,3},{2,4},{3,5},{4,6},{5,7},{6,8},{7,9},{8,10},{9,11},{10,... | collective-permute-start | bytes 786440 | tf_op jit(solution)/shard_map/ppermute | solution.py:27
  66.7 6.0 %collective-permute-start.16 = (bf16[128,512]{1,0:T(8,128)(2,1)S(1)}, bf16[128,512]{1,0:T(8,128)(2,1)S(1)}, u32[]{:S(2)}, u32[]{:S(2)}) collective-permute-start(bf16[128,512]{1,0:T(8,128)(2,1)S(1)} %slice.15), channel_id=1, source_target_pairs={{0,14},{1,15},{2,0},{3,1},{4,2},{5,3},{6,4},{7,5},{8,6},{9,7},{10,... | collective-permute-start | bytes 393224 | tf_op jit(solution)/shard_map/ppermute | solution.py:27
  69.9 7.5 %collective-permute-start.14 = (bf16[8,16,1280]{2,1,0:T(8,128)(2,1)S(1)}, bf16[8,16,1280]{2,1,0:T(8,128)(2,1)S(1)}, u32[]{:S(2)}, u32[]{:S(2)}) collective-permute-start(bf16[8,16,1280]{2,1,0:T(8,128)(2,1)S(1)} %constant_dynamic-update-slice_fusion), channel_id=1, source_target_pairs={{0,32},{1,33},{2,34},{3,35},{4,36},{5,37},{6,38},{7,39},{8,40},{9,... | collective-permute-start | bytes 983048 | tf_op jit(solution)/shard_map/ppermute | solution.py:27
  77.6 12.4 %collective-permute-start.17 = (bf16[8,8,16,1280]{3,2,1,0:T(8,128)(2,1)S(1)}, bf16[8,8,16,1280]{3,2,1,0:T(8,128)(2,1)}, u32[]{:S(2)}, u32[]{:S(2)}) collective-permute-start(bf16[8,8,16,1280]{3,2,1,0:T(8,128)(2,1)S(1)} %bitcast_dynamic-update-slice_fusion.own_s.refs_3_.refs_5_.refs_4_), channel_id=1, source_target_pairs={{0,16},{1,17},{2,18},{3,19},{4,20},{5,21},{6,22},{7,23},{8,24},{9,... | collective-permute-start | bytes 7864328 | tf_op jit(solution)/shard_map/ppermute | solution.py:27
  98.9 22.9 %all-to-all-start.1 = ((bf16[8,64,512]{2,1,0:T(8,128)(2,1)}), bf16[8,64,512]{2,1,0:T(8,128)(2,1)S(1)}, u32[]{:S(2)}, u32[]{:S(2)}) async-start(bf16[8,64,512]{2,1,0:T(8,128)(2,1)} %get-tuple-element.67), calls=%async_computation.1 | async-start | bytes 1048576 | tf_op jit(solution)/shard_map/all_to_all | solution.py:31
  122.7 21.4 %all-to-all-start.2 = ((bf16[8,64,512]{2,1,0:T(8,128)(2,1)}), bf16[8,64,512]{2,1,0:T(8,128)(2,1)S(1)}, u32[]{:S(2)}, u32[]{:S(2)}) async-start(bf16[8,64,512]{2,1,0:T(8,128)(2,1)} %broadcast_in_dim.20), calls=%async_computation.2 | async-start | bytes 1048576 | tf_op jit(solution)/shard_map/all_to_all | solution.py:31
  148.4 13.2 %collective-permute-start.18 = (bf16[512,512]{1,0:T(8,128)(2,1)}, bf16[512,512]{1,0:T(8,128)(2,1)S(1)}, u32[]{:S(2)}, u32[]{:S(2)}) collective-permute-start(bf16[512,512]{1,0:T(8,128)(2,1)} %get-tuple-element.79), channel_id=1, source_target_pairs={{0,1},{1,0},{2,3},{3,2},{4,5},{5,4},{6,7},{7,6},{8,9},{9,8},{10,11... | collective-permute-start | bytes 1572872 | tf_op jit(solution)/shard_map/ppermute | solution.py:27
  162.6 16.1 %all-to-all-start.3 = ((bf16[16,32,512]{2,1,0:T(8,128)(2,1)}), bf16[16,32,512]{2,1,0:T(8,128)(2,1)S(1)}, u32[]{:S(2)}, u32[]{:S(2)}) async-start(bf16[16,32,512]{2,1,0:T(8,128)(2,1)} %bitcast.17), calls=%async_computation.3 | async-start | bytes 1048576 | tf_op jit(solution)/shard_map/all_to_all | solution.py:369
  179.6 14.7 %all-to-all-start.4 = ((f32[8,32,512]{2,1,0:T(8,128)}), f32[8,32,512]{2,1,0:T(8,128)S(1)}, u32[]{:S(2)}, u32[]{:S(2)}) async-start(f32[8,32,512]{2,1,0:T(8,128)} %broadcast_in_dim.23), calls=%async_computation.4 | async-start | bytes 1048576 | tf_op jit(solution)/shard_map/all_to_all | solution.py:371
  183.6 17.8 %collective-permute-start.19 = (bf16[512,512]{1,0:T(8,128)(2,1)}, bf16[512,512]{1,0:T(8,128)(2,1)S(1)}, u32[]{:S(2)}, u32[]{:S(2)}) collective-permute-start(bf16[512,512]{1,0:T(8,128)(2,1)} %get-tuple-element.90), channel_id=1, source_target_pairs={{0,1},{1,0},{2,3},{3,2},{4,5},{5,4},{6,7},{7,6},{8,9},{9,8},{10,11... | collective-permute-start | bytes 1572872 | tf_op jit(solution)/shard_map/ppermute | solution.py:27
  194.3 8.3 %collective-permute-start.20 = (f32[8,32,512]{2,1,0:T(8,128)S(1)}, f32[8,32,512]{2,1,0:T(8,128)S(1)}, u32[]{:S(2)}, u32[]{:S(2)}) collective-permute-start(f32[8,32,512]{2,1,0:T(8,128)S(1)} %all-to-all-done.4), channel_id=1, source_target_pairs={{0,16},{1,17},{2,18},{3,19},{4,20},{5,21},{6,22},{7,23},{8,24},{9,... | collective-permute-start | bytes 1572872 | tf_op jit(solution)/shard_map/ppermute | solution.py:27
  (13 other events, 193.2 us)

commit v3 on v2

--- a/solution.py
+++ b/solution.py
@@ -12,7 +12,7 @@
 VMEM = 60 * 2**20
 AXES = ("mp", "shard")
 Z_GROUPS = [[z * 2 + xl for z in range(8)] for xl in range(2)]
-CORE_GROUPS = [[q * 2 + c for q in range(8)] for c in range(2)]
+XLO_GROUPS = [[p * 16 + z * 2 + xl for p in range(16) for xl in range(2)] for z in range(8)]
 
 
 def shift(x, y=0, xh=0, c=0, z=0, xl=0):
@@ -41,14 +41,11 @@
 
 def gather_both(piece, x, w):
     tie = lax.optimization_barrier
-    z = [x]
     zu, zd = shift(x, z=1), shift(x, z=-1)
-    piece, zu, zd, w = tie((swap_z(piece), zu, zd, shift(w, xl=1)))
-    z += [zu, zd]
+    piece, w = tie((swap_z(piece), shift(w, xl=1)))
     h, u, d = shift(piece, xh=1), shift(piece, y=1), shift(piece, y=-1)
-    zu, zd = shift(zu, z=1), shift(zd, z=-1)
     h, u, d, zu, zd = tie((h, u, d, zu, zd))
-    z += [zu, zd]
+    z = [zu, zd]
     half = piece.shape[0] // 2
     t0, t1 = shift(u[:half], y=1), shift(d[half:], y=-1)
     hu, hd = shift(h, y=1), shift(h, y=-1)
@@ -57,39 +54,47 @@
     z += [zu, zd]
     t = jnp.concatenate([t0, t1], 0)
     ht = shift(t, xh=1)
+    zu, zd = shift(zu, z=1), shift(zd, z=-1)
+    ht, zu, zd = tie((ht, zu, zd))
+    z += [zu, zd]
     zu, zd = shift(zu[:128], z=1), shift(zd[128:], z=-1)
-    ht, zu, zd = tie((ht, zu, zd))
     own = jnp.stack([piece, h, d, hd, t, ht, u, hu], 0)
-    return own, shift(own, c=1), w, [x, z[2], z[4], z[6], zu, zd, z[5], z[3], z[1]]
-
-
-def prepare_kernel(info, bank, ids, gains, piece_out, cols_out, total):
+    own, other, zu, zd = tie((own, shift(own, c=1), zu, zd))
+    return own, other, w, [x, z[1], z[3], z[5], zu, zd, z[4], z[2], z[0]]
+
+
+def prepare_kernel(info, bank, ids, gains, piece_out, cols_out, total, column, pick):
     zz = pl.program_id(0)
     p, s, xl = info[0], info[1], info[2]
-    i0 = lax.broadcasted_iota(jnp.int32, (64, 64), 0)
-    i1 = lax.broadcasted_iota(jnp.int32, (64, 64), 1)
-    row_ids = (ids[...] - s * 256).astype(F4)
-    row_ids = jnp.sum(jnp.where(i0 == i1, row_ids, 0.0), axis=1, keepdims=True)
-    pick = jnp.where(row_ids == lax.broadcasted_iota(jnp.int32, (64, 256), 1).astype(F4), 1.0, 0.0).astype(BF)
 
     @pl.when(zz == 0)
     def _():
+        i0 = lax.broadcasted_iota(jnp.int32, (64, 64), 0)
+        i1 = lax.broadcasted_iota(jnp.int32, (64, 64), 1)
+        row_ids = (ids[...] - s * 256).astype(F4)
+        row_ids = jnp.sum(jnp.where(i0 == i1, row_ids, 0.0), axis=1, keepdims=True)
+        lane = lax.broadcasted_iota(jnp.int32, (64, 256), 1).astype(F4)
+        column[...] = jnp.broadcast_to(row_ids, (64, 128))
+        pick[...] = jnp.where(row_ids == lane, 1.0, 0.0).astype(BF)
         total[...] = jnp.zeros_like(total)
 
-    got = dot(pick, bank[...])
-    total[...] += jnp.sum(got * got, axis=1, keepdims=True)
     own_row = pl.multiple_of(p * 16, 16)
-    for j in range(2):
-        at = pl.multiple_of((xl ^ j) * 512, 512)
-        piece_out[zz, :, j * 512 : j * 512 + 512] = bank[pl.ds(own_row, 16), pl.ds(at, 512)]
-
-    @pl.when(zz == p // 2)
-    def _():
-        cols_out[...] = bank[:, pl.ds(pl.multiple_of(p % 2 * 512, 512), 512)]
-
-    @pl.when(zz == 7)
-    def _():
-        scale = lax.rsqrt(total[:, 0:1] / 8192 + EPSILON)
+    for half in range(2):
+        got = dot(pick[...], bank[:, half * 1024 : half * 1024 + 1024])
+        got = got * got
+        total[...] += sum(got[:, i * 128 : i * 128 + 128] for i in range(8))
+        for j in range(2):
+            at = pl.multiple_of(half * 1024 + (xl ^ j) * 512, 512)
+            piece_out[zz * 2 + half, :, j * 512 : j * 512 + 512] = bank[pl.ds(own_row, 16), pl.ds(at, 512)]
+
+    @pl.when(zz == p // 4)
+    def _():
+        cols_out[...] = bank[:, pl.ds(pl.multiple_of(p % 4 * 512, 512), 512)]
+
+    @pl.when(zz == 3)
+    def _():
+        row_ids = column[:, 0:1]
+        scale = lax.rsqrt(jnp.sum(total[...], axis=1, keepdims=True) / 8192 + EPSILON)
         hi = scale.astype(BF).astype(F4)
         mid = (scale - hi).astype(BF).astype(F4)
         low = scale - hi - mid
@@ -115,10 +120,10 @@
         prepare_kernel,
         grid_spec=pltpu.PrefetchScalarGridSpec(
             num_scalar_prefetch=1,
-            grid=(8,),
-            in_specs=[pl.BlockSpec((256, 1024), lambda i, info: (0, i)), whole((1, 64)), whole((1, 8192))],
+            grid=(4,),
+            in_specs=[pl.BlockSpec((256, 2048), lambda i, info: (0, i)), whole((1, 64)), whole((1, 8192))],
             out_specs=[whole((8, 16, 1280)), whole((256, 512))],
-            scratch_shapes=[pltpu.VMEM((64, 128), F4)],
+            scratch_shapes=[pltpu.VMEM((64, 128), F4), pltpu.VMEM((64, 128), F4), pltpu.VMEM((64, 256), BF)],
         ),
         out_shape=[jax.ShapeDtypeStruct((8, 16, 1280), BF), jax.ShapeDtypeStruct((256, 512), BF)],
         compiler_params=pltpu.CompilerParams(dimension_semantics=("arbitrary",), vmem_limit_bytes=VMEM),
@@ -130,27 +135,28 @@
 def project_kernel(info, own_s, other_s, gains, weights, part_out, calib_out, diag_out, table, calib):
     zz = pl.program_id(0)
     xl, z = info[2], info[6]
-    for core in range(2):
-        src = own_s if core == 0 else other_s
-        for slot in range(8):
-            m = slot_model(info, core, slot)
-            table[pl.ds(pl.multiple_of(m * 16, 16), 16), :] = src[slot, 0, :, 0:1024]
-    extra = own_s[0, 0, :, 1024:1152].astype(F4)
     lane = lax.broadcasted_iota(jnp.int32, (16, 256), 1).astype(F4)
-    pick, scale = [], []
-    for t in range(4):
-        at = t * 32
-        pick.append(jnp.where(extra[:, at : at + 1] == lane, 1.0, 0.0))
-        scale.append(extra[:, at + 1 : at + 2] + extra[:, at + 2 : at + 3] + extra[:, at + 3 : at + 4])
-    pick = jnp.concatenate(pick, 0).astype(BF)
-    scale = jnp.concatenate(scale, 0)
-    rows = pl.ds(pl.multiple_of(zz * 64, 64), 64)
-    for j in range(2):
-        cols = slice(j * 512, j * 512 + 512)
-        g = gains[:, pl.ds(pl.multiple_of((z * 2 + (xl ^ j)) * 512, 512), 512)]
-        calib[rows, cols] = (dot(pick, table[:, cols]) * scale * g).astype(BF)
-
-    @pl.when(zz == 7)
+    for i in range(2):
+        for core in range(2):
+            src = own_s if core == 0 else other_s
+            for slot in range(8):
+                m = slot_model(info, core, slot)
+                table[i, pl.ds(pl.multiple_of(m * 16, 16), 16), :] = src[slot, i, :, 0:1024]
+        extra = own_s[0, i, :, 1024:1152].astype(F4)
+        pick, scale = [], []
+        for t in range(4):
+            at = t * 32
+            pick.append(jnp.where(extra[:, at : at + 1] == lane, 1.0, 0.0))
+            scale.append(extra[:, at + 1 : at + 2] + extra[:, at + 2 : at + 3] + extra[:, at + 3 : at + 4])
+        pick = jnp.concatenate(pick, 0).astype(BF)
+        scale = jnp.concatenate(scale, 0)
+        rows = pl.ds(pl.multiple_of(zz * 128 + i * 64, 64), 64)
+        for j in range(2):
+            cols = slice(j * 512, j * 512 + 512)
+            g = gains[:, pl.ds(pl.multiple_of((z * 2 + (xl ^ j)) * 512, 512), 512)]
+            calib[rows, cols] = (dot(pick, table[i, :, cols]) * scale * g).astype(BF)
+
+    @pl.when(zz == 3)
     def _():
         calib_out[...] = calib[...]
         part = dot(calib[...], weights[...]).astype(BF)
@@ -162,15 +168,15 @@
 
 def project(info, own_s, other_s, gains, weights):
     whole = lambda shape: pl.BlockSpec(shape, lambda i, info: (0,) * len(shape))
-    by_z = pl.BlockSpec((8, 1, 16, 1280), lambda i, info: (0, i, 0, 0))
+    by_z = pl.BlockSpec((8, 2, 16, 1280), lambda i, info: (0, i, 0, 0))
     return pl.pallas_call(
         project_kernel,
         grid_spec=pltpu.PrefetchScalarGridSpec(
             num_scalar_prefetch=1,
-            grid=(8,),
+            grid=(4,),
             in_specs=[by_z, by_z, whole((1, 8192)), whole((1024, 512))],
             out_specs=[whole((8, 64, 512)), whole((512, 1024)), whole((1, 1024))],
-            scratch_shapes=[pltpu.VMEM((256, 1024), BF), pltpu.VMEM((512, 1024), BF)],
+            scratch_shapes=[pltpu.VMEM((2, 256, 1024), BF), pltpu.VMEM((512, 1024), BF)],
         ),
         out_shape=[
             jax.ShapeDtypeStruct((8, 64, 512), BF),
@@ -183,7 +189,8 @@
     )(info, own_s, other_s, gains, weights)
 
 
-def numer_kernel(calib, model_out, diag, weights, near, far):
+def numer_kernel(info, calib, model_out, diag, weights, out):
+    xl = info[2]
     ratio = lax.broadcasted_iota(jnp.int32, (512, 512), 0) == lax.broadcasted_iota(jnp.int32, (512, 512), 1)
     for j in range(2):
         cols = slice(j * 512, j * 512 + 512)
@@ -191,22 +198,21 @@
         d = jnp.sum(jnp.where(ratio, d, 0.0), axis=1, keepdims=True)
         got = contract_rows(calib[:, cols], model_out[...]) * (ALPHA / 1024)
         got = got + d * weights[cols, :].astype(F4)
-        if j == 0:
-            near[...] = got
-        else:
-            far[...] = got.astype(BF)
-
-
-def numer_call(calib, model_out, diag, weights):
+        got = got.astype(BF)
+        for q in range(16):
+            out[q * 2 + (xl ^ j)] = got[q * 32 : q * 32 + 32]
+
+
+def numer_call(info, calib, model_out, diag, weights):
     return pl.pallas_call(
         numer_kernel,
-        in_specs=[pl.BlockSpec(memory_space=pltpu.VMEM)] * 4,
-        out_specs=[pl.BlockSpec(memory_space=pltpu.VMEM)] * 2,
-        out_shape=[jax.ShapeDtypeStruct((512, 512), F4), jax.ShapeDtypeStruct((512, 512), BF)],
+        in_specs=[pl.BlockSpec(memory_space=pltpu.SMEM)] + [pl.BlockSpec(memory_space=pltpu.VMEM)] * 4,
+        out_specs=pl.BlockSpec(memory_space=pltpu.VMEM),
+        out_shape=jax.ShapeDtypeStruct((32, 32, 512), BF),
         compiler_params=pltpu.CompilerParams(vmem_limit_bytes=VMEM),
         cost_estimate=pl.CostEstimate(flops=2**29, bytes_accessed=4 * 2**20, transcendentals=0),
         name="numer",
-    )(calib, model_out, diag, weights)
+    )(info, calib, model_out, diag, weights)
 
 
 ORDER = (0, 7, 1, 6, 2, 5, 3, 4)
@@ -359,20 +365,14 @@
     (acc,) = gram_call(1, info, [b[1], b[7]], own_s, other_s, gains, acc)
     model_out, acc = tie((swap_z(model_out), acc))
 
-    near, far = numer_call(calib, model_out.reshape(512, 512), diag, both)
-    far, info = tie((far, info))
+    numer = numer_call(info, calib, model_out.reshape(512, 512), diag, both)
+    numer, info = tie((numer, info))
     (acc,) = gram_call(2, info, [b[2], b[6]], own_s, other_s, gains, acc)
-    far, acc = tie((shift(far, xl=1), acc))
-    numer = (near + far.astype(F4)).astype(BF).reshape(16, 32, 512)
-    numer, info = tie((numer, info))
     near, far = gram_call(3, info, [b[3], b[4], b[5]], own_s, other_s, gains, acc)
-    numer, far = tie((lax.all_to_all(numer, "mp", 0, 0, tiled=True), far))
-    numer = jnp.sum(numer.astype(F4), 0)
-    mine = lax.all_to_all(
-        jnp.broadcast_to(numer[None], (8, 32, 512)), "mp", 0, 0, tiled=True, axis_index_groups=CORE_GROUPS
-    )
-    theirs = shift(mine, c=1)
-    numer = jnp.where(c == 0, jnp.stack([mine, theirs], 1), jnp.stack([theirs, mine], 1)).reshape(512, 512)
+    numer, near = tie((lax.all_to_all(numer, AXES, 0, 0, tiled=True, axis_index_groups=XLO_GROUPS), near))
+    numer = jnp.sum(numer.astype(F4), 0).astype(BF)
+    numer = lax.all_to_all(jnp.broadcast_to(numer[None], (16, 32, 512)), "mp", 0, 0, tiled=True)
+    numer = numer.reshape(512, 512).astype(F4)
 
     gram = near + shift(far, xl=1).astype(F4)
     on_diag = (p == s) & (

time: 205 us -> 191 us (0.932)
  waiting for transfers between devices: 79.4 us -> 64.6 us
  starting transfers between devices: 60.5 us -> 66.5 us
  Pallas kernels: 54.9 us -> 50.3 us
    ppermute x21 -> x19, waiting for transfers between devices: 47.5 us -> 37.1 us  [shift(): return lax.ppermute(x, AXES, pairs)]
    all_to_all x2, waiting for transfers between devices: 13.1 us -> 8.77 us  [the longest x1 8.76 us: local(): lax.all_to_all(jnp.broadcast_to(numer[None], (16, 32, 512)), 'mp', 0, 0,...]
    all_to_all x2, starting transfers between devices: 8.69 us -> 12 us  [the longest x1 7.02 us: local(): lax.all_to_all(jnp.broadcast_to(numer[None], (16, 32, 512)), 'mp', 0, 0,...]
    pallas_call x1, Pallas kernels: 7.89 us -> 5.24 us  [prepare(): pl.pallas_call(prepare_kernel, grid_spec=pltpu.PrefetchScalarGridSpec(num...]
    ppermute x21 -> x19, starting transfers between devices: 34.4 us -> 36.5 us  [shift(): return lax.ppermute(x, AXES, pairs)]
  transfers between devices with their start and end apart: 26 -> 24, of which waited for: 15 -> 15; matrix products, arithmetic and copies ran while one was open for 1% -> 2% of each run, Pallas kernels for 17% -> 18%
where the time goes in v3:
time: 191 us; the launch traced here: 190 us
  starting transfers between devices  66.5 us (35%)
  waiting for transfers between devices  64.6 us (34%)
  Pallas kernels  50.3 us (26%)
  local copies, waits for them, and re-layouts  4.11 us (2%)
  other arithmetic  3.58 us (2%)
    ppermute x19, waiting for transfers between devices, shift(): return lax.ppermute(x, AXES, pairs)  37.1 us
    ppermute x19, starting transfers between devices, shift(): return lax.ppermute(x, AXES, pairs)  36.5 us
    pallas_call x4, Pallas kernels, gram_call(): pl.pallas_call(lambda *refs: gram_kernel(first, last, *refs), grid_spec=p...  34.5 us
    all_to_all x3, waiting for transfers between devices, swap_z(): lax.all_to_all(x, 'shard', 0, 0, tiled=True, axis_index_groups=Z_GROUPS)  18.7 us
    all_to_all x3, starting transfers between devices, swap_z(): lax.all_to_all(x, 'shard', 0, 0, tiled=True, axis_index_groups=Z_GROUPS)  18 us
    all_to_all x1, waiting for transfers between devices, local(): lax.all_to_all(jnp.broadcast_to(numer[None], (16, 32, 512)), 'mp', 0, 0,...  8.76 us
    all_to_all x1, starting transfers between devices, local(): lax.all_to_all(jnp.broadcast_to(numer[None], (16, 32, 512)), 'mp', 0, 0,...  7.02 us
    pallas_call x1, Pallas kernels, project(): pl.pallas_call(project_kernel, grid_spec=pltpu.PrefetchScalarGridSpec(num...  6.89 us
  transfers between devices with their start and end apart: 24, of which 15 were waited for; matrix products, arithmetic and copies ran while one was open for 2% of the time, Pallas kernels for 18%

profile of v3, /device:TPU:1, one launch (start us, length us, event | category | flops | bytes accessed | tf_op | source)
XLA Modules:
  0.0 189.9 jit_solution(15493443510040014775)
XLA Ops:
  1.3 5.2 %prepare.1 = (bf16[8,16,1280]{2,1,0:T(8,128)(2,1)}, bf16[256,512]{1,0:T(8,128)(2,1)}) custom-call(s32[7]{0:T(128)} %stack.58.info.refs_0_, bf16[256,8192]{1,0:T(8,128)(2,1)} %bank.1, s32[1,64]{1,0:T(1,128)} %ids.1, f32[1,8192]{1,0:T(1,128)} %gains.3), custom_call_target="tpu_custom_call" | custom-call | flops 268435456 | bytes 5242880 | tf_op jit(solution)/shard_map/prepare/pallas_call | solution.py:119
  6.6 9.0 %all-to-all-start = ((bf16[8,16,1280]{2,1,0:T(8,128)(2,1)}), bf16[8,16,1280]{2,1,0:T(8,128)(2,1)S(1)}, u32[]{:S(2)}, u32[]{:S(2)}) async-start(bf16[8,16,1280]{2,1,0:T(8,128)(2,1)} %get-tuple-element.43), calls=%async_computation | async-start | bytes 655360 | tf_op jit(solution)/shard_map/all_to_all | solution.py:31
  19.5 8.8 %collective-permute-done = bf16[512,512]{1,0:T(8,128)(2,1)S(1)} collective-permute-done((bf16[512,512]{1,0:T(8,128)(2,1)S(1)}, bf16[512,512]{1,0:T(8,128)(2,1)S(1)}, u32[]{:S(2)}, u32[]{:S(2)}) %collective-permute-start) | collective-permute-done | bytes 524320 | tf_op jit(solution)/shard_map/ppermute | solution.py:27
  31.0 2.8 %collective-permute-start.1 = (bf16[8,16,1280]{2,1,0:T(8,128)(2,1)S(1)}, bf16[8,16,1280]{2,1,0:T(8,128)(2,1)S(1)}, u32[]{:S(2)}, u32[]{:S(2)}) collective-permute-start(bf16[8,16,1280]{2,1,0:T(8,128)(2,1)S(1)} %all-to-all-done), channel_id=1, source_target_pairs={{0,32},{1,33},{2,34},{3,35},{4,36},{5,37},{6,38},{7,39},{8,40},{9,... | collective-permute-start | bytes 983048 | tf_op jit(solution)/shard_map/ppermute | solution.py:27
  35.8 3.1 %collective-permute-done.2 = bf16[8,16,1280]{2,1,0:T(8,128)(2,1)S(1)} collective-permute-done((bf16[8,16,1280]{2,1,0:T(8,128)(2,1)S(1)}, bf16[8,16,1280]{2,1,0:T(8,128)(2,1)S(1)}, u32[]{:S(2)}, u32[]{:S(2)}) %collective-permute-start.2) | collective-permute-done | bytes 327712 | tf_op jit(solution)/shard_map/ppermute | solution.py:27
  45.7 5.9 %collective-permute-done.8 = bf16[4,16,1280]{2,1,0:T(8,128)(2,1)S(1)} collective-permute-done((bf16[4,16,1280]{2,1,0:T(8,128)(2,1)S(1)}, bf16[4,16,1280]{2,1,0:T(8,128)(2,1)S(1)}, u32[]{:S(2)}, u32[]{:S(2)}) %collective-permute-start.8) | collective-permute-done | bytes 163872 | tf_op jit(solution)/shard_map/ppermute | solution.py:27
  54.2 3.6 %collective-permute-done.11.refs_1_ = bf16[256,512]{1,0:T(8,128)(2,1)S(1)} collective-permute-done((bf16[256,512]{1,0:T(8,128)(2,1)}, bf16[256,512]{1,0:T(8,128)(2,1)S(1)}, u32[]{:S(2)}, u32[]{:S(2)}) %collective-permute-start.11) | collective-permute-done | bytes 262176 | tf_op jit(solution)/shard_map/ppermute | solution.py:27
  61.0 2.8 %collective-permute-start.12 = (bf16[8,16,1280]{2,1,0:T(8,128)(2,1)S(1)}, bf16[8,16,1280]{2,1,0:T(8,128)(2,1)S(1)}, u32[]{:S(2)}, u32[]{:S(2)}) collective-permute-start(bf16[8,16,1280]{2,1,0:T(8,128)(2,1)S(1)} %constant_dynamic-update-slice_fusion), channel_id=1, source_target_pairs={{0,32},{1,33},{2,34},{3,35},{4,36},{5,37},{6,38},{7,39},{8,40},{9,... | collective-permute-start | bytes 983048 | tf_op jit(solution)/shard_map/ppermute | solution.py:27
  65.7 2.8 %collective-permute-done.12 = bf16[8,16,1280]{2,1,0:T(8,128)(2,1)S(1)} collective-permute-done((bf16[8,16,1280]{2,1,0:T(8,128)(2,1)S(1)}, bf16[8,16,1280]{2,1,0:T(8,128)(2,1)S(1)}, u32[]{:S(2)}, u32[]{:S(2)}) %collective-permute-start.12) | collective-permute-done | bytes 327712 | tf_op jit(solution)/shard_map/ppermute | solution.py:27
  68.6 8.9 %collective-permute-start.15 = (bf16[8,8,16,1280]{3,2,1,0:T(8,128)(2,1)S(1)}, bf16[8,8,16,1280]{3,2,1,0:T(8,128)(2,1)}, u32[]{:S(2)}, u32[]{:S(2)}) collective-permute-start(bf16[8,8,16,1280]{3,2,1,0:T(8,128)(2,1)S(1)} %bitcast_dynamic-update-slice_fusion.own_s.refs_3_.refs_5_.refs_4_), channel_id=1, source_target_pairs={{0,16},{1,17},{2,18},{3,19},{4,20},{5,21},{6,22},{7,23},{8,24},{9,... | collective-permute-start | bytes 7864328 | tf_op jit(solution)/shard_map/ppermute | solution.py:27
  86.1 6.9 %project.1 = (bf16[8,64,512]{2,1,0:T(8,128)(2,1)}, bf16[512,1024]{1,0:T(8,128)(2,1)}, f32[1,1024]{1,0:T(1,128)}) custom-call(s32[7]{0:T(128)} %stack.58.info.refs_0_, bf16[8,8,16,1280]{3,2,1,0:T(8,128)(2,1)} %copy-done, bf16[8,8,16,1280]{3,2,1,0:T(8,128)(2,1)} %collective-permute-done.15.other_s.refs_4_.refs_6_.refs_5_, f32[1,8192]{1,0:T(1,128)} %gains.3, ...), custom_call_target="tpu_custom_call" | custom-call | flops 1073741824 | bytes 8388608 | tf_op jit(solution)/shard_map/project/pallas_call | solution.py:172
  93.0 5.5 %all-to-all-start.1 = ((bf16[8,64,512]{2,1,0:T(8,128)(2,1)}), bf16[8,64,512]{2,1,0:T(8,128)(2,1)S(1)}, u32[]{:S(2)}, u32[]{:S(2)}) async-start(bf16[8,64,512]{2,1,0:T(8,128)(2,1)} %get-tuple-element.64), calls=%async_computation.1 | async-start | bytes 1048576 | tf_op jit(solution)/shard_map/all_to_all | solution.py:31
  98.5 8.2 %gram0.1 = (f32[512,1024]{1,0:T(8,128)}, f32[16,1536]{1,0:T(8,128)}) custom-call(s32[7]{0:T(128)} %stack.58.info.refs_0_, bf16[256,512]{1,0:T(8,128)(2,1)} %get-tuple-element.45.refs_1_, bf16[256,512]{1,0:T(8,128)(2,1)} %collective-permute-done.4.refs_2_, bf16[8,8,16,1280]{3,2,1,0:T(8,128)(2,1)} %copy-done, ...), custom_call_target="tpu_custom_call" | custom-call | flops 4294967296 | bytes 6291456 | tf_op jit(solution)/shard_map/gram0/pallas_call | solution.py:323
  106.7 9.7 %all-to-all-done.1 = bf16[8,64,512]{2,1,0:T(8,128)(2,1)S(1)} async-done(((bf16[8,64,512]{2,1,0:T(8,128)(2,1)}), bf16[8,64,512]{2,1,0:T(8,128)(2,1)S(1)}, u32[]{:S(2)}, u32[]{:S(2)}) %all-to-all-start.1) | async-done | bytes 524320 | tf_op jit(solution)/shard_map/all_to_all | solution.py:31
  117.3 3.5 %all-to-all-start.2 = ((bf16[8,64,512]{2,1,0:T(8,128)(2,1)}), bf16[8,64,512]{2,1,0:T(8,128)(2,1)S(1)}, u32[]{:S(2)}, u32[]{:S(2)}) async-start(bf16[8,64,512]{2,1,0:T(8,128)(2,1)} %broadcast_in_dim.20), calls=%async_computation.2 | async-start | bytes 1048576 | tf_op jit(solution)/shard_map/all_to_all | solution.py:31
  120.8 8.8 %gram1.1.refs_6_ = f32[512,1024]{1,0:T(8,128)} custom-call(s32[7]{0:T(128)} %stack.58.info.refs_0_, bf16[256,512]{1,0:T(8,128)(2,1)} %collective-permute-done.5.refs_1_, bf16[256,512]{1,0:T(8,128)(2,1)} %copy-done.7, bf16[8,8,16,1280]{3,2,1,0:T(8,128)(2,1)} %copy-done, ...), custom_call_target="tpu_custom_call", output_to_operand_aliasing={{}: (6, {})} | custom-call | flops 4294967296 | bytes 6291456 | tf_op jit(solution)/shard_map/gram1/pallas_call | solution.py:323
  129.6 9.1 %all-to-all-done.2 = bf16[8,64,512]{2,1,0:T(8,128)(2,1)S(1)} async-done(((bf16[8,64,512]{2,1,0:T(8,128)(2,1)}), bf16[8,64,512]{2,1,0:T(8,128)(2,1)S(1)}, u32[]{:S(2)}, u32[]{:S(2)}) %all-to-all-start.2) | async-done | bytes 524320 | tf_op jit(solution)/shard_map/all_to_all | solution.py:31
  139.5 3.6 %numer.1 = bf16[32,32,512]{2,1,0:T(8,128)(2,1)} custom-call(s32[7]{0:T(128)} %stack.58.info.refs_0_, bf16[512,1024]{1,0:T(8,128)(2,1)} %get-tuple-element.69.calib, bf16[512,512]{1,0:T(8,128)(2,1)} %bitcast.28, f32[1,1024]{1,0:T(1,128)} %get-tuple-element.74.diag, bf16[1024,512]{1,0:T(8,128)(2,1)} %pad_maximum_fusion.weights), custom_call_target="tpu_custom_call" | custom-call | flops 536870912 | bytes 4194304 | tf_op jit(solution)/shard_map/numer/pallas_call | solution.py:207
  143.1 5.0 %all-to-all-start.3 = ((bf16[32,32,512]{2,1,0:T(8,128)(2,1)}), bf16[32,32,512]{2,1,0:T(8,128)(2,1)S(1)}, u32[]{:S(2)}, u32[]{:S(2)}) async-start(bf16[32,32,512]{2,1,0:T(8,128)(2,1)} %numer.1), calls=%async_computation.3 | async-start | bytes 2097152 | tf_op jit(solution)/shard_map/all_to_all | solution.py:372
  148.1 8.8 %gram2.1.refs_7_ = f32[512,1024]{1,0:T(8,128)} custom-call(s32[7]{0:T(128)} %stack.58.info.refs_0_, bf16[256,512]{1,0:T(8,128)(2,1)} %copy-done.6, bf16[256,512]{1,0:T(8,128)(2,1)} %copy-done.5, bf16[8,8,16,1280]{3,2,1,0:T(8,128)(2,1)} %copy-done, ...), custom_call_target="tpu_custom_call", output_to_operand_aliasing={{}: (6, {})} | custom-call | flops 4294967296 | bytes 6291456 | tf_op jit(solution)/shard_map/gram2/pallas_call | solution.py:323
  156.9 8.7 %gram3.1 = (f32[512,512]{1,0:T(8,128)}, bf16[512,512]{1,0:T(8,128)(2,1)}) custom-call(s32[7]{0:T(128)} %stack.58.info.refs_0_, bf16[256,512]{1,0:T(8,128)(2,1)} %copy-done.4, bf16[128,512]{1,0:T(8,128)(2,1)} %copy-done.9, bf16[128,512]{1,0:T(8,128)(2,1)} %copy-done.8, bf16[8,8,16,1280]{3,2,1,0:T(8,128)(2,1)} %copy-done, ...), custom_call_target="tpu_custom_call" | custom-call | flops 4294967296 | bytes 6291456 | tf_op jit(solution)/shard_map/gram3/pallas_call | solution.py:323
  168.0 7.0 %all-to-all-start.4 = ((bf16[16,32,512]{2,1,0:T(8,128)(2,1)}), bf16[16,32,512]{2,1,0:T(8,128)(2,1)S(1)}, u32[]{:S(2)}, u32[]{:S(2)}) async-start(bf16[16,32,512]{2,1,0:T(8,128)(2,1)} %broadcast_in_dim.23), calls=%async_computation.4 | async-start | bytes 1048576 | tf_op jit(solution)/shard_map/all_to_all | solution.py:374
  175.0 3.8 %collective-permute-done.18 = bf16[512,512]{1,0:T(8,128)(2,1)S(1)} collective-permute-done((bf16[512,512]{1,0:T(8,128)(2,1)}, bf16[512,512]{1,0:T(8,128)(2,1)S(1)}, u32[]{:S(2)}, u32[]{:S(2)}) %collective-permute-start.18) | collective-permute-done | bytes 524320 | tf_op jit(solution)/shard_map/ppermute | solution.py:27
  180.0 8.8 %all-to-all-done.4 = bf16[16,32,512]{2,1,0:T(8,128)(2,1)S(1)} async-done(((bf16[16,32,512]{2,1,0:T(8,128)(2,1)}), bf16[16,32,512]{2,1,0:T(8,128)(2,1)S(1)}, u32[]{:S(2)}, u32[]{:S(2)}) %all-to-all-start.4) | async-done | bytes 524320 | tf_op jit(solution)/shard_map/all_to_all | solution.py:374
  (73 shorter events, 38.7 us)
Async XLA Ops:
  6.6 21.7 %all-to-all-start = ((bf16[8,16,1280]{2,1,0:T(8,128)(2,1)}), bf16[8,16,1280]{2,1,0:T(8,128)(2,1)S(1)}, u32[]{:S(2)}, u32[]{:S(2)}) async-start(bf16[8,16,1280]{2,1,0:T(8,128)(2,1)} %get-tuple-element.43), calls=%async_computation | async-start | bytes 655360 | tf_op jit(solution)/shard_map/all_to_all | solution.py:31
  15.6 12.7 %collective-permute-start = (bf16[512,512]{1,0:T(8,128)(2,1)S(1)}, bf16[512,512]{1,0:T(8,128)(2,1)S(1)}, u32[]{:S(2)}, u32[]{:S(2)}) collective-permute-start(bf16[512,512]{1,0:T(8,128)(2,1)S(1)} %bitcast.29), channel_id=1, source_target_pairs={{0,1},{1,0},{2,3},{3,2},{4,5},{5,4},{6,7},{7,6},{8,9},{9,8},{10,11... | collective-permute-start | bytes 1572872 | tf_op jit(solution)/shard_map/ppermute | solution.py:27
  16.9 16.9 %collective-permute-start.5 = (bf16[256,512]{1,0:T(8,128)(2,1)}, bf16[256,512]{1,0:T(8,128)(2,1)}, u32[]{:S(2)}, u32[]{:S(2)}) collective-permute-start(bf16[256,512]{1,0:T(8,128)(2,1)} %get-tuple-element.45.refs_1_), channel_id=1, source_target_pairs={{0,14},{1,15},{2,0},{3,1},{4,2},{5,3},{6,4},{7,5},{8,6},{9,7},{10,... | collective-permute-start | bytes 786440 | tf_op jit(solution)/shard_map/ppermute | solution.py:27
  19.5 14.3 %collective-permute-start.4 = (bf16[256,512]{1,0:T(8,128)(2,1)}, bf16[256,512]{1,0:T(8,128)(2,1)}, u32[]{:S(2)}, u32[]{:S(2)}) collective-permute-start(bf16[256,512]{1,0:T(8,128)(2,1)} %get-tuple-element.45.refs_1_), channel_id=1, source_target_pairs={{0,2},{1,3},{2,4},{3,5},{4,6},{5,7},{6,8},{7,9},{8,10},{9,11},{10,... | collective-permute-start | bytes 786440 | tf_op jit(solution)/shard_map/ppermute | solution.py:27
  28.2 7.6 %collective-permute-start.3 = (bf16[8,16,1280]{2,1,0:T(8,128)(2,1)S(1)}, bf16[8,16,1280]{2,1,0:T(8,128)(2,1)S(1)}, u32[]{:S(2)}, u32[]{:S(2)}) collective-permute-start(bf16[8,16,1280]{2,1,0:T(8,128)(2,1)S(1)} %all-to-all-done), channel_id=1, source_target_pairs={{0,192},{1,193},{2,194},{3,195},{4,196},{5,197},{6,198},{7,199},{8... | collective-permute-start | bytes 983048 | tf_op jit(solution)/shard_map/ppermute | solution.py:27
  31.0 8.0 %collective-permute-start.2 = (bf16[8,16,1280]{2,1,0:T(8,128)(2,1)S(1)}, bf16[8,16,1280]{2,1,0:T(8,128)(2,1)S(1)}, u32[]{:S(2)}, u32[]{:S(2)}) collective-permute-start(bf16[8,16,1280]{2,1,0:T(8,128)(2,1)S(1)} %all-to-all-done), channel_id=1, source_target_pairs={{0,64},{1,65},{2,66},{3,67},{4,68},{5,69},{6,70},{7,71},{8,72},{9,... | collective-permute-start | bytes 983048 | tf_op jit(solution)/shard_map/ppermute | solution.py:27
  31.0 8.3 %collective-permute-start.1 = (bf16[8,16,1280]{2,1,0:T(8,128)(2,1)S(1)}, bf16[8,16,1280]{2,1,0:T(8,128)(2,1)S(1)}, u32[]{:S(2)}, u32[]{:S(2)}) collective-permute-start(bf16[8,16,1280]{2,1,0:T(8,128)(2,1)S(1)} %all-to-all-done), channel_id=1, source_target_pairs={{0,32},{1,33},{2,34},{3,35},{4,36},{5,37},{6,38},{7,39},{8,40},{9,... | collective-permute-start | bytes 983048 | tf_op jit(solution)/shard_map/ppermute | solution.py:27
  39.2 18.6 %collective-permute-start.7 = (bf16[8,16,1280]{2,1,0:T(8,128)(2,1)S(1)}, bf16[8,16,1280]{2,1,0:T(8,128)(2,1)S(1)}, u32[]{:S(2)}, u32[]{:S(2)}) collective-permute-start(bf16[8,16,1280]{2,1,0:T(8,128)(2,1)S(1)} %collective-permute-done.1), channel_id=1, source_target_pairs={{0,192},{1,193},{2,194},{3,195},{4,196},{5,197},{6,198},{7,199},{8... | collective-permute-start | bytes 983048 | tf_op jit(solution)/shard_map/ppermute | solution.py:27
  41.6 16.2 %collective-permute-start.6 = (bf16[8,16,1280]{2,1,0:T(8,128)(2,1)S(1)}, bf16[8,16,1280]{2,1,0:T(8,128)(2,1)S(1)}, u32[]{:S(2)}, u32[]{:S(2)}) collective-permute-start(bf16[8,16,1280]{2,1,0:T(8,128)(2,1)S(1)} %collective-permute-done.1), channel_id=1, source_target_pairs={{0,64},{1,65},{2,66},{3,67},{4,68},{5,69},{6,70},{7,71},{8,72},{9,... | collective-permute-start | bytes 983048 | tf_op jit(solution)/shard_map/ppermute | solution.py:27
  41.7 10.0 %collective-permute-start.8 = (bf16[4,16,1280]{2,1,0:T(8,128)(2,1)S(1)}, bf16[4,16,1280]{2,1,0:T(8,128)(2,1)S(1)}, u32[]{:S(2)}, u32[]{:S(2)}) collective-permute-start(bf16[4,16,1280]{2,1,0:T(8,128)(2,1)S(1)} %slice.12), channel_id=1, source_target_pairs={{0,64},{1,65},{2,66},{3,67},{4,68},{5,69},{6,70},{7,71},{8,72},{9,... | collective-permute-start | bytes 491528 | tf_op jit(solution)/shard_map/ppermute | solution.py:27
  41.8 12.4 %collective-permute-start.9 = (bf16[4,16,1280]{2,1,0:T(8,128)(2,1)S(1)}, bf16[4,16,1280]{2,1,0:T(8,128)(2,1)S(1)}, u32[]{:S(2)}, u32[]{:S(2)}) collective-permute-start(bf16[4,16,1280]{2,1,0:T(8,128)(2,1)S(1)} %slice.13), channel_id=1, source_target_pairs={{0,192},{1,193},{2,194},{3,195},{4,196},{5,197},{6,198},{7,199},{8... | collective-permute-start | bytes 491528 | tf_op jit(solution)/shard_map/ppermute | solution.py:27
  44.5 9.7 %collective-permute-start.10 = (bf16[256,512]{1,0:T(8,128)(2,1)}, bf16[256,512]{1,0:T(8,128)(2,1)S(1)}, u32[]{:S(2)}, u32[]{:S(2)}) collective-permute-start(bf16[256,512]{1,0:T(8,128)(2,1)} %collective-permute-done.4.refs_2_), channel_id=1, source_target_pairs={{0,2},{1,3},{2,4},{3,5},{4,6},{5,7},{6,8},{7,9},{8,10},{9,11},{10,... | collective-permute-start | bytes 786440 | tf_op jit(solution)/shard_map/ppermute | solution.py:27
  51.6 6.2 %collective-permute-start.11 = (bf16[256,512]{1,0:T(8,128)(2,1)}, bf16[256,512]{1,0:T(8,128)(2,1)S(1)}, u32[]{:S(2)}, u32[]{:S(2)}) collective-permute-start(bf16[256,512]{1,0:T(8,128)(2,1)} %collective-permute-done.5.refs_1_), channel_id=1, source_target_pairs={{0,14},{1,15},{2,0},{3,1},{4,2},{5,3},{6,4},{7,5},{8,6},{9,7},{10,... | collective-permute-start | bytes 786440 | tf_op jit(solution)/shard_map/ppermute | solution.py:27
  57.8 6.9 %collective-permute-start.13 = (bf16[256,512]{1,0:T(8,128)(2,1)S(1)}, bf16[256,512]{1,0:T(8,128)(2,1)S(1)}, u32[]{:S(2)}, u32[]{:S(2)}) collective-permute-start(bf16[256,512]{1,0:T(8,128)(2,1)S(1)} %collective-permute-done.10.refs_2_), channel_id=1, source_target_pairs={{0,2},{1,3},{2,4},{3,5},{4,6},{5,7},{6,8},{7,9},{8,10},{9,11},{10,... | collective-permute-start | bytes 786440 | tf_op jit(solution)/shard_map/ppermute | solution.py:27
  58.5 7.2 %collective-permute-start.14 = (bf16[256,512]{1,0:T(8,128)(2,1)S(1)}, bf16[256,512]{1,0:T(8,128)(2,1)S(1)}, u32[]{:S(2)}, u32[]{:S(2)}) collective-permute-start(bf16[256,512]{1,0:T(8,128)(2,1)S(1)} %collective-permute-done.11.refs_1_), channel_id=1, source_target_pairs={{0,14},{1,15},{2,0},{3,1},{4,2},{5,3},{6,4},{7,5},{8,6},{9,7},{10,... | collective-permute-start | bytes 786440 | tf_op jit(solution)/shard_map/ppermute | solution.py:27
  61.0 7.5 %collective-permute-start.12 = (bf16[8,16,1280]{2,1,0:T(8,128)(2,1)S(1)}, bf16[8,16,1280]{2,1,0:T(8,128)(2,1)S(1)}, u32[]{:S(2)}, u32[]{:S(2)}) collective-permute-start(bf16[8,16,1280]{2,1,0:T(8,128)(2,1)S(1)} %constant_dynamic-update-slice_fusion), channel_id=1, source_target_pairs={{0,32},{1,33},{2,34},{3,35},{4,36},{5,37},{6,38},{7,39},{8,40},{9,... | collective-permute-start | bytes 983048 | tf_op jit(solution)/shard_map/ppermute | solution.py:27
  68.6 17.4 %collective-permute-start.15 = (bf16[8,8,16,1280]{3,2,1,0:T(8,128)(2,1)S(1)}, bf16[8,8,16,1280]{3,2,1,0:T(8,128)(2,1)}, u32[]{:S(2)}, u32[]{:S(2)}) collective-permute-start(bf16[8,8,16,1280]{3,2,1,0:T(8,128)(2,1)S(1)} %bitcast_dynamic-update-slice_fusion.own_s.refs_3_.refs_5_.refs_4_), channel_id=1, source_target_pairs={{0,16},{1,17},{2,18},{3,19},{4,20},{5,21},{6,22},{7,23},{8,24},{9,... | collective-permute-start | bytes 7864328 | tf_op jit(solution)/shard_map/ppermute | solution.py:27
  77.6 5.2 %collective-permute-start.17 = (bf16[128,512]{1,0:T(8,128)(2,1)S(1)}, bf16[128,512]{1,0:T(8,128)(2,1)S(1)}, u32[]{:S(2)}, u32[]{:S(2)}) collective-permute-start(bf16[128,512]{1,0:T(8,128)(2,1)S(1)} %slice.15), channel_id=1, source_target_pairs={{0,14},{1,15},{2,0},{3,1},{4,2},{5,3},{6,4},{7,5},{8,6},{9,7},{10,... | collective-permute-start | bytes 393224 | tf_op jit(solution)/shard_map/ppermute | solution.py:27
  79.3 6.1 %collective-permute-start.16 = (bf16[128,512]{1,0:T(8,128)(2,1)S(1)}, bf16[128,512]{1,0:T(8,128)(2,1)S(1)}, u32[]{:S(2)}, u32[]{:S(2)}) collective-permute-start(bf16[128,512]{1,0:T(8,128)(2,1)S(1)} %slice.14), channel_id=1, source_target_pairs={{0,2},{1,3},{2,4},{3,5},{4,6},{5,7},{6,8},{7,9},{8,10},{9,11},{10,... | collective-permute-start | bytes 393224 | tf_op jit(solution)/shard_map/ppermute | solution.py:27
  93.0 23.4 %all-to-all-start.1 = ((bf16[8,64,512]{2,1,0:T(8,128)(2,1)}), bf16[8,64,512]{2,1,0:T(8,128)(2,1)S(1)}, u32[]{:S(2)}, u32[]{:S(2)}) async-start(bf16[8,64,512]{2,1,0:T(8,128)(2,1)} %get-tuple-element.64), calls=%async_computation.1 | async-start | bytes 1048576 | tf_op jit(solution)/shard_map/all_to_all | solution.py:31
  117.3 21.4 %all-to-all-start.2 = ((bf16[8,64,512]{2,1,0:T(8,128)(2,1)}), bf16[8,64,512]{2,1,0:T(8,128)(2,1)S(1)}, u32[]{:S(2)}, u32[]{:S(2)}) async-start(bf16[8,64,512]{2,1,0:T(8,128)(2,1)} %broadcast_in_dim.20), calls=%async_computation.2 | async-start | bytes 1048576 | tf_op jit(solution)/shard_map/all_to_all | solution.py:31
  143.1 23.9 %all-to-all-start.3 = ((bf16[32,32,512]{2,1,0:T(8,128)(2,1)}), bf16[32,32,512]{2,1,0:T(8,128)(2,1)S(1)}, u32[]{:S(2)}, u32[]{:S(2)}) async-start(bf16[32,32,512]{2,1,0:T(8,128)(2,1)} %numer.1), calls=%async_computation.3 | async-start | bytes 2097152 | tf_op jit(solution)/shard_map/all_to_all | solution.py:372
  165.6 13.3 %collective-permute-start.18 = (bf16[512,512]{1,0:T(8,128)(2,1)}, bf16[512,512]{1,0:T(8,128)(2,1)S(1)}, u32[]{:S(2)}, u32[]{:S(2)}) collective-permute-start(bf16[512,512]{1,0:T(8,128)(2,1)} %get-tuple-element.82), channel_id=1, source_target_pairs={{0,1},{1,0},{2,3},{3,2},{4,5},{5,4},{6,7},{7,6},{8,9},{9,8},{10,11... | collective-permute-start | bytes 1572872 | tf_op jit(solution)/shard_map/ppermute | solution.py:27
  168.0 20.8 %all-to-all-start.4 = ((bf16[16,32,512]{2,1,0:T(8,128)(2,1)}), bf16[16,32,512]{2,1,0:T(8,128)(2,1)S(1)}, u32[]{:S(2)}, u32[]{:S(2)}) async-start(bf16[16,32,512]{2,1,0:T(8,128)(2,1)} %broadcast_in_dim.23), calls=%async_computation.4 | async-start | bytes 1048576 | tf_op jit(solution)/shard_map/all_to_all | solution.py:374
  (10 other events, 132.3 us)

commit v4 on v3

--- a/solution.py
+++ b/solution.py
@@ -12,6 +12,7 @@
 VMEM = 60 * 2**20
 AXES = ("mp", "shard")
 Z_GROUPS = [[z * 2 + xl for z in range(8)] for xl in range(2)]
+CORE_GROUPS = [[q * 2 + c for q in range(8)] for c in range(2)]
 XLO_GROUPS = [[p * 16 + z * 2 + xl for p in range(16) for xl in range(2)] for z in range(8)]
 
 
@@ -39,28 +40,12 @@
     return lax.dot_general(a, b, (((0,), (0,)), ((), ())), preferred_element_type=F4)
 
 
-def gather_both(piece, x, w):
-    tie = lax.optimization_barrier
-    zu, zd = shift(x, z=1), shift(x, z=-1)
-    piece, w = tie((swap_z(piece), shift(w, xl=1)))
-    h, u, d = shift(piece, xh=1), shift(piece, y=1), shift(piece, y=-1)
-    h, u, d, zu, zd = tie((h, u, d, zu, zd))
-    z = [zu, zd]
-    half = piece.shape[0] // 2
-    t0, t1 = shift(u[:half], y=1), shift(d[half:], y=-1)
-    hu, hd = shift(h, y=1), shift(h, y=-1)
-    zu, zd = shift(zu, z=1), shift(zd, z=-1)
-    hu, hd, t0, t1, zu, zd = tie((hu, hd, t0, t1, zu, zd))
-    z += [zu, zd]
-    t = jnp.concatenate([t0, t1], 0)
-    ht = shift(t, xh=1)
-    zu, zd = shift(zu, z=1), shift(zd, z=-1)
-    ht, zu, zd = tie((ht, zu, zd))
-    z += [zu, zd]
-    zu, zd = shift(zu[:128], z=1), shift(zd[128:], z=-1)
-    own = jnp.stack([piece, h, d, hd, t, ht, u, hu], 0)
-    own, other, zu, zd = tie((own, shift(own, c=1), zu, zd))
-    return own, other, w, [x, z[1], z[3], z[5], zu, zd, z[4], z[2], z[0]]
+def gather_mp(piece, w):
+    n = len(CORE_GROUPS[0])
+    sent = jnp.broadcast_to(piece[None], (n, *piece.shape)).reshape(n * piece.shape[0], *piece.shape[1:])
+    own = lax.all_to_all(sent, "mp", 0, 0, tiled=True, axis_index_groups=CORE_GROUPS)
+    own, w = lax.optimization_barrier((own.reshape(n, *piece.shape), shift(w, xl=1)))
+    return own, shift(own, c=1), w
 
 
 def prepare_kernel(info, bank, ids, gains, piece_out, cols_out, total, column, pick):
@@ -142,7 +127,7 @@
             for slot in range(8):
                 m = slot_model(info, core, slot)
                 table[i, pl.ds(pl.multiple_of(m * 16, 16), 16), :] = src[slot, i, :, 0:1024]
-        extra = own_s[0, i, :, 1024:1152].astype(F4)
+        extra = own_s[info[3] * 2 + info[4], i, :, 1024:1152].astype(F4)
         pick, scale = [], []
         for t in range(4):
             at = t * 32
@@ -215,18 +200,13 @@
     )(info, calib, model_out, diag, weights)
 
 
-ORDER = (0, 7, 1, 6, 2, 5, 3, 4)
-
-
 def slot_model(info, core, slot):
-    y, xh, c = info[3], info[4], info[5]
-    return lax.rem(y + slot // 2, 4) * 4 + (xh ^ (slot % 2)) * 2 + (c ^ core)
+    return slot * 2 + (info[5] ^ core)
 
 
 def gram_kernel(first, last, info, *refs):
     refs = list(refs)
-    blocks = [refs.pop(0) for _ in range(3 if last else 2)]
-    own_s, other_s = refs.pop(0), refs.pop(0)
+    block, own_s, other_s = refs.pop(0), refs.pop(0), refs.pop(0)
     if first:
         own_g, other_g = refs.pop(0), refs.pop(0)
     else:
@@ -260,16 +240,8 @@
                         tile = jnp.where(b % 2 == 0, tile[0:4], tile[4:8])
                         row += [tile[i : i + 1] for i in range(4)]
                     gains[pl.ds(m, 1), :] = jnp.concatenate(row, 1)
-        table[:, 0:512] = blocks[0][...]
-
-    @pl.when(step == 1)
-    def _():
-        if last:
-            table[0:128, 0:512] = blocks[1][...]
-            table[128:256, 0:512] = blocks[2][...]
-        else:
-            table[:, 0:512] = blocks[1][...]
-
+
+    table[:, 0:512] = block[0]
     lane = lax.broadcasted_iota(jnp.int32, (16, 256), 1).astype(F4)
     models = []
     for core in range(2):
@@ -308,9 +280,9 @@
 
 def gram_call(i, info, blocks, own_s, other_s, gains, before):
     first, last = i == 0, i == 3
-    k0, k1 = ORDER[2 * i], ORDER[2 * i + 1]
     whole = lambda shape: pl.BlockSpec(shape, lambda j, info: (0,) * len(shape))
-    by_z = pl.BlockSpec((8, 1, 16, 1280), lambda j, info: (0, (info[6] + k0 + j * (k1 - k0) + 8) % 8, 0, 0))
+    by_z = pl.BlockSpec((8, 1, 16, 1280), lambda j, info: (0, 2 * i + j, 0, 0))
+    block = pl.BlockSpec((1, 256, 512), lambda j, info: (2 * i + j, 0, 0))
     gain_view = pl.BlockSpec((8, 8, 16, 128), lambda j, info: (0, 0, 0, 9))
     shapes = [jax.ShapeDtypeStruct((512, 1024), F4)]
     if last:
@@ -319,13 +291,13 @@
         shapes.append(jax.ShapeDtypeStruct((16, 1536), F4))
     extra = [own_s, other_s] if first else [gains, before]
     extra_specs = [gain_view, gain_view] if first else [whole((16, 1536)), whole((512, 1024))]
-    operands = [info, *blocks, own_s, other_s, *extra]
+    operands = [info, blocks, own_s, other_s, *extra]
     return pl.pallas_call(
         lambda *refs: gram_kernel(first, last, *refs),
         grid_spec=pltpu.PrefetchScalarGridSpec(
             num_scalar_prefetch=1,
             grid=(2,),
-            in_specs=[whole(b.shape) for b in blocks] + [by_z, by_z] + extra_specs,
+            in_specs=[block, by_z, by_z] + extra_specs,
             out_specs=[whole(o.shape) for o in shapes],
             scratch_shapes=([pltpu.VMEM((512, 1024), F4)] if last else [])
             + [
@@ -352,23 +324,24 @@
     weights = proj_slabs[0]
 
     piece, bank_cols = prepare(info, bank, calib_ids, norm_gains)
-    own_s, other_s, weights_other, b = gather_both(piece, bank_cols, weights)
+    blocks = lax.all_gather(bank_cols, "shard", axis=0, axis_index_groups=Z_GROUPS)
+    own_s, other_s, weights_other = gather_mp(swap_z(piece), weights)
     both = jnp.concatenate([weights, weights_other], 0)
 
     partial_out, calib, diag = project(info, own_s, other_s, norm_gains, both)
     tie = lax.optimization_barrier
     partial_out, info = tie((partial_out, info))
-    acc, gains = gram_call(0, info, [b[0], b[8]], own_s, other_s, None, None)
+    acc, gains = gram_call(0, info, blocks, own_s, other_s, None, None)
     partial_out, gains = tie((swap_z(partial_out), gains))
     model_out = jnp.sum(partial_out.astype(F4), 0).astype(BF)
     model_out, info = tie((jnp.broadcast_to(model_out[None], (8, 64, 512)), info))
-    (acc,) = gram_call(1, info, [b[1], b[7]], own_s, other_s, gains, acc)
+    (acc,) = gram_call(1, info, blocks, own_s, other_s, gains, acc)
     model_out, acc = tie((swap_z(model_out), acc))
 
     numer = numer_call(info, calib, model_out.reshape(512, 512), diag, both)
     numer, info = tie((numer, info))
-    (acc,) = gram_call(2, info, [b[2], b[6]], own_s, other_s, gains, acc)
-    near, far = gram_call(3, info, [b[3], b[4], b[5]], own_s, other_s, gains, acc)
+    (acc,) = gram_call(2, info, blocks, own_s, other_s, gains, acc)
+    near, far = gram_call(3, info, blocks, own_s, other_s, gains, acc)
     numer, near = tie((lax.all_to_all(numer, AXES, 0, 0, tiled=True, axis_index_groups=XLO_GROUPS), near))
     numer = jnp.sum(numer.astype(F4), 0).astype(BF)
     numer = lax.all_to_all(jnp.broadcast_to(numer[None], (16, 32, 512)), "mp", 0, 0, tiled=True)

time: 191 us -> 201 us (1.052)
  starting transfers between devices: 66.5 us -> 34.5 us
  blocking collectives: 0 us -> 20.7 us
  between operations: 0.9 us -> 14.1 us
  waiting for transfers between devices: 64.6 us -> 71.8 us
    ppermute x19 -> x3, starting transfers between devices: 36.5 us -> 5.26 us  [shift(): return lax.ppermute(x, AXES, pairs)]
    all_to_all x0 -> x1, blocking collectives: none -> 20.7 us  [swap_z(): lax.all_to_all(x, 'shard', 0, 0, tiled=True, axis_index_groups=Z_GROUPS)]
    all_to_all x3 -> x2, starting transfers between devices: 18 us -> 6.98 us  [swap_z(): lax.all_to_all(x, 'shard', 0, 0, tiled=True, axis_index_groups=Z_GROUPS)]
    all_to_all x0 -> x1, starting transfers between devices: none -> 6.76 us  [gather_mp(): lax.all_to_all(sent, 'mp', 0, 0, tiled=True, axis_index_groups=CORE_GROUPS)]
    ppermute x19 -> x3, waiting for transfers between devices: 37.1 us -> 43.8 us  [shift(): return lax.ppermute(x, AXES, pairs)]
    all_to_all x1, starting transfers between devices: 4.96 us -> 8.38 us  [local(): lax.all_to_all(numer, AXES, 0, 0, tiled=True, axis_index_groups=XLO_GROUPS)]
    all_to_all x3 -> x2, waiting for transfers between devices: 18.7 us -> 18.9 us  [swap_z(): lax.all_to_all(x, 'shard', 0, 0, tiled=True, axis_index_groups=Z_GROUPS)]
  transfers between devices with their start and end apart: 24 -> 9, of which waited for: 15 -> 6; matrix products, arithmetic and copies ran while one was open for 2% -> 2% of each run, Pallas kernels for 18% -> 20%
where the time goes in v4:
time: 201 us; the launch traced here: 200 us
  waiting for transfers between devices  71.8 us (36%)
  Pallas kernels  49.6 us (25%)
  starting transfers between devices  34.5 us (17%)
  blocking collectives  20.7 us (10%)
  between operations  14.1 us (7%)
  local copies, waits for them, and re-layouts  4.91 us (2%)
  other arithmetic  4.62 us (2%)
    ppermute x3, waiting for transfers between devices, shift(): return lax.ppermute(x, AXES, pairs)  43.8 us
    pallas_call x4, Pallas kernels, gram_call(): pl.pallas_call(lambda *refs: gram_kernel(first, last, *refs), grid_spec=p...  34 us
    all_to_all x1, blocking collectives, swap_z(): lax.all_to_all(x, 'shard', 0, 0, tiled=True, axis_index_groups=Z_GROUPS)  20.7 us
    all_to_all x2, waiting for transfers between devices, swap_z(): lax.all_to_all(x, 'shard', 0, 0, tiled=True, axis_index_groups=Z_GROUPS)  18.9 us
    all_to_all x1, waiting for transfers between devices, local(): lax.all_to_all(jnp.broadcast_to(numer[None], (16, 32, 512)), 'mp', 0, 0,...  8.72 us
    all_to_all x1, starting transfers between devices, local(): lax.all_to_all(numer, AXES, 0, 0, tiled=True, axis_index_groups=XLO_GROUPS)  8.38 us
    all_to_all x1, starting transfers between devices, local(): lax.all_to_all(jnp.broadcast_to(numer[None], (16, 32, 512)), 'mp', 0, 0,...  7.03 us
    all_to_all x2, starting transfers between devices, swap_z(): lax.all_to_all(x, 'shard', 0, 0, tiled=True, axis_index_groups=Z_GROUPS)  6.98 us
  transfers between devices with their start and end apart: 9, of which 6 were waited for; matrix products, arithmetic and copies ran while one was open for 2% of the time, Pallas kernels for 20%

profile of v4, /device:TPU:1, one launch (start us, length us, event | category | flops | bytes accessed | tf_op | source)
XLA Modules:
  0.0 200.1 jit_solution(16959767034963282629)
XLA Ops:
  7.9 5.3 %prepare.1 = (bf16[8,16,1280]{2,1,0:T(8,128)(2,1)}, bf16[256,512]{1,0:T(8,128)(2,1)}) custom-call(s32[7]{0:T(128)} %stack.31.info.refs_0_, bf16[256,8192]{1,0:T(8,128)(2,1)} %bank.1, s32[1,64]{1,0:T(1,128)} %ids.1, f32[1,8192]{1,0:T(1,128)} %gains.3), custom_call_target="tpu_custom_call" | custom-call | flops 268435456 | bytes 5242880 | tf_op jit(solution)/shard_map/prepare/pallas_call | solution.py:104
  13.1 20.7 %all_to_all.30 = bf16[8,16,1280]{2,1,0:T(8,128)(2,1)S(1)} all-to-all(bf16[8,16,1280]{2,1,0:T(8,128)(2,1)} %get-tuple-element.25), channel_id=1, replica_groups={{0,2,4,6,8,10,12,14},{1,3,5,7,9,11,13,15},{16,18,20,22,24,26,28,30},{17..., dimensions={0} | all-to-all | bytes 655360 | tf_op jit(solution)/shard_map/all_to_all | solution.py:32
  33.8 1.7 broadcast_in_dim.12
  35.6 6.8 %all-to-all-start.1 = ((bf16[64,16,1280]{2,1,0:T(8,128)(2,1)}), bf16[64,16,1280]{2,1,0:T(8,128)(2,1)S(1)}, u32[]{:S(2)}, u32[]{:S(2)}) async-start(bf16[64,16,1280]{2,1,0:T(8,128)(2,1)} %bitcast.22), calls=%async_computation.1 | async-start | bytes 5242880 | tf_op jit(solution)/shard_map/all_to_all | solution.py:46
  43.1 37.4 %collective-permute-done = bf16[512,512]{1,0:T(8,128)(2,1)} collective-permute-done((bf16[512,512]{1,0:T(8,128)(2,1)S(1)}, bf16[512,512]{1,0:T(8,128)(2,1)}, u32[]{:S(2)}, u32[]{:S(2)}) %collective-permute-start) | collective-permute-done | bytes 524320 | tf_op jit(solution)/shard_map/ppermute | solution.py:28
  80.4 3.5 %collective-permute-start.1 = (bf16[8,8,16,1280]{3,2,1,0:T(8,128)(2,1)S(1)}, bf16[8,8,16,1280]{3,2,1,0:T(8,128)(2,1)}, u32[]{:S(2)}, u32[]{:S(2)}) collective-permute-start(bf16[8,8,16,1280]{3,2,1,0:T(8,128)(2,1)S(1)} %bitcast.15), channel_id=1, source_target_pairs={{0,16},{1,17},{2,18},{3,19},{4,20},{5,21},{6,22},{7,23},{8,24},{9,... | collective-permute-start | bytes 7864328 | tf_op jit(solution)/shard_map/ppermute | solution.py:28
  83.9 2.1 %pad_maximum_fusion.weights = bf16[1024,512]{1,0:T(8,128)(2,1)} fusion(bf16[512,512]{1,0:T(8,128)(2,1)} %collective-permute-done, bf16[512,512]{1,0:T(8,128)(2,1)S(1)} %bitcast.25), kind=kLoop, calls=%fused_computation | loop fusion | flops 2097152 | bytes 2097152 | tf_op jit(solution)/shard_map/concatenate | solution.py:329
  86.0 2.6 %collective-permute-done.1.other_s.refs_3_.refs_5_ = bf16[8,8,16,1280]{3,2,1,0:T(8,128)(2,1)} collective-permute-done((bf16[8,8,16,1280]{3,2,1,0:T(8,128)(2,1)S(1)}, bf16[8,8,16,1280]{3,2,1,0:T(8,128)(2,1)}, u32[]{:S(2)}, u32[]{:S(2)}) %collective-permute-start.1) | collective-permute-done | bytes 2621472 | tf_op jit(solution)/shard_map/ppermute | solution.py:28
  88.6 6.8 %project.1 = (bf16[8,64,512]{2,1,0:T(8,128)(2,1)}, bf16[512,1024]{1,0:T(8,128)(2,1)}, f32[1,1024]{1,0:T(1,128)}) custom-call(s32[7]{0:T(128)} %stack.31.info.refs_0_, bf16[8,8,16,1280]{3,2,1,0:T(8,128)(2,1)} %bitcast.16, bf16[8,8,16,1280]{3,2,1,0:T(8,128)(2,1)} %collective-permute-done.1.other_s.refs_3_.refs_5_, f32[1,8192]{1,0:T(1,128)} %gains.3, ...), custom_call_target="tpu_custom_call" | custom-call | flops 1073741824 | bytes 8388608 | tf_op jit(solution)/shard_map/project/pallas_call | solution.py:157
  95.4 3.5 %all-to-all-start.2 = ((bf16[8,64,512]{2,1,0:T(8,128)(2,1)}), bf16[8,64,512]{2,1,0:T(8,128)(2,1)S(1)}, u32[]{:S(2)}, u32[]{:S(2)}) async-start(bf16[8,64,512]{2,1,0:T(8,128)(2,1)} %get-tuple-element.29), calls=%async_computation.2 | async-start | bytes 1048576 | tf_op jit(solution)/shard_map/all_to_all | solution.py:32
  98.9 8.2 %gram0.1 = (f32[512,1024]{1,0:T(8,128)}, f32[16,1536]{1,0:T(8,128)}) custom-call(s32[7]{0:T(128)} %stack.31.info.refs_0_, bf16[8,256,512]{2,1,0:T(8,128)(2,1)} %bitcast.26, bf16[8,8,16,1280]{3,2,1,0:T(8,128)(2,1)} %bitcast.17, bf16[8,8,16,1280]{3,2,1,0:T(8,128)(2,1)} %collective-permute-done.1.other_s.refs_3_.refs_5_, bf16[8,8,16,1280]{3,2,1,0:T(8,128)(2,1)} %bitcast.18, ...), custom_call_target="tpu_custom_call" | custom-call | flops 4294967296 | bytes 6291456 | tf_op jit(solution)/shard_map/gram0/pallas_call | solution.py:295
  107.1 9.7 %all-to-all-done.2 = bf16[8,64,512]{2,1,0:T(8,128)(2,1)S(1)} async-done(((bf16[8,64,512]{2,1,0:T(8,128)(2,1)}), bf16[8,64,512]{2,1,0:T(8,128)(2,1)S(1)}, u32[]{:S(2)}, u32[]{:S(2)}) %all-to-all-start.2) | async-done | bytes 524320 | tf_op jit(solution)/shard_map/all_to_all | solution.py:32
  117.7 3.5 %all-to-all-start.3 = ((bf16[8,64,512]{2,1,0:T(8,128)(2,1)}), bf16[8,64,512]{2,1,0:T(8,128)(2,1)S(1)}, u32[]{:S(2)}, u32[]{:S(2)}) async-start(bf16[8,64,512]{2,1,0:T(8,128)(2,1)} %broadcast_in_dim.13), calls=%async_computation.3 | async-start | bytes 1048576 | tf_op jit(solution)/shard_map/all_to_all | solution.py:32
  121.2 8.7 %gram1.1.refs_5_ = f32[512,1024]{1,0:T(8,128)} custom-call(s32[7]{0:T(128)} %stack.31.info.refs_0_, bf16[8,256,512]{2,1,0:T(8,128)(2,1)} %bitcast.27, bf16[8,8,16,1280]{3,2,1,0:T(8,128)(2,1)} %bitcast.19, bf16[8,8,16,1280]{3,2,1,0:T(8,128)(2,1)} %collective-permute-done.1.other_s.refs_3_.refs_5_, ...), custom_call_target="tpu_custom_call", output_to_operand_aliasing={{}: (5, {})} | custom-call | flops 4294967296 | bytes 6291456 | tf_op jit(solution)/shard_map/gram1/pallas_call | solution.py:295
  129.9 9.2 %all-to-all-done.3 = bf16[8,64,512]{2,1,0:T(8,128)(2,1)S(1)} async-done(((bf16[8,64,512]{2,1,0:T(8,128)(2,1)}), bf16[8,64,512]{2,1,0:T(8,128)(2,1)S(1)}, u32[]{:S(2)}, u32[]{:S(2)}) %all-to-all-start.3) | async-done | bytes 524320 | tf_op jit(solution)/shard_map/all_to_all | solution.py:32
  139.9 3.5 %numer.1 = bf16[32,32,512]{2,1,0:T(8,128)(2,1)} custom-call(s32[7]{0:T(128)} %stack.31.info.refs_0_, bf16[512,1024]{1,0:T(8,128)(2,1)} %get-tuple-element.35.calib, bf16[512,512]{1,0:T(8,128)(2,1)} %bitcast.23, f32[1,1024]{1,0:T(1,128)} %get-tuple-element.40.diag, bf16[1024,512]{1,0:T(8,128)(2,1)} %pad_maximum_fusion.weights), custom_call_target="tpu_custom_call" | custom-call | flops 536870912 | bytes 4194304 | tf_op jit(solution)/shard_map/numer/pallas_call | solution.py:192
  143.4 8.4 %all-to-all-start.4 = ((bf16[32,32,512]{2,1,0:T(8,128)(2,1)}), bf16[32,32,512]{2,1,0:T(8,128)(2,1)S(1)}, u32[]{:S(2)}, u32[]{:S(2)}) async-start(bf16[32,32,512]{2,1,0:T(8,128)(2,1)} %numer.1), calls=%async_computation.4 | async-start | bytes 2097152 | tf_op jit(solution)/shard_map/all_to_all | solution.py:345
  151.8 8.7 %gram2.1.refs_5_ = f32[512,1024]{1,0:T(8,128)} custom-call(s32[7]{0:T(128)} %stack.31.info.refs_0_, bf16[8,256,512]{2,1,0:T(8,128)(2,1)} %bitcast.28, bf16[8,8,16,1280]{3,2,1,0:T(8,128)(2,1)} %bitcast.20, bf16[8,8,16,1280]{3,2,1,0:T(8,128)(2,1)} %collective-permute-done.1.other_s.refs_3_.refs_5_, ...), custom_call_target="tpu_custom_call", output_to_operand_aliasing={{}: (5, {})} | custom-call | flops 4294967296 | bytes 6291456 | tf_op jit(solution)/shard_map/gram2/pallas_call | solution.py:295
  160.4 8.5 %gram3.1 = (f32[512,512]{1,0:T(8,128)}, bf16[512,512]{1,0:T(8,128)(2,1)}) custom-call(s32[7]{0:T(128)} %stack.31.info.refs_0_, bf16[8,256,512]{2,1,0:T(8,128)(2,1)} %bitcast.29, bf16[8,8,16,1280]{3,2,1,0:T(8,128)(2,1)} %bitcast.21, bf16[8,8,16,1280]{3,2,1,0:T(8,128)(2,1)} %collective-permute-done.1.other_s.refs_3_.refs_5_, ...), custom_call_target="tpu_custom_call" | custom-call | flops 4294967296 | bytes 6291456 | tf_op jit(solution)/shard_map/gram3/pallas_call | solution.py:295
  169.0 1.4 collective-permute-start.2
  171.4 7.0 %all-to-all-start.5 = ((bf16[16,32,512]{2,1,0:T(8,128)(2,1)}), bf16[16,32,512]{2,1,0:T(8,128)(2,1)S(1)}, u32[]{:S(2)}, u32[]{:S(2)}) async-start(bf16[16,32,512]{2,1,0:T(8,128)(2,1)} %broadcast_in_dim.30), calls=%async_computation.5 | async-start | bytes 1048576 | tf_op jit(solution)/shard_map/all_to_all | solution.py:347
  178.4 3.9 %collective-permute-done.2 = bf16[512,512]{1,0:T(8,128)(2,1)S(1)} collective-permute-done((bf16[512,512]{1,0:T(8,128)(2,1)}, bf16[512,512]{1,0:T(8,128)(2,1)S(1)}, u32[]{:S(2)}, u32[]{:S(2)}) %collective-permute-start.2) | collective-permute-done | bytes 524320 | tf_op jit(solution)/shard_map/ppermute | solution.py:28
  182.3 1.2 select_multiply_fusion
  183.4 8.7 %all-to-all-done.5 = bf16[16,32,512]{2,1,0:T(8,128)(2,1)S(1)} async-done(((bf16[16,32,512]{2,1,0:T(8,128)(2,1)}), bf16[16,32,512]{2,1,0:T(8,128)(2,1)S(1)}, u32[]{:S(2)}, u32[]{:S(2)}) %all-to-all-start.5) | async-done | bytes 524320 | tf_op jit(solution)/shard_map/all_to_all | solution.py:347
  (20 shorter events, 5.3 us)
Async XLA Ops:
  35.6 6.8 %copy-start.3 = (bf16[1,512,512]{2,1,0:T(8,128)(2,1)S(1)}, bf16[1,512,512]{2,1,0:T(8,128)(2,1)}, u32[]{:S(2)}) copy-start(bf16[1,512,512]{2,1,0:T(8,128)(2,1)} %param.7) | copy-start | bytes 1572868
  35.6 44.9 %all-to-all-start.1 = ((bf16[64,16,1280]{2,1,0:T(8,128)(2,1)}), bf16[64,16,1280]{2,1,0:T(8,128)(2,1)S(1)}, u32[]{:S(2)}, u32[]{:S(2)}) async-start(bf16[64,16,1280]{2,1,0:T(8,128)(2,1)} %bitcast.22), calls=%async_computation.1 | async-start | bytes 5242880 | tf_op jit(solution)/shard_map/all_to_all | solution.py:46
  42.3 56.6 %all-gather.3.cloned.1.call-start = ((), (), s32[]{:S(2)}) async-start(), calls=%async_computation.6 | async-start | bytes 2359296 | tf_op jit(solution)/shard_map/all_gather | solution.py:327
  42.4 38.0 %collective-permute-start = (bf16[512,512]{1,0:T(8,128)(2,1)S(1)}, bf16[512,512]{1,0:T(8,128)(2,1)}, u32[]{:S(2)}, u32[]{:S(2)}) collective-permute-start(bf16[512,512]{1,0:T(8,128)(2,1)S(1)} %bitcast.24), channel_id=1, source_target_pairs={{0,1},{1,0},{2,3},{3,2},{4,5},{5,4},{6,7},{7,6},{8,9},{9,8},{10,11... | collective-permute-start | bytes 1572872 | tf_op jit(solution)/shard_map/ppermute | solution.py:28
  80.4 8.2 %copy-start = (bf16[64,16,1280]{2,1,0:T(8,128)(2,1)}, bf16[64,16,1280]{2,1,0:T(8,128)(2,1)S(1)}, u32[]{:S(2)}) copy-start(bf16[64,16,1280]{2,1,0:T(8,128)(2,1)S(1)} %all-to-all-done.1) | copy-start | bytes 7864324
  80.4 8.2 %collective-permute-start.1 = (bf16[8,8,16,1280]{3,2,1,0:T(8,128)(2,1)S(1)}, bf16[8,8,16,1280]{3,2,1,0:T(8,128)(2,1)}, u32[]{:S(2)}, u32[]{:S(2)}) collective-permute-start(bf16[8,8,16,1280]{3,2,1,0:T(8,128)(2,1)S(1)} %bitcast.15), channel_id=1, source_target_pairs={{0,16},{1,17},{2,18},{3,19},{4,20},{5,21},{6,22},{7,23},{8,24},{9,... | collective-permute-start | bytes 7864328 | tf_op jit(solution)/shard_map/ppermute | solution.py:28
  95.4 21.4 %all-to-all-start.2 = ((bf16[8,64,512]{2,1,0:T(8,128)(2,1)}), bf16[8,64,512]{2,1,0:T(8,128)(2,1)S(1)}, u32[]{:S(2)}, u32[]{:S(2)}) async-start(bf16[8,64,512]{2,1,0:T(8,128)(2,1)} %get-tuple-element.29), calls=%async_computation.2 | async-start | bytes 1048576 | tf_op jit(solution)/shard_map/all_to_all | solution.py:32
  117.7 21.4 %all-to-all-start.3 = ((bf16[8,64,512]{2,1,0:T(8,128)(2,1)}), bf16[8,64,512]{2,1,0:T(8,128)(2,1)S(1)}, u32[]{:S(2)}, u32[]{:S(2)}) async-start(bf16[8,64,512]{2,1,0:T(8,128)(2,1)} %broadcast_in_dim.13), calls=%async_computation.3 | async-start | bytes 1048576 | tf_op jit(solution)/shard_map/all_to_all | solution.py:32
  139.1 0.8 copy-start.1
  143.4 27.0 %all-to-all-start.4 = ((bf16[32,32,512]{2,1,0:T(8,128)(2,1)}), bf16[32,32,512]{2,1,0:T(8,128)(2,1)S(1)}, u32[]{:S(2)}, u32[]{:S(2)}) async-start(bf16[32,32,512]{2,1,0:T(8,128)(2,1)} %numer.1), calls=%async_computation.4 | async-start | bytes 2097152 | tf_op jit(solution)/shard_map/all_to_all | solution.py:345
  169.0 13.3 %copy-start.2 = (f32[512,512]{1,0:T(8,128)S(1)}, f32[512,512]{1,0:T(8,128)}, u32[]{:S(2)}) copy-start(f32[512,512]{1,0:T(8,128)} %get-tuple-element.45) | copy-start | bytes 3145732
  169.0 13.3 %collective-permute-start.2 = (bf16[512,512]{1,0:T(8,128)(2,1)}, bf16[512,512]{1,0:T(8,128)(2,1)S(1)}, u32[]{:S(2)}, u32[]{:S(2)}) collective-permute-start(bf16[512,512]{1,0:T(8,128)(2,1)} %get-tuple-element.46), channel_id=1, source_target_pairs={{0,1},{1,0},{2,3},{3,2},{4,5},{5,4},{6,7},{7,6},{8,9},{9,8},{10,11... | collective-permute-start | bytes 1572872 | tf_op jit(solution)/shard_map/ppermute | solution.py:28
  171.4 20.8 %all-to-all-start.5 = ((bf16[16,32,512]{2,1,0:T(8,128)(2,1)}), bf16[16,32,512]{2,1,0:T(8,128)(2,1)S(1)}, u32[]{:S(2)}, u32[]{:S(2)}) async-start(bf16[16,32,512]{2,1,0:T(8,128)(2,1)} %broadcast_in_dim.30), calls=%async_computation.5 | async-start | bytes 1048576 | tf_op jit(solution)/shard_map/all_to_all | solution.py:347
Sparse Core Ops, SparseCore 0:
  44.9 36.1 all-gather.2

commit v5 on v4

--- a/solution.py
+++ b/solution.py
@@ -40,15 +40,13 @@
     return lax.dot_general(a, b, (((0,), (0,)), ((), ())), preferred_element_type=F4)
 
 
-def gather_mp(piece, w):
-    n = len(CORE_GROUPS[0])
-    sent = jnp.broadcast_to(piece[None], (n, *piece.shape)).reshape(n * piece.shape[0], *piece.shape[1:])
+def gather_mp(sent, w):
     own = lax.all_to_all(sent, "mp", 0, 0, tiled=True, axis_index_groups=CORE_GROUPS)
-    own, w = lax.optimization_barrier((own.reshape(n, *piece.shape), shift(w, xl=1)))
+    own, w = lax.optimization_barrier((own.reshape(8, 8, 16, 1152), shift(w, xl=1)))
     return own, shift(own, c=1), w
 
 
-def prepare_kernel(info, bank, ids, gains, piece_out, cols_out, total, column, pick):
+def prepare_kernel(info, bank, ids, piece_out, cols_out, total, pick):
     zz = pl.program_id(0)
     p, s, xl = info[0], info[1], info[2]
 
@@ -59,7 +57,6 @@
         row_ids = (ids[...] - s * 256).astype(F4)
         row_ids = jnp.sum(jnp.where(i0 == i1, row_ids, 0.0), axis=1, keepdims=True)
         lane = lax.broadcasted_iota(jnp.int32, (64, 256), 1).astype(F4)
-        column[...] = jnp.broadcast_to(row_ids, (64, 128))
         pick[...] = jnp.where(row_ids == lane, 1.0, 0.0).astype(BF)
         total[...] = jnp.zeros_like(total)
 
@@ -78,63 +75,86 @@
 
     @pl.when(zz == 3)
     def _():
-        row_ids = column[:, 0:1]
         scale = lax.rsqrt(jnp.sum(total[...], axis=1, keepdims=True) / 8192 + EPSILON)
+        i0 = lax.broadcasted_iota(jnp.int32, (64, 64), 0)
+        i1 = lax.broadcasted_iota(jnp.int32, (64, 64), 1)
+        scale = jnp.sum(jnp.where(i0 == i1, scale, 0.0), axis=0, keepdims=True)
         hi = scale.astype(BF).astype(F4)
         mid = (scale - hi).astype(BF).astype(F4)
         low = scale - hi - mid
-        lane = lax.broadcasted_iota(jnp.int32, (16, 128), 1)
-        extra = jnp.zeros((16, 128), F4)
-        for q in range(4):
-            part = slice(q * 16, q * 16 + 16)
-            for j, v in enumerate((row_ids, hi, mid, low)):
-                extra = jnp.where(lane == q * 32 + j, v[part], extra)
-        extra = extra.astype(BF)
-        own = gains[:, pl.ds(pl.multiple_of(s // 2 * 1024, 1024), 1024)]
-        own = jnp.concatenate([own[:, i * 128 : i * 128 + 128] for i in range(8)], 0)
-        own_hi = own.astype(BF).astype(F4)
-        own = jnp.concatenate([own_hi, own - own_hi], 0).astype(BF)
+        first = jnp.concatenate([(ids[...] - s * 256).astype(F4), hi], 1)
+        second = jnp.concatenate([mid, low], 1)
+        row = lax.broadcasted_iota(jnp.int32, (16, 128), 0)
+        extra = jnp.where(row == 0, first, jnp.where(row == 1, second, 0.0)).astype(BF)
         for to in range(8):
             piece_out[to, :, 1024:1152] = extra
-            piece_out[to, :, 1152:1280] = own
-
-
-def prepare(info, bank, ids, gains):
+
+
+def prepare(info, bank, ids):
     whole = lambda shape: pl.BlockSpec(shape, lambda i, info: (0,) * len(shape))
     return pl.pallas_call(
         prepare_kernel,
         grid_spec=pltpu.PrefetchScalarGridSpec(
             num_scalar_prefetch=1,
             grid=(4,),
-            in_specs=[pl.BlockSpec((256, 2048), lambda i, info: (0, i)), whole((1, 64)), whole((1, 8192))],
-            out_specs=[whole((8, 16, 1280)), whole((256, 512))],
-            scratch_shapes=[pltpu.VMEM((64, 128), F4), pltpu.VMEM((64, 128), F4), pltpu.VMEM((64, 256), BF)],
+            in_specs=[pl.BlockSpec((256, 2048), lambda i, info: (0, i)), whole((1, 64))],
+            out_specs=[whole((8, 16, 1152)), whole((256, 512))],
+            scratch_shapes=[pltpu.VMEM((64, 128), F4), pltpu.VMEM((64, 256), BF)],
         ),
-        out_shape=[jax.ShapeDtypeStruct((8, 16, 1280), BF), jax.ShapeDtypeStruct((256, 512), BF)],
+        out_shape=[jax.ShapeDtypeStruct((8, 16, 1152), BF), jax.ShapeDtypeStruct((256, 512), BF)],
         compiler_params=pltpu.CompilerParams(dimension_semantics=("arbitrary",), vmem_limit_bytes=VMEM),
         cost_estimate=pl.CostEstimate(flops=2**28, bytes_accessed=5 * 2**20, transcendentals=64),
         name="prepare",
-    )(info, bank, ids, gains)
+    )(info, bank, ids)
+
+
+def address_kernel(info, piece, gains, out):
+    z, xl = info[6], info[2]
+    for q in range(8):
+        out[q * 8 : q * 8 + 8] = piece[...]
+        for i, b in enumerate((2 * q, 2 * q + 1, z * 2 + xl, z * 2 + (1 - xl))):
+            at = b * 512 if i < 2 else pl.multiple_of(b * 512, 512)
+            g = gains[:, pl.ds(at, 512)]
+            g = jnp.concatenate([g[:, j * 128 : j * 128 + 128] for j in range(4)], 0)
+            hi = g.astype(BF).astype(F4)
+            top = piece[i, :, 1024:1152].astype(F4)[0:8]
+            out[q * 8 + i, :, 1024:1152] = jnp.concatenate([top, hi, g - hi], 0).astype(BF)
+
+
+def address(info, piece, gains):
+    return pl.pallas_call(
+        address_kernel,
+        in_specs=[pl.BlockSpec(memory_space=pltpu.SMEM)] + [pl.BlockSpec(memory_space=pltpu.VMEM)] * 2,
+        out_specs=pl.BlockSpec(memory_space=pltpu.VMEM),
+        out_shape=jax.ShapeDtypeStruct((64, 16, 1152), BF),
+        compiler_params=pltpu.CompilerParams(vmem_limit_bytes=VMEM),
+        cost_estimate=pl.CostEstimate(flops=2**20, bytes_accessed=3 * 2**20, transcendentals=0),
+        name="address",
+    )(info, piece, gains)
+
+
+def token_columns(tiles):
+    stacked = jnp.concatenate([t.astype(F4)[0:8] for t in tiles], 0).T
+    out = []
+    for m in range(16):
+        first, second = stacked[:, m * 8 : m * 8 + 1], stacked[:, m * 8 + 1 : m * 8 + 2]
+        out.append((first[0:64], first[64:128] + second[0:64] + second[64:128]))
+    return out
 
 
 def project_kernel(info, own_s, other_s, gains, weights, part_out, calib_out, diag_out, table, calib):
     zz = pl.program_id(0)
     xl, z = info[2], info[6]
-    lane = lax.broadcasted_iota(jnp.int32, (16, 256), 1).astype(F4)
+    lane = lax.broadcasted_iota(jnp.int32, (64, 256), 1).astype(F4)
     for i in range(2):
         for core in range(2):
             src = own_s if core == 0 else other_s
             for slot in range(8):
                 m = slot_model(info, core, slot)
                 table[i, pl.ds(pl.multiple_of(m * 16, 16), 16), :] = src[slot, i, :, 0:1024]
-        extra = own_s[info[3] * 2 + info[4], i, :, 1024:1152].astype(F4)
-        pick, scale = [], []
-        for t in range(4):
-            at = t * 32
-            pick.append(jnp.where(extra[:, at : at + 1] == lane, 1.0, 0.0))
-            scale.append(extra[:, at + 1 : at + 2] + extra[:, at + 2 : at + 3] + extra[:, at + 3 : at + 4])
-        pick = jnp.concatenate(pick, 0).astype(BF)
-        scale = jnp.concatenate(scale, 0)
+        extra = own_s[info[3] * 2 + info[4], i, :, 1024:1152]
+        column, scale = token_columns([extra] * 16)[0]
+        pick = jnp.where(column == lane, 1.0, 0.0).astype(BF)
         rows = pl.ds(pl.multiple_of(zz * 128 + i * 64, 64), 64)
         for j in range(2):
             cols = slice(j * 512, j * 512 + 512)
@@ -153,7 +173,7 @@
 
 def project(info, own_s, other_s, gains, weights):
     whole = lambda shape: pl.BlockSpec(shape, lambda i, info: (0,) * len(shape))
-    by_z = pl.BlockSpec((8, 2, 16, 1280), lambda i, info: (0, i, 0, 0))
+    by_z = pl.BlockSpec((8, 2, 16, 1152), lambda i, info: (0, i, 0, 0))
     return pl.pallas_call(
         project_kernel,
         grid_spec=pltpu.PrefetchScalarGridSpec(
@@ -200,6 +220,9 @@
     )(info, calib, model_out, diag, weights)
 
 
+STEPS = (3, 3, 2)
+
+
 def slot_model(info, core, slot):
     return slot * 2 + (info[5] ^ core)
 
@@ -221,7 +244,6 @@
         acc = refs.pop(0)
     table, pick, scale, calib = refs
     step = pl.program_id(0)
-    p, xl, z = info[0], info[2], info[6]
 
     @pl.when(step == 0)
     def _():
@@ -234,30 +256,26 @@
                 for slot in range(8):
                     m = slot_model(info, core, slot)
                     row = []
-                    for b in (p, z * 2 + xl, z * 2 + (1 - xl)):
-                        tile = src[slot, b // 2].astype(F4)
-                        tile = tile[0:8] + tile[8:16]
-                        tile = jnp.where(b % 2 == 0, tile[0:4], tile[4:8])
+                    for b in (info[5], 2, 3):
+                        tile = src[slot, b].astype(F4)
+                        tile = tile[8:12] + tile[12:16]
                         row += [tile[i : i + 1] for i in range(4)]
                     gains[pl.ds(m, 1), :] = jnp.concatenate(row, 1)
 
     table[:, 0:512] = block[0]
-    lane = lax.broadcasted_iota(jnp.int32, (16, 256), 1).astype(F4)
-    models = []
+    lane = lax.broadcasted_iota(jnp.int32, (64, 256), 1).astype(F4)
+    models, tiles = [], []
     for core in range(2):
         src = own_s if core == 0 else other_s
         for slot in range(8):
             m = slot_model(info, core, slot)
             models.append(m)
             table[pl.ds(pl.multiple_of(m * 16, 16), 16), 512:1536] = src[slot, 0, :, 0:1024]
-            extra = src[slot, 0, :, 1024:1152].astype(F4)
-            for t in range(4):
-                row = (core * 8 + slot) * 64 + t * 16
-                at = t * 32
-                hit = extra[:, at : at + 1] == lane
-                pick[row : row + 16, :] = jnp.where(hit, 1.0, 0.0).astype(BF)
-                value = extra[:, at + 1 : at + 2] + extra[:, at + 2 : at + 3] + extra[:, at + 3 : at + 4]
-                scale[row : row + 16, :] = jnp.broadcast_to(value, (16, 128))
+            tiles.append(src[slot, 0, :, 1024:1152])
+    for m, (column, value) in enumerate(token_columns(tiles)):
+        part = slice(m * 64, m * 64 + 64)
+        pick[part, :] = jnp.where(column == lane, 1.0, 0.0).astype(BF)
+        scale[part, :] = jnp.broadcast_to(value, (64, 128))
 
     for n in range(6):
         cols = slice(n * 256, n * 256 + 256)
@@ -272,18 +290,19 @@
 
     if last:
 
-        @pl.when(step == 1)
+        @pl.when(step == STEPS[-1] - 1)
         def _():
             near[...] = acc[:, 0:512]
             far[...] = acc[:, 512:1024].astype(BF)
 
 
 def gram_call(i, info, blocks, own_s, other_s, gains, before):
-    first, last = i == 0, i == 3
+    first, last = i == 0, i == len(STEPS) - 1
+    start, steps = sum(STEPS[:i]), STEPS[i]
     whole = lambda shape: pl.BlockSpec(shape, lambda j, info: (0,) * len(shape))
-    by_z = pl.BlockSpec((8, 1, 16, 1280), lambda j, info: (0, 2 * i + j, 0, 0))
-    block = pl.BlockSpec((1, 256, 512), lambda j, info: (2 * i + j, 0, 0))
-    gain_view = pl.BlockSpec((8, 8, 16, 128), lambda j, info: (0, 0, 0, 9))
+    by_z = pl.BlockSpec((8, 1, 16, 1152), lambda j, info: (0, start + j, 0, 0))
+    block = pl.BlockSpec((1, 256, 512), lambda j, info: (start + j, 0, 0))
+    gain_view = pl.BlockSpec((8, 8, 16, 128), lambda j, info: (0, 0, 0, 8))
     shapes = [jax.ShapeDtypeStruct((512, 1024), F4)]
     if last:
         shapes = [jax.ShapeDtypeStruct((512, 512), F4), jax.ShapeDtypeStruct((512, 512), BF)]
@@ -296,7 +315,7 @@
         lambda *refs: gram_kernel(first, last, *refs),
         grid_spec=pltpu.PrefetchScalarGridSpec(
             num_scalar_prefetch=1,
-            grid=(2,),
+            grid=(steps,),
             in_specs=[block, by_z, by_z] + extra_specs,
             out_specs=[whole(o.shape) for o in shapes],
             scratch_shapes=([pltpu.VMEM((512, 1024), F4)] if last else [])
@@ -310,7 +329,7 @@
         out_shape=shapes,
         input_output_aliases={} if first or last else {len(operands) - 1: 0},
         compiler_params=pltpu.CompilerParams(dimension_semantics=("arbitrary",), vmem_limit_bytes=VMEM),
-        cost_estimate=pl.CostEstimate(flops=4 * 2**30, bytes_accessed=6 * 2**20, transcendentals=0),
+        cost_estimate=pl.CostEstimate(flops=steps * 2**31, bytes_accessed=6 * 2**20, transcendentals=0),
         name="gram" + str(i),
     )(*operands)
 
@@ -323,9 +342,9 @@
     info = jnp.stack([p, s, xl, y, xh, c, z]).astype(jnp.int32)
     weights = proj_slabs[0]
 
-    piece, bank_cols = prepare(info, bank, calib_ids, norm_gains)
+    piece, bank_cols = prepare(info, bank, calib_ids)
     blocks = lax.all_gather(bank_cols, "shard", axis=0, axis_index_groups=Z_GROUPS)
-    own_s, other_s, weights_other = gather_mp(swap_z(piece), weights)
+    own_s, other_s, weights_other = gather_mp(address(info, swap_z(piece), norm_gains), weights)
     both = jnp.concatenate([weights, weights_other], 0)
 
     partial_out, calib, diag = project(info, own_s, other_s, norm_gains, both)
@@ -340,8 +359,7 @@
 
     numer = numer_call(info, calib, model_out.reshape(512, 512), diag, both)
     numer, info = tie((numer, info))
-    (acc,) = gram_call(2, info, blocks, own_s, other_s, gains, acc)
-    near, far = gram_call(3, info, blocks, own_s, other_s, gains, acc)
+    near, far = gram_call(2, info, blocks, own_s, other_s, gains, acc)
     numer, near = tie((lax.all_to_all(numer, AXES, 0, 0, tiled=True, axis_index_groups=XLO_GROUPS), near))
     numer = jnp.sum(numer.astype(F4), 0).astype(BF)
     numer = lax.all_to_all(jnp.broadcast_to(numer[None], (16, 32, 512)), "mp", 0, 0, tiled=True)

time: 201 us -> 192 us (0.955)
  waiting for transfers between devices: 71.8 us -> 67.6 us
    all_to_all x1, waiting for transfers between devices: 0.01 us -> 5.53 us  [local(): lax.all_to_all(numer, AXES, 0, 0, tiled=True, axis_index_groups=XLO_GROUPS)]
    all_to_all x2, waiting for transfers between devices: 18.9 us -> 14 us  [swap_z(): lax.all_to_all(x, 'shard', 0, 0, tiled=True, axis_index_groups=Z_GROUPS)]
    ppermute x3, waiting for transfers between devices: 43.8 us -> 39.3 us  [shift(): return lax.ppermute(x, AXES, pairs)]
    pallas_call x4 -> x3, Pallas kernels: 34 us -> 30.3 us  [gram_call(): pl.pallas_call(lambda *refs: gram_kernel(first, last, *refs), grid_spec=p...]
    pallas_call x0 -> x1, Pallas kernels: none -> 2.59 us  [address(): pl.pallas_call(address_kernel, in_specs=[pl.BlockSpec(memory_space=pltpu....]
  transfers between devices with their start and end apart: 9 -> 9, of which waited for: 6 -> 7; matrix products, arithmetic and copies ran while one was open for 2% -> 2% of each run, Pallas kernels for 20% -> 20%
where the time goes in v5:
time: 192 us; the launch traced here: 191 us
  waiting for transfers between devices  67.6 us (35%)
  Pallas kernels  48.6 us (25%)
  starting transfers between devices  33.7 us (18%)
  blocking collectives  20 us (10%)
  between operations  14.1 us (7%)
  other arithmetic  3.57 us (2%)
  local copies, waits for them, and re-layouts  3.14 us (2%)
    ppermute x3, waiting for transfers between devices, shift(): return lax.ppermute(x, AXES, pairs)  39.3 us
    pallas_call x3, Pallas kernels, gram_call(): pl.pallas_call(lambda *refs: gram_kernel(first, last, *refs), grid_spec=p...  30.3 us
    all_to_all x1, blocking collectives, swap_z(): lax.all_to_all(x, 'shard', 0, 0, tiled=True, axis_index_groups=Z_GROUPS)  20 us
    all_to_all x2, waiting for transfers between devices, swap_z(): lax.all_to_all(x, 'shard', 0, 0, tiled=True, axis_index_groups=Z_GROUPS)  14 us
    all_to_all x1, starting transfers between devices, local(): lax.all_to_all(numer, AXES, 0, 0, tiled=True, axis_index_groups=XLO_GROUPS)  8.55 us
    all_to_all x1, waiting for transfers between devices, local(): lax.all_to_all(jnp.broadcast_to(numer[None], (16, 32, 512)), 'mp', 0, 0,...  8.06 us
    all_to_all x2, starting transfers between devices, swap_z(): lax.all_to_all(x, 'shard', 0, 0, tiled=True, axis_index_groups=Z_GROUPS)  6.98 us
    pallas_call x1, Pallas kernels, project(): pl.pallas_call(project_kernel, grid_spec=pltpu.PrefetchScalarGridSpec(num...  6.94 us
  transfers between devices with their start and end apart: 9, of which 7 were waited for; matrix products, arithmetic and copies ran while one was open for 2% of the time, Pallas kernels for 20%

profile of v5, /device:TPU:1, one launch (start us, length us, event | category | flops | bytes accessed | tf_op | source)
XLA Modules:
  0.0 190.8 jit_solution(4746166856641539061)
XLA Ops:
  7.8 5.3 %prepare.1 = (bf16[8,16,1152]{2,1,0:T(8,128)(2,1)}, bf16[256,512]{1,0:T(8,128)(2,1)}) custom-call(s32[7]{0:T(128)} %stack.31.info.refs_0_, bf16[256,8192]{1,0:T(8,128)(2,1)} %bank.1, s32[1,64]{1,0:T(1,128)} %ids.1), custom_call_target="tpu_custom_call" | custom-call | flops 268435456 | bytes 5242880 | tf_op jit(solution)/shard_map/prepare/pallas_call | solution.py:95
  13.1 20.0 %all_to_all.30.piece = bf16[8,16,1152]{2,1,0:T(8,128)(2,1)} all-to-all(bf16[8,16,1152]{2,1,0:T(8,128)(2,1)} %get-tuple-element.25), channel_id=1, replica_groups={{0,2,4,6,8,10,12,14},{1,3,5,7,9,11,13,15},{16,18,20,22,24,26,28,30},{17..., dimensions={0} | all-to-all | bytes 589824 | tf_op jit(solution)/shard_map/all_to_all | solution.py:32
  33.1 2.6 %address.1 = bf16[64,16,1152]{2,1,0:T(8,128)(2,1)} custom-call(s32[7]{0:T(128)} %stack.31.info.refs_0_, bf16[8,16,1152]{2,1,0:T(8,128)(2,1)} %all_to_all.30.piece, f32[1,8192]{1,0:T(1,128)} %gains.3), custom_call_target="tpu_custom_call" | custom-call | flops 1048576 | bytes 3145728 | tf_op jit(solution)/shard_map/address/pallas_call | solution.py:125
  35.7 6.8 %all-to-all-start.1 = ((bf16[64,16,1152]{2,1,0:T(8,128)(2,1)}), bf16[64,16,1152]{2,1,0:T(8,128)(2,1)S(1)}, u32[]{:S(2)}, u32[]{:S(2)}) async-start(bf16[64,16,1152]{2,1,0:T(8,128)(2,1)} %address.1), calls=%async_computation.1 | async-start | bytes 4718592 | tf_op jit(solution)/shard_map/all_to_all | solution.py:44
  43.5 34.0 %collective-permute-done = bf16[512,512]{1,0:T(8,128)(2,1)S(1)} collective-permute-done((bf16[512,512]{1,0:T(8,128)(2,1)S(1)}, bf16[512,512]{1,0:T(8,128)(2,1)S(1)}, u32[]{:S(2)}, u32[]{:S(2)}) %collective-permute-start) | collective-permute-done | bytes 524320 | tf_op jit(solution)/shard_map/ppermute | solution.py:28
  77.6 3.5 %collective-permute-start.1 = (bf16[8,8,16,1152]{3,2,1,0:T(8,128)(2,1)S(1)}, bf16[8,8,16,1152]{3,2,1,0:T(8,128)(2,1)}, u32[]{:S(2)}, u32[]{:S(2)}) collective-permute-start(bf16[8,8,16,1152]{3,2,1,0:T(8,128)(2,1)S(1)} %bitcast.14), channel_id=1, source_target_pairs={{0,16},{1,17},{2,18},{3,19},{4,20},{5,21},{6,22},{7,23},{8,24},{9,... | collective-permute-start | bytes 7077896 | tf_op jit(solution)/shard_map/ppermute | solution.py:28
  82.1 3.3 %collective-permute-done.1.other_s.refs_3_.refs_5_ = bf16[8,8,16,1152]{3,2,1,0:T(8,128)(2,1)} collective-permute-done((bf16[8,8,16,1152]{3,2,1,0:T(8,128)(2,1)S(1)}, bf16[8,8,16,1152]{3,2,1,0:T(8,128)(2,1)}, u32[]{:S(2)}, u32[]{:S(2)}) %collective-permute-start.1) | collective-permute-done | bytes 2359328 | tf_op jit(solution)/shard_map/ppermute | solution.py:28
  85.4 6.9 %project.1 = (bf16[8,64,512]{2,1,0:T(8,128)(2,1)}, bf16[512,1024]{1,0:T(8,128)(2,1)}, f32[1,1024]{1,0:T(1,128)}) custom-call(s32[7]{0:T(128)} %stack.31.info.refs_0_, bf16[8,8,16,1152]{3,2,1,0:T(8,128)(2,1)} %bitcast.15, bf16[8,8,16,1152]{3,2,1,0:T(8,128)(2,1)} %collective-permute-done.1.other_s.refs_3_.refs_5_, f32[1,8192]{1,0:T(1,128)} %gains.3, ...), custom_call_target="tpu_custom_call" | custom-call | flops 1073741824 | bytes 8388608 | tf_op jit(solution)/shard_map/project/pallas_call | solution.py:177
  92.3 3.5 %all-to-all-start.2 = ((bf16[8,64,512]{2,1,0:T(8,128)(2,1)}), bf16[8,64,512]{2,1,0:T(8,128)(2,1)S(1)}, u32[]{:S(2)}, u32[]{:S(2)}) async-start(bf16[8,64,512]{2,1,0:T(8,128)(2,1)} %get-tuple-element.29), calls=%async_computation.2 | async-start | bytes 1048576 | tf_op jit(solution)/shard_map/all_to_all | solution.py:32
  95.9 10.6 %gram0.1 = (f32[512,1024]{1,0:T(8,128)}, f32[16,1536]{1,0:T(8,128)}) custom-call(s32[7]{0:T(128)} %stack.31.info.refs_0_, bf16[8,256,512]{2,1,0:T(8,128)(2,1)} %bitcast.23, bf16[8,8,16,1152]{3,2,1,0:T(8,128)(2,1)} %bitcast.16, bf16[8,8,16,1152]{3,2,1,0:T(8,128)(2,1)} %collective-permute-done.1.other_s.refs_3_.refs_5_, bf16[8,8,16,1152]{3,2,1,0:T(8,128)(2,1)} %bitcast.17, ...), custom_call_target="tpu_custom_call" | custom-call | flops 6442450944 | bytes 6291456 | tf_op jit(solution)/shard_map/gram0/pallas_call | solution.py:314
  106.4 7.3 %all-to-all-done.2 = bf16[8,64,512]{2,1,0:T(8,128)(2,1)S(1)} async-done(((bf16[8,64,512]{2,1,0:T(8,128)(2,1)}), bf16[8,64,512]{2,1,0:T(8,128)(2,1)S(1)}, u32[]{:S(2)}, u32[]{:S(2)}) %all-to-all-start.2) | async-done | bytes 524320 | tf_op jit(solution)/shard_map/all_to_all | solution.py:32
  114.6 3.5 %all-to-all-start.3 = ((bf16[8,64,512]{2,1,0:T(8,128)(2,1)}), bf16[8,64,512]{2,1,0:T(8,128)(2,1)S(1)}, u32[]{:S(2)}, u32[]{:S(2)}) async-start(bf16[8,64,512]{2,1,0:T(8,128)(2,1)} %broadcast_in_dim.20), calls=%async_computation.3 | async-start | bytes 1048576 | tf_op jit(solution)/shard_map/all_to_all | solution.py:32
  118.1 11.1 %gram1.1.refs_5_ = f32[512,1024]{1,0:T(8,128)} custom-call(s32[7]{0:T(128)} %stack.31.info.refs_0_, bf16[8,256,512]{2,1,0:T(8,128)(2,1)} %bitcast.24, bf16[8,8,16,1152]{3,2,1,0:T(8,128)(2,1)} %bitcast.18, bf16[8,8,16,1152]{3,2,1,0:T(8,128)(2,1)} %collective-permute-done.1.other_s.refs_3_.refs_5_, ...), custom_call_target="tpu_custom_call", output_to_operand_aliasing={{}: (5, {})} | custom-call | flops 6442450944 | bytes 6291456 | tf_op jit(solution)/shard_map/gram1/pallas_call | solution.py:314
  129.2 6.8 %all-to-all-done.3 = bf16[8,64,512]{2,1,0:T(8,128)(2,1)S(1)} async-done(((bf16[8,64,512]{2,1,0:T(8,128)(2,1)}), bf16[8,64,512]{2,1,0:T(8,128)(2,1)S(1)}, u32[]{:S(2)}, u32[]{:S(2)}) %all-to-all-start.3) | async-done | bytes 524320 | tf_op jit(solution)/shard_map/all_to_all | solution.py:32
  136.8 3.5 %numer.1 = bf16[32,32,512]{2,1,0:T(8,128)(2,1)} custom-call(s32[7]{0:T(128)} %stack.31.info.refs_0_, bf16[512,1024]{1,0:T(8,128)(2,1)} %get-tuple-element.35.calib, bf16[512,512]{1,0:T(8,128)(2,1)} %bitcast.20, f32[1,1024]{1,0:T(1,128)} %get-tuple-element.40.diag, bf16[1024,512]{1,0:T(8,128)(2,1)} %pad_maximum_fusion.weights), custom_call_target="tpu_custom_call" | custom-call | flops 536870912 | bytes 4194304 | tf_op jit(solution)/shard_map/numer/pallas_call | solution.py:212
  140.3 8.5 %all-to-all-start.4 = ((bf16[32,32,512]{2,1,0:T(8,128)(2,1)}), bf16[32,32,512]{2,1,0:T(8,128)(2,1)S(1)}, u32[]{:S(2)}, u32[]{:S(2)}) async-start(bf16[32,32,512]{2,1,0:T(8,128)(2,1)} %numer.1), calls=%async_computation.4 | async-start | bytes 2097152 | tf_op jit(solution)/shard_map/all_to_all | solution.py:363
  148.9 8.6 %gram2.1 = (f32[512,512]{1,0:T(8,128)}, bf16[512,512]{1,0:T(8,128)(2,1)}) custom-call(s32[7]{0:T(128)} %stack.31.info.refs_0_, bf16[8,256,512]{2,1,0:T(8,128)(2,1)} %bitcast.25, bf16[8,8,16,1152]{3,2,1,0:T(8,128)(2,1)} %bitcast.19, bf16[8,8,16,1152]{3,2,1,0:T(8,128)(2,1)} %collective-permute-done.1.other_s.refs_3_.refs_5_, ...), custom_call_target="tpu_custom_call" | custom-call | flops 4294967296 | bytes 6291456 | tf_op jit(solution)/shard_map/gram2/pallas_call | solution.py:314
  157.5 1.4 collective-permute-start.2
  158.9 5.5 %all-to-all-done.4 = bf16[32,32,512]{2,1,0:T(8,128)(2,1)S(1)} async-done(((bf16[32,32,512]{2,1,0:T(8,128)(2,1)}), bf16[32,32,512]{2,1,0:T(8,128)(2,1)S(1)}, u32[]{:S(2)}, u32[]{:S(2)}) %all-to-all-start.4) | async-done | bytes 1048608 | tf_op jit(solution)/shard_map/all_to_all | solution.py:363
  165.4 6.1 %all-to-all-start.5 = ((bf16[16,32,512]{2,1,0:T(8,128)(2,1)}), bf16[16,32,512]{2,1,0:T(8,128)(2,1)S(1)}, u32[]{:S(2)}, u32[]{:S(2)}) async-start(bf16[16,32,512]{2,1,0:T(8,128)(2,1)} %broadcast_in_dim.23), calls=%async_computation.5 | async-start | bytes 1048576 | tf_op jit(solution)/shard_map/all_to_all | solution.py:365
  171.5 2.1 %collective-permute-done.2 = bf16[512,512]{1,0:T(8,128)(2,1)S(1)} collective-permute-done((bf16[512,512]{1,0:T(8,128)(2,1)}, bf16[512,512]{1,0:T(8,128)(2,1)S(1)}, u32[]{:S(2)}, u32[]{:S(2)}) %collective-permute-start.2) | collective-permute-done | bytes 524320 | tf_op jit(solution)/shard_map/ppermute | solution.py:28
  173.6 1.2 select_multiply_fusion
  174.7 8.1 %all-to-all-done.5 = bf16[16,32,512]{2,1,0:T(8,128)(2,1)S(1)} async-done(((bf16[16,32,512]{2,1,0:T(8,128)(2,1)}), bf16[16,32,512]{2,1,0:T(8,128)(2,1)S(1)}, u32[]{:S(2)}, u32[]{:S(2)}) %all-to-all-start.5) | async-done | bytes 524320 | tf_op jit(solution)/shard_map/all_to_all | solution.py:365
  182.8 1.1 bitcast_convert_fusion
  (19 shorter events, 5.5 us)
Async XLA Ops:
  35.7 7.5 %copy-start.3 = (bf16[1,512,512]{2,1,0:T(8,128)(2,1)S(1)}, bf16[1,512,512]{2,1,0:T(8,128)(2,1)}, u32[]{:S(2)}) copy-start(bf16[1,512,512]{2,1,0:T(8,128)(2,1)} %param.7) | copy-start | bytes 1572868
  35.7 41.9 %all-to-all-start.1 = ((bf16[64,16,1152]{2,1,0:T(8,128)(2,1)}), bf16[64,16,1152]{2,1,0:T(8,128)(2,1)S(1)}, u32[]{:S(2)}, u32[]{:S(2)}) async-start(bf16[64,16,1152]{2,1,0:T(8,128)(2,1)} %address.1), calls=%async_computation.1 | async-start | bytes 4718592 | tf_op jit(solution)/shard_map/all_to_all | solution.py:44
  42.4 53.4 %all-gather.3.cloned.1.call-start = ((), (), s32[]{:S(2)}) async-start(), calls=%async_computation.6 | async-start | bytes 2359296 | tf_op jit(solution)/shard_map/all_gather | solution.py:346
  43.2 34.4 %collective-permute-start = (bf16[512,512]{1,0:T(8,128)(2,1)S(1)}, bf16[512,512]{1,0:T(8,128)(2,1)S(1)}, u32[]{:S(2)}, u32[]{:S(2)}) collective-permute-start(bf16[512,512]{1,0:T(8,128)(2,1)S(1)} %bitcast.21), channel_id=1, source_target_pairs={{0,1},{1,0},{2,3},{3,2},{4,5},{5,4},{6,7},{7,6},{8,9},{9,8},{10,11... | collective-permute-start | bytes 1572872 | tf_op jit(solution)/shard_map/ppermute | solution.py:28
  77.6 7.8 %copy-start = (bf16[64,16,1152]{2,1,0:T(8,128)(2,1)}, bf16[64,16,1152]{2,1,0:T(8,128)(2,1)S(1)}, u32[]{:S(2)}) copy-start(bf16[64,16,1152]{2,1,0:T(8,128)(2,1)S(1)} %all-to-all-done.1) | copy-start | bytes 7077892
  77.6 7.8 %collective-permute-start.1 = (bf16[8,8,16,1152]{3,2,1,0:T(8,128)(2,1)S(1)}, bf16[8,8,16,1152]{3,2,1,0:T(8,128)(2,1)}, u32[]{:S(2)}, u32[]{:S(2)}) collective-permute-start(bf16[8,8,16,1152]{3,2,1,0:T(8,128)(2,1)S(1)} %bitcast.14), channel_id=1, source_target_pairs={{0,16},{1,17},{2,18},{3,19},{4,20},{5,21},{6,22},{7,23},{8,24},{9,... | collective-permute-start | bytes 7077896 | tf_op jit(solution)/shard_map/ppermute | solution.py:28
  92.3 21.4 %all-to-all-start.2 = ((bf16[8,64,512]{2,1,0:T(8,128)(2,1)}), bf16[8,64,512]{2,1,0:T(8,128)(2,1)S(1)}, u32[]{:S(2)}, u32[]{:S(2)}) async-start(bf16[8,64,512]{2,1,0:T(8,128)(2,1)} %get-tuple-element.29), calls=%async_computation.2 | async-start | bytes 1048576 | tf_op jit(solution)/shard_map/all_to_all | solution.py:32
  114.6 21.4 %all-to-all-start.3 = ((bf16[8,64,512]{2,1,0:T(8,128)(2,1)}), bf16[8,64,512]{2,1,0:T(8,128)(2,1)S(1)}, u32[]{:S(2)}, u32[]{:S(2)}) async-start(bf16[8,64,512]{2,1,0:T(8,128)(2,1)} %broadcast_in_dim.20), calls=%async_computation.3 | async-start | bytes 1048576 | tf_op jit(solution)/shard_map/all_to_all | solution.py:32
  136.0 0.8 copy-start.1
  140.3 24.1 %all-to-all-start.4 = ((bf16[32,32,512]{2,1,0:T(8,128)(2,1)}), bf16[32,32,512]{2,1,0:T(8,128)(2,1)S(1)}, u32[]{:S(2)}, u32[]{:S(2)}) async-start(bf16[32,32,512]{2,1,0:T(8,128)(2,1)} %numer.1), calls=%async_computation.4 | async-start | bytes 2097152 | tf_op jit(solution)/shard_map/all_to_all | solution.py:363
  157.5 16.1 %copy-start.2 = (f32[512,512]{1,0:T(8,128)S(1)}, f32[512,512]{1,0:T(8,128)}, u32[]{:S(2)}) copy-start(f32[512,512]{1,0:T(8,128)} %get-tuple-element.45) | copy-start | bytes 3145732
  157.5 16.1 %collective-permute-start.2 = (bf16[512,512]{1,0:T(8,128)(2,1)}, bf16[512,512]{1,0:T(8,128)(2,1)S(1)}, u32[]{:S(2)}, u32[]{:S(2)}) collective-permute-start(bf16[512,512]{1,0:T(8,128)(2,1)} %get-tuple-element.46), channel_id=1, source_target_pairs={{0,1},{1,0},{2,3},{3,2},{4,5},{5,4},{6,7},{7,6},{8,9},{9,8},{10,11... | collective-permute-start | bytes 1572872 | tf_op jit(solution)/shard_map/ppermute | solution.py:28
  165.4 17.4 %all-to-all-start.5 = ((bf16[16,32,512]{2,1,0:T(8,128)(2,1)}), bf16[16,32,512]{2,1,0:T(8,128)(2,1)S(1)}, u32[]{:S(2)}, u32[]{:S(2)}) async-start(bf16[16,32,512]{2,1,0:T(8,128)(2,1)} %broadcast_in_dim.23), calls=%async_computation.5 | async-start | bytes 1048576 | tf_op jit(solution)/shard_map/all_to_all | solution.py:365
Sparse Core Ops, SparseCore 0:
  45.1 36.2 all-gather.2

commit v6 on v5

--- a/solution.py
+++ b/solution.py
@@ -40,10 +40,16 @@
     return lax.dot_general(a, b, (((0,), (0,)), ((), ())), preferred_element_type=F4)
 
 
-def gather_mp(sent, w):
+def gather(sent, w, x):
     own = lax.all_to_all(sent, "mp", 0, 0, tiled=True, axis_index_groups=CORE_GROUPS)
-    own, w = lax.optimization_barrier((own.reshape(8, 8, 16, 1152), shift(w, xl=1)))
-    return own, shift(own, c=1), w
+    z = [x]
+    u = d = x
+    for _ in range(3):
+        u, d = shift(u, z=1), shift(d, z=-1)
+        z += [u, d]
+    z += [shift(u[:128], z=1), shift(d[128:], z=-1)]
+    own, w, *z = lax.optimization_barrier((own.reshape(8, 8, 16, 1152), shift(w, xl=1), *z))
+    return own, shift(own, c=1), w, z
 
 
 def prepare_kernel(info, bank, ids, piece_out, cols_out, total, pick):
@@ -220,6 +226,7 @@
     )(info, calib, model_out, diag, weights)
 
 
+ORDER = (0, 7, 1, 6, 2, 5, 3, 4)
 STEPS = (3, 3, 2)
 
 
@@ -229,7 +236,8 @@
 
 def gram_kernel(first, last, info, *refs):
     refs = list(refs)
-    block, own_s, other_s = refs.pop(0), refs.pop(0), refs.pop(0)
+    blocks = [refs.pop(0) for _ in range(3)]
+    own_s, other_s = refs.pop(0), refs.pop(0)
     if first:
         own_g, other_g = refs.pop(0), refs.pop(0)
     else:
@@ -262,7 +270,16 @@
                         row += [tile[i : i + 1] for i in range(4)]
                     gains[pl.ds(m, 1), :] = jnp.concatenate(row, 1)
 
-    table[:, 0:512] = block[0]
+    for i in range(2 if last else 3):
+
+        @pl.when(step == i)
+        def _(i=i):
+            if last and i == 1:
+                table[0:128, 0:512] = blocks[1][...]
+                table[128:256, 0:512] = blocks[2][...]
+            else:
+                table[:, 0:512] = blocks[i][...]
+
     lane = lax.broadcasted_iota(jnp.int32, (64, 256), 1).astype(F4)
     models, tiles = [], []
     for core in range(2):
@@ -300,8 +317,7 @@
     first, last = i == 0, i == len(STEPS) - 1
     start, steps = sum(STEPS[:i]), STEPS[i]
     whole = lambda shape: pl.BlockSpec(shape, lambda j, info: (0,) * len(shape))
-    by_z = pl.BlockSpec((8, 1, 16, 1152), lambda j, info: (0, start + j, 0, 0))
-    block = pl.BlockSpec((1, 256, 512), lambda j, info: (start + j, 0, 0))
+    by_z = pl.BlockSpec((8, 1, 16, 1152), lambda j, info: (0, info[7 + start + j], 0, 0))
     gain_view = pl.BlockSpec((8, 8, 16, 128), lambda j, info: (0, 0, 0, 8))
     shapes = [jax.ShapeDtypeStruct((512, 1024), F4)]
     if last:
@@ -310,13 +326,14 @@
         shapes.append(jax.ShapeDtypeStruct((16, 1536), F4))
     extra = [own_s, other_s] if first else [gains, before]
     extra_specs = [gain_view, gain_view] if first else [whole((16, 1536)), whole((512, 1024))]
-    operands = [info, blocks, own_s, other_s, *extra]
+    blocks = blocks[start : start + 3]
+    operands = [info, *blocks, own_s, other_s, *extra]
     return pl.pallas_call(
         lambda *refs: gram_kernel(first, last, *refs),
         grid_spec=pltpu.PrefetchScalarGridSpec(
             num_scalar_prefetch=1,
             grid=(steps,),
-            in_specs=[block, by_z, by_z] + extra_specs,
+            in_specs=[whole(b.shape) for b in blocks] + [by_z, by_z] + extra_specs,
             out_specs=[whole(o.shape) for o in shapes],
             scratch_shapes=([pltpu.VMEM((512, 1024), F4)] if last else [])
             + [
@@ -339,12 +356,12 @@
     s = lax.axis_index("shard")
     y, xh, c = p // 4, p // 2 % 2, p % 2
     z, xl = s // 2, s % 2
-    info = jnp.stack([p, s, xl, y, xh, c, z]).astype(jnp.int32)
+    info = jnp.stack([p, s, xl, y, xh, c, z] + [(z + k) % 8 for k in ORDER]).astype(jnp.int32)
     weights = proj_slabs[0]
 
     piece, bank_cols = prepare(info, bank, calib_ids)
-    blocks = lax.all_gather(bank_cols, "shard", axis=0, axis_index_groups=Z_GROUPS)
-    own_s, other_s, weights_other = gather_mp(address(info, swap_z(piece), norm_gains), weights)
+    sent = address(info, swap_z(piece), norm_gains)
+    own_s, other_s, weights_other, blocks = gather(sent, weights, bank_cols)
     both = jnp.concatenate([weights, weights_other], 0)
 
     partial_out, calib, diag = project(info, own_s, other_s, norm_gains, both)

time: 192 us -> 177 us (0.922)
  between operations: 14.1 us -> 0.95 us
  waiting for transfers between devices: 67.6 us -> 58.7 us
  starting transfers between devices: 33.7 us -> 40.7 us
    ppermute x3 -> x11, starting transfers between devices: 5.28 us -> 12.1 us  [shift(): return lax.ppermute(x, AXES, pairs)]
    ppermute x3 -> x11, waiting for transfers between devices: 39.3 us -> 33.3 us  [shift(): return lax.ppermute(x, AXES, pairs)]
    all_to_all x2, waiting for transfers between devices: 14 us -> 12 us  [swap_z(): lax.all_to_all(x, 'shard', 0, 0, tiled=True, axis_index_groups=Z_GROUPS)]
  transfers between devices with their start and end apart: 9 -> 16, of which waited for: 7 -> 11; matrix products, arithmetic and copies ran while one was open for 2% -> 2% of each run, Pallas kernels for 20% -> 18%
where the time goes in v6:
time: 177 us; the launch traced here: 176 us
  waiting for transfers between devices  58.7 us (33%)
  Pallas kernels  49.3 us (28%)
  starting transfers between devices  40.7 us (23%)
  blocking collectives  20 us (11%)
  other arithmetic  3.57 us (2%)
  local copies, waits for them, and re-layouts  3.22 us (2%)
    ppermute x11, waiting for transfers between devices, shift(): return lax.ppermute(x, AXES, pairs)  33.3 us
    pallas_call x3, Pallas kernels, gram_call(): pl.pallas_call(lambda *refs: gram_kernel(first, last, *refs), grid_spec=p...  31 us
    all_to_all x1, blocking collectives, swap_z(): lax.all_to_all(x, 'shard', 0, 0, tiled=True, axis_index_groups=Z_GROUPS)  20 us
    ppermute x11, starting transfers between devices, shift(): return lax.ppermute(x, AXES, pairs)  12.1 us
    all_to_all x2, waiting for transfers between devices, swap_z(): lax.all_to_all(x, 'shard', 0, 0, tiled=True, axis_index_groups=Z_GROUPS)  12 us
    all_to_all x1, starting transfers between devices, local(): lax.all_to_all(numer, AXES, 0, 0, tiled=True, axis_index_groups=XLO_GROUPS)  8.52 us
    all_to_all x1, waiting for transfers between devices, local(): lax.all_to_all(jnp.broadcast_to(numer[None], (16, 32, 512)), 'mp', 0, 0,...  8.07 us
    all_to_all x2, starting transfers between devices, swap_z(): lax.all_to_all(x, 'shard', 0, 0, tiled=True, axis_index_groups=Z_GROUPS)  7.18 us
  transfers between devices with their start and end apart: 16, of which 11 were waited for; matrix products, arithmetic and copies ran while one was open for 2% of the time, Pallas kernels for 18%

profile of v6, /device:TPU:1, one launch (start us, length us, event | category | flops | bytes accessed | tf_op | source)
XLA Modules:
  0.0 176.4 jit_solution(1684325389093022297)
XLA Ops:
  1.5 5.3 %prepare.1 = (bf16[8,16,1152]{2,1,0:T(8,128)(2,1)}, bf16[256,512]{1,0:T(8,128)(2,1)}) custom-call(s32[15]{0:T(128)} %stack.63.info.refs_0_, bf16[256,8192]{1,0:T(8,128)(2,1)} %bank.1, s32[1,64]{1,0:T(1,128)} %ids.1), custom_call_target="tpu_custom_call" | custom-call | flops 268435456 | bytes 5242880 | tf_op jit(solution)/shard_map/prepare/pallas_call | solution.py:101
  6.7 20.0 %all_to_all.30.piece = bf16[8,16,1152]{2,1,0:T(8,128)(2,1)} all-to-all(bf16[8,16,1152]{2,1,0:T(8,128)(2,1)} %get-tuple-element.34), channel_id=1, replica_groups={{0,2,4,6,8,10,12,14},{1,3,5,7,9,11,13,15},{16,18,20,22,24,26,28,30},{17..., dimensions={0} | all-to-all | bytes 589824 | tf_op jit(solution)/shard_map/all_to_all | solution.py:32
  26.7 2.6 %address.1 = bf16[64,16,1152]{2,1,0:T(8,128)(2,1)} custom-call(s32[15]{0:T(128)} %stack.63.info.refs_0_, bf16[8,16,1152]{2,1,0:T(8,128)(2,1)} %all_to_all.30.piece, f32[1,8192]{1,0:T(1,128)} %gains.3), custom_call_target="tpu_custom_call" | custom-call | flops 1048576 | bytes 3145728 | tf_op jit(solution)/shard_map/address/pallas_call | solution.py:131
  29.3 6.8 %all-to-all-start.1 = ((bf16[64,16,1152]{2,1,0:T(8,128)(2,1)}), bf16[64,16,1152]{2,1,0:T(8,128)(2,1)S(1)}, u32[]{:S(2)}, u32[]{:S(2)}) async-start(bf16[64,16,1152]{2,1,0:T(8,128)(2,1)} %address.1), calls=%async_computation.1 | async-start | bytes 4718592 | tf_op jit(solution)/shard_map/all_to_all | solution.py:44
  37.6 3.8 %collective-permute-done.2.refs_3_ = bf16[256,512]{1,0:T(8,128)(2,1)S(1)} collective-permute-done((bf16[256,512]{1,0:T(8,128)(2,1)S(1)}, bf16[256,512]{1,0:T(8,128)(2,1)S(1)}, u32[]{:S(2)}, u32[]{:S(2)}) %collective-permute-start.2) | collective-permute-done | bytes 262176 | tf_op jit(solution)/shard_map/ppermute | solution.py:28
  43.4 4.4 %collective-permute-done.4.refs_2_ = bf16[256,512]{1,0:T(8,128)(2,1)S(1)} collective-permute-done((bf16[256,512]{1,0:T(8,128)(2,1)S(1)}, bf16[256,512]{1,0:T(8,128)(2,1)S(1)}, u32[]{:S(2)}, u32[]{:S(2)}) %collective-permute-start.4) | collective-permute-done | bytes 262176 | tf_op jit(solution)/shard_map/ppermute | solution.py:28
  49.6 5.6 %collective-permute-done.6.refs_1_ = bf16[256,512]{1,0:T(8,128)(2,1)S(1)} collective-permute-done((bf16[256,512]{1,0:T(8,128)(2,1)S(1)}, bf16[256,512]{1,0:T(8,128)(2,1)S(1)}, u32[]{:S(2)}, u32[]{:S(2)}) %collective-permute-start.6) | collective-permute-done | bytes 262176 | tf_op jit(solution)/shard_map/ppermute | solution.py:28
  57.1 14.0 %collective-permute-done = bf16[512,512]{1,0:T(8,128)(2,1)S(1)} collective-permute-done((bf16[512,512]{1,0:T(8,128)(2,1)S(1)}, bf16[512,512]{1,0:T(8,128)(2,1)S(1)}, u32[]{:S(2)}, u32[]{:S(2)}) %collective-permute-start) | collective-permute-done | bytes 524320 | tf_op jit(solution)/shard_map/ppermute | solution.py:28
  71.1 3.7 %collective-permute-start.9 = (bf16[8,8,16,1152]{3,2,1,0:T(8,128)(2,1)S(1)}, bf16[8,8,16,1152]{3,2,1,0:T(8,128)(2,1)}, u32[]{:S(2)}, u32[]{:S(2)}) collective-permute-start(bf16[8,8,16,1152]{3,2,1,0:T(8,128)(2,1)S(1)} %bitcast.21), channel_id=1, source_target_pairs={{0,16},{1,17},{2,18},{3,19},{4,20},{5,21},{6,22},{7,23},{8,24},{9,... | collective-permute-start | bytes 7077896 | tf_op jit(solution)/shard_map/ppermute | solution.py:28
  75.9 3.3 %collective-permute-done.9.other_s.refs_5_.refs_7_ = bf16[8,8,16,1152]{3,2,1,0:T(8,128)(2,1)} collective-permute-done((bf16[8,8,16,1152]{3,2,1,0:T(8,128)(2,1)S(1)}, bf16[8,8,16,1152]{3,2,1,0:T(8,128)(2,1)}, u32[]{:S(2)}, u32[]{:S(2)}) %collective-permute-start.9) | collective-permute-done | bytes 2359328 | tf_op jit(solution)/shard_map/ppermute | solution.py:28
  79.1 6.9 %project.1 = (bf16[8,64,512]{2,1,0:T(8,128)(2,1)}, bf16[512,1024]{1,0:T(8,128)(2,1)}, f32[1,1024]{1,0:T(1,128)}) custom-call(s32[15]{0:T(128)} %stack.63.info.refs_0_, bf16[8,8,16,1152]{3,2,1,0:T(8,128)(2,1)} %bitcast.22, bf16[8,8,16,1152]{3,2,1,0:T(8,128)(2,1)} %collective-permute-done.9.other_s.refs_5_.refs_7_, f32[1,8192]{1,0:T(1,128)} %gains.3, ...), custom_call_target="tpu_custom_call" | custom-call | flops 1073741824 | bytes 8388608 | tf_op jit(solution)/shard_map/project/pallas_call | solution.py:183
  86.1 3.5 %all-to-all-start.2 = ((bf16[8,64,512]{2,1,0:T(8,128)(2,1)}), bf16[8,64,512]{2,1,0:T(8,128)(2,1)S(1)}, u32[]{:S(2)}, u32[]{:S(2)}) async-start(bf16[8,64,512]{2,1,0:T(8,128)(2,1)} %get-tuple-element.39), calls=%async_computation.2 | async-start | bytes 1048576 | tf_op jit(solution)/shard_map/all_to_all | solution.py:32
  89.6 10.8 %gram0.1 = (f32[512,1024]{1,0:T(8,128)}, f32[16,1536]{1,0:T(8,128)}) custom-call(s32[15]{0:T(128)} %stack.63.info.refs_0_, bf16[256,512]{1,0:T(8,128)(2,1)} %get-tuple-element.41.refs_1_, bf16[256,512]{1,0:T(8,128)(2,1)} %copy-done.10, bf16[256,512]{1,0:T(8,128)(2,1)} %copy-done.9, bf16[8,8,16,1152]{3,2,1,0:T(8,128)(2,1)} %bitcast.23, ...), custom_call_target="tpu_custom_call" | custom-call | flops 6442450944 | bytes 6291456 | tf_op jit(solution)/shard_map/gram0/pallas_call | solution.py:331
  100.4 7.0 %all-to-all-done.2 = bf16[8,64,512]{2,1,0:T(8,128)(2,1)S(1)} async-done(((bf16[8,64,512]{2,1,0:T(8,128)(2,1)}), bf16[8,64,512]{2,1,0:T(8,128)(2,1)S(1)}, u32[]{:S(2)}, u32[]{:S(2)}) %all-to-all-start.2) | async-done | bytes 524320 | tf_op jit(solution)/shard_map/all_to_all | solution.py:32
  108.4 3.7 %all-to-all-start.3 = ((bf16[8,64,512]{2,1,0:T(8,128)(2,1)}), bf16[8,64,512]{2,1,0:T(8,128)(2,1)S(1)}, u32[]{:S(2)}, u32[]{:S(2)}) async-start(bf16[8,64,512]{2,1,0:T(8,128)(2,1)} %broadcast_in_dim.20), calls=%async_computation.3 | async-start | bytes 1048576 | tf_op jit(solution)/shard_map/all_to_all | solution.py:32
  112.0 11.4 %gram1.1.refs_7_ = f32[512,1024]{1,0:T(8,128)} custom-call(s32[15]{0:T(128)} %stack.63.info.refs_0_, bf16[256,512]{1,0:T(8,128)(2,1)} %copy-done.8, bf16[256,512]{1,0:T(8,128)(2,1)} %copy-done.7, bf16[256,512]{1,0:T(8,128)(2,1)} %copy-done.5, bf16[8,8,16,1152]{3,2,1,0:T(8,128)(2,1)} %bitcast.25, ...), custom_call_target="tpu_custom_call", output_to_operand_aliasing={{}: (7, {})} | custom-call | flops 6442450944 | bytes 6291456 | tf_op jit(solution)/shard_map/gram1/pallas_call | solution.py:331
  123.4 5.0 %all-to-all-done.3 = bf16[8,64,512]{2,1,0:T(8,128)(2,1)S(1)} async-done(((bf16[8,64,512]{2,1,0:T(8,128)(2,1)}), bf16[8,64,512]{2,1,0:T(8,128)(2,1)S(1)}, u32[]{:S(2)}, u32[]{:S(2)}) %all-to-all-start.3) | async-done | bytes 524320 | tf_op jit(solution)/shard_map/all_to_all | solution.py:32
  129.3 3.5 %numer.1 = bf16[32,32,512]{2,1,0:T(8,128)(2,1)} custom-call(s32[15]{0:T(128)} %stack.63.info.refs_0_, bf16[512,1024]{1,0:T(8,128)(2,1)} %get-tuple-element.47.calib, bf16[512,512]{1,0:T(8,128)(2,1)} %bitcast.27, f32[1,1024]{1,0:T(1,128)} %get-tuple-element.55.diag, bf16[1024,512]{1,0:T(8,128)(2,1)} %pad_maximum_fusion.weights), custom_call_target="tpu_custom_call" | custom-call | flops 536870912 | bytes 4194304 | tf_op jit(solution)/shard_map/numer/pallas_call | solution.py:218
  132.8 8.5 %all-to-all-start.4 = ((bf16[32,32,512]{2,1,0:T(8,128)(2,1)}), bf16[32,32,512]{2,1,0:T(8,128)(2,1)S(1)}, u32[]{:S(2)}, u32[]{:S(2)}) async-start(bf16[32,32,512]{2,1,0:T(8,128)(2,1)} %numer.1), calls=%async_computation.4 | async-start | bytes 2097152 | tf_op jit(solution)/shard_map/all_to_all | solution.py:380
  141.3 8.8 %gram2.1 = (f32[512,512]{1,0:T(8,128)}, bf16[512,512]{1,0:T(8,128)(2,1)}) custom-call(s32[15]{0:T(128)} %stack.63.info.refs_0_, bf16[256,512]{1,0:T(8,128)(2,1)} %copy-done.4, bf16[128,512]{1,0:T(8,128)(2,1)} %collective-permute-done.7.refs_2_, bf16[128,512]{1,0:T(8,128)(2,1)} %copy-done.11, bf16[8,8,16,1152]{3,2,1,0:T(8,128)(2,1)} %bitcast.26, ...), custom_call_target="tpu_custom_call" | custom-call | flops 4294967296 | bytes 6291456 | tf_op jit(solution)/shard_map/gram2/pallas_call | solution.py:331
  151.5 5.4 %all-to-all-done.4 = bf16[32,32,512]{2,1,0:T(8,128)(2,1)S(1)} async-done(((bf16[32,32,512]{2,1,0:T(8,128)(2,1)}), bf16[32,32,512]{2,1,0:T(8,128)(2,1)S(1)}, u32[]{:S(2)}, u32[]{:S(2)}) %all-to-all-start.4) | async-done | bytes 1048608 | tf_op jit(solution)/shard_map/all_to_all | solution.py:380
  157.9 6.1 %all-to-all-start.5 = ((bf16[16,32,512]{2,1,0:T(8,128)(2,1)}), bf16[16,32,512]{2,1,0:T(8,128)(2,1)S(1)}, u32[]{:S(2)}, u32[]{:S(2)}) async-start(bf16[16,32,512]{2,1,0:T(8,128)(2,1)} %broadcast_in_dim.23), calls=%async_computation.5 | async-start | bytes 1048576 | tf_op jit(solution)/shard_map/all_to_all | solution.py:382
  164.0 2.1 %collective-permute-done.10 = bf16[512,512]{1,0:T(8,128)(2,1)S(1)} collective-permute-done((bf16[512,512]{1,0:T(8,128)(2,1)}, bf16[512,512]{1,0:T(8,128)(2,1)S(1)}, u32[]{:S(2)}, u32[]{:S(2)}) %collective-permute-start.10) | collective-permute-done | bytes 524320 | tf_op jit(solution)/shard_map/ppermute | solution.py:28
  167.2 8.1 %all-to-all-done.5 = bf16[16,32,512]{2,1,0:T(8,128)(2,1)S(1)} async-done(((bf16[16,32,512]{2,1,0:T(8,128)(2,1)}), bf16[16,32,512]{2,1,0:T(8,128)(2,1)S(1)}, u32[]{:S(2)}, u32[]{:S(2)}) %all-to-all-start.5) | async-done | bytes 524320 | tf_op jit(solution)/shard_map/all_to_all | solution.py:382
  (50 shorter events, 15.4 us)
Async XLA Ops:
  29.3 6.8 %copy-start.6 = (bf16[256,512]{1,0:T(8,128)(2,1)S(1)}, bf16[256,512]{1,0:T(8,128)(2,1)}, u32[]{:S(2)}) copy-start(bf16[256,512]{1,0:T(8,128)(2,1)} %get-tuple-element.41.refs_1_) | copy-start | bytes 786436
  29.3 13.8 %copy-start.3 = (bf16[1,512,512]{2,1,0:T(8,128)(2,1)S(1)}, bf16[1,512,512]{2,1,0:T(8,128)(2,1)}, u32[]{:S(2)}) copy-start(bf16[1,512,512]{2,1,0:T(8,128)(2,1)} %param.7) | copy-start | bytes 1572868
  29.3 41.9 %all-to-all-start.1 = ((bf16[64,16,1152]{2,1,0:T(8,128)(2,1)}), bf16[64,16,1152]{2,1,0:T(8,128)(2,1)S(1)}, u32[]{:S(2)}, u32[]{:S(2)}) async-start(bf16[64,16,1152]{2,1,0:T(8,128)(2,1)} %address.1), calls=%async_computation.1 | async-start | bytes 4718592 | tf_op jit(solution)/shard_map/all_to_all | solution.py:44
  36.0 5.3 %collective-permute-start.2 = (bf16[256,512]{1,0:T(8,128)(2,1)S(1)}, bf16[256,512]{1,0:T(8,128)(2,1)S(1)}, u32[]{:S(2)}, u32[]{:S(2)}) collective-permute-start(bf16[256,512]{1,0:T(8,128)(2,1)S(1)} %copy-done.6), channel_id=1, source_target_pairs={{0,14},{1,15},{2,0},{3,1},{4,2},{5,3},{6,4},{7,5},{8,6},{9,7},{10,... | collective-permute-start | bytes 786440 | tf_op jit(solution)/shard_map/ppermute | solution.py:28
  36.3 6.4 %collective-permute-start.1 = (bf16[256,512]{1,0:T(8,128)(2,1)S(1)}, bf16[256,512]{1,0:T(8,128)(2,1)S(1)}, u32[]{:S(2)}, u32[]{:S(2)}) collective-permute-start(bf16[256,512]{1,0:T(8,128)(2,1)S(1)} %copy-done.6), channel_id=1, source_target_pairs={{0,2},{1,3},{2,4},{3,5},{4,6},{5,7},{6,8},{7,9},{8,10},{9,11},{10,... | collective-permute-start | bytes 786440 | tf_op jit(solution)/shard_map/ppermute | solution.py:28
  41.3 8.3 %copy-start.9 = (bf16[256,512]{1,0:T(8,128)(2,1)}, bf16[256,512]{1,0:T(8,128)(2,1)S(1)}, u32[]{:S(2)}) copy-start(bf16[256,512]{1,0:T(8,128)(2,1)S(1)} %collective-permute-done.2.refs_3_) | copy-start | bytes 786436
  41.3 6.5 %collective-permute-start.4 = (bf16[256,512]{1,0:T(8,128)(2,1)S(1)}, bf16[256,512]{1,0:T(8,128)(2,1)S(1)}, u32[]{:S(2)}, u32[]{:S(2)}) collective-permute-start(bf16[256,512]{1,0:T(8,128)(2,1)S(1)} %collective-permute-done.2.refs_3_), channel_id=1, source_target_pairs={{0,14},{1,15},{2,0},{3,1},{4,2},{5,3},{6,4},{7,5},{8,6},{9,7},{10,... | collective-permute-start | bytes 786440 | tf_op jit(solution)/shard_map/ppermute | solution.py:28
  42.7 6.7 %collective-permute-start.3 = (bf16[256,512]{1,0:T(8,128)(2,1)S(1)}, bf16[256,512]{1,0:T(8,128)(2,1)S(1)}, u32[]{:S(2)}, u32[]{:S(2)}) collective-permute-start(bf16[256,512]{1,0:T(8,128)(2,1)S(1)} %collective-permute-done.1.refs_2_), channel_id=1, source_target_pairs={{0,2},{1,3},{2,4},{3,5},{4,6},{5,7},{6,8},{7,9},{8,10},{9,11},{10,... | collective-permute-start | bytes 786440 | tf_op jit(solution)/shard_map/ppermute | solution.py:28
  43.1 28.0 %collective-permute-start = (bf16[512,512]{1,0:T(8,128)(2,1)S(1)}, bf16[512,512]{1,0:T(8,128)(2,1)S(1)}, u32[]{:S(2)}, u32[]{:S(2)}) collective-permute-start(bf16[512,512]{1,0:T(8,128)(2,1)S(1)} %bitcast.28), channel_id=1, source_target_pairs={{0,1},{1,0},{2,3},{3,2},{4,5},{5,4},{6,7},{7,6},{8,9},{9,8},{10,11... | collective-permute-start | bytes 1572872 | tf_op jit(solution)/shard_map/ppermute | solution.py:28
  47.9 7.3 %collective-permute-start.6 = (bf16[256,512]{1,0:T(8,128)(2,1)S(1)}, bf16[256,512]{1,0:T(8,128)(2,1)S(1)}, u32[]{:S(2)}, u32[]{:S(2)}) collective-permute-start(bf16[256,512]{1,0:T(8,128)(2,1)S(1)} %collective-permute-done.4.refs_2_), channel_id=1, source_target_pairs={{0,14},{1,15},{2,0},{3,1},{4,2},{5,3},{6,4},{7,5},{8,6},{9,7},{10,... | collective-permute-start | bytes 786440 | tf_op jit(solution)/shard_map/ppermute | solution.py:28
  49.5 21.6 %copy-start.8 = (bf16[256,512]{1,0:T(8,128)(2,1)}, bf16[256,512]{1,0:T(8,128)(2,1)S(1)}, u32[]{:S(2)}) copy-start(bf16[256,512]{1,0:T(8,128)(2,1)S(1)} %collective-permute-done.3.refs_1_) | copy-start | bytes 786436
  49.5 7.5 %collective-permute-start.5 = (bf16[256,512]{1,0:T(8,128)(2,1)S(1)}, bf16[256,512]{1,0:T(8,128)(2,1)S(1)}, u32[]{:S(2)}, u32[]{:S(2)}) collective-permute-start(bf16[256,512]{1,0:T(8,128)(2,1)S(1)} %collective-permute-done.3.refs_1_), channel_id=1, source_target_pairs={{0,2},{1,3},{2,4},{3,5},{4,6},{5,7},{6,8},{7,9},{8,10},{9,11},{10,... | collective-permute-start | bytes 786440 | tf_op jit(solution)/shard_map/ppermute | solution.py:28
  55.2 15.9 %collective-permute-start.8 = (bf16[128,512]{1,0:T(8,128)(2,1)S(1)}, bf16[128,512]{1,0:T(8,128)(2,1)S(1)}, u32[]{:S(2)}, u32[]{:S(2)}) collective-permute-start(bf16[128,512]{1,0:T(8,128)(2,1)S(1)} %slice.9), channel_id=1, source_target_pairs={{0,14},{1,15},{2,0},{3,1},{4,2},{5,3},{6,4},{7,5},{8,6},{9,7},{10,... | collective-permute-start | bytes 393224 | tf_op jit(solution)/shard_map/ppermute | solution.py:28
  57.0 14.1 %copy-start.5 = (bf16[256,512]{1,0:T(8,128)(2,1)}, bf16[256,512]{1,0:T(8,128)(2,1)S(1)}, u32[]{:S(2)}) copy-start(bf16[256,512]{1,0:T(8,128)(2,1)S(1)} %collective-permute-done.5.refs_3_) | copy-start | bytes 786436
  57.0 14.1 %collective-permute-start.7 = (bf16[128,512]{1,0:T(8,128)(2,1)S(1)}, bf16[128,512]{1,0:T(8,128)(2,1)}, u32[]{:S(2)}, u32[]{:S(2)}) collective-permute-start(bf16[128,512]{1,0:T(8,128)(2,1)S(1)} %slice.8), channel_id=1, source_target_pairs={{0,2},{1,3},{2,4},{3,5},{4,6},{5,7},{6,8},{7,9},{8,10},{9,11},{10,... | collective-permute-start | bytes 393224 | tf_op jit(solution)/shard_map/ppermute | solution.py:28
  71.1 15.0 %copy-start.11 = (bf16[128,512]{1,0:T(8,128)(2,1)}, bf16[128,512]{1,0:T(8,128)(2,1)S(1)}, u32[]{:S(2)}) copy-start(bf16[128,512]{1,0:T(8,128)(2,1)S(1)} %collective-permute-done.8.refs_3_) | copy-start | bytes 393220
  71.1 8.0 %copy-start = (bf16[64,16,1152]{2,1,0:T(8,128)(2,1)}, bf16[64,16,1152]{2,1,0:T(8,128)(2,1)S(1)}, u32[]{:S(2)}) copy-start(bf16[64,16,1152]{2,1,0:T(8,128)(2,1)S(1)} %all-to-all-done.1) | copy-start | bytes 7077892
  71.1 8.0 %collective-permute-start.9 = (bf16[8,8,16,1152]{3,2,1,0:T(8,128)(2,1)S(1)}, bf16[8,8,16,1152]{3,2,1,0:T(8,128)(2,1)}, u32[]{:S(2)}, u32[]{:S(2)}) collective-permute-start(bf16[8,8,16,1152]{3,2,1,0:T(8,128)(2,1)S(1)} %bitcast.21), channel_id=1, source_target_pairs={{0,16},{1,17},{2,18},{3,19},{4,20},{5,21},{6,22},{7,23},{8,24},{9,... | collective-permute-start | bytes 7077896 | tf_op jit(solution)/shard_map/ppermute | solution.py:28
  86.1 21.4 %all-to-all-start.2 = ((bf16[8,64,512]{2,1,0:T(8,128)(2,1)}), bf16[8,64,512]{2,1,0:T(8,128)(2,1)S(1)}, u32[]{:S(2)}, u32[]{:S(2)}) async-start(bf16[8,64,512]{2,1,0:T(8,128)(2,1)} %get-tuple-element.39), calls=%async_computation.2 | async-start | bytes 1048576 | tf_op jit(solution)/shard_map/all_to_all | solution.py:32
  108.4 20.1 %all-to-all-start.3 = ((bf16[8,64,512]{2,1,0:T(8,128)(2,1)}), bf16[8,64,512]{2,1,0:T(8,128)(2,1)S(1)}, u32[]{:S(2)}, u32[]{:S(2)}) async-start(bf16[8,64,512]{2,1,0:T(8,128)(2,1)} %broadcast_in_dim.20), calls=%async_computation.3 | async-start | bytes 1048576 | tf_op jit(solution)/shard_map/all_to_all | solution.py:32
  132.8 24.1 %all-to-all-start.4 = ((bf16[32,32,512]{2,1,0:T(8,128)(2,1)}), bf16[32,32,512]{2,1,0:T(8,128)(2,1)S(1)}, u32[]{:S(2)}, u32[]{:S(2)}) async-start(bf16[32,32,512]{2,1,0:T(8,128)(2,1)} %numer.1), calls=%async_computation.4 | async-start | bytes 2097152 | tf_op jit(solution)/shard_map/all_to_all | solution.py:380
  150.1 15.9 %copy-start.2 = (f32[512,512]{1,0:T(8,128)S(1)}, f32[512,512]{1,0:T(8,128)}, u32[]{:S(2)}) copy-start(f32[512,512]{1,0:T(8,128)} %get-tuple-element.63) | copy-start | bytes 3145732
  150.1 15.9 %collective-permute-start.10 = (bf16[512,512]{1,0:T(8,128)(2,1)}, bf16[512,512]{1,0:T(8,128)(2,1)S(1)}, u32[]{:S(2)}, u32[]{:S(2)}) collective-permute-start(bf16[512,512]{1,0:T(8,128)(2,1)} %get-tuple-element.64), channel_id=1, source_target_pairs={{0,1},{1,0},{2,3},{3,2},{4,5},{5,4},{6,7},{7,6},{8,9},{9,8},{10,11... | collective-permute-start | bytes 1572872 | tf_op jit(solution)/shard_map/ppermute | solution.py:28
  157.9 17.4 %all-to-all-start.5 = ((bf16[16,32,512]{2,1,0:T(8,128)(2,1)}), bf16[16,32,512]{2,1,0:T(8,128)(2,1)S(1)}, u32[]{:S(2)}, u32[]{:S(2)}) async-start(bf16[16,32,512]{2,1,0:T(8,128)(2,1)} %broadcast_in_dim.23), calls=%async_computation.5 | async-start | bytes 1048576 | tf_op jit(solution)/shard_map/all_to_all | solution.py:382
  (4 other events, 11.0 us)

commit v7 on v6

v7 whole, which is shorter than its diff:
```python
import jax
import jax.numpy as jnp
from jax import lax
from jax.experimental import pallas as pl
from jax.experimental.pallas import tpu as pltpu
from jax.sharding import PartitionSpec as P

ALPHA = 0.9
EPSILON = 1e-05
BF = jnp.bfloat16
F4 = jnp.float32
VMEM = 60 * 2**20
AXES = ("mp", "shard")
Z_GROUPS = [[z * 2 + xl for z in range(8)] for xl in range(2)]
XLO_GROUPS = [[p * 16 + z * 2 + xl for p in range(16) for xl in range(2)] for z in range(8)]


def shift(x, yp=0, xh=0, c=0, z=0, xl=0):
    pairs = []
    for p in range(16):
        for s in range(16):
            py, pxh, pc = p // 4, p // 2 % 2, p % 2
            sz, sxl = s // 2, s % 2
            tp = (py ^ yp) * 4 + (pxh ^ xh) * 2 + (pc ^ c)
            ts = (sz + z) % 8 * 2 + (sxl ^ xl)
            pairs.append((p * 16 + s, tp * 16 + ts))
    return lax.ppermute(x, AXES, pairs)


def swap_z(x):
    return lax.all_to_all(x, "shard", 0, 0, tiled=True, axis_index_groups=Z_GROUPS)


def dot(a, b):
    return jnp.dot(a, b, preferred_element_type=F4)


def contract_rows(a, b):
    return lax.dot_general(a, b, (((0,), (0,)), ((), ())), preferred_element_type=F4)


def ring(x):
    z = [x]
    u = d = x
    for _ in range(3):
        u, d = shift(u, z=1), shift(d, z=-1)
        z += [u, d]
    return z + [shift(u[:128], z=1), shift(d[128:], z=-1)]


def quarter(info, other_core, other_pair, high):
    y, xh, c = info[3], info[4], info[5]
    pair = y % 2 if high else xh
    return pl.multiple_of((c ^ other_core) * 64 + (pair ^ other_pair) * 128, 64)


def prepare_kernel(info, bank, ids, piece_out, cols_out, total, pick):
    zz = pl.program_id(0)
    p, s, xl = info[0], info[1], info[2]

    @pl.when(zz == 0)
    def _():
        i0 = lax.broadcasted_iota(jnp.int32, (64, 64), 0)
        i1 = lax.broadcasted_iota(jnp.int32, (64, 64), 1)
        row_ids = (ids[...] - s * 256).astype(F4)
        row_ids = jnp.sum(jnp.where(i0 == i1, row_ids, 0.0), axis=1, keepdims=True)
        lane = lax.broadcasted_iota(jnp.int32, (64, 256), 1).astype(F4)
        pick[...] = jnp.where(row_ids == lane, 1.0, 0.0).astype(BF)
        total[...] = jnp.zeros_like(total)

    own_row = jnp.where(info[6] < 4, quarter(info, 0, 0, False), quarter(info, 0, 0, True))
    own_row = pl.multiple_of(own_row, 64)
    for half in range(2):
        got = dot(pick[...], bank[:, half * 1024 : half * 1024 + 1024])
        got = got * got
        total[...] += sum(got[:, i * 128 : i * 128 + 128] for i in range(8))
        for j in range(2):
            at = pl.multiple_of(half * 1024 + (xl ^ j) * 512, 512)
            piece_out[zz * 2 + half, :, j * 512 : j * 512 + 512] = bank[pl.ds(own_row, 64), pl.ds(at, 512)]

    @pl.when(zz == p // 4)
    def _():
        cols_out[...] = bank[:, pl.ds(pl.multiple_of(p % 4 * 512, 512), 512)]

    @pl.when(zz == 3)
    def _():
        scale = lax.rsqrt(jnp.sum(total[...], axis=1, keepdims=True) / 8192 + EPSILON)
        i0 = lax.broadcasted_iota(jnp.int32, (64, 64), 0)
        i1 = lax.broadcasted_iota(jnp.int32, (64, 64), 1)
        scale = jnp.sum(jnp.where(i0 == i1, scale, 0.0), axis=0, keepdims=True)
        hi = scale.astype(BF).astype(F4)
        mid = (scale - hi).astype(BF).astype(F4)
        low = scale - hi - mid
        first = jnp.concatenate([(ids[...] - s * 256).astype(F4), hi], 1)
        second = jnp.concatenate([mid, low], 1)
        row = lax.broadcasted_iota(jnp.int32, (64, 128), 0)
        extra = jnp.where(row == 0, first, jnp.where(row == 1, second, 0.0)).astype(BF)
        for to in range(8):
            piece_out[to, :, 1024:1152] = extra


def prepare(info, bank, ids):
    whole = lambda shape: pl.BlockSpec(shape, lambda i, info: (0,) * len(shape))
    return pl.pallas_call(
        prepare_kernel,
        grid_spec=pltpu.PrefetchScalarGridSpec(
            num_scalar_prefetch=1,
            grid=(4,),
            in_specs=[pl.BlockSpec((256, 2048), lambda i, info: (0, i)), whole((1, 64))],
            out_specs=[whole((8, 64, 1152)), whole((256, 512))],
            scratch_shapes=[pltpu.VMEM((64, 128), F4), pltpu.VMEM((64, 256), BF)],
        ),
        out_shape=[jax.ShapeDtypeStruct((8, 64, 1152), BF), jax.ShapeDtypeStruct((256, 512), BF)],
        compiler_params=pltpu.CompilerParams(dimension_semantics=("arbitrary",), vmem_limit_bytes=VMEM),
        cost_estimate=pl.CostEstimate(flops=2**28, bytes_accessed=5 * 2**20, transcendentals=64),
        name="prepare",
    )(info, bank, ids)


def address_kernel(info, extra, gains, out):
    z, xl = info[6], info[2]
    tokens = []
    for i in range(8):
        e = extra[i].astype(F4)
        scale = e[0:1, 64:128] + e[1:2, 0:64] + e[1:2, 64:128]
        tokens.append(jnp.concatenate([e[0:1, 0:64], scale], 1))
    tokens = jnp.concatenate(tokens, 0)

    def rows(b):
        g = gains[:, pl.ds(b, 512)]
        return [g[:, j * 128 : j * 128 + 128] for j in range(4)]

    mine = rows(pl.multiple_of((z * 2 + xl) * 512, 512)) + rows(pl.multiple_of((z * 2 + 1 - xl) * 512, 512))
    mine = jnp.concatenate(mine, 0)
    for q in range(16):
        out[q, 0:8] = tokens
        out[q, 8:16] = mine
        out[q, 16:24] = jnp.concatenate(rows(q * 512) * 2, 0)


def address(info, pieces, gains):
    whole = lambda shape: pl.BlockSpec(shape, lambda i, info: (0,) * len(shape))
    return pl.pallas_call(
        address_kernel,
        grid_spec=pltpu.PrefetchScalarGridSpec(
            num_scalar_prefetch=1,
            grid=(1,),
            in_specs=[pl.BlockSpec((8, 16, 128), lambda i, info: (0, 0, 8)), whole((1, 8192))],
            out_specs=whole((16, 24, 128)),
        ),
        out_shape=jax.ShapeDtypeStruct((16, 24, 128), F4),
        cost_estimate=pl.CostEstimate(flops=2**20, bytes_accessed=2**18, transcendentals=0),
        name="address",
    )(info, pieces, gains)


def fill(info, table, i, cols, high, own, core, pair, both):
    for j, src in enumerate((own, core, pair, both)):
        table[pl.ds(quarter(info, j % 2, j // 2, high), 64), cols] = src[i, :, 0:1024]


def project_kernel(
    info, own, core, xp, yp, xc, yc, gains, weights, part_out, calib_out, diag_out, table, calib
):
    zz = pl.program_id(0)
    xl, z = info[2], info[6]
    lane = lax.broadcasted_iota(jnp.int32, (64, 256), 1).astype(F4)
    for i in range(2):

        @pl.when(zz < 2)
        def _():
            fill(info, table.at[i], i, slice(0, 1024), False, own, core, xp, xc)

        @pl.when(zz >= 2)
        def _():
            fill(info, table.at[i], i, slice(0, 1024), True, own, core, yp, yc)

        extra = own[i, 0:16, 1024:1152].astype(F4)[0:8]
        extra = jnp.concatenate([extra] * 16, 0).T
        column = extra[0:64, 0:1]
        scale = extra[64:128, 0:1] + extra[0:64, 1:2] + extra[64:128, 1:2]
        pick = jnp.where(column == lane, 1.0, 0.0).astype(BF)
        rows = pl.ds(pl.multiple_of(zz * 128 + i * 64, 64), 64)
        for j in range(2):
            cols = slice(j * 512, j * 512 + 512)
            g = gains[:, pl.ds(pl.multiple_of((z * 2 + (xl ^ j)) * 512, 512), 512)]
            calib[rows, cols] = (dot(pick, table[i, :, cols]) * scale * g).astype(BF)

    @pl.when(zz == 3)
    def _():
        calib_out[...] = calib[...]
        part = dot(calib[...], weights[...]).astype(BF)
        for to in range(8):
            part_out[to] = part[to * 64 : to * 64 + 64]
        whole = calib[...].astype(F4)
        diag_out[...] = jnp.sum(whole * whole, axis=0, keepdims=True)


def project(info, pieces, gains, weights):
    whole = lambda shape: pl.BlockSpec(shape, lambda i, info: (0,) * len(shape))
    by_z = pl.BlockSpec((2, 64, 1152), lambda i, info: (i, 0, 0))
    low = pl.BlockSpec((2, 64, 1152), lambda i, info: (jnp.minimum(i, 1), 0, 0))
    high = pl.BlockSpec((2, 64, 1152), lambda i, info: (jnp.maximum(i - 2, 0), 0, 0))
    return pl.pallas_call(
        project_kernel,
        grid_spec=pltpu.PrefetchScalarGridSpec(
            num_scalar_prefetch=1,
            grid=(4,),
            in_specs=[by_z, by_z, low, high, low, high, whole((1, 8192)), whole((1024, 512))],
            out_specs=[whole((8, 64, 512)), whole((512, 1024)), whole((1, 1024))],
            scratch_shapes=[pltpu.VMEM((2, 256, 1024), BF), pltpu.VMEM((512, 1024), BF)],
        ),
        out_shape=[
            jax.ShapeDtypeStruct((8, 64, 512), BF),
            jax.ShapeDtypeStruct((512, 1024), BF),
            jax.ShapeDtypeStruct((1, 1024), F4),
        ],
        compiler_params=pltpu.CompilerParams(dimension_semantics=("arbitrary",), vmem_limit_bytes=VMEM),
        cost_estimate=pl.CostEstimate(flops=2**30, bytes_accessed=8 * 2**20, transcendentals=0),
        name="project",
    )(info, *pieces, gains, weights)


def numer_kernel(info, calib, model_out, diag, weights, out):
    xl = info[2]
    ratio = lax.broadcasted_iota(jnp.int32, (512, 512), 0) == lax.broadcasted_iota(jnp.int32, (512, 512), 1)
    for j in range(2):
        cols = slice(j * 512, j * 512 + 512)
        d = diag[:, cols] * ((1.0 - ALPHA) / 1024)
        d = jnp.sum(jnp.where(ratio, d, 0.0), axis=1, keepdims=True)
        got = contract_rows(calib[:, cols], model_out[...]) * (ALPHA / 1024)
        got = got + d * weights[cols, :].astype(F4)
        got = got.astype(BF)
        for q in range(16):
            out[q * 2 + (xl ^ j)] = got[q * 32 : q * 32 + 32]


def numer_call(info, calib, model_out, diag, weights):
    return pl.pallas_call(
        numer_kernel,
        in_specs=[pl.BlockSpec(memory_space=pltpu.SMEM)] + [pl.BlockSpec(memory_space=pltpu.VMEM)] * 4,
        out_specs=pl.BlockSpec(memory_space=pltpu.VMEM),
        out_shape=jax.ShapeDtypeStruct((32, 32, 512), BF),
        compiler_params=pltpu.CompilerParams(vmem_limit_bytes=VMEM),
        cost_estimate=pl.CostEstimate(flops=2**29, bytes_accessed=4 * 2**20, transcendentals=0),
        name="numer",
    )(info, calib, model_out, diag, weights)


ORDER = (0, 7, 1, 6, 2, 5, 3, 4)
STEPS = (3, 3, 2)


def gram_kernel(first, last, start, info, *refs):
    refs = list(refs)
    blocks = [refs.pop(0) for _ in range(3)]
    own, core, xp, yp, xc, yc, tokens, gains = [refs.pop(0) for _ in range(8)]
    if not first:
        before = refs.pop(0)
    if last:
        near, far = refs.pop(0), refs.pop(0)
    acc, table, pick, scale, calib = refs
    step = pl.program_id(0)
    at = info[7 + start + step]

    @pl.when(step == 0)
    def _():
        acc[...] = jnp.zeros_like(acc) if first else before[...]

    for i in range(2 if last else 3):

        @pl.when(step == i)
        def _(i=i):
            if last and i == 1:
                table[0:128, 0:512] = blocks[1][...]
                table[128:256, 0:512] = blocks[2][...]
            else:
                table[:, 0:512] = blocks[i][...]

    @pl.when(at < 4)
    def _():
        fill(info, table, 0, slice(512, 1536), False, own, core, xp, xc)

    @pl.when(at >= 4)
    def _():
        fill(info, table, 0, slice(512, 1536), True, own, core, yp, yc)

    lane = lax.broadcasted_iota(jnp.int32, (64, 256), 1).astype(F4)
    z_row = lax.broadcasted_iota(jnp.int32, (16, 8, 128), 1)
    token = jnp.sum(jnp.where(z_row == at, tokens[...], 0.0), axis=1)
    token = jnp.concatenate([token, jnp.zeros((112, 128), F4)], 0).T
    for m in range(16):
        part = slice(m * 64, m * 64 + 64)
        pick[part, :] = jnp.where(token[0:64, m : m + 1] == lane, 1.0, 0.0).astype(BF)
        scale[part, :] = jnp.broadcast_to(token[64:128, m : m + 1], (64, 128))

    for n in range(6):
        cols = slice(n * 256, n * 256 + 256)
        got = dot(pick[...], table[:, cols])
        for m in range(16):
            part = slice(m * 64, m * 64 + 64)
            r = scale[part, :]
            r = jnp.concatenate([r, r], 1)
            g = gains[m : m + 1, cols]
            calib[part, cols] = (got[part] * r * g).astype(BF)
    acc[...] += contract_rows(calib[:, 0:512], calib[:, 512:1536])

    if last:

        @pl.when(step == STEPS[-1] - 1)
        def _():
            near[...] = acc[:, 0:512]
            far[...] = acc[:, 512:1024].astype(BF)


def gram_call(i, info, blocks, pieces, tokens, gains, before):
    first, last = i == 0, i == len(STEPS) - 1
    start, steps = sum(STEPS[:i]), STEPS[i]
    whole = lambda shape: pl.BlockSpec(shape, lambda j, info: (0,) * len(shape))
    by_z = pl.BlockSpec((1, 64, 1152), lambda j, info: (info[7 + start + j], 0, 0))
    low = pl.BlockSpec((1, 64, 1152), lambda j, info: (jnp.minimum(info[7 + start + j], 3), 0, 0))
    high = pl.BlockSpec((1, 64, 1152), lambda j, info: (jnp.maximum(info[7 + start + j] - 4, 0), 0, 0))
    shapes = [jax.ShapeDtypeStruct((512, 1024), F4)]
    if last:
        shapes = [jax.ShapeDtypeStruct((512, 512), F4), jax.ShapeDtypeStruct((512, 512), BF)]
    blocks = blocks[start : start + 3]
    operands = [info, *blocks, *pieces, tokens, gains] + ([] if first else [before])
    return pl.pallas_call(
        lambda *refs: gram_kernel(first, last, start, *refs),
        grid_spec=pltpu.PrefetchScalarGridSpec(
            num_scalar_prefetch=1,
            grid=(steps,),
            in_specs=[whole(b.shape) for b in blocks]
            + [by_z, by_z, low, high, low, high, whole((16, 8, 128)), whole((16, 1536))]
            + ([] if first else [whole((512, 1024))]),
            out_specs=[whole(o.shape) for o in shapes],
            scratch_shapes=([pltpu.VMEM((512, 1024), F4)] if last else [])
            + [
                pltpu.VMEM((256, 1536), BF),
                pltpu.VMEM((1024, 256), BF),
                pltpu.VMEM((1024, 128), F4),
                pltpu.VMEM((1024, 1536), BF),
            ],
        ),
        out_shape=shapes,
        input_output_aliases={} if first or last else {len(operands) - 1: 0},
        compiler_params=pltpu.CompilerParams(dimension_semantics=("arbitrary",), vmem_limit_bytes=VMEM),
        cost_estimate=pl.CostEstimate(flops=steps * 2**31, bytes_accessed=6 * 2**20, transcendentals=0),
        name="gram" + str(i),
    )(*operands)


def local(bank, calib_ids, norm_gains, proj_slabs):
    p = lax.axis_index("mp")
    s = lax.axis_index("shard")
    y, xh, c = p // 4, p // 2 % 2, p % 2
    z, xl = s // 2, s % 2
    info = jnp.stack([p, s, xl, y, xh, c, z] + [(z + k) % 8 for k in ORDER]).astype(jnp.int32)
    weights = proj_slabs[0]

    tie = lax.optimization_barrier
    piece, bank_cols = prepare(info, bank, calib_ids)
    own, weights_other = tie((swap_z(piece), shift(weights, xl=1)))
    both = jnp.concatenate([weights, weights_other], 0)
    xp, yp, core = shift(own[:4], xh=1), shift(own[4:], yp=1), shift(own, c=1)
    tokens = lax.all_to_all(address(info, own, norm_gains), "mp", 0, 0, tiled=True)
    blocks = ring(bank_cols)
    xp, yp, core, tokens = tie((xp, yp, core, tokens))
    pieces = [own, core, xp, yp, shift(xp, c=1), shift(yp, c=1)]
    gains = jnp.concatenate([tokens[:, 16:20], tokens[:, 8:16]], 1).reshape(16, 1536)
    tokens = tokens[:, 0:8]

    partial_out, calib, diag = project(info, pieces, norm_gains, both)
    partial_out, info, *blocks = tie((partial_out, info, *blocks))
    (acc,) = gram_call(0, info, blocks, pieces, tokens, gains, None)
    partial_out, acc = tie((swap_z(partial_out), acc))
    model_out = jnp.sum(partial_out.astype(F4), 0).astype(BF)
    model_out, info = tie((jnp.broadcast_to(model_out[None], (8, 64, 512)), info))
    (acc,) = gram_call(1, info, blocks, pieces, tokens, gains, acc)
    model_out, acc = tie((swap_z(model_out), acc))

    numer = numer_call(info, calib, model_out.reshape(512, 512), diag, both)
    numer, info = tie((numer, info))
    near, far = gram_call(2, info, blocks, pieces, tokens, gains, acc)
    numer, near = tie((lax.all_to_all(numer, AXES, 0, 0, tiled=True, axis_index_groups=XLO_GROUPS), near))
    numer = jnp.sum(numer.astype(F4), 0).astype(BF)
    numer = lax.all_to_all(jnp.broadcast_to(numer[None], (16, 32, 512)), "mp", 0, 0, tiled=True)
    numer = numer.reshape(512, 512).astype(F4)

    gram = near + shift(far, xl=1).astype(F4)
    on_diag = (p == s) & (
        lax.broadcasted_iota(jnp.int32, (512, 512), 0) == lax.broadcasted_iota(jnp.int32, (512, 512), 1)
    )
    merged_gram = gram * jnp.where(on_diag, 1.0 / 1024, ALPHA / 1024)

    return (merged_gram, numer)


def solution(mesh):
    placed = (P("shard", None), P("mp", "shard"), P("mp", None), P("mp", "shard", None))
    return jax.shard_map(
        local,
        mesh=mesh,
        in_specs=placed,
        out_specs=(P("mp", "shard"), P("shard", None)),
        check_vma=False,
    )
```

time: 177 us -> 184 us (1.040)
  blocking collectives: 20 us -> 0 us
  starting transfers between devices: 40.7 us -> 54.1 us
  local copies, waits for them, and re-layouts: 3.22 us -> 8.04 us
  waiting for transfers between devices: 58.7 us -> 63 us
  Pallas kernels: 49.3 us -> 52 us
    all_to_all x1 -> x0, blocking collectives: 20 us -> none  [swap_z(): lax.all_to_all(x, 'shard', 0, 0, tiled=True, axis_index_groups=Z_GROUPS)]
    ppermute x11 -> x15, waiting for transfers between devices: 33.3 us -> 19.7 us  [shift(): return lax.ppermute(x, AXES, pairs)]
    all_to_all x2 -> x3, waiting for transfers between devices: 12 us -> 23.1 us  [swap_z(): lax.all_to_all(x, 'shard', 0, 0, tiled=True, axis_index_groups=Z_GROUPS)]
    all_to_all x2 -> x3, starting transfers between devices: 7.18 us -> 17.5 us  [swap_z(): lax.all_to_all(x, 'shard', 0, 0, tiled=True, axis_index_groups=Z_GROUPS)]
    all_to_all x1, waiting for transfers between devices: 0.01 us -> 7.41 us  [local(): lax.all_to_all(address(info, own, norm_gains), 'mp', 0, 0, tiled=True)]
    unnamed x24 -> x25, local copies, waits for them, and re-layouts: 0.89 us -> 3.98 us
    all_to_all x1, starting transfers between devices: 8.52 us -> 11.1 us  [local(): lax.all_to_all(numer, AXES, 0, 0, tiled=True, axis_index_groups=XLO_GROUPS)]
    ppermute x11 -> x15, starting transfers between devices: 12.1 us -> 14 us  [shift(): return lax.ppermute(x, AXES, pairs)]
  transfers between devices with their start and end apart: 16 -> 21, of which waited for: 11 -> 9; matrix products, arithmetic and copies ran while one was open for 2% -> 4% of each run, Pallas kernels for 18% -> 23%
where the time goes in v7:
time: 184 us; the launch traced here: 183 us
  waiting for transfers between devices  63 us (34%)
  starting transfers between devices  54.1 us (29%)
  Pallas kernels  52 us (28%)
  local copies, waits for them, and re-layouts  8.04 us (4%)
  other arithmetic  4.79 us (3%)
    pallas_call x3, Pallas kernels, gram_call(): pl.pallas_call(lambda *refs: gram_kernel(first, last, start, *refs), grid...  32.6 us
    all_to_all x3, waiting for transfers between devices, swap_z(): lax.all_to_all(x, 'shard', 0, 0, tiled=True, axis_index_groups=Z_GROUPS)  23.1 us
    ppermute x15, waiting for transfers between devices, shift(): return lax.ppermute(x, AXES, pairs)  19.7 us
    all_to_all x3, starting transfers between devices, swap_z(): lax.all_to_all(x, 'shard', 0, 0, tiled=True, axis_index_groups=Z_GROUPS)  17.5 us
    ppermute x15, starting transfers between devices, shift(): return lax.ppermute(x, AXES, pairs)  14 us
    all_to_all x1, starting transfers between devices, local(): lax.all_to_all(numer, AXES, 0, 0, tiled=True, axis_index_groups=XLO_GROUPS)  11.1 us
    pallas_call x1, Pallas kernels, project(): pl.pallas_call(project_kernel, grid_spec=pltpu.PrefetchScalarGridSpec(num...  8.08 us
    all_to_all x1, waiting for transfers between devices, local(): lax.all_to_all(jnp.broadcast_to(numer[None], (16, 32, 512)), 'mp', 0, 0,...  8.05 us
  transfers between devices with their start and end apart: 21, of which 9 were waited for; matrix products, arithmetic and copies ran while one was open for 4% of the time, Pallas kernels for 23%

profile of v7, /device:TPU:1, one launch (start us, length us, event | category | flops | bytes accessed | tf_op | source)
XLA Modules:
  0.0 182.9 jit_solution(879743401877474172)
XLA Ops:
  1.4 5.5 %prepare.1 = (bf16[8,64,1152]{2,1,0:T(8,128)(2,1)}, bf16[256,512]{1,0:T(8,128)(2,1)}) custom-call(s32[15]{0:T(128)} %stack.63.info.refs_0_, bf16[256,8192]{1,0:T(8,128)(2,1)} %bank.1, s32[1,64]{1,0:T(1,128)} %ids.1), custom_call_target="tpu_custom_call" | custom-call | flops 268435456 | bytes 5242880 | tf_op jit(solution)/shard_map/prepare/pallas_call | solution.py:104
  7.0 9.1 %all-to-all-start = ((bf16[8,64,1152]{2,1,0:T(8,128)(2,1)}), bf16[8,64,1152]{2,1,0:T(8,128)(2,1)S(1)}, u32[]{:S(2)}, u32[]{:S(2)}) async-start(bf16[8,64,1152]{2,1,0:T(8,128)(2,1)} %get-tuple-element.36), calls=%async_computation | async-start | bytes 2359296 | tf_op jit(solution)/shard_map/all_to_all | solution.py:31
  17.4 11.3 %collective-permute-done = bf16[512,512]{1,0:T(8,128)(2,1)S(1)} collective-permute-done((bf16[512,512]{1,0:T(8,128)(2,1)S(1)}, bf16[512,512]{1,0:T(8,128)(2,1)S(1)}, u32[]{:S(2)}, u32[]{:S(2)}) %collective-permute-start) | collective-permute-done | bytes 524320 | tf_op jit(solution)/shard_map/ppermute | solution.py:27
  29.5 18.7 %all-to-all-done.extra.own.refs_4_ = bf16[8,64,1152]{2,1,0:T(8,128)(2,1)S(1)} async-done(((bf16[8,64,1152]{2,1,0:T(8,128)(2,1)}), bf16[8,64,1152]{2,1,0:T(8,128)(2,1)S(1)}, u32[]{:S(2)}, u32[]{:S(2)}) %all-to-all-start) | async-done | bytes 1179680 | tf_op jit(solution)/shard_map/all_to_all | solution.py:31
  51.1 2.7 %collective-permute-start.1 = (bf16[4,64,1152]{2,1,0:T(8,128)(2,1)}, bf16[4,64,1152]{2,1,0:T(8,128)(2,1)}, u32[]{:S(2)}, u32[]{:S(2)}) collective-permute-start(bf16[4,64,1152]{2,1,0:T(8,128)(2,1)} %get-tuple-element.71), channel_id=1, source_target_pairs={{0,32},{1,33},{2,34},{3,35},{4,36},{5,37},{6,38},{7,39},{8,40},{9,... | collective-permute-start | bytes 1769480 | tf_op jit(solution)/shard_map/ppermute | solution.py:27
  55.3 2.2 %address.1 = f32[16,24,128]{2,1,0:T(8,128)} custom-call(s32[15]{0:T(128)} %stack.63.info.refs_0_, bf16[8,64,1152]{2,1,0:T(8,128)(2,1)} %copy-done, f32[1,8192]{1,0:T(1,128)} %gains.3), custom_call_target="tpu_custom_call" | custom-call | flops 1048576 | bytes 262144 | tf_op jit(solution)/shard_map/address/pallas_call | solution.py:143
  57.6 5.4 %all-to-all-start.1 = ((f32[16,24,128]{2,1,0:T(8,128)}), f32[16,24,128]{2,1,0:T(8,128)S(1)}, u32[]{:S(2)}, u32[]{:S(2)}) async-start(f32[16,24,128]{2,1,0:T(8,128)} %address.1), calls=%async_computation.1 | async-start | bytes 393216 | tf_op jit(solution)/shard_map/all_to_all | solution.py:366
  64.5 7.4 %all-to-all-done.1 = f32[16,24,128]{2,1,0:T(8,128)S(1)} async-done(((f32[16,24,128]{2,1,0:T(8,128)}), f32[16,24,128]{2,1,0:T(8,128)S(1)}, u32[]{:S(2)}, u32[]{:S(2)}) %all-to-all-start.1) | async-done | bytes 196640 | tf_op jit(solution)/shard_map/all_to_all | solution.py:366
  74.0 6.3 %collective-permute-done.11.refs_1_ = bf16[256,512]{1,0:T(8,128)(2,1)S(1)} collective-permute-done((bf16[256,512]{1,0:T(8,128)(2,1)}, bf16[256,512]{1,0:T(8,128)(2,1)S(1)}, u32[]{:S(2)}, u32[]{:S(2)}) %collective-permute-start.11) | collective-permute-done | bytes 262176 | tf_op jit(solution)/shard_map/ppermute | solution.py:27
  82.0 2.2 %pad_maximum_fusion.weights = bf16[1024,512]{1,0:T(8,128)(2,1)} fusion(bf16[512,512]{1,0:T(8,128)(2,1)} %copy-done.8, bf16[512,512]{1,0:T(8,128)(2,1)} %bitcast.26), kind=kLoop, calls=%fused_computation | loop fusion | flops 2097152 | bytes 2097152 | tf_op jit(solution)/shard_map/concatenate | solution.py:364
  85.9 8.1 %project.1 = (bf16[8,64,512]{2,1,0:T(8,128)(2,1)}, bf16[512,1024]{1,0:T(8,128)(2,1)}, f32[1,1024]{1,0:T(1,128)}) custom-call(s32[15]{0:T(128)} %stack.63.info.refs_0_, bf16[8,64,1152]{2,1,0:T(8,128)(2,1)} %copy-done, bf16[8,64,1152]{2,1,0:T(8,128)(2,1)} %copy-done.2, bf16[4,64,1152]{2,1,0:T(8,128)(2,1)} %collective-permute-done.1.xp.refs_6_, ...), custom_call_target="tpu_custom_call" | custom-call | flops 1073741824 | bytes 8388608 | tf_op jit(solution)/shard_map/project/pallas_call | solution.py:204
  94.0 3.9 %all-to-all-start.2 = ((bf16[8,64,512]{2,1,0:T(8,128)(2,1)}), bf16[8,64,512]{2,1,0:T(8,128)(2,1)S(1)}, u32[]{:S(2)}, u32[]{:S(2)}) async-start(bf16[8,64,512]{2,1,0:T(8,128)(2,1)} %get-tuple-element.44), calls=%async_computation.2 | async-start | bytes 1048576 | tf_op jit(solution)/shard_map/all_to_all | solution.py:31
  99.3 11.3 %gram0.1.refs_12_ = f32[512,1024]{1,0:T(8,128)} custom-call(s32[15]{0:T(128)} %stack.63.info.refs_0_, bf16[256,512]{1,0:T(8,128)(2,1)} %get-tuple-element.46.refs_1_, bf16[256,512]{1,0:T(8,128)(2,1)} %collective-permute-done.6.refs_2_, bf16[256,512]{1,0:T(8,128)(2,1)} %collective-permute-done.7.refs_3_, bf16[8,64,1152]{2,1,0:T(8,128)(2,1)} %copy-done, ...), custom_call_target="tpu_custom_call" | custom-call | flops 6442450944 | bytes 6291456 | tf_op jit(solution)/shard_map/gram0/pallas_call | solution.py:328
  110.5 2.2 %all-to-all-done.2 = bf16[8,64,512]{2,1,0:T(8,128)(2,1)S(1)} async-done(((bf16[8,64,512]{2,1,0:T(8,128)(2,1)}), bf16[8,64,512]{2,1,0:T(8,128)(2,1)S(1)}, u32[]{:S(2)}, u32[]{:S(2)}) %all-to-all-start.2) | async-done | bytes 524320 | tf_op jit(solution)/shard_map/all_to_all | solution.py:31
  113.7 4.4 %all-to-all-start.3 = ((bf16[8,64,512]{2,1,0:T(8,128)(2,1)}), bf16[8,64,512]{2,1,0:T(8,128)(2,1)S(1)}, u32[]{:S(2)}, u32[]{:S(2)}) async-start(bf16[8,64,512]{2,1,0:T(8,128)(2,1)} %broadcast_in_dim.20), calls=%async_computation.3 | async-start | bytes 1048576 | tf_op jit(solution)/shard_map/all_to_all | solution.py:31
  118.1 12.1 %gram1.1.refs_12_ = f32[512,1024]{1,0:T(8,128)} custom-call(s32[15]{0:T(128)} %stack.63.info.refs_0_, bf16[256,512]{1,0:T(8,128)(2,1)} %collective-permute-done.8.refs_1_, bf16[256,512]{1,0:T(8,128)(2,1)} %collective-permute-done.9.refs_2_, bf16[256,512]{1,0:T(8,128)(2,1)} %copy-done.10, ...), custom_call_target="tpu_custom_call", output_to_operand_aliasing={{}: (12, {})} | custom-call | flops 6442450944 | bytes 6291456 | tf_op jit(solution)/shard_map/gram1/pallas_call | solution.py:328
  130.2 2.2 %all-to-all-done.3 = bf16[8,64,512]{2,1,0:T(8,128)(2,1)S(1)} async-done(((bf16[8,64,512]{2,1,0:T(8,128)(2,1)}), bf16[8,64,512]{2,1,0:T(8,128)(2,1)S(1)}, u32[]{:S(2)}, u32[]{:S(2)}) %all-to-all-start.3) | async-done | bytes 524320 | tf_op jit(solution)/shard_map/all_to_all | solution.py:31
  133.2 3.5 %numer.1 = bf16[32,32,512]{2,1,0:T(8,128)(2,1)} custom-call(s32[15]{0:T(128)} %stack.63.info.refs_0_, bf16[512,1024]{1,0:T(8,128)(2,1)} %get-tuple-element.52.calib, bf16[512,512]{1,0:T(8,128)(2,1)} %bitcast.24, f32[1,1024]{1,0:T(1,128)} %get-tuple-element.59.diag, bf16[1024,512]{1,0:T(8,128)(2,1)} %pad_maximum_fusion.weights), custom_call_target="tpu_custom_call" | custom-call | flops 536870912 | bytes 4194304 | tf_op jit(solution)/shard_map/numer/pallas_call | solution.py:239
  136.7 11.1 %all-to-all-start.4 = ((bf16[32,32,512]{2,1,0:T(8,128)(2,1)}), bf16[32,32,512]{2,1,0:T(8,128)(2,1)S(1)}, u32[]{:S(2)}, u32[]{:S(2)}) async-start(bf16[32,32,512]{2,1,0:T(8,128)(2,1)} %numer.1), calls=%async_computation.4 | async-start | bytes 2097152 | tf_op jit(solution)/shard_map/all_to_all | solution.py:385
  147.8 9.3 %gram2.1 = (f32[512,512]{1,0:T(8,128)}, bf16[512,512]{1,0:T(8,128)(2,1)}) custom-call(s32[15]{0:T(128)} %stack.63.info.refs_0_, bf16[256,512]{1,0:T(8,128)(2,1)} %copy-done.9, bf16[128,512]{1,0:T(8,128)(2,1)} %collective-permute-done.12.refs_2_, bf16[128,512]{1,0:T(8,128)(2,1)} %collective-permute-done.13.refs_3_, bf16[8,64,1152]{2,1,0:T(8,128)(2,1)} %copy-done, ...), custom_call_target="tpu_custom_call" | custom-call | flops 4294967296 | bytes 6291456 | tf_op jit(solution)/shard_map/gram2/pallas_call | solution.py:328
  158.6 4.8 %all-to-all-done.4 = bf16[32,32,512]{2,1,0:T(8,128)(2,1)S(1)} async-done(((bf16[32,32,512]{2,1,0:T(8,128)(2,1)}), bf16[32,32,512]{2,1,0:T(8,128)(2,1)S(1)}, u32[]{:S(2)}, u32[]{:S(2)}) %all-to-all-start.4) | async-done | bytes 1048608 | tf_op jit(solution)/shard_map/all_to_all | solution.py:385
  164.4 6.1 %all-to-all-start.5 = ((bf16[16,32,512]{2,1,0:T(8,128)(2,1)}), bf16[16,32,512]{2,1,0:T(8,128)(2,1)S(1)}, u32[]{:S(2)}, u32[]{:S(2)}) async-start(bf16[16,32,512]{2,1,0:T(8,128)(2,1)} %broadcast_in_dim.23), calls=%async_computation.5 | async-start | bytes 1048576 | tf_op jit(solution)/shard_map/all_to_all | solution.py:387
  170.5 2.1 %collective-permute-done.14 = bf16[512,512]{1,0:T(8,128)(2,1)S(1)} collective-permute-done((bf16[512,512]{1,0:T(8,128)(2,1)}, bf16[512,512]{1,0:T(8,128)(2,1)S(1)}, u32[]{:S(2)}, u32[]{:S(2)}) %collective-permute-start.14) | collective-permute-done | bytes 524320 | tf_op jit(solution)/shard_map/ppermute | solution.py:27
  173.7 8.1 %all-to-all-done.5 = bf16[16,32,512]{2,1,0:T(8,128)(2,1)S(1)} async-done(((bf16[16,32,512]{2,1,0:T(8,128)(2,1)}), bf16[16,32,512]{2,1,0:T(8,128)(2,1)S(1)}, u32[]{:S(2)}, u32[]{:S(2)}) %all-to-all-start.5) | async-done | bytes 524320 | tf_op jit(solution)/shard_map/all_to_all | solution.py:387
  (64 shorter events, 21.9 us)
Async XLA Ops:
  7.0 46.9 %copy-start.11 = (bf16[256,512]{1,0:T(8,128)(2,1)S(1)}, bf16[256,512]{1,0:T(8,128)(2,1)}, u32[]{:S(2)}) copy-start(bf16[256,512]{1,0:T(8,128)(2,1)} %get-tuple-element.46.refs_1_) | copy-start | bytes 786436
  7.0 41.2 %all-to-all-start = ((bf16[8,64,1152]{2,1,0:T(8,128)(2,1)}), bf16[8,64,1152]{2,1,0:T(8,128)(2,1)S(1)}, u32[]{:S(2)}, u32[]{:S(2)}) async-start(bf16[8,64,1152]{2,1,0:T(8,128)(2,1)} %get-tuple-element.36), calls=%async_computation | async-start | bytes 2359296 | tf_op jit(solution)/shard_map/all_to_all | solution.py:31
  16.2 12.6 %collective-permute-start = (bf16[512,512]{1,0:T(8,128)(2,1)S(1)}, bf16[512,512]{1,0:T(8,128)(2,1)S(1)}, u32[]{:S(2)}, u32[]{:S(2)}) collective-permute-start(bf16[512,512]{1,0:T(8,128)(2,1)S(1)} %bitcast.27), channel_id=1, source_target_pairs={{0,1},{1,0},{2,3},{3,2},{4,5},{5,4},{6,7},{7,6},{8,9},{9,8},{10,11... | collective-permute-start | bytes 1572872 | tf_op jit(solution)/shard_map/ppermute | solution.py:27
  48.2 23.7 %collective-permute-start.3 = (bf16[8,64,1152]{2,1,0:T(8,128)(2,1)S(1)}, bf16[8,64,1152]{2,1,0:T(8,128)(2,1)S(1)}, u32[]{:S(2)}, u32[]{:S(2)}) collective-permute-start(bf16[8,64,1152]{2,1,0:T(8,128)(2,1)S(1)} %all-to-all-done.extra.own.refs_4_), channel_id=1, source_target_pairs={{0,16},{1,17},{2,18},{3,19},{4,20},{5,21},{6,22},{7,23},{8,24},{9,... | collective-permute-start | bytes 3538952 | tf_op jit(solution)/shard_map/ppermute | solution.py:27
  49.8 22.1 %collective-permute-start.2 = (bf16[4,64,1152]{2,1,0:T(8,128)(2,1)}, bf16[4,64,1152]{2,1,0:T(8,128)(2,1)S(1)}, u32[]{:S(2)}, u32[]{:S(2)}) collective-permute-start(bf16[4,64,1152]{2,1,0:T(8,128)(2,1)} %get-tuple-element.70), channel_id=1, source_target_pairs={{0,64},{1,65},{2,66},{3,67},{4,68},{5,69},{6,70},{7,71},{8,72},{9,... | collective-permute-start | bytes 1769480 | tf_op jit(solution)/shard_map/ppermute | solution.py:27
  51.1 20.8 %collective-permute-start.1 = (bf16[4,64,1152]{2,1,0:T(8,128)(2,1)}, bf16[4,64,1152]{2,1,0:T(8,128)(2,1)}, u32[]{:S(2)}, u32[]{:S(2)}) collective-permute-start(bf16[4,64,1152]{2,1,0:T(8,128)(2,1)} %get-tuple-element.71), channel_id=1, source_target_pairs={{0,32},{1,33},{2,34},{3,35},{4,36},{5,37},{6,38},{7,39},{8,40},{9,... | collective-permute-start | bytes 1769480 | tf_op jit(solution)/shard_map/ppermute | solution.py:27
  53.9 9.1 %collective-permute-start.7 = (bf16[256,512]{1,0:T(8,128)(2,1)S(1)}, bf16[256,512]{1,0:T(8,128)(2,1)}, u32[]{:S(2)}, u32[]{:S(2)}) collective-permute-start(bf16[256,512]{1,0:T(8,128)(2,1)S(1)} %copy-done.11), channel_id=1, source_target_pairs={{0,14},{1,15},{2,0},{3,1},{4,2},{5,3},{6,4},{7,5},{8,6},{9,7},{10,... | collective-permute-start | bytes 786440 | tf_op jit(solution)/shard_map/ppermute | solution.py:27
  53.9 10.1 %collective-permute-start.6 = (bf16[256,512]{1,0:T(8,128)(2,1)S(1)}, bf16[256,512]{1,0:T(8,128)(2,1)}, u32[]{:S(2)}, u32[]{:S(2)}) collective-permute-start(bf16[256,512]{1,0:T(8,128)(2,1)S(1)} %copy-done.11), channel_id=1, source_target_pairs={{0,2},{1,3},{2,4},{3,5},{4,6},{5,7},{6,8},{7,9},{8,10},{9,11},{10,... | collective-permute-start | bytes 786440 | tf_op jit(solution)/shard_map/ppermute | solution.py:27
  57.6 14.4 %all-to-all-start.1 = ((f32[16,24,128]{2,1,0:T(8,128)}), f32[16,24,128]{2,1,0:T(8,128)S(1)}, u32[]{:S(2)}, u32[]{:S(2)}) async-start(f32[16,24,128]{2,1,0:T(8,128)} %address.1), calls=%async_computation.1 | async-start | bytes 393216 | tf_op jit(solution)/shard_map/all_to_all | solution.py:366
  62.9 9.6 %collective-permute-start.9 = (bf16[256,512]{1,0:T(8,128)(2,1)}, bf16[256,512]{1,0:T(8,128)(2,1)}, u32[]{:S(2)}, u32[]{:S(2)}) collective-permute-start(bf16[256,512]{1,0:T(8,128)(2,1)} %collective-permute-done.7.refs_3_), channel_id=1, source_target_pairs={{0,14},{1,15},{2,0},{3,1},{4,2},{5,3},{6,4},{7,5},{8,6},{9,7},{10,... | collective-permute-start | bytes 786440 | tf_op jit(solution)/shard_map/ppermute | solution.py:27
  64.0 9.4 %collective-permute-start.8 = (bf16[256,512]{1,0:T(8,128)(2,1)}, bf16[256,512]{1,0:T(8,128)(2,1)}, u32[]{:S(2)}, u32[]{:S(2)}) collective-permute-start(bf16[256,512]{1,0:T(8,128)(2,1)} %collective-permute-done.6.refs_2_), channel_id=1, source_target_pairs={{0,2},{1,3},{2,4},{3,5},{4,6},{5,7},{6,8},{7,9},{8,10},{9,11},{10,... | collective-permute-start | bytes 786440 | tf_op jit(solution)/shard_map/ppermute | solution.py:27
  72.0 12.3 %collective-permute-start.4 = (bf16[4,64,1152]{2,1,0:T(8,128)(2,1)}, bf16[4,64,1152]{2,1,0:T(8,128)(2,1)S(1)}, u32[]{:S(2)}, u32[]{:S(2)}) collective-permute-start(bf16[4,64,1152]{2,1,0:T(8,128)(2,1)} %collective-permute-done.1.xp.refs_6_), channel_id=1, source_target_pairs={{0,16},{1,17},{2,18},{3,19},{4,20},{5,21},{6,22},{7,23},{8,24},{9,... | collective-permute-start | bytes 1769480 | tf_op jit(solution)/shard_map/ppermute | solution.py:27
  72.4 11.8 %collective-permute-start.5 = (bf16[4,64,1152]{2,1,0:T(8,128)(2,1)S(1)}, bf16[4,64,1152]{2,1,0:T(8,128)(2,1)S(1)}, u32[]{:S(2)}, u32[]{:S(2)}) collective-permute-start(bf16[4,64,1152]{2,1,0:T(8,128)(2,1)S(1)} %collective-permute-done.2.yp.refs_7_), channel_id=1, source_target_pairs={{0,16},{1,17},{2,18},{3,19},{4,20},{5,21},{6,22},{7,23},{8,24},{9,... | collective-permute-start | bytes 1769480 | tf_op jit(solution)/shard_map/ppermute | solution.py:27
  72.6 7.8 %collective-permute-start.11 = (bf16[256,512]{1,0:T(8,128)(2,1)}, bf16[256,512]{1,0:T(8,128)(2,1)S(1)}, u32[]{:S(2)}, u32[]{:S(2)}) collective-permute-start(bf16[256,512]{1,0:T(8,128)(2,1)} %collective-permute-done.9.refs_2_), channel_id=1, source_target_pairs={{0,14},{1,15},{2,0},{3,1},{4,2},{5,3},{6,4},{7,5},{8,6},{9,7},{10,... | collective-permute-start | bytes 786440 | tf_op jit(solution)/shard_map/ppermute | solution.py:27
  73.4 8.5 %collective-permute-start.10 = (bf16[256,512]{1,0:T(8,128)(2,1)}, bf16[256,512]{1,0:T(8,128)(2,1)S(1)}, u32[]{:S(2)}, u32[]{:S(2)}) collective-permute-start(bf16[256,512]{1,0:T(8,128)(2,1)} %collective-permute-done.8.refs_1_), channel_id=1, source_target_pairs={{0,2},{1,3},{2,4},{3,5},{4,6},{5,7},{6,8},{7,9},{8,10},{9,11},{10,... | collective-permute-start | bytes 786440 | tf_op jit(solution)/shard_map/ppermute | solution.py:27
  80.3 13.7 %copy-start.9 = (bf16[256,512]{1,0:T(8,128)(2,1)}, bf16[256,512]{1,0:T(8,128)(2,1)S(1)}, u32[]{:S(2)}) copy-start(bf16[256,512]{1,0:T(8,128)(2,1)S(1)} %collective-permute-done.11.refs_1_) | copy-start | bytes 786436
  80.3 13.7 %collective-permute-start.13 = (bf16[128,512]{1,0:T(8,128)(2,1)S(1)}, bf16[128,512]{1,0:T(8,128)(2,1)}, u32[]{:S(2)}, u32[]{:S(2)}) collective-permute-start(bf16[128,512]{1,0:T(8,128)(2,1)S(1)} %slice.29), channel_id=1, source_target_pairs={{0,14},{1,15},{2,0},{3,1},{4,2},{5,3},{6,4},{7,5},{8,6},{9,7},{10,... | collective-permute-start | bytes 393224 | tf_op jit(solution)/shard_map/ppermute | solution.py:27
  81.8 12.2 %collective-permute-start.12 = (bf16[128,512]{1,0:T(8,128)(2,1)S(1)}, bf16[128,512]{1,0:T(8,128)(2,1)}, u32[]{:S(2)}, u32[]{:S(2)}) collective-permute-start(bf16[128,512]{1,0:T(8,128)(2,1)S(1)} %slice.28), channel_id=1, source_target_pairs={{0,2},{1,3},{2,4},{3,5},{4,6},{5,7},{6,8},{7,9},{8,10},{9,11},{10,... | collective-permute-start | bytes 393224 | tf_op jit(solution)/shard_map/ppermute | solution.py:27
  94.0 18.7 %all-to-all-start.2 = ((bf16[8,64,512]{2,1,0:T(8,128)(2,1)}), bf16[8,64,512]{2,1,0:T(8,128)(2,1)S(1)}, u32[]{:S(2)}, u32[]{:S(2)}) async-start(bf16[8,64,512]{2,1,0:T(8,128)(2,1)} %get-tuple-element.44), calls=%async_computation.2 | async-start | bytes 1048576 | tf_op jit(solution)/shard_map/all_to_all | solution.py:31
  113.7 18.7 %all-to-all-start.3 = ((bf16[8,64,512]{2,1,0:T(8,128)(2,1)}), bf16[8,64,512]{2,1,0:T(8,128)(2,1)S(1)}, u32[]{:S(2)}, u32[]{:S(2)}) async-start(bf16[8,64,512]{2,1,0:T(8,128)(2,1)} %broadcast_in_dim.20), calls=%async_computation.3 | async-start | bytes 1048576 | tf_op jit(solution)/shard_map/all_to_all | solution.py:31
  136.7 26.7 %all-to-all-start.4 = ((bf16[32,32,512]{2,1,0:T(8,128)(2,1)}), bf16[32,32,512]{2,1,0:T(8,128)(2,1)S(1)}, u32[]{:S(2)}, u32[]{:S(2)}) async-start(bf16[32,32,512]{2,1,0:T(8,128)(2,1)} %numer.1), calls=%async_computation.4 | async-start | bytes 2097152 | tf_op jit(solution)/shard_map/all_to_all | solution.py:385
  157.1 15.4 %copy-start.3 = (f32[512,512]{1,0:T(8,128)S(1)}, f32[512,512]{1,0:T(8,128)}, u32[]{:S(2)}) copy-start(f32[512,512]{1,0:T(8,128)} %get-tuple-element.67) | copy-start | bytes 3145732
  157.1 15.4 %collective-permute-start.14 = (bf16[512,512]{1,0:T(8,128)(2,1)}, bf16[512,512]{1,0:T(8,128)(2,1)S(1)}, u32[]{:S(2)}, u32[]{:S(2)}) collective-permute-start(bf16[512,512]{1,0:T(8,128)(2,1)} %get-tuple-element.68), channel_id=1, source_target_pairs={{0,1},{1,0},{2,3},{3,2},{4,5},{5,4},{6,7},{7,6},{8,9},{9,8},{10,11... | collective-permute-start | bytes 1572872 | tf_op jit(solution)/shard_map/ppermute | solution.py:27
  164.4 17.4 %all-to-all-start.5 = ((bf16[16,32,512]{2,1,0:T(8,128)(2,1)}), bf16[16,32,512]{2,1,0:T(8,128)(2,1)S(1)}, u32[]{:S(2)}, u32[]{:S(2)}) async-start(bf16[16,32,512]{2,1,0:T(8,128)(2,1)} %broadcast_in_dim.23), calls=%async_computation.5 | async-start | bytes 1048576 | tf_op jit(solution)/shard_map/all_to_all | solution.py:387
  (9 other events, 56.4 us)

commit v8 on v7

--- a/solution.py
+++ b/solution.py
@@ -37,15 +37,6 @@
 
 def contract_rows(a, b):
     return lax.dot_general(a, b, (((0,), (0,)), ((), ())), preferred_element_type=F4)
-
-
-def ring(x):
-    z = [x]
-    u = d = x
-    for _ in range(3):
-        u, d = shift(u, z=1), shift(d, z=-1)
-        z += [u, d]
-    return z + [shift(u[:128], z=1), shift(d[128:], z=-1)]
 
 
 def quarter(info, other_core, other_pair, high):
@@ -215,7 +206,7 @@
             jax.ShapeDtypeStruct((512, 1024), BF),
             jax.ShapeDtypeStruct((1, 1024), F4),
         ],
-        compiler_params=pltpu.CompilerParams(dimension_semantics=("arbitrary",), vmem_limit_bytes=VMEM),
+        compiler_params=pltpu.CompilerParams(dimension_semantics=("arbitrary",), vmem_limit_bytes=20 * 2**20),
         cost_estimate=pl.CostEstimate(flops=2**30, bytes_accessed=8 * 2**20, transcendentals=0),
         name="project",
     )(info, *pieces, gains, weights)
@@ -323,7 +314,6 @@
     shapes = [jax.ShapeDtypeStruct((512, 1024), F4)]
     if last:
         shapes = [jax.ShapeDtypeStruct((512, 512), F4), jax.ShapeDtypeStruct((512, 512), BF)]
-    blocks = blocks[start : start + 3]
     operands = [info, *blocks, *pieces, tokens, gains] + ([] if first else [before])
     return pl.pallas_call(
         lambda *refs: gram_kernel(first, last, start, *refs),
@@ -360,28 +350,30 @@
 
     tie = lax.optimization_barrier
     piece, bank_cols = prepare(info, bank, calib_ids)
-    own, weights_other = tie((swap_z(piece), shift(weights, xl=1)))
-    both = jnp.concatenate([weights, weights_other], 0)
+    own, both = tie((swap_z(piece), jnp.concatenate([weights, shift(weights, xl=1)], 0)))
     xp, yp, core = shift(own[:4], xh=1), shift(own[4:], yp=1), shift(own, c=1)
     tokens = lax.all_to_all(address(info, own, norm_gains), "mp", 0, 0, tiled=True)
-    blocks = ring(bank_cols)
-    xp, yp, core, tokens = tie((xp, yp, core, tokens))
+    u1, d1 = shift(bank_cols, z=1), shift(bank_cols, z=-1)
+    xp, yp, core, tokens, u1, d1 = tie((xp, yp, core, tokens, u1, d1))
     pieces = [own, core, xp, yp, shift(xp, c=1), shift(yp, c=1)]
     gains = jnp.concatenate([tokens[:, 16:20], tokens[:, 8:16]], 1).reshape(16, 1536)
     tokens = tokens[:, 0:8]
 
     partial_out, calib, diag = project(info, pieces, norm_gains, both)
-    partial_out, info, *blocks = tie((partial_out, info, *blocks))
-    (acc,) = gram_call(0, info, blocks, pieces, tokens, gains, None)
-    partial_out, acc = tie((swap_z(partial_out), acc))
+    u2, d2 = shift(u1, z=1), shift(d1, z=-1)
+    partial_out, info, u2, d2 = tie((partial_out, info, u2, d2))
+    (acc,) = gram_call(0, info, [bank_cols, u1, d1], pieces, tokens, gains, None)
+    u3, d3 = shift(u2, z=1), shift(d2, z=-1)
+    partial_out, acc, u3, d3 = tie((swap_z(partial_out), acc, u3, d3))
     model_out = jnp.sum(partial_out.astype(F4), 0).astype(BF)
     model_out, info = tie((jnp.broadcast_to(model_out[None], (8, 64, 512)), info))
-    (acc,) = gram_call(1, info, blocks, pieces, tokens, gains, acc)
-    model_out, acc = tie((swap_z(model_out), acc))
+    (acc,) = gram_call(1, info, [u2, d2, u3], pieces, tokens, gains, acc)
+    far = [shift(u3[:128], z=1), shift(d3[128:], z=-1)]
+    model_out, acc, *far = tie((swap_z(model_out), acc, *far))
 
     numer = numer_call(info, calib, model_out.reshape(512, 512), diag, both)
     numer, info = tie((numer, info))
-    near, far = gram_call(2, info, blocks, pieces, tokens, gains, acc)
+    near, far = gram_call(2, info, [d3, *far], pieces, tokens, gains, acc)
     numer, near = tie((lax.all_to_all(numer, AXES, 0, 0, tiled=True, axis_index_groups=XLO_GROUPS), near))
     numer = jnp.sum(numer.astype(F4), 0).astype(BF)
     numer = lax.all_to_all(jnp.broadcast_to(numer[None], (16, 32, 512)), "mp", 0, 0, tiled=True)

time: 184 us -> 178 us (0.967)
  waiting for transfers between devices: 63 us -> 60.4 us
  other arithmetic: 4.79 us -> 2.63 us
  local copies, waits for them, and re-layouts: 8.04 us -> 9.91 us
    all_to_all x1, starting transfers between devices: 11.1 us -> 4.54 us  [local(): lax.all_to_all(numer, AXES, 0, 0, tiled=True, axis_index_groups=XLO_GROUPS)]
    ppermute x15, starting transfers between devices: 14 us -> 19.2 us  [shift(): return lax.ppermute(x, AXES, pairs)]
    concatenate x1, other arithmetic: 2.24 us -> 0.07 us  [local(): jnp.concatenate([weights, shift(weights, xl=1)], 0)]
    ppermute x15, waiting for transfers between devices: 19.7 us -> 17.7 us  [shift(): return lax.ppermute(x, AXES, pairs)]
    unnamed x25 -> x39, local copies, waits for them, and re-layouts: 3.98 us -> 3.98 us
where the time goes in v8:
time: 178 us; the launch traced here: 177 us
  waiting for transfers between devices  60.4 us (34%)
  starting transfers between devices  53.1 us (30%)
  Pallas kernels  50.3 us (28%)
  local copies, waits for them, and re-layouts  9.91 us (6%)
  other arithmetic  2.63 us (1%)
    pallas_call x3, Pallas kernels, gram_call(): pl.pallas_call(lambda *refs: gram_kernel(first, last, start, *refs), grid...  32.6 us
    all_to_all x3, waiting for transfers between devices, swap_z(): lax.all_to_all(x, 'shard', 0, 0, tiled=True, axis_index_groups=Z_GROUPS)  21.4 us
    ppermute x15, starting transfers between devices, shift(): return lax.ppermute(x, AXES, pairs)  19.2 us
    all_to_all x3, starting transfers between devices, swap_z(): lax.all_to_all(x, 'shard', 0, 0, tiled=True, axis_index_groups=Z_GROUPS)  17.8 us
    ppermute x15, waiting for transfers between devices, shift(): return lax.ppermute(x, AXES, pairs)  17.7 us
    all_to_all x1, waiting for transfers between devices, local(): lax.all_to_all(address(info, own, norm_gains), 'mp', 0, 0, tiled=True)  8.28 us
    all_to_all x1, waiting for transfers between devices, local(): lax.all_to_all(jnp.broadcast_to(numer[None], (16, 32, 512)), 'mp', 0, 0,...  8.15 us
    pallas_call x1, Pallas kernels, project(): pl.pallas_call(project_kernel, grid_spec=pltpu.PrefetchScalarGridSpec(num...  6.36 us
  transfers between devices with their start and end apart: 21, of which 9 were waited for; matrix products, arithmetic and copies ran while one was open for 4% of the time, Pallas kernels for 23%

profile of v8, /device:TPU:1, one launch (start us, length us, event | category | flops | bytes accessed | tf_op | source)
XLA Modules:
  0.0 177.3 jit_solution(1032104006305138323)
XLA Ops:
  1.5 5.6 %prepare.1 = (bf16[8,64,1152]{2,1,0:T(8,128)(2,1)}, bf16[256,512]{1,0:T(8,128)(2,1)}) custom-call(s32[15]{0:T(128)} %stack.63.info.refs_0_, bf16[256,8192]{1,0:T(8,128)(2,1)} %bank.1, s32[1,64]{1,0:T(1,128)} %ids.1), custom_call_target="tpu_custom_call" | custom-call | flops 268435456 | bytes 5242880 | tf_op jit(solution)/shard_map/prepare/pallas_call | solution.py:95
  7.1 9.1 %all-to-all-start = ((bf16[8,64,1152]{2,1,0:T(8,128)(2,1)}), bf16[8,64,1152]{2,1,0:T(8,128)(2,1)S(1)}, u32[]{:S(2)}, u32[]{:S(2)}) async-start(bf16[8,64,1152]{2,1,0:T(8,128)(2,1)} %get-tuple-element.35), calls=%async_computation | async-start | bytes 2359296 | tf_op jit(solution)/shard_map/all_to_all | solution.py:31
  17.5 11.3 %collective-permute-done = bf16[512,512]{1,0:T(8,128)(2,1)S(1)} collective-permute-done((bf16[512,512]{1,0:T(8,128)(2,1)S(1)}, bf16[512,512]{1,0:T(8,128)(2,1)S(1)}, u32[]{:S(2)}, u32[]{:S(2)}) %collective-permute-start) | collective-permute-done | bytes 524320 | tf_op jit(solution)/shard_map/ppermute | solution.py:27
  28.9 19.4 %all-to-all-done.extra.own.refs_4_ = bf16[8,64,1152]{2,1,0:T(8,128)(2,1)S(1)} async-done(((bf16[8,64,1152]{2,1,0:T(8,128)(2,1)}), bf16[8,64,1152]{2,1,0:T(8,128)(2,1)S(1)}, u32[]{:S(2)}, u32[]{:S(2)}) %all-to-all-start) | async-done | bytes 1179680 | tf_op jit(solution)/shard_map/all_to_all | solution.py:31
  49.9 2.7 %collective-permute-start.1 = (bf16[4,64,1152]{2,1,0:T(8,128)(2,1)}, bf16[4,64,1152]{2,1,0:T(8,128)(2,1)}, u32[]{:S(2)}, u32[]{:S(2)}) collective-permute-start(bf16[4,64,1152]{2,1,0:T(8,128)(2,1)} %get-tuple-element.69), channel_id=1, source_target_pairs={{0,32},{1,33},{2,34},{3,35},{4,36},{5,37},{6,38},{7,39},{8,40},{9,... | collective-permute-start | bytes 1769480 | tf_op jit(solution)/shard_map/ppermute | solution.py:27
  54.2 2.5 %collective-permute-start.5 = (bf16[256,512]{1,0:T(8,128)(2,1)}, bf16[256,512]{1,0:T(8,128)(2,1)}, u32[]{:S(2)}, u32[]{:S(2)}) collective-permute-start(bf16[256,512]{1,0:T(8,128)(2,1)} %get-tuple-element.37.refs_1_), channel_id=1, source_target_pairs={{0,14},{1,15},{2,0},{3,1},{4,2},{5,3},{6,4},{7,5},{8,6},{9,7},{10,... | collective-permute-start | bytes 786440 | tf_op jit(solution)/shard_map/ppermute | solution.py:27
  56.6 2.2 %address.1 = f32[16,24,128]{2,1,0:T(8,128)} custom-call(s32[15]{0:T(128)} %stack.63.info.refs_0_, bf16[8,64,1152]{2,1,0:T(8,128)(2,1)} %copy-done, f32[1,8192]{1,0:T(1,128)} %gains.3), custom_call_target="tpu_custom_call" | custom-call | flops 1048576 | bytes 262144 | tf_op jit(solution)/shard_map/address/pallas_call | solution.py:134
  58.8 5.5 %all-to-all-start.1 = ((f32[16,24,128]{2,1,0:T(8,128)}), f32[16,24,128]{2,1,0:T(8,128)}, u32[]{:S(2)}, u32[]{:S(2)}) async-start(f32[16,24,128]{2,1,0:T(8,128)} %address.1), calls=%async_computation.1 | async-start | bytes 393216 | tf_op jit(solution)/shard_map/all_to_all | solution.py:355
  64.3 8.3 %all-to-all-done.1 = f32[16,24,128]{2,1,0:T(8,128)} async-done(((f32[16,24,128]{2,1,0:T(8,128)}), f32[16,24,128]{2,1,0:T(8,128)}, u32[]{:S(2)}, u32[]{:S(2)}) %all-to-all-start.1) | async-done | bytes 196640 | tf_op jit(solution)/shard_map/all_to_all | solution.py:355
  73.6 2.7 %collective-permute-start.9 = (bf16[256,512]{1,0:T(8,128)(2,1)}, bf16[256,512]{1,0:T(8,128)(2,1)S(1)}, u32[]{:S(2)}, u32[]{:S(2)}) collective-permute-start(bf16[256,512]{1,0:T(8,128)(2,1)} %collective-permute-done.5.refs_3_), channel_id=1, source_target_pairs={{0,14},{1,15},{2,0},{3,1},{4,2},{5,3},{6,4},{7,5},{8,6},{9,7},{10,... | collective-permute-start | bytes 786440 | tf_op jit(solution)/shard_map/ppermute | solution.py:27
  78.6 6.4 %project.1 = (bf16[8,64,512]{2,1,0:T(8,128)(2,1)}, bf16[512,1024]{1,0:T(8,128)(2,1)S(1)}, f32[1,1024]{1,0:T(1,128)S(1)}) custom-call(s32[15]{0:T(128)S(1)} %copy-done.8, bf16[8,64,1152]{2,1,0:T(8,128)(2,1)S(1)} %copy-done.1, bf16[8,64,1152]{2,1,0:T(8,128)(2,1)S(1)} %collective-permute-done.3.core.refs_5_, ...), custom_call_target="tpu_custom_call" | custom-call | flops 1073741824 | bytes 8388608 | tf_op jit(solution)/shard_map/project/pallas_call | solution.py:195
  86.0 3.5 %all-to-all-start.2 = ((bf16[8,64,512]{2,1,0:T(8,128)(2,1)}), bf16[8,64,512]{2,1,0:T(8,128)(2,1)S(1)}, u32[]{:S(2)}, u32[]{:S(2)}) async-start(bf16[8,64,512]{2,1,0:T(8,128)(2,1)} %get-tuple-element.45), calls=%async_computation.2 | async-start | bytes 1048576 | tf_op jit(solution)/shard_map/all_to_all | solution.py:31
  94.4 11.2 %gram0.1.refs_12_ = f32[512,1024]{1,0:T(8,128)} custom-call(s32[15]{0:T(128)} %stack.63.info.refs_0_, bf16[256,512]{1,0:T(8,128)(2,1)} %get-tuple-element.37.refs_1_, bf16[256,512]{1,0:T(8,128)(2,1)} %collective-permute-done.4.refs_2_, bf16[256,512]{1,0:T(8,128)(2,1)} %collective-permute-done.5.refs_3_, bf16[8,64,1152]{2,1,0:T(8,128)(2,1)} %copy-done, ...), custom_call_target="tpu_custom_call" | custom-call | flops 6442450944 | bytes 6291456 | tf_op jit(solution)/shard_map/gram0/pallas_call | solution.py:318
  105.6 3.7 %collective-permute-done.10.refs_3_ = bf16[256,512]{1,0:T(8,128)(2,1)S(1)} collective-permute-done((bf16[256,512]{1,0:T(8,128)(2,1)S(1)}, bf16[256,512]{1,0:T(8,128)(2,1)S(1)}, u32[]{:S(2)}, u32[]{:S(2)}) %collective-permute-start.10) | collective-permute-done | bytes 262176 | tf_op jit(solution)/shard_map/ppermute | solution.py:27
  110.4 5.2 %all-to-all-start.3 = ((bf16[8,64,512]{2,1,0:T(8,128)(2,1)}), bf16[8,64,512]{2,1,0:T(8,128)(2,1)S(1)}, u32[]{:S(2)}, u32[]{:S(2)}) async-start(bf16[8,64,512]{2,1,0:T(8,128)(2,1)} %broadcast_in_dim.20), calls=%async_computation.3 | async-start | bytes 1048576 | tf_op jit(solution)/shard_map/all_to_all | solution.py:31
  118.4 12.1 %gram1.1.refs_12_ = f32[512,1024]{1,0:T(8,128)} custom-call(s32[15]{0:T(128)} %stack.63.info.refs_0_, bf16[256,512]{1,0:T(8,128)(2,1)} %copy-done.15, bf16[256,512]{1,0:T(8,128)(2,1)} %copy-done.16, bf16[256,512]{1,0:T(8,128)(2,1)} %copy-done.14, bf16[8,64,1152]{2,1,0:T(8,128)(2,1)} %copy-done, ...), custom_call_target="tpu_custom_call", output_to_operand_aliasing={{}: (12, {})} | custom-call | flops 6442450944 | bytes 6291456 | tf_op jit(solution)/shard_map/gram1/pallas_call | solution.py:318
  131.2 2.0 %all-to-all-done.3 = bf16[8,64,512]{2,1,0:T(8,128)(2,1)S(1)} async-done(((bf16[8,64,512]{2,1,0:T(8,128)(2,1)}), bf16[8,64,512]{2,1,0:T(8,128)(2,1)S(1)}, u32[]{:S(2)}, u32[]{:S(2)}) %all-to-all-start.3) | async-done | bytes 524320 | tf_op jit(solution)/shard_map/all_to_all | solution.py:31
  134.1 3.5 %numer.1 = bf16[32,32,512]{2,1,0:T(8,128)(2,1)} custom-call(s32[15]{0:T(128)} %stack.63.info.refs_0_, bf16[512,1024]{1,0:T(8,128)(2,1)} %copy-done.4, bf16[512,512]{1,0:T(8,128)(2,1)} %bitcast.24, f32[1,1024]{1,0:T(1,128)} %copy-done.9, bf16[1024,512]{1,0:T(8,128)(2,1)} %copy-done.2), custom_call_target="tpu_custom_call" | custom-call | flops 536870912 | bytes 4194304 | tf_op jit(solution)/shard_map/numer/pallas_call | solution.py:230
  137.6 4.5 %all-to-all-start.4 = ((bf16[32,32,512]{2,1,0:T(8,128)(2,1)}), bf16[32,32,512]{2,1,0:T(8,128)(2,1)S(1)}, u32[]{:S(2)}, u32[]{:S(2)}) async-start(bf16[32,32,512]{2,1,0:T(8,128)(2,1)} %numer.1), calls=%async_computation.4 | async-start | bytes 2097152 | tf_op jit(solution)/shard_map/all_to_all | solution.py:377
  142.2 9.3 %gram2.1 = (f32[512,512]{1,0:T(8,128)}, bf16[512,512]{1,0:T(8,128)(2,1)}) custom-call(s32[15]{0:T(128)} %stack.63.info.refs_0_, bf16[256,512]{1,0:T(8,128)(2,1)} %copy-done.13, bf16[128,512]{1,0:T(8,128)(2,1)} %copy-done.17, bf16[128,512]{1,0:T(8,128)(2,1)} %copy-done.18, bf16[8,64,1152]{2,1,0:T(8,128)(2,1)} %copy-done, bf16[8,64,1152]{2,1,0:T(8,128)(2,1)} %copy-done.3, ...), custom_call_target="tpu_custom_call" | custom-call | flops 4294967296 | bytes 6291456 | tf_op jit(solution)/shard_map/gram2/pallas_call | solution.py:318
  152.9 4.8 %all-to-all-done.4 = bf16[32,32,512]{2,1,0:T(8,128)(2,1)S(1)} async-done(((bf16[32,32,512]{2,1,0:T(8,128)(2,1)}), bf16[32,32,512]{2,1,0:T(8,128)(2,1)S(1)}, u32[]{:S(2)}, u32[]{:S(2)}) %all-to-all-start.4) | async-done | bytes 1048608 | tf_op jit(solution)/shard_map/all_to_all | solution.py:377
  158.8 6.1 %all-to-all-start.5 = ((bf16[16,32,512]{2,1,0:T(8,128)(2,1)}), bf16[16,32,512]{2,1,0:T(8,128)(2,1)S(1)}, u32[]{:S(2)}, u32[]{:S(2)}) async-start(bf16[16,32,512]{2,1,0:T(8,128)(2,1)} %broadcast_in_dim.23), calls=%async_computation.5 | async-start | bytes 1048576 | tf_op jit(solution)/shard_map/all_to_all | solution.py:379
  164.9 2.0 %collective-permute-done.14 = bf16[512,512]{1,0:T(8,128)(2,1)S(1)} collective-permute-done((bf16[512,512]{1,0:T(8,128)(2,1)}, bf16[512,512]{1,0:T(8,128)(2,1)S(1)}, u32[]{:S(2)}, u32[]{:S(2)}) %collective-permute-start.14) | collective-permute-done | bytes 524320 | tf_op jit(solution)/shard_map/ppermute | solution.py:27
  168.0 8.1 %all-to-all-done.5 = bf16[16,32,512]{2,1,0:T(8,128)(2,1)S(1)} async-done(((bf16[16,32,512]{2,1,0:T(8,128)(2,1)}), bf16[16,32,512]{2,1,0:T(8,128)(2,1)S(1)}, u32[]{:S(2)}, u32[]{:S(2)}) %all-to-all-start.5) | async-done | bytes 524320 | tf_op jit(solution)/shard_map/all_to_all | solution.py:379
  (78 shorter events, 24.6 us)
Async XLA Ops:
  7.1 41.2 %all-to-all-start = ((bf16[8,64,1152]{2,1,0:T(8,128)(2,1)}), bf16[8,64,1152]{2,1,0:T(8,128)(2,1)S(1)}, u32[]{:S(2)}, u32[]{:S(2)}) async-start(bf16[8,64,1152]{2,1,0:T(8,128)(2,1)} %get-tuple-element.35), calls=%async_computation | async-start | bytes 2359296 | tf_op jit(solution)/shard_map/all_to_all | solution.py:31
  16.2 12.6 %collective-permute-start = (bf16[512,512]{1,0:T(8,128)(2,1)S(1)}, bf16[512,512]{1,0:T(8,128)(2,1)S(1)}, u32[]{:S(2)}, u32[]{:S(2)}) collective-permute-start(bf16[512,512]{1,0:T(8,128)(2,1)S(1)} %bitcast.26), channel_id=1, source_target_pairs={{0,1},{1,0},{2,3},{3,2},{4,5},{5,4},{6,7},{7,6},{8,9},{9,8},{10,11... | collective-permute-start | bytes 1572872 | tf_op jit(solution)/shard_map/ppermute | solution.py:27
  28.9 48.3 %copy-start.2 = (bf16[1024,512]{1,0:T(8,128)(2,1)}, bf16[1024,512]{1,0:T(8,128)(2,1)S(1)}, u32[]{:S(2)}) copy-start(bf16[1024,512]{1,0:T(8,128)(2,1)S(1)} %pad_maximum_fusion.weights) | copy-start | bytes 3145732
  28.9 48.3 %copy-start.7 = (f32[1,8192]{1,0:T(1,128)S(1)}, f32[1,8192]{1,0:T(1,128)}, u32[]{:S(2)}) copy-start(f32[1,8192]{1,0:T(1,128)} %gains.3) | copy-start | bytes 98308
  28.9 48.3 %copy-start.8 = (s32[15]{0:T(128)S(1)}, s32[15]{0:T(128)}, u32[]{:S(2)}) copy-start(s32[15]{0:T(128)} %stack.63.info.refs_0_) | copy-start | bytes 184
  48.3 24.3 %collective-permute-start.3 = (bf16[8,64,1152]{2,1,0:T(8,128)(2,1)S(1)}, bf16[8,64,1152]{2,1,0:T(8,128)(2,1)S(1)}, u32[]{:S(2)}, u32[]{:S(2)}) collective-permute-start(bf16[8,64,1152]{2,1,0:T(8,128)(2,1)S(1)} %all-to-all-done.extra.own.refs_4_), channel_id=1, source_target_pairs={{0,16},{1,17},{2,18},{3,19},{4,20},{5,21},{6,22},{7,23},{8,24},{9,... | collective-permute-start | bytes 3538952 | tf_op jit(solution)/shard_map/ppermute | solution.py:27
  49.9 22.7 %collective-permute-start.1 = (bf16[4,64,1152]{2,1,0:T(8,128)(2,1)}, bf16[4,64,1152]{2,1,0:T(8,128)(2,1)}, u32[]{:S(2)}, u32[]{:S(2)}) collective-permute-start(bf16[4,64,1152]{2,1,0:T(8,128)(2,1)} %get-tuple-element.69), channel_id=1, source_target_pairs={{0,32},{1,33},{2,34},{3,35},{4,36},{5,37},{6,38},{7,39},{8,40},{9,... | collective-permute-start | bytes 1769480 | tf_op jit(solution)/shard_map/ppermute | solution.py:27
  52.7 20.0 %collective-permute-start.2 = (bf16[4,64,1152]{2,1,0:T(8,128)(2,1)}, bf16[4,64,1152]{2,1,0:T(8,128)(2,1)}, u32[]{:S(2)}, u32[]{:S(2)}) collective-permute-start(bf16[4,64,1152]{2,1,0:T(8,128)(2,1)} %get-tuple-element.68), channel_id=1, source_target_pairs={{0,64},{1,65},{2,66},{3,67},{4,68},{5,69},{6,70},{7,71},{8,72},{9,... | collective-permute-start | bytes 1769480 | tf_op jit(solution)/shard_map/ppermute | solution.py:27
  54.0 10.4 %collective-permute-start.4 = (bf16[256,512]{1,0:T(8,128)(2,1)}, bf16[256,512]{1,0:T(8,128)(2,1)}, u32[]{:S(2)}, u32[]{:S(2)}) collective-permute-start(bf16[256,512]{1,0:T(8,128)(2,1)} %get-tuple-element.37.refs_1_), channel_id=1, source_target_pairs={{0,2},{1,3},{2,4},{3,5},{4,6},{5,7},{6,8},{7,9},{8,10},{9,11},{10,... | collective-permute-start | bytes 786440 | tf_op jit(solution)/shard_map/ppermute | solution.py:27
  54.2 10.1 %collective-permute-start.5 = (bf16[256,512]{1,0:T(8,128)(2,1)}, bf16[256,512]{1,0:T(8,128)(2,1)}, u32[]{:S(2)}, u32[]{:S(2)}) collective-permute-start(bf16[256,512]{1,0:T(8,128)(2,1)} %get-tuple-element.37.refs_1_), channel_id=1, source_target_pairs={{0,14},{1,15},{2,0},{3,1},{4,2},{5,3},{6,4},{7,5},{8,6},{9,7},{10,... | collective-permute-start | bytes 786440 | tf_op jit(solution)/shard_map/ppermute | solution.py:27
  58.8 13.8 %all-to-all-start.1 = ((f32[16,24,128]{2,1,0:T(8,128)}), f32[16,24,128]{2,1,0:T(8,128)}, u32[]{:S(2)}, u32[]{:S(2)}) async-start(f32[16,24,128]{2,1,0:T(8,128)} %address.1), calls=%async_computation.1 | async-start | bytes 393216 | tf_op jit(solution)/shard_map/all_to_all | solution.py:355
  72.6 4.5 %collective-permute-start.6 = (bf16[4,64,1152]{2,1,0:T(8,128)(2,1)}, bf16[4,64,1152]{2,1,0:T(8,128)(2,1)S(1)}, u32[]{:S(2)}, u32[]{:S(2)}) collective-permute-start(bf16[4,64,1152]{2,1,0:T(8,128)(2,1)} %collective-permute-done.1.xp.refs_6_), channel_id=1, source_target_pairs={{0,16},{1,17},{2,18},{3,19},{4,20},{5,21},{6,22},{7,23},{8,24},{9,... | collective-permute-start | bytes 1769480 | tf_op jit(solution)/shard_map/ppermute | solution.py:27
  73.5 3.6 %collective-permute-start.7 = (bf16[4,64,1152]{2,1,0:T(8,128)(2,1)}, bf16[4,64,1152]{2,1,0:T(8,128)(2,1)S(1)}, u32[]{:S(2)}, u32[]{:S(2)}) collective-permute-start(bf16[4,64,1152]{2,1,0:T(8,128)(2,1)} %collective-permute-done.2.yp.refs_7_), channel_id=1, source_target_pairs={{0,16},{1,17},{2,18},{3,19},{4,20},{5,21},{6,22},{7,23},{8,24},{9,... | collective-permute-start | bytes 1769480 | tf_op jit(solution)/shard_map/ppermute | solution.py:27
  73.6 12.4 %collective-permute-start.8 = (bf16[256,512]{1,0:T(8,128)(2,1)}, bf16[256,512]{1,0:T(8,128)(2,1)S(1)}, u32[]{:S(2)}, u32[]{:S(2)}) collective-permute-start(bf16[256,512]{1,0:T(8,128)(2,1)} %collective-permute-done.4.refs_2_), channel_id=1, source_target_pairs={{0,2},{1,3},{2,4},{3,5},{4,6},{5,7},{6,8},{7,9},{8,10},{9,11},{10,... | collective-permute-start | bytes 786440 | tf_op jit(solution)/shard_map/ppermute | solution.py:27
  73.6 12.4 %collective-permute-start.9 = (bf16[256,512]{1,0:T(8,128)(2,1)}, bf16[256,512]{1,0:T(8,128)(2,1)S(1)}, u32[]{:S(2)}, u32[]{:S(2)}) collective-permute-start(bf16[256,512]{1,0:T(8,128)(2,1)} %collective-permute-done.5.refs_3_), channel_id=1, source_target_pairs={{0,14},{1,15},{2,0},{3,1},{4,2},{5,3},{6,4},{7,5},{8,6},{9,7},{10,... | collective-permute-start | bytes 786440 | tf_op jit(solution)/shard_map/ppermute | solution.py:27
  86.0 23.4 %all-to-all-start.2 = ((bf16[8,64,512]{2,1,0:T(8,128)(2,1)}), bf16[8,64,512]{2,1,0:T(8,128)(2,1)S(1)}, u32[]{:S(2)}, u32[]{:S(2)}) async-start(bf16[8,64,512]{2,1,0:T(8,128)(2,1)} %get-tuple-element.45), calls=%async_computation.2 | async-start | bytes 1048576 | tf_op jit(solution)/shard_map/all_to_all | solution.py:31
  91.7 17.7 %collective-permute-start.10 = (bf16[256,512]{1,0:T(8,128)(2,1)S(1)}, bf16[256,512]{1,0:T(8,128)(2,1)S(1)}, u32[]{:S(2)}, u32[]{:S(2)}) collective-permute-start(bf16[256,512]{1,0:T(8,128)(2,1)S(1)} %collective-permute-done.8.refs_1_), channel_id=1, source_target_pairs={{0,2},{1,3},{2,4},{3,5},{4,6},{5,7},{6,8},{7,9},{8,10},{9,11},{10,... | collective-permute-start | bytes 786440 | tf_op jit(solution)/shard_map/ppermute | solution.py:27
  93.1 16.3 %collective-permute-start.11 = (bf16[256,512]{1,0:T(8,128)(2,1)S(1)}, bf16[256,512]{1,0:T(8,128)(2,1)S(1)}, u32[]{:S(2)}, u32[]{:S(2)}) collective-permute-start(bf16[256,512]{1,0:T(8,128)(2,1)S(1)} %collective-permute-done.9.refs_2_), channel_id=1, source_target_pairs={{0,14},{1,15},{2,0},{3,1},{4,2},{5,3},{6,4},{7,5},{8,6},{9,7},{10,... | collective-permute-start | bytes 786440 | tf_op jit(solution)/shard_map/ppermute | solution.py:27
  110.4 22.8 %all-to-all-start.3 = ((bf16[8,64,512]{2,1,0:T(8,128)(2,1)}), bf16[8,64,512]{2,1,0:T(8,128)(2,1)S(1)}, u32[]{:S(2)}, u32[]{:S(2)}) async-start(bf16[8,64,512]{2,1,0:T(8,128)(2,1)} %broadcast_in_dim.20), calls=%async_computation.3 | async-start | bytes 1048576 | tf_op jit(solution)/shard_map/all_to_all | solution.py:31
  115.6 15.7 %collective-permute-start.12 = (bf16[128,512]{1,0:T(8,128)(2,1)S(1)}, bf16[128,512]{1,0:T(8,128)(2,1)S(1)}, u32[]{:S(2)}, u32[]{:S(2)}) collective-permute-start(bf16[128,512]{1,0:T(8,128)(2,1)S(1)} %slice.26), channel_id=1, source_target_pairs={{0,2},{1,3},{2,4},{3,5},{4,6},{5,7},{6,8},{7,9},{8,10},{9,11},{10,... | collective-permute-start | bytes 393224 | tf_op jit(solution)/shard_map/ppermute | solution.py:27
  117.1 14.1 %collective-permute-start.13 = (bf16[128,512]{1,0:T(8,128)(2,1)S(1)}, bf16[128,512]{1,0:T(8,128)(2,1)S(1)}, u32[]{:S(2)}, u32[]{:S(2)}) collective-permute-start(bf16[128,512]{1,0:T(8,128)(2,1)S(1)} %slice.27), channel_id=1, source_target_pairs={{0,14},{1,15},{2,0},{3,1},{4,2},{5,3},{6,4},{7,5},{8,6},{9,7},{10,... | collective-permute-start | bytes 393224 | tf_op jit(solution)/shard_map/ppermute | solution.py:27
  137.6 20.2 %all-to-all-start.4 = ((bf16[32,32,512]{2,1,0:T(8,128)(2,1)}), bf16[32,32,512]{2,1,0:T(8,128)(2,1)S(1)}, u32[]{:S(2)}, u32[]{:S(2)}) async-start(bf16[32,32,512]{2,1,0:T(8,128)(2,1)} %numer.1), calls=%async_computation.4 | async-start | bytes 2097152 | tf_op jit(solution)/shard_map/all_to_all | solution.py:377
  151.5 15.4 %collective-permute-start.14 = (bf16[512,512]{1,0:T(8,128)(2,1)}, bf16[512,512]{1,0:T(8,128)(2,1)S(1)}, u32[]{:S(2)}, u32[]{:S(2)}) collective-permute-start(bf16[512,512]{1,0:T(8,128)(2,1)} %get-tuple-element.66), channel_id=1, source_target_pairs={{0,1},{1,0},{2,3},{3,2},{4,5},{5,4},{6,7},{7,6},{8,9},{9,8},{10,11... | collective-permute-start | bytes 1572872 | tf_op jit(solution)/shard_map/ppermute | solution.py:27
  158.8 17.4 %all-to-all-start.5 = ((bf16[16,32,512]{2,1,0:T(8,128)(2,1)}), bf16[16,32,512]{2,1,0:T(8,128)(2,1)S(1)}, u32[]{:S(2)}, u32[]{:S(2)}) async-start(bf16[16,32,512]{2,1,0:T(8,128)(2,1)} %broadcast_in_dim.23), calls=%async_computation.5 | async-start | bytes 1048576 | tf_op jit(solution)/shard_map/all_to_all | solution.py:379
  (16 other events, 173.7 us)

commit v9 on v8

--- a/solution.py
+++ b/solution.py
@@ -355,18 +355,18 @@
     tokens = lax.all_to_all(address(info, own, norm_gains), "mp", 0, 0, tiled=True)
     u1, d1 = shift(bank_cols, z=1), shift(bank_cols, z=-1)
     xp, yp, core, tokens, u1, d1 = tie((xp, yp, core, tokens, u1, d1))
-    pieces = [own, core, xp, yp, shift(xp, c=1), shift(yp, c=1)]
     gains = jnp.concatenate([tokens[:, 16:20], tokens[:, 8:16]], 1).reshape(16, 1536)
-    tokens = tokens[:, 0:8]
+    xc, yc, gains, tokens = tie((shift(xp, c=1), shift(yp, c=1), gains, tokens[:, 0:8]))
+    pieces = [own, core, xp, yp, xc, yc]
 
     partial_out, calib, diag = project(info, pieces, norm_gains, both)
     u2, d2 = shift(u1, z=1), shift(d1, z=-1)
     partial_out, info, u2, d2 = tie((partial_out, info, u2, d2))
     (acc,) = gram_call(0, info, [bank_cols, u1, d1], pieces, tokens, gains, None)
     u3, d3 = shift(u2, z=1), shift(d2, z=-1)
-    partial_out, acc, u3, d3 = tie((swap_z(partial_out), acc, u3, d3))
+    partial_out, acc = tie((swap_z(partial_out), acc))
     model_out = jnp.sum(partial_out.astype(F4), 0).astype(BF)
-    model_out, info = tie((jnp.broadcast_to(model_out[None], (8, 64, 512)), info))
+    model_out, info, u3, d3 = tie((jnp.broadcast_to(model_out[None], (8, 64, 512)), info, u3, d3))
     (acc,) = gram_call(1, info, [u2, d2, u3], pieces, tokens, gains, acc)
     far = [shift(u3[:128], z=1), shift(d3[128:], z=-1)]
     model_out, acc, *far = tie((swap_z(model_out), acc, *far))

time: 178 us -> 181 us (1.017)
  waiting for transfers between devices: 60.4 us -> 63.1 us
    all_to_all x3, waiting for transfers between devices: 21.4 us -> 24.9 us  [swap_z(): lax.all_to_all(x, 'shard', 0, 0, tiled=True, axis_index_groups=Z_GROUPS)]
  transfers between devices with their start and end apart: 21 -> 21, of which waited for: 9 -> 11; matrix products, arithmetic and copies ran while one was open for 4% -> 4% of each run, Pallas kernels for 23% -> 23%
where the time goes in v9:
time: 181 us; the launch traced here: 180 us
  waiting for transfers between devices  63.1 us (35%)
  starting transfers between devices  53 us (29%)
  Pallas kernels  50.3 us (28%)
  local copies, waits for them, and re-layouts  10.1 us (6%)
  other arithmetic  2.62 us (1%)
    pallas_call x3, Pallas kernels, gram_call(): pl.pallas_call(lambda *refs: gram_kernel(first, last, start, *refs), grid...  32.6 us
    all_to_all x3, waiting for transfers between devices, swap_z(): lax.all_to_all(x, 'shard', 0, 0, tiled=True, axis_index_groups=Z_GROUPS)  24.9 us
    all_to_all x3, starting transfers between devices, swap_z(): lax.all_to_all(x, 'shard', 0, 0, tiled=True, axis_index_groups=Z_GROUPS)  17.8 us
    ppermute x15, starting transfers between devices, shift(): return lax.ppermute(x, AXES, pairs)  17.5 us
    ppermute x15, waiting for transfers between devices, shift(): return lax.ppermute(x, AXES, pairs)  16.4 us
    all_to_all x1, waiting for transfers between devices, local(): lax.all_to_all(address(info, own, norm_gains), 'mp', 0, 0, tiled=True)  9.02 us
    all_to_all x1, waiting for transfers between devices, local(): lax.all_to_all(jnp.broadcast_to(numer[None], (16, 32, 512)), 'mp', 0, 0,...  8.05 us
    pallas_call x1, Pallas kernels, project(): pl.pallas_call(project_kernel, grid_spec=pltpu.PrefetchScalarGridSpec(num...  6.36 us
  transfers between devices with their start and end apart: 21, of which 11 were waited for; matrix products, arithmetic and copies ran while one was open for 4% of the time, Pallas kernels for 23%

profile of v9, /device:TPU:1, one launch (start us, length us, event | category | flops | bytes accessed | tf_op | source)
XLA Modules:
  0.0 180.2 jit_solution(2335097703588605419)
XLA Ops:
  1.5 5.6 %prepare.1 = (bf16[8,64,1152]{2,1,0:T(8,128)(2,1)}, bf16[256,512]{1,0:T(8,128)(2,1)}) custom-call(s32[15]{0:T(128)} %stack.63.info.refs_0_, bf16[256,8192]{1,0:T(8,128)(2,1)} %bank.1, s32[1,64]{1,0:T(1,128)} %ids.1), custom_call_target="tpu_custom_call" | custom-call | flops 268435456 | bytes 5242880 | tf_op jit(solution)/shard_map/prepare/pallas_call | solution.py:95
  7.1 9.1 %all-to-all-start = ((bf16[8,64,1152]{2,1,0:T(8,128)(2,1)}), bf16[8,64,1152]{2,1,0:T(8,128)(2,1)S(1)}, u32[]{:S(2)}, u32[]{:S(2)}) async-start(bf16[8,64,1152]{2,1,0:T(8,128)(2,1)} %get-tuple-element.39), calls=%async_computation | async-start | bytes 2359296 | tf_op jit(solution)/shard_map/all_to_all | solution.py:31
  17.5 11.3 %collective-permute-done = bf16[512,512]{1,0:T(8,128)(2,1)S(1)} collective-permute-done((bf16[512,512]{1,0:T(8,128)(2,1)S(1)}, bf16[512,512]{1,0:T(8,128)(2,1)S(1)}, u32[]{:S(2)}, u32[]{:S(2)}) %collective-permute-start) | collective-permute-done | bytes 524320 | tf_op jit(solution)/shard_map/ppermute | solution.py:27
  28.9 19.4 %all-to-all-done.extra.own.refs_4_ = bf16[8,64,1152]{2,1,0:T(8,128)(2,1)S(1)} async-done(((bf16[8,64,1152]{2,1,0:T(8,128)(2,1)}), bf16[8,64,1152]{2,1,0:T(8,128)(2,1)S(1)}, u32[]{:S(2)}, u32[]{:S(2)}) %all-to-all-start) | async-done | bytes 1179680 | tf_op jit(solution)/shard_map/all_to_all | solution.py:31
  51.2 2.7 %collective-permute-start.1 = (bf16[4,64,1152]{2,1,0:T(8,128)(2,1)}, bf16[4,64,1152]{2,1,0:T(8,128)(2,1)}, u32[]{:S(2)}, u32[]{:S(2)}) collective-permute-start(bf16[4,64,1152]{2,1,0:T(8,128)(2,1)} %get-tuple-element.77), channel_id=1, source_target_pairs={{0,32},{1,33},{2,34},{3,35},{4,36},{5,37},{6,38},{7,39},{8,40},{9,... | collective-permute-start | bytes 1769480 | tf_op jit(solution)/shard_map/ppermute | solution.py:27
  55.4 2.2 %address.1 = f32[16,24,128]{2,1,0:T(8,128)} custom-call(s32[15]{0:T(128)} %stack.63.info.refs_0_, bf16[8,64,1152]{2,1,0:T(8,128)(2,1)} %copy-done, f32[1,8192]{1,0:T(1,128)} %gains.3), custom_call_target="tpu_custom_call" | custom-call | flops 1048576 | bytes 262144 | tf_op jit(solution)/shard_map/address/pallas_call | solution.py:134
  57.6 5.5 %all-to-all-start.1 = ((f32[16,24,128]{2,1,0:T(8,128)}), f32[16,24,128]{2,1,0:T(8,128)}, u32[]{:S(2)}, u32[]{:S(2)}) async-start(f32[16,24,128]{2,1,0:T(8,128)} %address.1), calls=%async_computation.1 | async-start | bytes 393216 | tf_op jit(solution)/shard_map/all_to_all | solution.py:355
  63.1 9.0 %all-to-all-done.1 = f32[16,24,128]{2,1,0:T(8,128)} async-done(((f32[16,24,128]{2,1,0:T(8,128)}), f32[16,24,128]{2,1,0:T(8,128)}, u32[]{:S(2)}, u32[]{:S(2)}) %all-to-all-start.1) | async-done | bytes 196640 | tf_op jit(solution)/shard_map/all_to_all | solution.py:355
  73.0 2.5 %collective-permute-start.9 = (bf16[256,512]{1,0:T(8,128)(2,1)}, bf16[256,512]{1,0:T(8,128)(2,1)S(1)}, u32[]{:S(2)}, u32[]{:S(2)}) collective-permute-start(bf16[256,512]{1,0:T(8,128)(2,1)} %collective-permute-done.5.refs_3_), channel_id=1, source_target_pairs={{0,14},{1,15},{2,0},{3,1},{4,2},{5,3},{6,4},{7,5},{8,6},{9,7},{10,... | collective-permute-start | bytes 786440 | tf_op jit(solution)/shard_map/ppermute | solution.py:27
  80.2 6.4 %project.1 = (bf16[8,64,512]{2,1,0:T(8,128)(2,1)}, bf16[512,1024]{1,0:T(8,128)(2,1)S(1)}, f32[1,1024]{1,0:T(1,128)S(1)}) custom-call(s32[15]{0:T(128)S(1)} %copy-done.8, bf16[8,64,1152]{2,1,0:T(8,128)(2,1)S(1)} %copy-done.1, bf16[8,64,1152]{2,1,0:T(8,128)(2,1)S(1)} %collective-permute-done.3.core.refs_5_, ...), custom_call_target="tpu_custom_call" | custom-call | flops 1073741824 | bytes 8388608 | tf_op jit(solution)/shard_map/project/pallas_call | solution.py:195
  87.5 3.5 %all-to-all-start.2 = ((bf16[8,64,512]{2,1,0:T(8,128)(2,1)}), bf16[8,64,512]{2,1,0:T(8,128)(2,1)S(1)}, u32[]{:S(2)}, u32[]{:S(2)}) async-start(bf16[8,64,512]{2,1,0:T(8,128)(2,1)} %get-tuple-element.52), calls=%async_computation.2 | async-start | bytes 1048576 | tf_op jit(solution)/shard_map/all_to_all | solution.py:31
  93.8 11.2 %gram0.1.refs_12_ = f32[512,1024]{1,0:T(8,128)} custom-call(s32[15]{0:T(128)} %stack.63.info.refs_0_, bf16[256,512]{1,0:T(8,128)(2,1)} %get-tuple-element.41.refs_1_, bf16[256,512]{1,0:T(8,128)(2,1)} %collective-permute-done.4.refs_2_, bf16[256,512]{1,0:T(8,128)(2,1)} %collective-permute-done.5.refs_3_, bf16[8,64,1152]{2,1,0:T(8,128)(2,1)} %copy-done, ...), custom_call_target="tpu_custom_call" | custom-call | flops 6442450944 | bytes 6291456 | tf_op jit(solution)/shard_map/gram0/pallas_call | solution.py:318
  105.1 3.5 %all-to-all-done.2 = bf16[8,64,512]{2,1,0:T(8,128)(2,1)S(1)} async-done(((bf16[8,64,512]{2,1,0:T(8,128)(2,1)}), bf16[8,64,512]{2,1,0:T(8,128)(2,1)S(1)}, u32[]{:S(2)}, u32[]{:S(2)}) %all-to-all-start.2) | async-done | bytes 524320 | tf_op jit(solution)/shard_map/all_to_all | solution.py:31
  108.6 2.3 %collective-permute-done.10.refs_3_ = bf16[256,512]{1,0:T(8,128)(2,1)S(1)} collective-permute-done((bf16[256,512]{1,0:T(8,128)(2,1)S(1)}, bf16[256,512]{1,0:T(8,128)(2,1)S(1)}, u32[]{:S(2)}, u32[]{:S(2)}) %collective-permute-start.10) | collective-permute-done | bytes 262176 | tf_op jit(solution)/shard_map/ppermute | solution.py:27
  111.8 5.2 %all-to-all-start.3 = ((bf16[8,64,512]{2,1,0:T(8,128)(2,1)}), bf16[8,64,512]{2,1,0:T(8,128)(2,1)S(1)}, u32[]{:S(2)}, u32[]{:S(2)}) async-start(bf16[8,64,512]{2,1,0:T(8,128)(2,1)} %broadcast_in_dim.20), calls=%async_computation.3 | async-start | bytes 1048576 | tf_op jit(solution)/shard_map/all_to_all | solution.py:31
  117.0 2.8 %collective-permute-start.13 = (bf16[128,512]{1,0:T(8,128)(2,1)S(1)}, bf16[128,512]{1,0:T(8,128)(2,1)S(1)}, u32[]{:S(2)}, u32[]{:S(2)}) collective-permute-start(bf16[128,512]{1,0:T(8,128)(2,1)S(1)} %slice.27), channel_id=1, source_target_pairs={{0,14},{1,15},{2,0},{3,1},{4,2},{5,3},{6,4},{7,5},{8,6},{9,7},{10,... | collective-permute-start | bytes 393224 | tf_op jit(solution)/shard_map/ppermute | solution.py:27
  119.8 12.1 %gram1.1.refs_12_ = f32[512,1024]{1,0:T(8,128)} custom-call(s32[15]{0:T(128)} %stack.63.info.refs_0_, bf16[256,512]{1,0:T(8,128)(2,1)} %copy-done.15, bf16[256,512]{1,0:T(8,128)(2,1)} %copy-done.16, bf16[256,512]{1,0:T(8,128)(2,1)} %copy-done.14, bf16[8,64,1152]{2,1,0:T(8,128)(2,1)} %copy-done, ...), custom_call_target="tpu_custom_call", output_to_operand_aliasing={{}: (12, {})} | custom-call | flops 6442450944 | bytes 6291456 | tf_op jit(solution)/shard_map/gram1/pallas_call | solution.py:318
  135.5 3.5 %numer.1 = bf16[32,32,512]{2,1,0:T(8,128)(2,1)} custom-call(s32[15]{0:T(128)} %stack.63.info.refs_0_, bf16[512,1024]{1,0:T(8,128)(2,1)} %copy-done.4, bf16[512,512]{1,0:T(8,128)(2,1)} %bitcast.24, f32[1,1024]{1,0:T(1,128)} %copy-done.9, bf16[1024,512]{1,0:T(8,128)(2,1)} %copy-done.2), custom_call_target="tpu_custom_call" | custom-call | flops 536870912 | bytes 4194304 | tf_op jit(solution)/shard_map/numer/pallas_call | solution.py:230
  139.0 6.1 %all-to-all-start.4 = ((bf16[32,32,512]{2,1,0:T(8,128)(2,1)}), bf16[32,32,512]{2,1,0:T(8,128)(2,1)S(1)}, u32[]{:S(2)}, u32[]{:S(2)}) async-start(bf16[32,32,512]{2,1,0:T(8,128)(2,1)} %numer.1), calls=%async_computation.4 | async-start | bytes 2097152 | tf_op jit(solution)/shard_map/all_to_all | solution.py:377
  145.1 9.3 %gram2.1 = (f32[512,512]{1,0:T(8,128)}, bf16[512,512]{1,0:T(8,128)(2,1)}) custom-call(s32[15]{0:T(128)} %stack.63.info.refs_0_, bf16[256,512]{1,0:T(8,128)(2,1)} %copy-done.13, bf16[128,512]{1,0:T(8,128)(2,1)} %copy-done.18, bf16[128,512]{1,0:T(8,128)(2,1)} %copy-done.17, bf16[8,64,1152]{2,1,0:T(8,128)(2,1)} %copy-done, bf16[8,64,1152]{2,1,0:T(8,128)(2,1)} %copy-done.3, ...), custom_call_target="tpu_custom_call" | custom-call | flops 4294967296 | bytes 6291456 | tf_op jit(solution)/shard_map/gram2/pallas_call | solution.py:318
  155.9 4.7 %all-to-all-done.4 = bf16[32,32,512]{2,1,0:T(8,128)(2,1)S(1)} async-done(((bf16[32,32,512]{2,1,0:T(8,128)(2,1)}), bf16[32,32,512]{2,1,0:T(8,128)(2,1)S(1)}, u32[]{:S(2)}, u32[]{:S(2)}) %all-to-all-start.4) | async-done | bytes 1048608 | tf_op jit(solution)/shard_map/all_to_all | solution.py:377
  161.7 6.1 %all-to-all-start.5 = ((bf16[16,32,512]{2,1,0:T(8,128)(2,1)}), bf16[16,32,512]{2,1,0:T(8,128)(2,1)S(1)}, u32[]{:S(2)}, u32[]{:S(2)}) async-start(bf16[16,32,512]{2,1,0:T(8,128)(2,1)} %broadcast_in_dim.23), calls=%async_computation.5 | async-start | bytes 1048576 | tf_op jit(solution)/shard_map/all_to_all | solution.py:379
  167.7 2.1 %collective-permute-done.14 = bf16[512,512]{1,0:T(8,128)(2,1)S(1)} collective-permute-done((bf16[512,512]{1,0:T(8,128)(2,1)}, bf16[512,512]{1,0:T(8,128)(2,1)S(1)}, u32[]{:S(2)}, u32[]{:S(2)}) %collective-permute-start.14) | collective-permute-done | bytes 524320 | tf_op jit(solution)/shard_map/ppermute | solution.py:27
  171.0 8.0 %all-to-all-done.5 = bf16[16,32,512]{2,1,0:T(8,128)(2,1)S(1)} async-done(((bf16[16,32,512]{2,1,0:T(8,128)(2,1)}), bf16[16,32,512]{2,1,0:T(8,128)(2,1)S(1)}, u32[]{:S(2)}, u32[]{:S(2)}) %all-to-all-start.5) | async-done | bytes 524320 | tf_op jit(solution)/shard_map/all_to_all | solution.py:379
  (78 shorter events, 25.2 us)
Async XLA Ops:
  7.1 41.2 %all-to-all-start = ((bf16[8,64,1152]{2,1,0:T(8,128)(2,1)}), bf16[8,64,1152]{2,1,0:T(8,128)(2,1)S(1)}, u32[]{:S(2)}, u32[]{:S(2)}) async-start(bf16[8,64,1152]{2,1,0:T(8,128)(2,1)} %get-tuple-element.39), calls=%async_computation | async-start | bytes 2359296 | tf_op jit(solution)/shard_map/all_to_all | solution.py:31
  16.2 12.6 %collective-permute-start = (bf16[512,512]{1,0:T(8,128)(2,1)S(1)}, bf16[512,512]{1,0:T(8,128)(2,1)S(1)}, u32[]{:S(2)}, u32[]{:S(2)}) collective-permute-start(bf16[512,512]{1,0:T(8,128)(2,1)S(1)} %bitcast.26), channel_id=1, source_target_pairs={{0,1},{1,0},{2,3},{3,2},{4,5},{5,4},{6,7},{7,6},{8,9},{9,8},{10,11... | collective-permute-start | bytes 1572872 | tf_op jit(solution)/shard_map/ppermute | solution.py:27
  28.9 49.6 %copy-start.2 = (bf16[1024,512]{1,0:T(8,128)(2,1)}, bf16[1024,512]{1,0:T(8,128)(2,1)S(1)}, u32[]{:S(2)}) copy-start(bf16[1024,512]{1,0:T(8,128)(2,1)S(1)} %pad_maximum_fusion.weights) | copy-start | bytes 3145732
  28.9 49.6 %copy-start.7 = (f32[1,8192]{1,0:T(1,128)S(1)}, f32[1,8192]{1,0:T(1,128)}, u32[]{:S(2)}) copy-start(f32[1,8192]{1,0:T(1,128)} %gains.3) | copy-start | bytes 98308
  28.9 49.6 %copy-start.8 = (s32[15]{0:T(128)S(1)}, s32[15]{0:T(128)}, u32[]{:S(2)}) copy-start(s32[15]{0:T(128)} %stack.63.info.refs_0_) | copy-start | bytes 184
  48.3 23.9 %collective-permute-start.3 = (bf16[8,64,1152]{2,1,0:T(8,128)(2,1)S(1)}, bf16[8,64,1152]{2,1,0:T(8,128)(2,1)S(1)}, u32[]{:S(2)}, u32[]{:S(2)}) collective-permute-start(bf16[8,64,1152]{2,1,0:T(8,128)(2,1)S(1)} %all-to-all-done.extra.own.refs_4_), channel_id=1, source_target_pairs={{0,16},{1,17},{2,18},{3,19},{4,20},{5,21},{6,22},{7,23},{8,24},{9,... | collective-permute-start | bytes 3538952 | tf_op jit(solution)/shard_map/ppermute | solution.py:27
  49.9 22.2 %collective-permute-start.2 = (bf16[4,64,1152]{2,1,0:T(8,128)(2,1)}, bf16[4,64,1152]{2,1,0:T(8,128)(2,1)}, u32[]{:S(2)}, u32[]{:S(2)}) collective-permute-start(bf16[4,64,1152]{2,1,0:T(8,128)(2,1)} %get-tuple-element.76), channel_id=1, source_target_pairs={{0,64},{1,65},{2,66},{3,67},{4,68},{5,69},{6,70},{7,71},{8,72},{9,... | collective-permute-start | bytes 1769480 | tf_op jit(solution)/shard_map/ppermute | solution.py:27
  51.2 20.9 %collective-permute-start.1 = (bf16[4,64,1152]{2,1,0:T(8,128)(2,1)}, bf16[4,64,1152]{2,1,0:T(8,128)(2,1)}, u32[]{:S(2)}, u32[]{:S(2)}) collective-permute-start(bf16[4,64,1152]{2,1,0:T(8,128)(2,1)} %get-tuple-element.77), channel_id=1, source_target_pairs={{0,32},{1,33},{2,34},{3,35},{4,36},{5,37},{6,38},{7,39},{8,40},{9,... | collective-permute-start | bytes 1769480 | tf_op jit(solution)/shard_map/ppermute | solution.py:27
  54.0 9.1 %collective-permute-start.5 = (bf16[256,512]{1,0:T(8,128)(2,1)}, bf16[256,512]{1,0:T(8,128)(2,1)}, u32[]{:S(2)}, u32[]{:S(2)}) collective-permute-start(bf16[256,512]{1,0:T(8,128)(2,1)} %get-tuple-element.41.refs_1_), channel_id=1, source_target_pairs={{0,14},{1,15},{2,0},{3,1},{4,2},{5,3},{6,4},{7,5},{8,6},{9,7},{10,... | collective-permute-start | bytes 786440 | tf_op jit(solution)/shard_map/ppermute | solution.py:27
  54.0 9.1 %collective-permute-start.4 = (bf16[256,512]{1,0:T(8,128)(2,1)}, bf16[256,512]{1,0:T(8,128)(2,1)}, u32[]{:S(2)}, u32[]{:S(2)}) collective-permute-start(bf16[256,512]{1,0:T(8,128)(2,1)} %get-tuple-element.41.refs_1_), channel_id=1, source_target_pairs={{0,2},{1,3},{2,4},{3,5},{4,6},{5,7},{6,8},{7,9},{8,10},{9,11},{10,... | collective-permute-start | bytes 786440 | tf_op jit(solution)/shard_map/ppermute | solution.py:27
  57.6 14.5 %all-to-all-start.1 = ((f32[16,24,128]{2,1,0:T(8,128)}), f32[16,24,128]{2,1,0:T(8,128)}, u32[]{:S(2)}, u32[]{:S(2)}) async-start(f32[16,24,128]{2,1,0:T(8,128)} %address.1), calls=%async_computation.1 | async-start | bytes 393216 | tf_op jit(solution)/shard_map/all_to_all | solution.py:355
  72.2 6.3 %collective-permute-start.6 = (bf16[4,64,1152]{2,1,0:T(8,128)(2,1)}, bf16[4,64,1152]{2,1,0:T(8,128)(2,1)S(1)}, u32[]{:S(2)}, u32[]{:S(2)}) collective-permute-start(bf16[4,64,1152]{2,1,0:T(8,128)(2,1)} %collective-permute-done.1.xp.refs_6_), channel_id=1, source_target_pairs={{0,16},{1,17},{2,18},{3,19},{4,20},{5,21},{6,22},{7,23},{8,24},{9,... | collective-permute-start | bytes 1769480 | tf_op jit(solution)/shard_map/ppermute | solution.py:27
  72.6 5.9 %collective-permute-start.7 = (bf16[4,64,1152]{2,1,0:T(8,128)(2,1)}, bf16[4,64,1152]{2,1,0:T(8,128)(2,1)S(1)}, u32[]{:S(2)}, u32[]{:S(2)}) collective-permute-start(bf16[4,64,1152]{2,1,0:T(8,128)(2,1)} %collective-permute-done.2.yp.refs_7_), channel_id=1, source_target_pairs={{0,16},{1,17},{2,18},{3,19},{4,20},{5,21},{6,22},{7,23},{8,24},{9,... | collective-permute-start | bytes 1769480 | tf_op jit(solution)/shard_map/ppermute | solution.py:27
  72.8 14.8 %collective-permute-start.8 = (bf16[256,512]{1,0:T(8,128)(2,1)}, bf16[256,512]{1,0:T(8,128)(2,1)S(1)}, u32[]{:S(2)}, u32[]{:S(2)}) collective-permute-start(bf16[256,512]{1,0:T(8,128)(2,1)} %collective-permute-done.4.refs_2_), channel_id=1, source_target_pairs={{0,2},{1,3},{2,4},{3,5},{4,6},{5,7},{6,8},{7,9},{8,10},{9,11},{10,... | collective-permute-start | bytes 786440 | tf_op jit(solution)/shard_map/ppermute | solution.py:27
  73.0 14.6 %collective-permute-start.9 = (bf16[256,512]{1,0:T(8,128)(2,1)}, bf16[256,512]{1,0:T(8,128)(2,1)S(1)}, u32[]{:S(2)}, u32[]{:S(2)}) collective-permute-start(bf16[256,512]{1,0:T(8,128)(2,1)} %collective-permute-done.5.refs_3_), channel_id=1, source_target_pairs={{0,14},{1,15},{2,0},{3,1},{4,2},{5,3},{6,4},{7,5},{8,6},{9,7},{10,... | collective-permute-start | bytes 786440 | tf_op jit(solution)/shard_map/ppermute | solution.py:27
  87.5 21.0 %all-to-all-start.2 = ((bf16[8,64,512]{2,1,0:T(8,128)(2,1)}), bf16[8,64,512]{2,1,0:T(8,128)(2,1)S(1)}, u32[]{:S(2)}, u32[]{:S(2)}) async-start(bf16[8,64,512]{2,1,0:T(8,128)(2,1)} %get-tuple-element.52), calls=%async_computation.2 | async-start | bytes 1048576 | tf_op jit(solution)/shard_map/all_to_all | solution.py:31
  91.0 19.9 %collective-permute-start.10 = (bf16[256,512]{1,0:T(8,128)(2,1)S(1)}, bf16[256,512]{1,0:T(8,128)(2,1)S(1)}, u32[]{:S(2)}, u32[]{:S(2)}) collective-permute-start(bf16[256,512]{1,0:T(8,128)(2,1)S(1)} %collective-permute-done.8.refs_1_), channel_id=1, source_target_pairs={{0,2},{1,3},{2,4},{3,5},{4,6},{5,7},{6,8},{7,9},{8,10},{9,11},{10,... | collective-permute-start | bytes 786440 | tf_op jit(solution)/shard_map/ppermute | solution.py:27
  92.4 18.5 %collective-permute-start.11 = (bf16[256,512]{1,0:T(8,128)(2,1)S(1)}, bf16[256,512]{1,0:T(8,128)(2,1)S(1)}, u32[]{:S(2)}, u32[]{:S(2)}) collective-permute-start(bf16[256,512]{1,0:T(8,128)(2,1)S(1)} %collective-permute-done.9.refs_2_), channel_id=1, source_target_pairs={{0,14},{1,15},{2,0},{3,1},{4,2},{5,3},{6,4},{7,5},{8,6},{9,7},{10,... | collective-permute-start | bytes 786440 | tf_op jit(solution)/shard_map/ppermute | solution.py:27
  111.8 22.8 %all-to-all-start.3 = ((bf16[8,64,512]{2,1,0:T(8,128)(2,1)}), bf16[8,64,512]{2,1,0:T(8,128)(2,1)S(1)}, u32[]{:S(2)}, u32[]{:S(2)}) async-start(bf16[8,64,512]{2,1,0:T(8,128)(2,1)} %broadcast_in_dim.20), calls=%async_computation.3 | async-start | bytes 1048576 | tf_op jit(solution)/shard_map/all_to_all | solution.py:31
  117.0 15.5 %collective-permute-start.13 = (bf16[128,512]{1,0:T(8,128)(2,1)S(1)}, bf16[128,512]{1,0:T(8,128)(2,1)S(1)}, u32[]{:S(2)}, u32[]{:S(2)}) collective-permute-start(bf16[128,512]{1,0:T(8,128)(2,1)S(1)} %slice.27), channel_id=1, source_target_pairs={{0,14},{1,15},{2,0},{3,1},{4,2},{5,3},{6,4},{7,5},{8,6},{9,7},{10,... | collective-permute-start | bytes 393224 | tf_op jit(solution)/shard_map/ppermute | solution.py:27
  119.8 12.9 %collective-permute-start.12 = (bf16[128,512]{1,0:T(8,128)(2,1)S(1)}, bf16[128,512]{1,0:T(8,128)(2,1)S(1)}, u32[]{:S(2)}, u32[]{:S(2)}) collective-permute-start(bf16[128,512]{1,0:T(8,128)(2,1)S(1)} %slice.26), channel_id=1, source_target_pairs={{0,2},{1,3},{2,4},{3,5},{4,6},{5,7},{6,8},{7,9},{8,10},{9,11},{10,... | collective-permute-start | bytes 393224 | tf_op jit(solution)/shard_map/ppermute | solution.py:27
  139.0 21.6 %all-to-all-start.4 = ((bf16[32,32,512]{2,1,0:T(8,128)(2,1)}), bf16[32,32,512]{2,1,0:T(8,128)(2,1)S(1)}, u32[]{:S(2)}, u32[]{:S(2)}) async-start(bf16[32,32,512]{2,1,0:T(8,128)(2,1)} %numer.1), calls=%async_computation.4 | async-start | bytes 2097152 | tf_op jit(solution)/shard_map/all_to_all | solution.py:377
  154.4 15.4 %collective-permute-start.14 = (bf16[512,512]{1,0:T(8,128)(2,1)}, bf16[512,512]{1,0:T(8,128)(2,1)S(1)}, u32[]{:S(2)}, u32[]{:S(2)}) collective-permute-start(bf16[512,512]{1,0:T(8,128)(2,1)} %get-tuple-element.74), channel_id=1, source_target_pairs={{0,1},{1,0},{2,3},{3,2},{4,5},{5,4},{6,7},{7,6},{8,9},{9,8},{10,11... | collective-permute-start | bytes 1572872 | tf_op jit(solution)/shard_map/ppermute | solution.py:27
  161.7 17.4 %all-to-all-start.5 = ((bf16[16,32,512]{2,1,0:T(8,128)(2,1)}), bf16[16,32,512]{2,1,0:T(8,128)(2,1)S(1)}, u32[]{:S(2)}, u32[]{:S(2)}) async-start(bf16[16,32,512]{2,1,0:T(8,128)(2,1)} %broadcast_in_dim.23), calls=%async_computation.5 | async-start | bytes 1048576 | tf_op jit(solution)/shard_map/all_to_all | solution.py:379
  (16 other events, 173.1 us)

commit v10 on v6

--- a/solution.py
+++ b/solution.py
@@ -41,6 +41,7 @@
 
 
 def gather(sent, w, x):
+    sent, other = lax.optimization_barrier((sent, shift(w, xl=1)))
     own = lax.all_to_all(sent, "mp", 0, 0, tiled=True, axis_index_groups=CORE_GROUPS)
     z = [x]
     u = d = x
@@ -48,8 +49,9 @@
         u, d = shift(u, z=1), shift(d, z=-1)
         z += [u, d]
     z += [shift(u[:128], z=1), shift(d[128:], z=-1)]
-    own, w, *z = lax.optimization_barrier((own.reshape(8, 8, 16, 1152), shift(w, xl=1), *z))
-    return own, shift(own, c=1), w, z
+    both = jnp.concatenate([w, other], 0)
+    own, both, *z = lax.optimization_barrier((own.reshape(8, 8, 16, 1152), both, *z))
+    return own, shift(own, c=1), both, z
 
 
 def prepare_kernel(info, bank, ids, piece_out, cols_out, total, pick):
@@ -361,8 +363,7 @@
 
     piece, bank_cols = prepare(info, bank, calib_ids)
     sent = address(info, swap_z(piece), norm_gains)
-    own_s, other_s, weights_other, blocks = gather(sent, weights, bank_cols)
-    both = jnp.concatenate([weights, weights_other], 0)
+    own_s, other_s, both, blocks = gather(sent, weights, bank_cols)
 
     partial_out, calib, diag = project(info, own_s, other_s, norm_gains, both)
     tie = lax.optimization_barrier

time: 177 us -> 174 us (0.983)
  waiting for transfers between devices: 58.7 us -> 51.7 us
  starting transfers between devices: 40.7 us -> 45.1 us
    ppermute x11, waiting for transfers between devices: 33.3 us -> 26.2 us  [shift(): return lax.ppermute(x, AXES, pairs)]
    ppermute x11, starting transfers between devices: 12.1 us -> 17.3 us  [shift(): return lax.ppermute(x, AXES, pairs)]
  transfers between devices with their start and end apart: 16 -> 16, of which waited for: 11 -> 12; matrix products, arithmetic and copies ran while one was open for 2% -> 2% of each run, Pallas kernels for 18% -> 22%
where the time goes in v10:
time: 174 us; the launch traced here: 173 us
  waiting for transfers between devices  51.7 us (30%)
  Pallas kernels  49.3 us (28%)
  starting transfers between devices  45.1 us (26%)
  blocking collectives  18.9 us (11%)
  local copies, waits for them, and re-layouts  3.9 us (2%)
  other arithmetic  3.58 us (2%)
    pallas_call x3, Pallas kernels, gram_call(): pl.pallas_call(lambda *refs: gram_kernel(first, last, *refs), grid_spec=p...  31 us
    ppermute x11, waiting for transfers between devices, shift(): return lax.ppermute(x, AXES, pairs)  26.2 us
    all_to_all x1, blocking collectives, swap_z(): lax.all_to_all(x, 'shard', 0, 0, tiled=True, axis_index_groups=Z_GROUPS)  18.9 us
    ppermute x11, starting transfers between devices, shift(): return lax.ppermute(x, AXES, pairs)  17.3 us
    all_to_all x2, waiting for transfers between devices, swap_z(): lax.all_to_all(x, 'shard', 0, 0, tiled=True, axis_index_groups=Z_GROUPS)  12.1 us
    all_to_all x1, starting transfers between devices, local(): lax.all_to_all(numer, AXES, 0, 0, tiled=True, axis_index_groups=XLO_GROUPS)  8.11 us
    all_to_all x1, waiting for transfers between devices, local(): lax.all_to_all(jnp.broadcast_to(numer[None], (16, 32, 512)), 'mp', 0, 0,...  8.08 us
    all_to_all x2, starting transfers between devices, swap_z(): lax.all_to_all(x, 'shard', 0, 0, tiled=True, axis_index_groups=Z_GROUPS)  7.16 us
  transfers between devices with their start and end apart: 16, of which 12 were waited for; matrix products, arithmetic and copies ran while one was open for 2% of the time, Pallas kernels for 22%

profile of v10, /device:TPU:1, one launch (start us, length us, event | category | flops | bytes accessed | tf_op | source)
XLA Modules:
  0.0 173.2 jit_solution(5866341103180114498)
XLA Ops:
  0.6 2.1 %collective-permute-start = (bf16[512,512]{1,0:T(8,128)(2,1)}, bf16[512,512]{1,0:T(8,128)(2,1)S(1)}, u32[]{:S(2)}, u32[]{:S(2)}) collective-permute-start(bf16[512,512]{1,0:T(8,128)(2,1)} %bitcast.28), channel_id=1, source_target_pairs={{0,1},{1,0},{2,3},{3,2},{4,5},{5,4},{6,7},{7,6},{8,9},{9,8},{10,11... | collective-permute-start | bytes 1572872 | tf_op jit(solution)/shard_map/ppermute | solution.py:28
  3.3 5.3 %prepare.1 = (bf16[8,16,1152]{2,1,0:T(8,128)(2,1)}, bf16[256,512]{1,0:T(8,128)(2,1)}) custom-call(s32[15]{0:T(128)} %stack.63.info.refs_0_, bf16[256,8192]{1,0:T(8,128)(2,1)} %bank.1, s32[1,64]{1,0:T(1,128)} %ids.1), custom_call_target="tpu_custom_call" | custom-call | flops 268435456 | bytes 5242880 | tf_op jit(solution)/shard_map/prepare/pallas_call | solution.py:103
  8.6 18.9 %all_to_all.30.piece = bf16[8,16,1152]{2,1,0:T(8,128)(2,1)} all-to-all(bf16[8,16,1152]{2,1,0:T(8,128)(2,1)} %get-tuple-element.36), channel_id=1, replica_groups={{0,2,4,6,8,10,12,14},{1,3,5,7,9,11,13,15},{16,18,20,22,24,26,28,30},{17..., dimensions={0} | all-to-all | bytes 589824 | tf_op jit(solution)/shard_map/all_to_all | solution.py:32
  27.5 2.6 %address.1 = bf16[64,16,1152]{2,1,0:T(8,128)(2,1)} custom-call(s32[15]{0:T(128)} %stack.63.info.refs_0_, bf16[8,16,1152]{2,1,0:T(8,128)(2,1)} %all_to_all.30.piece, f32[1,8192]{1,0:T(1,128)} %gains.3), custom_call_target="tpu_custom_call" | custom-call | flops 1048576 | bytes 3145728 | tf_op jit(solution)/shard_map/address/pallas_call | solution.py:133
  30.1 6.5 %all-to-all-start.1 = ((bf16[64,16,1152]{2,1,0:T(8,128)(2,1)}), bf16[64,16,1152]{2,1,0:T(8,128)(2,1)S(1)}, u32[]{:S(2)}, u32[]{:S(2)}) async-start(bf16[64,16,1152]{2,1,0:T(8,128)(2,1)} %address.1), calls=%async_computation.1 | async-start | bytes 4718592 | tf_op jit(solution)/shard_map/all_to_all | solution.py:45
  38.0 4.0 %collective-permute-done.2.refs_3_ = bf16[256,512]{1,0:T(8,128)(2,1)S(1)} collective-permute-done((bf16[256,512]{1,0:T(8,128)(2,1)}, bf16[256,512]{1,0:T(8,128)(2,1)S(1)}, u32[]{:S(2)}, u32[]{:S(2)}) %collective-permute-start.2) | collective-permute-done | bytes 262176 | tf_op jit(solution)/shard_map/ppermute | solution.py:28
  43.7 5.0 %collective-permute-done.4.refs_2_ = bf16[256,512]{1,0:T(8,128)(2,1)S(1)} collective-permute-done((bf16[256,512]{1,0:T(8,128)(2,1)S(1)}, bf16[256,512]{1,0:T(8,128)(2,1)S(1)}, u32[]{:S(2)}, u32[]{:S(2)}) %collective-permute-start.4) | collective-permute-done | bytes 262176 | tf_op jit(solution)/shard_map/ppermute | solution.py:28
  50.5 5.8 %collective-permute-done.6.refs_1_ = bf16[256,512]{1,0:T(8,128)(2,1)S(1)} collective-permute-done((bf16[256,512]{1,0:T(8,128)(2,1)S(1)}, bf16[256,512]{1,0:T(8,128)(2,1)S(1)}, u32[]{:S(2)}, u32[]{:S(2)}) %collective-permute-start.6) | collective-permute-done | bytes 262176 | tf_op jit(solution)/shard_map/ppermute | solution.py:28
  61.9 2.8 %collective-permute-done.7.refs_2_ = bf16[128,512]{1,0:T(8,128)(2,1)} collective-permute-done((bf16[128,512]{1,0:T(8,128)(2,1)S(1)}, bf16[128,512]{1,0:T(8,128)(2,1)}, u32[]{:S(2)}, u32[]{:S(2)}) %collective-permute-start.7) | collective-permute-done | bytes 131104 | tf_op jit(solution)/shard_map/ppermute | solution.py:28
  64.7 7.3 %collective-permute-start.9 = (bf16[8,8,16,1152]{3,2,1,0:T(8,128)(2,1)S(1)}, bf16[8,8,16,1152]{3,2,1,0:T(8,128)(2,1)}, u32[]{:S(2)}, u32[]{:S(2)}) collective-permute-start(bf16[8,8,16,1152]{3,2,1,0:T(8,128)(2,1)S(1)} %bitcast.21), channel_id=1, source_target_pairs={{0,16},{1,17},{2,18},{3,19},{4,20},{5,21},{6,22},{7,23},{8,24},{9,... | collective-permute-start | bytes 7077896 | tf_op jit(solution)/shard_map/ppermute | solution.py:28
  72.0 4.3 %collective-permute-done.9.other_s.refs_5_.refs_7_ = bf16[8,8,16,1152]{3,2,1,0:T(8,128)(2,1)} collective-permute-done((bf16[8,8,16,1152]{3,2,1,0:T(8,128)(2,1)S(1)}, bf16[8,8,16,1152]{3,2,1,0:T(8,128)(2,1)}, u32[]{:S(2)}, u32[]{:S(2)}) %collective-permute-start.9) | collective-permute-done | bytes 2359328 | tf_op jit(solution)/shard_map/ppermute | solution.py:28
  76.3 6.9 %project.1 = (bf16[8,64,512]{2,1,0:T(8,128)(2,1)}, bf16[512,1024]{1,0:T(8,128)(2,1)}, f32[1,1024]{1,0:T(1,128)}) custom-call(s32[15]{0:T(128)} %stack.63.info.refs_0_, bf16[8,8,16,1152]{3,2,1,0:T(8,128)(2,1)} %bitcast.22, bf16[8,8,16,1152]{3,2,1,0:T(8,128)(2,1)} %collective-permute-done.9.other_s.refs_5_.refs_7_, f32[1,8192]{1,0:T(1,128)} %gains.3, ...), custom_call_target="tpu_custom_call" | custom-call | flops 1073741824 | bytes 8388608 | tf_op jit(solution)/shard_map/project/pallas_call | solution.py:185
  83.2 3.5 %all-to-all-start.2 = ((bf16[8,64,512]{2,1,0:T(8,128)(2,1)}), bf16[8,64,512]{2,1,0:T(8,128)(2,1)S(1)}, u32[]{:S(2)}, u32[]{:S(2)}) async-start(bf16[8,64,512]{2,1,0:T(8,128)(2,1)} %get-tuple-element.43), calls=%async_computation.2 | async-start | bytes 1048576 | tf_op jit(solution)/shard_map/all_to_all | solution.py:32
  86.7 10.8 %gram0.1 = (f32[512,1024]{1,0:T(8,128)}, f32[16,1536]{1,0:T(8,128)}) custom-call(s32[15]{0:T(128)} %stack.63.info.refs_0_, bf16[256,512]{1,0:T(8,128)(2,1)} %get-tuple-element.45.refs_1_, bf16[256,512]{1,0:T(8,128)(2,1)} %copy-done.9, bf16[256,512]{1,0:T(8,128)(2,1)} %copy-done.8, bf16[8,8,16,1152]{3,2,1,0:T(8,128)(2,1)} %bitcast.23, ...), custom_call_target="tpu_custom_call" | custom-call | flops 6442450944 | bytes 6291456 | tf_op jit(solution)/shard_map/gram0/pallas_call | solution.py:333
  97.6 7.1 %all-to-all-done.2 = bf16[8,64,512]{2,1,0:T(8,128)(2,1)S(1)} async-done(((bf16[8,64,512]{2,1,0:T(8,128)(2,1)}), bf16[8,64,512]{2,1,0:T(8,128)(2,1)S(1)}, u32[]{:S(2)}, u32[]{:S(2)}) %all-to-all-start.2) | async-done | bytes 524320 | tf_op jit(solution)/shard_map/all_to_all | solution.py:32
  105.6 3.7 %all-to-all-start.3 = ((bf16[8,64,512]{2,1,0:T(8,128)(2,1)}), bf16[8,64,512]{2,1,0:T(8,128)(2,1)S(1)}, u32[]{:S(2)}, u32[]{:S(2)}) async-start(bf16[8,64,512]{2,1,0:T(8,128)(2,1)} %broadcast_in_dim.20), calls=%async_computation.3 | async-start | bytes 1048576 | tf_op jit(solution)/shard_map/all_to_all | solution.py:32
  109.2 11.4 %gram1.1.refs_7_ = f32[512,1024]{1,0:T(8,128)} custom-call(s32[15]{0:T(128)} %stack.63.info.refs_0_, bf16[256,512]{1,0:T(8,128)(2,1)} %copy-done.7, bf16[256,512]{1,0:T(8,128)(2,1)} %copy-done.6, bf16[256,512]{1,0:T(8,128)(2,1)} %copy-done.5, bf16[8,8,16,1152]{3,2,1,0:T(8,128)(2,1)} %bitcast.25, ...), custom_call_target="tpu_custom_call", output_to_operand_aliasing={{}: (7, {})} | custom-call | flops 6442450944 | bytes 6291456 | tf_op jit(solution)/shard_map/gram1/pallas_call | solution.py:333
  120.6 5.0 %all-to-all-done.3 = bf16[8,64,512]{2,1,0:T(8,128)(2,1)S(1)} async-done(((bf16[8,64,512]{2,1,0:T(8,128)(2,1)}), bf16[8,64,512]{2,1,0:T(8,128)(2,1)S(1)}, u32[]{:S(2)}, u32[]{:S(2)}) %all-to-all-start.3) | async-done | bytes 524320 | tf_op jit(solution)/shard_map/all_to_all | solution.py:32
  126.5 3.5 %numer.1 = bf16[32,32,512]{2,1,0:T(8,128)(2,1)} custom-call(s32[15]{0:T(128)} %stack.63.info.refs_0_, bf16[512,1024]{1,0:T(8,128)(2,1)} %get-tuple-element.51.calib, bf16[512,512]{1,0:T(8,128)(2,1)} %bitcast.27, f32[1,1024]{1,0:T(1,128)} %get-tuple-element.59.diag, bf16[1024,512]{1,0:T(8,128)(2,1)} %pad_maximum_fusion.weights), custom_call_target="tpu_custom_call" | custom-call | flops 536870912 | bytes 4194304 | tf_op jit(solution)/shard_map/numer/pallas_call | solution.py:220
  130.0 8.1 %all-to-all-start.4 = ((bf16[32,32,512]{2,1,0:T(8,128)(2,1)}), bf16[32,32,512]{2,1,0:T(8,128)(2,1)S(1)}, u32[]{:S(2)}, u32[]{:S(2)}) async-start(bf16[32,32,512]{2,1,0:T(8,128)(2,1)} %numer.1), calls=%async_computation.4 | async-start | bytes 2097152 | tf_op jit(solution)/shard_map/all_to_all | solution.py:381
  138.1 8.8 %gram2.1 = (f32[512,512]{1,0:T(8,128)}, bf16[512,512]{1,0:T(8,128)(2,1)}) custom-call(s32[15]{0:T(128)} %stack.63.info.refs_0_, bf16[256,512]{1,0:T(8,128)(2,1)} %copy-done.4, bf16[128,512]{1,0:T(8,128)(2,1)} %collective-permute-done.7.refs_2_, bf16[128,512]{1,0:T(8,128)(2,1)} %copy-done.10, bf16[8,8,16,1152]{3,2,1,0:T(8,128)(2,1)} %bitcast.26, ...), custom_call_target="tpu_custom_call" | custom-call | flops 4294967296 | bytes 6291456 | tf_op jit(solution)/shard_map/gram2/pallas_call | solution.py:333
  148.3 5.4 %all-to-all-done.4 = bf16[32,32,512]{2,1,0:T(8,128)(2,1)S(1)} async-done(((bf16[32,32,512]{2,1,0:T(8,128)(2,1)}), bf16[32,32,512]{2,1,0:T(8,128)(2,1)S(1)}, u32[]{:S(2)}, u32[]{:S(2)}) %all-to-all-start.4) | async-done | bytes 1048608 | tf_op jit(solution)/shard_map/all_to_all | solution.py:381
  154.7 6.1 %all-to-all-start.5 = ((bf16[16,32,512]{2,1,0:T(8,128)(2,1)}), bf16[16,32,512]{2,1,0:T(8,128)(2,1)S(1)}, u32[]{:S(2)}, u32[]{:S(2)}) async-start(bf16[16,32,512]{2,1,0:T(8,128)(2,1)} %broadcast_in_dim.23), calls=%async_computation.5 | async-start | bytes 1048576 | tf_op jit(solution)/shard_map/all_to_all | solution.py:383
  164.0 8.1 %all-to-all-done.5 = bf16[16,32,512]{2,1,0:T(8,128)(2,1)S(1)} async-done(((bf16[16,32,512]{2,1,0:T(8,128)(2,1)}), bf16[16,32,512]{2,1,0:T(8,128)(2,1)S(1)}, u32[]{:S(2)}, u32[]{:S(2)}) %all-to-all-start.5) | async-done | bytes 524320 | tf_op jit(solution)/shard_map/all_to_all | solution.py:383
  (48 shorter events, 19.7 us)
Async XLA Ops:
  0.6 29.4 %collective-permute-start = (bf16[512,512]{1,0:T(8,128)(2,1)}, bf16[512,512]{1,0:T(8,128)(2,1)S(1)}, u32[]{:S(2)}, u32[]{:S(2)}) collective-permute-start(bf16[512,512]{1,0:T(8,128)(2,1)} %bitcast.28), channel_id=1, source_target_pairs={{0,1},{1,0},{2,3},{3,2},{4,5},{5,4},{6,7},{7,6},{8,9},{9,8},{10,11... | collective-permute-start | bytes 1572872 | tf_op jit(solution)/shard_map/ppermute | solution.py:28
  30.1 28.8 %copy-start.3 = (bf16[1,512,512]{2,1,0:T(8,128)(2,1)S(1)}, bf16[1,512,512]{2,1,0:T(8,128)(2,1)}, u32[]{:S(2)}) copy-start(bf16[1,512,512]{2,1,0:T(8,128)(2,1)} %param.7) | copy-start | bytes 1572868
  30.1 34.6 %all-to-all-start.1 = ((bf16[64,16,1152]{2,1,0:T(8,128)(2,1)}), bf16[64,16,1152]{2,1,0:T(8,128)(2,1)S(1)}, u32[]{:S(2)}, u32[]{:S(2)}) async-start(bf16[64,16,1152]{2,1,0:T(8,128)(2,1)} %address.1), calls=%async_computation.1 | async-start | bytes 4718592 | tf_op jit(solution)/shard_map/all_to_all | solution.py:45
  36.5 5.4 %collective-permute-start.2 = (bf16[256,512]{1,0:T(8,128)(2,1)}, bf16[256,512]{1,0:T(8,128)(2,1)S(1)}, u32[]{:S(2)}, u32[]{:S(2)}) collective-permute-start(bf16[256,512]{1,0:T(8,128)(2,1)} %get-tuple-element.45.refs_1_), channel_id=1, source_target_pairs={{0,14},{1,15},{2,0},{3,1},{4,2},{5,3},{6,4},{7,5},{8,6},{9,7},{10,... | collective-permute-start | bytes 786440 | tf_op jit(solution)/shard_map/ppermute | solution.py:28
  36.8 6.8 %collective-permute-start.1 = (bf16[256,512]{1,0:T(8,128)(2,1)}, bf16[256,512]{1,0:T(8,128)(2,1)S(1)}, u32[]{:S(2)}, u32[]{:S(2)}) collective-permute-start(bf16[256,512]{1,0:T(8,128)(2,1)} %get-tuple-element.45.refs_1_), channel_id=1, source_target_pairs={{0,2},{1,3},{2,4},{3,5},{4,6},{5,7},{6,8},{7,9},{8,10},{9,11},{10,... | collective-permute-start | bytes 786440 | tf_op jit(solution)/shard_map/ppermute | solution.py:28
  42.0 8.5 %copy-start.8 = (bf16[256,512]{1,0:T(8,128)(2,1)}, bf16[256,512]{1,0:T(8,128)(2,1)S(1)}, u32[]{:S(2)}) copy-start(bf16[256,512]{1,0:T(8,128)(2,1)S(1)} %collective-permute-done.2.refs_3_) | copy-start | bytes 786436
  42.0 6.8 %collective-permute-start.4 = (bf16[256,512]{1,0:T(8,128)(2,1)S(1)}, bf16[256,512]{1,0:T(8,128)(2,1)S(1)}, u32[]{:S(2)}, u32[]{:S(2)}) collective-permute-start(bf16[256,512]{1,0:T(8,128)(2,1)S(1)} %collective-permute-done.2.refs_3_), channel_id=1, source_target_pairs={{0,14},{1,15},{2,0},{3,1},{4,2},{5,3},{6,4},{7,5},{8,6},{9,7},{10,... | collective-permute-start | bytes 786440 | tf_op jit(solution)/shard_map/ppermute | solution.py:28
  43.5 6.7 %copy-start.9 = (bf16[256,512]{1,0:T(8,128)(2,1)}, bf16[256,512]{1,0:T(8,128)(2,1)S(1)}, u32[]{:S(2)}) copy-start(bf16[256,512]{1,0:T(8,128)(2,1)S(1)} %collective-permute-done.1.refs_2_) | copy-start | bytes 786436
  43.5 6.8 %collective-permute-start.3 = (bf16[256,512]{1,0:T(8,128)(2,1)S(1)}, bf16[256,512]{1,0:T(8,128)(2,1)S(1)}, u32[]{:S(2)}, u32[]{:S(2)}) collective-permute-start(bf16[256,512]{1,0:T(8,128)(2,1)S(1)} %collective-permute-done.1.refs_2_), channel_id=1, source_target_pairs={{0,2},{1,3},{2,4},{3,5},{4,6},{5,7},{6,8},{7,9},{8,10},{9,11},{10,... | collective-permute-start | bytes 786440 | tf_op jit(solution)/shard_map/ppermute | solution.py:28
  48.8 1.8 %copy-start.6 = (bf16[256,512]{1,0:T(8,128)(2,1)}, bf16[256,512]{1,0:T(8,128)(2,1)S(1)}, u32[]{:S(2)}) copy-start(bf16[256,512]{1,0:T(8,128)(2,1)S(1)} %collective-permute-done.4.refs_2_) | copy-start | bytes 786436
  48.8 7.6 %collective-permute-start.6 = (bf16[256,512]{1,0:T(8,128)(2,1)S(1)}, bf16[256,512]{1,0:T(8,128)(2,1)S(1)}, u32[]{:S(2)}, u32[]{:S(2)}) collective-permute-start(bf16[256,512]{1,0:T(8,128)(2,1)S(1)} %collective-permute-done.4.refs_2_), channel_id=1, source_target_pairs={{0,14},{1,15},{2,0},{3,1},{4,2},{5,3},{6,4},{7,5},{8,6},{9,7},{10,... | collective-permute-start | bytes 786440 | tf_op jit(solution)/shard_map/ppermute | solution.py:28
  50.3 7.6 %copy-start.7 = (bf16[256,512]{1,0:T(8,128)(2,1)}, bf16[256,512]{1,0:T(8,128)(2,1)S(1)}, u32[]{:S(2)}) copy-start(bf16[256,512]{1,0:T(8,128)(2,1)S(1)} %collective-permute-done.3.refs_1_) | copy-start | bytes 786436
  50.3 7.6 %collective-permute-start.5 = (bf16[256,512]{1,0:T(8,128)(2,1)S(1)}, bf16[256,512]{1,0:T(8,128)(2,1)S(1)}, u32[]{:S(2)}, u32[]{:S(2)}) collective-permute-start(bf16[256,512]{1,0:T(8,128)(2,1)S(1)} %collective-permute-done.3.refs_1_), channel_id=1, source_target_pairs={{0,2},{1,3},{2,4},{3,5},{4,6},{5,7},{6,8},{7,9},{8,10},{9,11},{10,... | collective-permute-start | bytes 786440 | tf_op jit(solution)/shard_map/ppermute | solution.py:28
  56.3 5.5 %collective-permute-start.8 = (bf16[128,512]{1,0:T(8,128)(2,1)S(1)}, bf16[128,512]{1,0:T(8,128)(2,1)S(1)}, u32[]{:S(2)}, u32[]{:S(2)}) collective-permute-start(bf16[128,512]{1,0:T(8,128)(2,1)S(1)} %slice.9), channel_id=1, source_target_pairs={{0,14},{1,15},{2,0},{3,1},{4,2},{5,3},{6,4},{7,5},{8,6},{9,7},{10,... | collective-permute-start | bytes 393224 | tf_op jit(solution)/shard_map/ppermute | solution.py:28
  58.6 6.0 %collective-permute-start.7 = (bf16[128,512]{1,0:T(8,128)(2,1)S(1)}, bf16[128,512]{1,0:T(8,128)(2,1)}, u32[]{:S(2)}, u32[]{:S(2)}) collective-permute-start(bf16[128,512]{1,0:T(8,128)(2,1)S(1)} %slice.8), channel_id=1, source_target_pairs={{0,2},{1,3},{2,4},{3,5},{4,6},{5,7},{6,8},{7,9},{8,10},{9,11},{10,... | collective-permute-start | bytes 393224 | tf_op jit(solution)/shard_map/ppermute | solution.py:28
  61.9 35.7 %copy-start.10 = (bf16[128,512]{1,0:T(8,128)(2,1)}, bf16[128,512]{1,0:T(8,128)(2,1)S(1)}, u32[]{:S(2)}) copy-start(bf16[128,512]{1,0:T(8,128)(2,1)S(1)} %collective-permute-done.8.refs_3_) | copy-start | bytes 393220
  64.7 11.6 %copy-start = (bf16[64,16,1152]{2,1,0:T(8,128)(2,1)}, bf16[64,16,1152]{2,1,0:T(8,128)(2,1)S(1)}, u32[]{:S(2)}) copy-start(bf16[64,16,1152]{2,1,0:T(8,128)(2,1)S(1)} %all-to-all-done.1) | copy-start | bytes 7077892
  64.7 11.6 %collective-permute-start.9 = (bf16[8,8,16,1152]{3,2,1,0:T(8,128)(2,1)S(1)}, bf16[8,8,16,1152]{3,2,1,0:T(8,128)(2,1)}, u32[]{:S(2)}, u32[]{:S(2)}) collective-permute-start(bf16[8,8,16,1152]{3,2,1,0:T(8,128)(2,1)S(1)} %bitcast.21), channel_id=1, source_target_pairs={{0,16},{1,17},{2,18},{3,19},{4,20},{5,21},{6,22},{7,23},{8,24},{9,... | collective-permute-start | bytes 7077896 | tf_op jit(solution)/shard_map/ppermute | solution.py:28
  83.2 21.4 %all-to-all-start.2 = ((bf16[8,64,512]{2,1,0:T(8,128)(2,1)}), bf16[8,64,512]{2,1,0:T(8,128)(2,1)S(1)}, u32[]{:S(2)}, u32[]{:S(2)}) async-start(bf16[8,64,512]{2,1,0:T(8,128)(2,1)} %get-tuple-element.43), calls=%async_computation.2 | async-start | bytes 1048576 | tf_op jit(solution)/shard_map/all_to_all | solution.py:32
  105.6 20.1 %all-to-all-start.3 = ((bf16[8,64,512]{2,1,0:T(8,128)(2,1)}), bf16[8,64,512]{2,1,0:T(8,128)(2,1)S(1)}, u32[]{:S(2)}, u32[]{:S(2)}) async-start(bf16[8,64,512]{2,1,0:T(8,128)(2,1)} %broadcast_in_dim.20), calls=%async_computation.3 | async-start | bytes 1048576 | tf_op jit(solution)/shard_map/all_to_all | solution.py:32
  130.0 23.7 %all-to-all-start.4 = ((bf16[32,32,512]{2,1,0:T(8,128)(2,1)}), bf16[32,32,512]{2,1,0:T(8,128)(2,1)S(1)}, u32[]{:S(2)}, u32[]{:S(2)}) async-start(bf16[32,32,512]{2,1,0:T(8,128)(2,1)} %numer.1), calls=%async_computation.4 | async-start | bytes 2097152 | tf_op jit(solution)/shard_map/all_to_all | solution.py:381
  146.9 15.9 %copy-start.2 = (f32[512,512]{1,0:T(8,128)S(1)}, f32[512,512]{1,0:T(8,128)}, u32[]{:S(2)}) copy-start(f32[512,512]{1,0:T(8,128)} %get-tuple-element.67) | copy-start | bytes 3145732
  146.9 15.9 %collective-permute-start.10 = (bf16[512,512]{1,0:T(8,128)(2,1)}, bf16[512,512]{1,0:T(8,128)(2,1)S(1)}, u32[]{:S(2)}, u32[]{:S(2)}) collective-permute-start(bf16[512,512]{1,0:T(8,128)(2,1)} %get-tuple-element.68), channel_id=1, source_target_pairs={{0,1},{1,0},{2,3},{3,2},{4,5},{5,4},{6,7},{7,6},{8,9},{9,8},{10,11... | collective-permute-start | bytes 1572872 | tf_op jit(solution)/shard_map/ppermute | solution.py:28
  154.7 17.4 %all-to-all-start.5 = ((bf16[16,32,512]{2,1,0:T(8,128)(2,1)}), bf16[16,32,512]{2,1,0:T(8,128)(2,1)S(1)}, u32[]{:S(2)}, u32[]{:S(2)}) async-start(bf16[16,32,512]{2,1,0:T(8,128)(2,1)} %broadcast_in_dim.23), calls=%async_computation.5 | async-start | bytes 1048576 | tf_op jit(solution)/shard_map/all_to_all | solution.py:383
  (3 other events, 3.2 us)

commit v11 on v10

--- a/solution.py
+++ b/solution.py
@@ -41,11 +41,11 @@
 
 
 def gather(sent, w, x):
-    sent, other = lax.optimization_barrier((sent, shift(w, xl=1)))
+    u, d = shift(x, z=1), shift(x, z=-1)
+    sent, other, u, d = lax.optimization_barrier((sent, shift(w, xl=1), u, d))
     own = lax.all_to_all(sent, "mp", 0, 0, tiled=True, axis_index_groups=CORE_GROUPS)
-    z = [x]
-    u = d = x
-    for _ in range(3):
+    z = [x, u, d]
+    for _ in range(2):
         u, d = shift(u, z=1), shift(d, z=-1)
         z += [u, d]
     z += [shift(u[:128], z=1), shift(d[128:], z=-1)]

time: 174 us -> 171 us (0.983)
  blocking collectives: 18.9 us -> 0 us
  waiting for transfers between devices: 51.7 us -> 58.7 us
  starting transfers between devices: 45.1 us -> 52 us
    all_to_all x1 -> x0, blocking collectives: 18.9 us -> none  [swap_z(): lax.all_to_all(x, 'shard', 0, 0, tiled=True, axis_index_groups=Z_GROUPS)]
    ppermute x11, waiting for transfers between devices: 26.2 us -> 16.2 us  [shift(): return lax.ppermute(x, AXES, pairs)]
    all_to_all x2 -> x3, starting transfers between devices: 7.16 us -> 16.4 us  [swap_z(): lax.all_to_all(x, 'shard', 0, 0, tiled=True, axis_index_groups=Z_GROUPS)]
    all_to_all x1, waiting for transfers between devices: 0.01 us -> 8.62 us  [gather(): lax.all_to_all(sent, 'mp', 0, 0, tiled=True, axis_index_groups=CORE_GROUPS)]
    all_to_all x2 -> x3, waiting for transfers between devices: 12.1 us -> 20.2 us  [swap_z(): lax.all_to_all(x, 'shard', 0, 0, tiled=True, axis_index_groups=Z_GROUPS)]
    all_to_all x1, starting transfers between devices: 8.11 us -> 4.08 us  [local(): lax.all_to_all(numer, AXES, 0, 0, tiled=True, axis_index_groups=XLO_GROUPS)]
  transfers between devices with their start and end apart: 16 -> 17, of which waited for: 12 -> 12; matrix products, arithmetic and copies ran while one was open for 2% -> 2% of each run, Pallas kernels for 22% -> 23%
where the time goes in v11:
time: 171 us; the launch traced here: 170 us
  waiting for transfers between devices  58.7 us (34%)
  starting transfers between devices  52 us (30%)
  Pallas kernels  49.3 us (29%)
  local copies, waits for them, and re-layouts  5.32 us (3%)
  other arithmetic  3.58 us (2%)
    pallas_call x3, Pallas kernels, gram_call(): pl.pallas_call(lambda *refs: gram_kernel(first, last, *refs), grid_spec=p...  31 us
    all_to_all x3, waiting for transfers between devices, swap_z(): lax.all_to_all(x, 'shard', 0, 0, tiled=True, axis_index_groups=Z_GROUPS)  20.2 us
    ppermute x11, starting transfers between devices, shift(): return lax.ppermute(x, AXES, pairs)  19 us
    all_to_all x3, starting transfers between devices, swap_z(): lax.all_to_all(x, 'shard', 0, 0, tiled=True, axis_index_groups=Z_GROUPS)  16.4 us
    ppermute x11, waiting for transfers between devices, shift(): return lax.ppermute(x, AXES, pairs)  16.2 us
    all_to_all x1, waiting for transfers between devices, gather(): lax.all_to_all(sent, 'mp', 0, 0, tiled=True, axis_index_groups=CORE_GROUPS)  8.62 us
    all_to_all x1, waiting for transfers between devices, local(): lax.all_to_all(jnp.broadcast_to(numer[None], (16, 32, 512)), 'mp', 0, 0,...  8.16 us
    pallas_call x1, Pallas kernels, project(): pl.pallas_call(project_kernel, grid_spec=pltpu.PrefetchScalarGridSpec(num...  6.91 us
  transfers between devices with their start and end apart: 17, of which 12 were waited for; matrix products, arithmetic and copies ran while one was open for 2% of the time, Pallas kernels for 23%

profile of v11, /device:TPU:1, one launch (start us, length us, event | category | flops | bytes accessed | tf_op | source)
XLA Modules:
  0.0 169.6 jit_solution(14737356155150426492)
XLA Ops:
  3.4 5.3 %prepare.1 = (bf16[8,16,1152]{2,1,0:T(8,128)(2,1)}, bf16[256,512]{1,0:T(8,128)(2,1)}) custom-call(s32[15]{0:T(128)} %stack.63.info.refs_0_, bf16[256,8192]{1,0:T(8,128)(2,1)} %bank.1, s32[1,64]{1,0:T(1,128)} %ids.1), custom_call_target="tpu_custom_call" | custom-call | flops 268435456 | bytes 5242880 | tf_op jit(solution)/shard_map/prepare/pallas_call | solution.py:103
  8.6 8.2 %all-to-all-start = ((bf16[8,16,1152]{2,1,0:T(8,128)(2,1)}), bf16[8,16,1152]{2,1,0:T(8,128)(2,1)S(1)}, u32[]{:S(2)}, u32[]{:S(2)}) async-start(bf16[8,16,1152]{2,1,0:T(8,128)(2,1)} %get-tuple-element.38), calls=%async_computation | async-start | bytes 589824 | tf_op jit(solution)/shard_map/all_to_all | solution.py:32
  19.5 8.1 %all-to-all-done.piece = bf16[8,16,1152]{2,1,0:T(8,128)(2,1)S(1)} async-done(((bf16[8,16,1152]{2,1,0:T(8,128)(2,1)}), bf16[8,16,1152]{2,1,0:T(8,128)(2,1)S(1)}, u32[]{:S(2)}, u32[]{:S(2)}) %all-to-all-start) | async-done | bytes 294944 | tf_op jit(solution)/shard_map/all_to_all | solution.py:32
  32.7 6.3 %all-to-all-start.1 = ((bf16[64,16,1152]{2,1,0:T(8,128)(2,1)}), bf16[64,16,1152]{2,1,0:T(8,128)(2,1)S(1)}, u32[]{:S(2)}, u32[]{:S(2)}) async-start(bf16[64,16,1152]{2,1,0:T(8,128)(2,1)} %address.1), calls=%async_computation.1 | async-start | bytes 4718592 | tf_op jit(solution)/shard_map/all_to_all | solution.py:46
  41.7 4.0 %collective-permute-done.3.refs_1_ = bf16[256,512]{1,0:T(8,128)(2,1)S(1)} collective-permute-done((bf16[256,512]{1,0:T(8,128)(2,1)}, bf16[256,512]{1,0:T(8,128)(2,1)S(1)}, u32[]{:S(2)}, u32[]{:S(2)}) %collective-permute-start.3) | collective-permute-done | bytes 262176 | tf_op jit(solution)/shard_map/ppermute | solution.py:28
  45.7 3.0 %collective-permute-start.6 = (bf16[256,512]{1,0:T(8,128)(2,1)S(1)}, bf16[256,512]{1,0:T(8,128)(2,1)S(1)}, u32[]{:S(2)}, u32[]{:S(2)}) collective-permute-start(bf16[256,512]{1,0:T(8,128)(2,1)S(1)} %collective-permute-done.4.refs_2_), channel_id=1, source_target_pairs={{0,14},{1,15},{2,0},{3,1},{4,2},{5,3},{6,4},{7,5},{8,6},{9,7},{10,... | collective-permute-start | bytes 786440 | tf_op jit(solution)/shard_map/ppermute | solution.py:28
  48.7 3.8 %collective-permute-done.5.refs_3_ = bf16[256,512]{1,0:T(8,128)(2,1)S(1)} collective-permute-done((bf16[256,512]{1,0:T(8,128)(2,1)S(1)}, bf16[256,512]{1,0:T(8,128)(2,1)S(1)}, u32[]{:S(2)}, u32[]{:S(2)}) %collective-permute-start.5) | collective-permute-done | bytes 262176 | tf_op jit(solution)/shard_map/ppermute | solution.py:28
  53.3 2.9 %collective-permute-start.8 = (bf16[128,512]{1,0:T(8,128)(2,1)S(1)}, bf16[128,512]{1,0:T(8,128)(2,1)}, u32[]{:S(2)}, u32[]{:S(2)}) collective-permute-start(bf16[128,512]{1,0:T(8,128)(2,1)S(1)} %slice.9), channel_id=1, source_target_pairs={{0,14},{1,15},{2,0},{3,1},{4,2},{5,3},{6,4},{7,5},{8,6},{9,7},{10,... | collective-permute-start | bytes 393224 | tf_op jit(solution)/shard_map/ppermute | solution.py:28
  58.4 8.6 %all-to-all-done.1 = bf16[64,16,1152]{2,1,0:T(8,128)(2,1)S(1)} async-done(((bf16[64,16,1152]{2,1,0:T(8,128)(2,1)}), bf16[64,16,1152]{2,1,0:T(8,128)(2,1)S(1)}, u32[]{:S(2)}, u32[]{:S(2)}) %all-to-all-start.1) | async-done | bytes 2359328 | tf_op jit(solution)/shard_map/all_to_all | solution.py:46
  67.1 4.2 %collective-permute-start.9 = (bf16[8,8,16,1152]{3,2,1,0:T(8,128)(2,1)S(1)}, bf16[8,8,16,1152]{3,2,1,0:T(8,128)(2,1)}, u32[]{:S(2)}, u32[]{:S(2)}) collective-permute-start(bf16[8,8,16,1152]{3,2,1,0:T(8,128)(2,1)S(1)} %bitcast.21), channel_id=1, source_target_pairs={{0,16},{1,17},{2,18},{3,19},{4,20},{5,21},{6,22},{7,23},{8,24},{9,... | collective-permute-start | bytes 7077896 | tf_op jit(solution)/shard_map/ppermute | solution.py:28
  71.3 4.3 %collective-permute-done.9.other_s.refs_5_.refs_7_ = bf16[8,8,16,1152]{3,2,1,0:T(8,128)(2,1)} collective-permute-done((bf16[8,8,16,1152]{3,2,1,0:T(8,128)(2,1)S(1)}, bf16[8,8,16,1152]{3,2,1,0:T(8,128)(2,1)}, u32[]{:S(2)}, u32[]{:S(2)}) %collective-permute-start.9) | collective-permute-done | bytes 2359328 | tf_op jit(solution)/shard_map/ppermute | solution.py:28
  75.6 6.9 %project.1 = (bf16[8,64,512]{2,1,0:T(8,128)(2,1)}, bf16[512,1024]{1,0:T(8,128)(2,1)}, f32[1,1024]{1,0:T(1,128)}) custom-call(s32[15]{0:T(128)} %stack.63.info.refs_0_, bf16[8,8,16,1152]{3,2,1,0:T(8,128)(2,1)} %bitcast.22, bf16[8,8,16,1152]{3,2,1,0:T(8,128)(2,1)} %collective-permute-done.9.other_s.refs_5_.refs_7_, f32[1,8192]{1,0:T(1,128)} %gains.3, ...), custom_call_target="tpu_custom_call" | custom-call | flops 1073741824 | bytes 8388608 | tf_op jit(solution)/shard_map/project/pallas_call | solution.py:185
  82.5 4.6 %all-to-all-start.2 = ((bf16[8,64,512]{2,1,0:T(8,128)(2,1)}), bf16[8,64,512]{2,1,0:T(8,128)(2,1)S(1)}, u32[]{:S(2)}, u32[]{:S(2)}) async-start(bf16[8,64,512]{2,1,0:T(8,128)(2,1)} %get-tuple-element.47), calls=%async_computation.2 | async-start | bytes 1048576 | tf_op jit(solution)/shard_map/all_to_all | solution.py:32
  87.1 10.8 %gram0.1 = (f32[512,1024]{1,0:T(8,128)}, f32[16,1536]{1,0:T(8,128)}) custom-call(s32[15]{0:T(128)} %stack.63.info.refs_0_, bf16[256,512]{1,0:T(8,128)(2,1)} %get-tuple-element.49.refs_1_, bf16[256,512]{1,0:T(8,128)(2,1)} %copy-done.8, bf16[256,512]{1,0:T(8,128)(2,1)} %copy-done.7, bf16[8,8,16,1152]{3,2,1,0:T(8,128)(2,1)} %bitcast.23, ...), custom_call_target="tpu_custom_call" | custom-call | flops 6442450944 | bytes 6291456 | tf_op jit(solution)/shard_map/gram0/pallas_call | solution.py:333
  97.9 7.1 %all-to-all-done.2 = bf16[8,64,512]{2,1,0:T(8,128)(2,1)S(1)} async-done(((bf16[8,64,512]{2,1,0:T(8,128)(2,1)}), bf16[8,64,512]{2,1,0:T(8,128)(2,1)S(1)}, u32[]{:S(2)}, u32[]{:S(2)}) %all-to-all-start.2) | async-done | bytes 524320 | tf_op jit(solution)/shard_map/all_to_all | solution.py:32
  105.9 3.7 %all-to-all-start.3 = ((bf16[8,64,512]{2,1,0:T(8,128)(2,1)}), bf16[8,64,512]{2,1,0:T(8,128)(2,1)S(1)}, u32[]{:S(2)}, u32[]{:S(2)}) async-start(bf16[8,64,512]{2,1,0:T(8,128)(2,1)} %broadcast_in_dim.20), calls=%async_computation.3 | async-start | bytes 1048576 | tf_op jit(solution)/shard_map/all_to_all | solution.py:32
  109.6 11.4 %gram1.1.refs_7_ = f32[512,1024]{1,0:T(8,128)} custom-call(s32[15]{0:T(128)} %stack.63.info.refs_0_, bf16[256,512]{1,0:T(8,128)(2,1)} %copy-done.9, bf16[256,512]{1,0:T(8,128)(2,1)} %copy-done.10, bf16[256,512]{1,0:T(8,128)(2,1)} %copy-done.6, bf16[8,8,16,1152]{3,2,1,0:T(8,128)(2,1)} %bitcast.25, ...), custom_call_target="tpu_custom_call", output_to_operand_aliasing={{}: (7, {})} | custom-call | flops 6442450944 | bytes 6291456 | tf_op jit(solution)/shard_map/gram1/pallas_call | solution.py:333
  121.0 5.0 %all-to-all-done.3 = bf16[8,64,512]{2,1,0:T(8,128)(2,1)S(1)} async-done(((bf16[8,64,512]{2,1,0:T(8,128)(2,1)}), bf16[8,64,512]{2,1,0:T(8,128)(2,1)S(1)}, u32[]{:S(2)}, u32[]{:S(2)}) %all-to-all-start.3) | async-done | bytes 524320 | tf_op jit(solution)/shard_map/all_to_all | solution.py:32
  126.9 3.5 %numer.1 = bf16[32,32,512]{2,1,0:T(8,128)(2,1)} custom-call(s32[15]{0:T(128)} %stack.63.info.refs_0_, bf16[512,1024]{1,0:T(8,128)(2,1)} %get-tuple-element.55.calib, bf16[512,512]{1,0:T(8,128)(2,1)} %bitcast.27, f32[1,1024]{1,0:T(1,128)} %get-tuple-element.63.diag, bf16[1024,512]{1,0:T(8,128)(2,1)} %pad_maximum_fusion.weights), custom_call_target="tpu_custom_call" | custom-call | flops 536870912 | bytes 4194304 | tf_op jit(solution)/shard_map/numer/pallas_call | solution.py:220
  130.4 4.1 %all-to-all-start.4 = ((bf16[32,32,512]{2,1,0:T(8,128)(2,1)}), bf16[32,32,512]{2,1,0:T(8,128)(2,1)S(1)}, u32[]{:S(2)}, u32[]{:S(2)}) async-start(bf16[32,32,512]{2,1,0:T(8,128)(2,1)} %numer.1), calls=%async_computation.4 | async-start | bytes 2097152 | tf_op jit(solution)/shard_map/all_to_all | solution.py:381
  134.5 8.8 %gram2.1 = (f32[512,512]{1,0:T(8,128)}, bf16[512,512]{1,0:T(8,128)(2,1)}) custom-call(s32[15]{0:T(128)} %stack.63.info.refs_0_, bf16[256,512]{1,0:T(8,128)(2,1)} %copy-done.5, bf16[128,512]{1,0:T(8,128)(2,1)} %copy-done.11, bf16[128,512]{1,0:T(8,128)(2,1)} %collective-permute-done.8.refs_3_, bf16[8,8,16,1152]{3,2,1,0:T(8,128)(2,1)} %bitcast.26, ...), custom_call_target="tpu_custom_call" | custom-call | flops 4294967296 | bytes 6291456 | tf_op jit(solution)/shard_map/gram2/pallas_call | solution.py:333
  144.6 5.5 %all-to-all-done.4 = bf16[32,32,512]{2,1,0:T(8,128)(2,1)S(1)} async-done(((bf16[32,32,512]{2,1,0:T(8,128)(2,1)}), bf16[32,32,512]{2,1,0:T(8,128)(2,1)S(1)}, u32[]{:S(2)}, u32[]{:S(2)}) %all-to-all-start.4) | async-done | bytes 1048608 | tf_op jit(solution)/shard_map/all_to_all | solution.py:381
  151.1 6.1 %all-to-all-start.5 = ((bf16[16,32,512]{2,1,0:T(8,128)(2,1)}), bf16[16,32,512]{2,1,0:T(8,128)(2,1)S(1)}, u32[]{:S(2)}, u32[]{:S(2)}) async-start(bf16[16,32,512]{2,1,0:T(8,128)(2,1)} %broadcast_in_dim.23), calls=%async_computation.5 | async-start | bytes 1048576 | tf_op jit(solution)/shard_map/all_to_all | solution.py:383
  160.3 8.2 %all-to-all-done.5 = bf16[16,32,512]{2,1,0:T(8,128)(2,1)S(1)} async-done(((bf16[16,32,512]{2,1,0:T(8,128)(2,1)}), bf16[16,32,512]{2,1,0:T(8,128)(2,1)S(1)}, u32[]{:S(2)}, u32[]{:S(2)}) %all-to-all-start.5) | async-done | bytes 524320 | tf_op jit(solution)/shard_map/all_to_all | solution.py:383
  (51 shorter events, 24.6 us)
Async XLA Ops:
  0.6 31.4 %collective-permute-start = (bf16[512,512]{1,0:T(8,128)(2,1)}, bf16[512,512]{1,0:T(8,128)(2,1)S(1)}, u32[]{:S(2)}, u32[]{:S(2)}) collective-permute-start(bf16[512,512]{1,0:T(8,128)(2,1)} %bitcast.28), channel_id=1, source_target_pairs={{0,1},{1,0},{2,3},{3,2},{4,5},{5,4},{6,7},{7,6},{8,9},{9,8},{10,11... | collective-permute-start | bytes 1572872 | tf_op jit(solution)/shard_map/ppermute | solution.py:28
  8.6 19.0 %all-to-all-start = ((bf16[8,16,1152]{2,1,0:T(8,128)(2,1)}), bf16[8,16,1152]{2,1,0:T(8,128)(2,1)S(1)}, u32[]{:S(2)}, u32[]{:S(2)}) async-start(bf16[8,16,1152]{2,1,0:T(8,128)(2,1)} %get-tuple-element.38), calls=%async_computation | async-start | bytes 589824 | tf_op jit(solution)/shard_map/all_to_all | solution.py:32
  16.8 14.1 %collective-permute-start.2 = (bf16[256,512]{1,0:T(8,128)(2,1)}, bf16[256,512]{1,0:T(8,128)(2,1)S(1)}, u32[]{:S(2)}, u32[]{:S(2)}) collective-permute-start(bf16[256,512]{1,0:T(8,128)(2,1)} %get-tuple-element.49.refs_1_), channel_id=1, source_target_pairs={{0,14},{1,15},{2,0},{3,1},{4,2},{5,3},{6,4},{7,5},{8,6},{9,7},{10,... | collective-permute-start | bytes 786440 | tf_op jit(solution)/shard_map/ppermute | solution.py:28
  19.5 12.5 %collective-permute-start.1 = (bf16[256,512]{1,0:T(8,128)(2,1)}, bf16[256,512]{1,0:T(8,128)(2,1)S(1)}, u32[]{:S(2)}, u32[]{:S(2)}) collective-permute-start(bf16[256,512]{1,0:T(8,128)(2,1)} %get-tuple-element.49.refs_1_), channel_id=1, source_target_pairs={{0,2},{1,3},{2,4},{3,5},{4,6},{5,7},{6,8},{7,9},{8,10},{9,11},{10,... | collective-permute-start | bytes 786440 | tf_op jit(solution)/shard_map/ppermute | solution.py:28
  30.9 25.3 %copy-start.4 = (bf16[1,512,512]{2,1,0:T(8,128)(2,1)S(1)}, bf16[1,512,512]{2,1,0:T(8,128)(2,1)}, u32[]{:S(2)}) copy-start(bf16[1,512,512]{2,1,0:T(8,128)(2,1)} %param.7) | copy-start | bytes 1572868
  30.9 1.1 copy-start.7
  32.7 34.3 %all-to-all-start.1 = ((bf16[64,16,1152]{2,1,0:T(8,128)(2,1)}), bf16[64,16,1152]{2,1,0:T(8,128)(2,1)S(1)}, u32[]{:S(2)}, u32[]{:S(2)}) async-start(bf16[64,16,1152]{2,1,0:T(8,128)(2,1)} %address.1), calls=%async_computation.1 | async-start | bytes 4718592 | tf_op jit(solution)/shard_map/all_to_all | solution.py:46
  39.1 6.6 %collective-permute-start.3 = (bf16[256,512]{1,0:T(8,128)(2,1)}, bf16[256,512]{1,0:T(8,128)(2,1)S(1)}, u32[]{:S(2)}, u32[]{:S(2)}) collective-permute-start(bf16[256,512]{1,0:T(8,128)(2,1)} %copy-done.8), channel_id=1, source_target_pairs={{0,2},{1,3},{2,4},{3,5},{4,6},{5,7},{6,8},{7,9},{8,10},{9,11},{10,... | collective-permute-start | bytes 786440 | tf_op jit(solution)/shard_map/ppermute | solution.py:28
  39.1 6.6 %collective-permute-start.4 = (bf16[256,512]{1,0:T(8,128)(2,1)}, bf16[256,512]{1,0:T(8,128)(2,1)S(1)}, u32[]{:S(2)}, u32[]{:S(2)}) collective-permute-start(bf16[256,512]{1,0:T(8,128)(2,1)} %copy-done.7), channel_id=1, source_target_pairs={{0,14},{1,15},{2,0},{3,1},{4,2},{5,3},{6,4},{7,5},{8,6},{9,7},{10,... | collective-permute-start | bytes 786440 | tf_op jit(solution)/shard_map/ppermute | solution.py:28
  45.7 3.0 %copy-start.9 = (bf16[256,512]{1,0:T(8,128)(2,1)}, bf16[256,512]{1,0:T(8,128)(2,1)S(1)}, u32[]{:S(2)}) copy-start(bf16[256,512]{1,0:T(8,128)(2,1)S(1)} %collective-permute-done.3.refs_1_) | copy-start | bytes 786436
  45.7 6.7 %collective-permute-start.5 = (bf16[256,512]{1,0:T(8,128)(2,1)S(1)}, bf16[256,512]{1,0:T(8,128)(2,1)S(1)}, u32[]{:S(2)}, u32[]{:S(2)}) collective-permute-start(bf16[256,512]{1,0:T(8,128)(2,1)S(1)} %collective-permute-done.3.refs_1_), channel_id=1, source_target_pairs={{0,2},{1,3},{2,4},{3,5},{4,6},{5,7},{6,8},{7,9},{8,10},{9,11},{10,... | collective-permute-start | bytes 786440 | tf_op jit(solution)/shard_map/ppermute | solution.py:28
  45.7 7.6 %copy-start.10 = (bf16[256,512]{1,0:T(8,128)(2,1)}, bf16[256,512]{1,0:T(8,128)(2,1)S(1)}, u32[]{:S(2)}) copy-start(bf16[256,512]{1,0:T(8,128)(2,1)S(1)} %collective-permute-done.4.refs_2_) | copy-start | bytes 786436
  45.7 6.8 %collective-permute-start.6 = (bf16[256,512]{1,0:T(8,128)(2,1)S(1)}, bf16[256,512]{1,0:T(8,128)(2,1)S(1)}, u32[]{:S(2)}, u32[]{:S(2)}) collective-permute-start(bf16[256,512]{1,0:T(8,128)(2,1)S(1)} %collective-permute-done.4.refs_2_), channel_id=1, source_target_pairs={{0,14},{1,15},{2,0},{3,1},{4,2},{5,3},{6,4},{7,5},{8,6},{9,7},{10,... | collective-permute-start | bytes 786440 | tf_op jit(solution)/shard_map/ppermute | solution.py:28
  52.4 6.0 %collective-permute-start.7 = (bf16[128,512]{1,0:T(8,128)(2,1)S(1)}, bf16[128,512]{1,0:T(8,128)(2,1)S(1)}, u32[]{:S(2)}, u32[]{:S(2)}) collective-permute-start(bf16[128,512]{1,0:T(8,128)(2,1)S(1)} %slice.8), channel_id=1, source_target_pairs={{0,2},{1,3},{2,4},{3,5},{4,6},{5,7},{6,8},{7,9},{8,10},{9,11},{10,... | collective-permute-start | bytes 393224 | tf_op jit(solution)/shard_map/ppermute | solution.py:28
  53.3 5.1 %collective-permute-start.8 = (bf16[128,512]{1,0:T(8,128)(2,1)S(1)}, bf16[128,512]{1,0:T(8,128)(2,1)}, u32[]{:S(2)}, u32[]{:S(2)}) collective-permute-start(bf16[128,512]{1,0:T(8,128)(2,1)S(1)} %slice.9), channel_id=1, source_target_pairs={{0,14},{1,15},{2,0},{3,1},{4,2},{5,3},{6,4},{7,5},{8,6},{9,7},{10,... | collective-permute-start | bytes 393224 | tf_op jit(solution)/shard_map/ppermute | solution.py:28
  58.4 39.5 %copy-start.11 = (bf16[128,512]{1,0:T(8,128)(2,1)}, bf16[128,512]{1,0:T(8,128)(2,1)S(1)}, u32[]{:S(2)}) copy-start(bf16[128,512]{1,0:T(8,128)(2,1)S(1)} %collective-permute-done.7.refs_2_) | copy-start | bytes 393220
  67.1 8.5 %copy-start = (bf16[64,16,1152]{2,1,0:T(8,128)(2,1)}, bf16[64,16,1152]{2,1,0:T(8,128)(2,1)S(1)}, u32[]{:S(2)}) copy-start(bf16[64,16,1152]{2,1,0:T(8,128)(2,1)S(1)} %all-to-all-done.1) | copy-start | bytes 7077892
  67.1 8.5 %collective-permute-start.9 = (bf16[8,8,16,1152]{3,2,1,0:T(8,128)(2,1)S(1)}, bf16[8,8,16,1152]{3,2,1,0:T(8,128)(2,1)}, u32[]{:S(2)}, u32[]{:S(2)}) collective-permute-start(bf16[8,8,16,1152]{3,2,1,0:T(8,128)(2,1)S(1)} %bitcast.21), channel_id=1, source_target_pairs={{0,16},{1,17},{2,18},{3,19},{4,20},{5,21},{6,22},{7,23},{8,24},{9,... | collective-permute-start | bytes 7077896 | tf_op jit(solution)/shard_map/ppermute | solution.py:28
  82.5 22.6 %all-to-all-start.2 = ((bf16[8,64,512]{2,1,0:T(8,128)(2,1)}), bf16[8,64,512]{2,1,0:T(8,128)(2,1)S(1)}, u32[]{:S(2)}, u32[]{:S(2)}) async-start(bf16[8,64,512]{2,1,0:T(8,128)(2,1)} %get-tuple-element.47), calls=%async_computation.2 | async-start | bytes 1048576 | tf_op jit(solution)/shard_map/all_to_all | solution.py:32
  105.9 20.1 %all-to-all-start.3 = ((bf16[8,64,512]{2,1,0:T(8,128)(2,1)}), bf16[8,64,512]{2,1,0:T(8,128)(2,1)S(1)}, u32[]{:S(2)}, u32[]{:S(2)}) async-start(bf16[8,64,512]{2,1,0:T(8,128)(2,1)} %broadcast_in_dim.20), calls=%async_computation.3 | async-start | bytes 1048576 | tf_op jit(solution)/shard_map/all_to_all | solution.py:32
  130.4 19.7 %all-to-all-start.4 = ((bf16[32,32,512]{2,1,0:T(8,128)(2,1)}), bf16[32,32,512]{2,1,0:T(8,128)(2,1)S(1)}, u32[]{:S(2)}, u32[]{:S(2)}) async-start(bf16[32,32,512]{2,1,0:T(8,128)(2,1)} %numer.1), calls=%async_computation.4 | async-start | bytes 2097152 | tf_op jit(solution)/shard_map/all_to_all | solution.py:381
  143.3 15.9 %copy-start.3 = (f32[512,512]{1,0:T(8,128)S(1)}, f32[512,512]{1,0:T(8,128)}, u32[]{:S(2)}) copy-start(f32[512,512]{1,0:T(8,128)} %get-tuple-element.71) | copy-start | bytes 3145732
  143.3 15.9 %collective-permute-start.10 = (bf16[512,512]{1,0:T(8,128)(2,1)}, bf16[512,512]{1,0:T(8,128)(2,1)S(1)}, u32[]{:S(2)}, u32[]{:S(2)}) collective-permute-start(bf16[512,512]{1,0:T(8,128)(2,1)} %get-tuple-element.72), channel_id=1, source_target_pairs={{0,1},{1,0},{2,3},{3,2},{4,5},{5,4},{6,7},{7,6},{8,9},{9,8},{10,11... | collective-permute-start | bytes 1572872 | tf_op jit(solution)/shard_map/ppermute | solution.py:28
  151.1 17.4 %all-to-all-start.5 = ((bf16[16,32,512]{2,1,0:T(8,128)(2,1)}), bf16[16,32,512]{2,1,0:T(8,128)(2,1)S(1)}, u32[]{:S(2)}, u32[]{:S(2)}) async-start(bf16[16,32,512]{2,1,0:T(8,128)(2,1)} %broadcast_in_dim.23), calls=%async_computation.5 | async-start | bytes 1048576 | tf_op jit(solution)/shard_map/all_to_all | solution.py:383
  (5 other events, 3.9 us)

commit v12 on v11

--- a/solution.py
+++ b/solution.py
@@ -135,7 +135,7 @@
         in_specs=[pl.BlockSpec(memory_space=pltpu.SMEM)] + [pl.BlockSpec(memory_space=pltpu.VMEM)] * 2,
         out_specs=pl.BlockSpec(memory_space=pltpu.VMEM),
         out_shape=jax.ShapeDtypeStruct((64, 16, 1152), BF),
-        compiler_params=pltpu.CompilerParams(vmem_limit_bytes=VMEM),
+        compiler_params=pltpu.CompilerParams(vmem_limit_bytes=16 * 2**20),
         cost_estimate=pl.CostEstimate(flops=2**20, bytes_accessed=3 * 2**20, transcendentals=0),
         name="address",
     )(info, piece, gains)
@@ -203,26 +203,32 @@
 
 
 def numer_kernel(info, calib, model_out, diag, weights, out):
-    xl = info[2]
-    ratio = lax.broadcasted_iota(jnp.int32, (512, 512), 0) == lax.broadcasted_iota(jnp.int32, (512, 512), 1)
-    for j in range(2):
-        cols = slice(j * 512, j * 512 + 512)
-        d = diag[:, cols] * ((1.0 - ALPHA) / 1024)
-        d = jnp.sum(jnp.where(ratio, d, 0.0), axis=1, keepdims=True)
-        got = contract_rows(calib[:, cols], model_out[...]) * (ALPHA / 1024)
-        got = got + d * weights[cols, :].astype(F4)
-        got = got.astype(BF)
-        for q in range(16):
-            out[q * 2 + (xl ^ j)] = got[q * 32 : q * 32 + 32]
+    i = pl.program_id(0)
+    side = info[2] ^ (i // 2)
+    on = lax.broadcasted_iota(jnp.int32, (256, 256), 0) == lax.broadcasted_iota(jnp.int32, (256, 256), 1)
+    d = jnp.sum(jnp.where(on, diag[...] * ((1.0 - ALPHA) / 1024), 0.0), axis=1, keepdims=True)
+    got = contract_rows(calib[...], model_out[...]) * (ALPHA / 1024) + d * weights[...].astype(F4)
+    got = got.astype(BF)
+    for q in range(8):
+        out[(i % 2 * 8 + q) * 2 + side] = got[q * 32 : q * 32 + 32]
 
 
 def numer_call(info, calib, model_out, diag, weights):
     return pl.pallas_call(
         numer_kernel,
-        in_specs=[pl.BlockSpec(memory_space=pltpu.SMEM)] + [pl.BlockSpec(memory_space=pltpu.VMEM)] * 4,
-        out_specs=pl.BlockSpec(memory_space=pltpu.VMEM),
+        grid_spec=pltpu.PrefetchScalarGridSpec(
+            num_scalar_prefetch=1,
+            grid=(4,),
+            in_specs=[
+                pl.BlockSpec((512, 256), lambda i, info: (0, i)),
+                pl.BlockSpec((512, 512), lambda i, info: (0, 0)),
+                pl.BlockSpec((1, 256), lambda i, info: (0, i)),
+                pl.BlockSpec((256, 512), lambda i, info: (i, 0)),
+            ],
+            out_specs=pl.BlockSpec((32, 32, 512), lambda i, info: (0, 0, 0)),
+        ),
         out_shape=jax.ShapeDtypeStruct((32, 32, 512), BF),
-        compiler_params=pltpu.CompilerParams(vmem_limit_bytes=VMEM),
+        compiler_params=pltpu.CompilerParams(dimension_semantics=("arbitrary",), vmem_limit_bytes=16 * 2**20),
         cost_estimate=pl.CostEstimate(flops=2**29, bytes_accessed=4 * 2**20, transcendentals=0),
         name="numer",
     )(info, calib, model_out, diag, weights)

time: 171 us -> 169 us (0.988)
  waiting for transfers between devices: 58.7 us -> 61.6 us
  starting transfers between devices: 52 us -> 50.1 us
    ppermute x11, waiting for transfers between devices: 16.2 us -> 18.1 us  [shift(): return lax.ppermute(x, AXES, pairs)]
    ppermute x11, starting transfers between devices: 19 us -> 17.2 us  [shift(): return lax.ppermute(x, AXES, pairs)]
  transfers between devices with their start and end apart: 17 -> 17, of which waited for: 12 -> 14; matrix products, arithmetic and copies ran while one was open for 2% -> 2% of each run, Pallas kernels for 23% -> 23%
where the time goes in v12:
time: 169 us
  waiting for transfers between devices  61.6 us (36%)
  starting transfers between devices  50.1 us (30%)
  Pallas kernels  48.6 us (29%)
  local copies, waits for them, and re-layouts  3.81 us (2%)
  other arithmetic  3.58 us (2%)
    pallas_call x3, Pallas kernels, gram_call(): pl.pallas_call(lambda *refs: gram_kernel(first, last, *refs), grid_spec=p...  31.1 us
    all_to_all x3, waiting for transfers between devices, swap_z(): lax.all_to_all(x, 'shard', 0, 0, tiled=True, axis_index_groups=Z_GROUPS)  20.1 us
    ppermute x11, waiting for transfers between devices, shift(): return lax.ppermute(x, AXES, pairs)  18.1 us
    ppermute x11, starting transfers between devices, shift(): return lax.ppermute(x, AXES, pairs)  17.2 us
    all_to_all x3, starting transfers between devices, swap_z(): lax.all_to_all(x, 'shard', 0, 0, tiled=True, axis_index_groups=Z_GROUPS)  16.4 us
    all_to_all x1, waiting for transfers between devices, gather(): lax.all_to_all(sent, 'mp', 0, 0, tiled=True, axis_index_groups=CORE_GROUPS)  9.79 us
    all_to_all x1, waiting for transfers between devices, local(): lax.all_to_all(jnp.broadcast_to(numer[None], (16, 32, 512)), 'mp', 0, 0,...  8.16 us
    pallas_call x1, Pallas kernels, project(): pl.pallas_call(project_kernel, grid_spec=pltpu.PrefetchScalarGridSpec(num...  6.91 us
  transfers between devices with their start and end apart: 17, of which 14 were waited for; matrix products, arithmetic and copies ran while one was open for 2% of the time, Pallas kernels for 23%

profile of v12, /device:TPU:1, one launch (start us, length us, event | category | flops | bytes accessed | tf_op | source)
XLA Modules:
  0.0 168.6 jit_solution(4939058588008215710)
XLA Ops:
  3.5 5.4 %prepare.1 = (bf16[8,16,1152]{2,1,0:T(8,128)(2,1)}, bf16[256,512]{1,0:T(8,128)(2,1)}) custom-call(s32[15]{0:T(128)} %stack.63.info.refs_0_, bf16[256,8192]{1,0:T(8,128)(2,1)} %bank.1, s32[1,64]{1,0:T(1,128)} %ids.1), custom_call_target="tpu_custom_call" | custom-call | flops 268435456 | bytes 5242880 | tf_op jit(solution)/shard_map/prepare/pallas_call | solution.py:103
  8.9 8.2 %all-to-all-start = ((bf16[8,16,1152]{2,1,0:T(8,128)(2,1)}), bf16[8,16,1152]{2,1,0:T(8,128)(2,1)S(1)}, u32[]{:S(2)}, u32[]{:S(2)}) async-start(bf16[8,16,1152]{2,1,0:T(8,128)(2,1)} %get-tuple-element.38), calls=%async_computation | async-start | bytes 589824 | tf_op jit(solution)/shard_map/all_to_all | solution.py:32
  17.0 2.7 %collective-permute-start.2 = (bf16[256,512]{1,0:T(8,128)(2,1)}, bf16[256,512]{1,0:T(8,128)(2,1)S(1)}, u32[]{:S(2)}, u32[]{:S(2)}) collective-permute-start(bf16[256,512]{1,0:T(8,128)(2,1)} %get-tuple-element.49.refs_1_), channel_id=1, source_target_pairs={{0,14},{1,15},{2,0},{3,1},{4,2},{5,3},{6,4},{7,5},{8,6},{9,7},{10,... | collective-permute-start | bytes 786440 | tf_op jit(solution)/shard_map/ppermute | solution.py:28
  19.7 8.1 %all-to-all-done.piece = bf16[8,16,1152]{2,1,0:T(8,128)(2,1)S(1)} async-done(((bf16[8,16,1152]{2,1,0:T(8,128)(2,1)}), bf16[8,16,1152]{2,1,0:T(8,128)(2,1)S(1)}, u32[]{:S(2)}, u32[]{:S(2)}) %all-to-all-start) | async-done | bytes 294944 | tf_op jit(solution)/shard_map/all_to_all | solution.py:32
  32.9 6.3 %all-to-all-start.1 = ((bf16[64,16,1152]{2,1,0:T(8,128)(2,1)}), bf16[64,16,1152]{2,1,0:T(8,128)(2,1)S(1)}, u32[]{:S(2)}, u32[]{:S(2)}) async-start(bf16[64,16,1152]{2,1,0:T(8,128)(2,1)} %address.1), calls=%async_computation.1 | async-start | bytes 4718592 | tf_op jit(solution)/shard_map/all_to_all | solution.py:46
  41.9 4.7 %collective-permute-done.3.refs_1_ = bf16[256,512]{1,0:T(8,128)(2,1)S(1)} collective-permute-done((bf16[256,512]{1,0:T(8,128)(2,1)}, bf16[256,512]{1,0:T(8,128)(2,1)S(1)}, u32[]{:S(2)}, u32[]{:S(2)}) %collective-permute-start.3) | collective-permute-done | bytes 262176 | tf_op jit(solution)/shard_map/ppermute | solution.py:28
  49.3 4.0 %collective-permute-done.5.refs_3_ = bf16[256,512]{1,0:T(8,128)(2,1)S(1)} collective-permute-done((bf16[256,512]{1,0:T(8,128)(2,1)S(1)}, bf16[256,512]{1,0:T(8,128)(2,1)S(1)}, u32[]{:S(2)}, u32[]{:S(2)}) %collective-permute-start.5) | collective-permute-done | bytes 262176 | tf_op jit(solution)/shard_map/ppermute | solution.py:28
  54.2 2.7 %collective-permute-start.8 = (bf16[128,512]{1,0:T(8,128)(2,1)S(1)}, bf16[128,512]{1,0:T(8,128)(2,1)}, u32[]{:S(2)}, u32[]{:S(2)}) collective-permute-start(bf16[128,512]{1,0:T(8,128)(2,1)S(1)} %slice.9), channel_id=1, source_target_pairs={{0,14},{1,15},{2,0},{3,1},{4,2},{5,3},{6,4},{7,5},{8,6},{9,7},{10,... | collective-permute-start | bytes 393224 | tf_op jit(solution)/shard_map/ppermute | solution.py:28
  58.9 9.8 %all-to-all-done.1 = bf16[64,16,1152]{2,1,0:T(8,128)(2,1)S(1)} async-done(((bf16[64,16,1152]{2,1,0:T(8,128)(2,1)}), bf16[64,16,1152]{2,1,0:T(8,128)(2,1)S(1)}, u32[]{:S(2)}, u32[]{:S(2)}) %all-to-all-start.1) | async-done | bytes 2359328 | tf_op jit(solution)/shard_map/all_to_all | solution.py:46
  68.7 2.8 %collective-permute-start.9 = (bf16[8,8,16,1152]{3,2,1,0:T(8,128)(2,1)S(1)}, bf16[8,8,16,1152]{3,2,1,0:T(8,128)(2,1)}, u32[]{:S(2)}, u32[]{:S(2)}) collective-permute-start(bf16[8,8,16,1152]{3,2,1,0:T(8,128)(2,1)S(1)} %bitcast.22), channel_id=1, source_target_pairs={{0,16},{1,17},{2,18},{3,19},{4,20},{5,21},{6,22},{7,23},{8,24},{9,... | collective-permute-start | bytes 7077896 | tf_op jit(solution)/shard_map/ppermute | solution.py:28
  71.5 4.3 %collective-permute-done.9.other_s.refs_5_.refs_7_ = bf16[8,8,16,1152]{3,2,1,0:T(8,128)(2,1)} collective-permute-done((bf16[8,8,16,1152]{3,2,1,0:T(8,128)(2,1)S(1)}, bf16[8,8,16,1152]{3,2,1,0:T(8,128)(2,1)}, u32[]{:S(2)}, u32[]{:S(2)}) %collective-permute-start.9) | collective-permute-done | bytes 2359328 | tf_op jit(solution)/shard_map/ppermute | solution.py:28
  75.8 6.9 %project.1 = (bf16[8,64,512]{2,1,0:T(8,128)(2,1)}, bf16[512,1024]{1,0:T(8,128)(2,1)}, f32[1,1024]{1,0:T(1,128)}) custom-call(s32[15]{0:T(128)} %stack.63.info.refs_0_, bf16[8,8,16,1152]{3,2,1,0:T(8,128)(2,1)} %bitcast.23, bf16[8,8,16,1152]{3,2,1,0:T(8,128)(2,1)} %collective-permute-done.9.other_s.refs_5_.refs_7_, f32[1,8192]{1,0:T(1,128)} %gains.3, ...), custom_call_target="tpu_custom_call" | custom-call | flops 1073741824 | bytes 8388608 | tf_op jit(solution)/shard_map/project/pallas_call | solution.py:185
  82.7 4.6 %all-to-all-start.2 = ((bf16[8,64,512]{2,1,0:T(8,128)(2,1)}), bf16[8,64,512]{2,1,0:T(8,128)(2,1)S(1)}, u32[]{:S(2)}, u32[]{:S(2)}) async-start(bf16[8,64,512]{2,1,0:T(8,128)(2,1)} %get-tuple-element.47), calls=%async_computation.2 | async-start | bytes 1048576 | tf_op jit(solution)/shard_map/all_to_all | solution.py:32
  87.3 10.8 %gram0.1 = (f32[512,1024]{1,0:T(8,128)}, f32[16,1536]{1,0:T(8,128)}) custom-call(s32[15]{0:T(128)} %stack.63.info.refs_0_, bf16[256,512]{1,0:T(8,128)(2,1)} %get-tuple-element.49.refs_1_, bf16[256,512]{1,0:T(8,128)(2,1)} %copy-done.12, bf16[256,512]{1,0:T(8,128)(2,1)} %copy-done.11, bf16[8,8,16,1152]{3,2,1,0:T(8,128)(2,1)} %bitcast.24, ...), custom_call_target="tpu_custom_call" | custom-call | flops 6442450944 | bytes 6291456 | tf_op jit(solution)/shard_map/gram0/pallas_call | solution.py:339
  98.1 7.1 %all-to-all-done.2 = bf16[8,64,512]{2,1,0:T(8,128)(2,1)S(1)} async-done(((bf16[8,64,512]{2,1,0:T(8,128)(2,1)}), bf16[8,64,512]{2,1,0:T(8,128)(2,1)S(1)}, u32[]{:S(2)}, u32[]{:S(2)}) %all-to-all-start.2) | async-done | bytes 524320 | tf_op jit(solution)/shard_map/all_to_all | solution.py:32
  106.1 3.7 %all-to-all-start.3 = ((bf16[8,64,512]{2,1,0:T(8,128)(2,1)}), bf16[8,64,512]{2,1,0:T(8,128)(2,1)S(1)}, u32[]{:S(2)}, u32[]{:S(2)}) async-start(bf16[8,64,512]{2,1,0:T(8,128)(2,1)} %broadcast_in_dim.20), calls=%async_computation.3 | async-start | bytes 1048576 | tf_op jit(solution)/shard_map/all_to_all | solution.py:32
  109.8 11.5 %gram1.1.refs_7_ = f32[512,1024]{1,0:T(8,128)} custom-call(s32[15]{0:T(128)} %stack.63.info.refs_0_, bf16[256,512]{1,0:T(8,128)(2,1)} %copy-done.13, bf16[256,512]{1,0:T(8,128)(2,1)} %copy-done.14, bf16[256,512]{1,0:T(8,128)(2,1)} %copy-done.10, bf16[8,8,16,1152]{3,2,1,0:T(8,128)(2,1)} %bitcast.26, ...), custom_call_target="tpu_custom_call", output_to_operand_aliasing={{}: (7, {})} | custom-call | flops 6442450944 | bytes 6291456 | tf_op jit(solution)/shard_map/gram1/pallas_call | solution.py:339
  121.4 4.8 %all-to-all-done.3 = bf16[8,64,512]{2,1,0:T(8,128)(2,1)S(1)} async-done(((bf16[8,64,512]{2,1,0:T(8,128)(2,1)}), bf16[8,64,512]{2,1,0:T(8,128)(2,1)S(1)}, u32[]{:S(2)}, u32[]{:S(2)}) %all-to-all-start.3) | async-done | bytes 524320 | tf_op jit(solution)/shard_map/all_to_all | solution.py:32
  126.2 3.0 %numer.1 = bf16[32,32,512]{2,1,0:T(8,128)(2,1)} custom-call(s32[15]{0:T(128)S(1)} %copy-done.4, bf16[512,1024]{1,0:T(8,128)(2,1)S(1)} %copy-done.1, bf16[512,512]{1,0:T(8,128)(2,1)S(1)} %bitcast.21, f32[1,1024]{1,0:T(1,128)S(1)} %copy-done.5, bf16[1024,512]{1,0:T(8,128)(2,1)S(1)} %copy-done), custom_call_target="tpu_custom_call" | custom-call | flops 536870912 | bytes 4194304 | tf_op jit(solution)/shard_map/numer/pallas_call | solution.py:217
  129.3 4.1 %all-to-all-start.4 = ((bf16[32,32,512]{2,1,0:T(8,128)(2,1)}), bf16[32,32,512]{2,1,0:T(8,128)(2,1)S(1)}, u32[]{:S(2)}, u32[]{:S(2)}) async-start(bf16[32,32,512]{2,1,0:T(8,128)(2,1)} %numer.1), calls=%async_computation.4 | async-start | bytes 2097152 | tf_op jit(solution)/shard_map/all_to_all | solution.py:387
  133.4 8.8 %gram2.1 = (f32[512,512]{1,0:T(8,128)}, bf16[512,512]{1,0:T(8,128)(2,1)}) custom-call(s32[15]{0:T(128)} %stack.63.info.refs_0_, bf16[256,512]{1,0:T(8,128)(2,1)} %copy-done.9, bf16[128,512]{1,0:T(8,128)(2,1)} %copy-done.15, bf16[128,512]{1,0:T(8,128)(2,1)} %collective-permute-done.8.refs_3_, bf16[8,8,16,1152]{3,2,1,0:T(8,128)(2,1)} %bitcast.27, ...), custom_call_target="tpu_custom_call" | custom-call | flops 4294967296 | bytes 6291456 | tf_op jit(solution)/shard_map/gram2/pallas_call | solution.py:339
  143.5 5.5 %all-to-all-done.4 = bf16[32,32,512]{2,1,0:T(8,128)(2,1)S(1)} async-done(((bf16[32,32,512]{2,1,0:T(8,128)(2,1)}), bf16[32,32,512]{2,1,0:T(8,128)(2,1)S(1)}, u32[]{:S(2)}, u32[]{:S(2)}) %all-to-all-start.4) | async-done | bytes 1048608 | tf_op jit(solution)/shard_map/all_to_all | solution.py:387
  150.0 6.1 %all-to-all-start.5 = ((bf16[16,32,512]{2,1,0:T(8,128)(2,1)}), bf16[16,32,512]{2,1,0:T(8,128)(2,1)S(1)}, u32[]{:S(2)}, u32[]{:S(2)}) async-start(bf16[16,32,512]{2,1,0:T(8,128)(2,1)} %broadcast_in_dim.23), calls=%async_computation.5 | async-start | bytes 1048576 | tf_op jit(solution)/shard_map/all_to_all | solution.py:389
  159.2 8.2 %all-to-all-done.5 = bf16[16,32,512]{2,1,0:T(8,128)(2,1)S(1)} async-done(((bf16[16,32,512]{2,1,0:T(8,128)(2,1)}), bf16[16,32,512]{2,1,0:T(8,128)(2,1)S(1)}, u32[]{:S(2)}, u32[]{:S(2)}) %all-to-all-start.5) | async-done | bytes 524320 | tf_op jit(solution)/shard_map/all_to_all | solution.py:389
  (59 shorter events, 23.6 us)
Async XLA Ops:
  0.6 31.6 %collective-permute-start = (bf16[512,512]{1,0:T(8,128)(2,1)}, bf16[512,512]{1,0:T(8,128)(2,1)S(1)}, u32[]{:S(2)}, u32[]{:S(2)}) collective-permute-start(bf16[512,512]{1,0:T(8,128)(2,1)} %bitcast.28), channel_id=1, source_target_pairs={{0,1},{1,0},{2,3},{3,2},{4,5},{5,4},{6,7},{7,6},{8,9},{9,8},{10,11... | collective-permute-start | bytes 1572872 | tf_op jit(solution)/shard_map/ppermute | solution.py:28
  3.4 24.4 %copy-start.2 = (f32[1,8192]{1,0:T(1,128)S(1)}, f32[1,8192]{1,0:T(1,128)}, u32[]{:S(2)}) copy-start(f32[1,8192]{1,0:T(1,128)} %gains.3) | copy-start | bytes 98308
  3.5 24.4 %copy-start.3 = (s32[15]{0:T(128)S(1)}, s32[15]{0:T(128)}, u32[]{:S(2)}) copy-start(s32[15]{0:T(128)} %stack.63.info.refs_0_) | copy-start | bytes 184
  8.9 19.0 %all-to-all-start = ((bf16[8,16,1152]{2,1,0:T(8,128)(2,1)}), bf16[8,16,1152]{2,1,0:T(8,128)(2,1)S(1)}, u32[]{:S(2)}, u32[]{:S(2)}) async-start(bf16[8,16,1152]{2,1,0:T(8,128)(2,1)} %get-tuple-element.38), calls=%async_computation | async-start | bytes 589824 | tf_op jit(solution)/shard_map/all_to_all | solution.py:32
  17.0 13.4 %collective-permute-start.2 = (bf16[256,512]{1,0:T(8,128)(2,1)}, bf16[256,512]{1,0:T(8,128)(2,1)S(1)}, u32[]{:S(2)}, u32[]{:S(2)}) collective-permute-start(bf16[256,512]{1,0:T(8,128)(2,1)} %get-tuple-element.49.refs_1_), channel_id=1, source_target_pairs={{0,14},{1,15},{2,0},{3,1},{4,2},{5,3},{6,4},{7,5},{8,6},{9,7},{10,... | collective-permute-start | bytes 786440 | tf_op jit(solution)/shard_map/ppermute | solution.py:28
  19.7 12.5 %collective-permute-start.1 = (bf16[256,512]{1,0:T(8,128)(2,1)}, bf16[256,512]{1,0:T(8,128)(2,1)S(1)}, u32[]{:S(2)}, u32[]{:S(2)}) collective-permute-start(bf16[256,512]{1,0:T(8,128)(2,1)} %get-tuple-element.49.refs_1_), channel_id=1, source_target_pairs={{0,2},{1,3},{2,4},{3,5},{4,6},{5,7},{6,8},{7,9},{8,10},{9,11},{10,... | collective-permute-start | bytes 786440 | tf_op jit(solution)/shard_map/ppermute | solution.py:28
  30.0 26.9 %copy-start.8 = (bf16[1,512,512]{2,1,0:T(8,128)(2,1)S(1)}, bf16[1,512,512]{2,1,0:T(8,128)(2,1)}, u32[]{:S(2)}) copy-start(bf16[1,512,512]{2,1,0:T(8,128)(2,1)} %param.7) | copy-start | bytes 1572868
  32.9 35.8 %all-to-all-start.1 = ((bf16[64,16,1152]{2,1,0:T(8,128)(2,1)}), bf16[64,16,1152]{2,1,0:T(8,128)(2,1)S(1)}, u32[]{:S(2)}, u32[]{:S(2)}) async-start(bf16[64,16,1152]{2,1,0:T(8,128)(2,1)} %address.1), calls=%async_computation.1 | async-start | bytes 4718592 | tf_op jit(solution)/shard_map/all_to_all | solution.py:46
  39.3 7.4 %collective-permute-start.3 = (bf16[256,512]{1,0:T(8,128)(2,1)}, bf16[256,512]{1,0:T(8,128)(2,1)S(1)}, u32[]{:S(2)}, u32[]{:S(2)}) collective-permute-start(bf16[256,512]{1,0:T(8,128)(2,1)} %copy-done.12), channel_id=1, source_target_pairs={{0,2},{1,3},{2,4},{3,5},{4,6},{5,7},{6,8},{7,9},{8,10},{9,11},{10,... | collective-permute-start | bytes 786440 | tf_op jit(solution)/shard_map/ppermute | solution.py:28
  39.3 7.4 %collective-permute-start.4 = (bf16[256,512]{1,0:T(8,128)(2,1)}, bf16[256,512]{1,0:T(8,128)(2,1)S(1)}, u32[]{:S(2)}, u32[]{:S(2)}) collective-permute-start(bf16[256,512]{1,0:T(8,128)(2,1)} %copy-done.11), channel_id=1, source_target_pairs={{0,14},{1,15},{2,0},{3,1},{4,2},{5,3},{6,4},{7,5},{8,6},{9,7},{10,... | collective-permute-start | bytes 786440 | tf_op jit(solution)/shard_map/ppermute | solution.py:28
  46.6 6.7 %collective-permute-start.5 = (bf16[256,512]{1,0:T(8,128)(2,1)S(1)}, bf16[256,512]{1,0:T(8,128)(2,1)S(1)}, u32[]{:S(2)}, u32[]{:S(2)}) collective-permute-start(bf16[256,512]{1,0:T(8,128)(2,1)S(1)} %collective-permute-done.3.refs_1_), channel_id=1, source_target_pairs={{0,2},{1,3},{2,4},{3,5},{4,6},{5,7},{6,8},{7,9},{8,10},{9,11},{10,... | collective-permute-start | bytes 786440 | tf_op jit(solution)/shard_map/ppermute | solution.py:28
  46.6 6.8 %collective-permute-start.6 = (bf16[256,512]{1,0:T(8,128)(2,1)S(1)}, bf16[256,512]{1,0:T(8,128)(2,1)S(1)}, u32[]{:S(2)}, u32[]{:S(2)}) collective-permute-start(bf16[256,512]{1,0:T(8,128)(2,1)S(1)} %collective-permute-done.4.refs_2_), channel_id=1, source_target_pairs={{0,14},{1,15},{2,0},{3,1},{4,2},{5,3},{6,4},{7,5},{8,6},{9,7},{10,... | collective-permute-start | bytes 786440 | tf_op jit(solution)/shard_map/ppermute | solution.py:28
  53.4 5.4 %collective-permute-start.7 = (bf16[128,512]{1,0:T(8,128)(2,1)S(1)}, bf16[128,512]{1,0:T(8,128)(2,1)S(1)}, u32[]{:S(2)}, u32[]{:S(2)}) collective-permute-start(bf16[128,512]{1,0:T(8,128)(2,1)S(1)} %slice.8), channel_id=1, source_target_pairs={{0,2},{1,3},{2,4},{3,5},{4,6},{5,7},{6,8},{7,9},{8,10},{9,11},{10,... | collective-permute-start | bytes 393224 | tf_op jit(solution)/shard_map/ppermute | solution.py:28
  54.2 4.7 %collective-permute-start.8 = (bf16[128,512]{1,0:T(8,128)(2,1)S(1)}, bf16[128,512]{1,0:T(8,128)(2,1)}, u32[]{:S(2)}, u32[]{:S(2)}) collective-permute-start(bf16[128,512]{1,0:T(8,128)(2,1)S(1)} %slice.9), channel_id=1, source_target_pairs={{0,14},{1,15},{2,0},{3,1},{4,2},{5,3},{6,4},{7,5},{8,6},{9,7},{10,... | collective-permute-start | bytes 393224 | tf_op jit(solution)/shard_map/ppermute | solution.py:28
  58.8 39.3 %copy-start.15 = (bf16[128,512]{1,0:T(8,128)(2,1)}, bf16[128,512]{1,0:T(8,128)(2,1)S(1)}, u32[]{:S(2)}) copy-start(bf16[128,512]{1,0:T(8,128)(2,1)S(1)} %collective-permute-done.7.refs_2_) | copy-start | bytes 393220
  68.7 7.1 %collective-permute-start.9 = (bf16[8,8,16,1152]{3,2,1,0:T(8,128)(2,1)S(1)}, bf16[8,8,16,1152]{3,2,1,0:T(8,128)(2,1)}, u32[]{:S(2)}, u32[]{:S(2)}) collective-permute-start(bf16[8,8,16,1152]{3,2,1,0:T(8,128)(2,1)S(1)} %bitcast.22), channel_id=1, source_target_pairs={{0,16},{1,17},{2,18},{3,19},{4,20},{5,21},{6,22},{7,23},{8,24},{9,... | collective-permute-start | bytes 7077896 | tf_op jit(solution)/shard_map/ppermute | solution.py:28
  82.7 22.5 %all-to-all-start.2 = ((bf16[8,64,512]{2,1,0:T(8,128)(2,1)}), bf16[8,64,512]{2,1,0:T(8,128)(2,1)S(1)}, u32[]{:S(2)}, u32[]{:S(2)}) async-start(bf16[8,64,512]{2,1,0:T(8,128)(2,1)} %get-tuple-element.47), calls=%async_computation.2 | async-start | bytes 1048576 | tf_op jit(solution)/shard_map/all_to_all | solution.py:32
  106.1 20.1 %all-to-all-start.3 = ((bf16[8,64,512]{2,1,0:T(8,128)(2,1)}), bf16[8,64,512]{2,1,0:T(8,128)(2,1)S(1)}, u32[]{:S(2)}, u32[]{:S(2)}) async-start(bf16[8,64,512]{2,1,0:T(8,128)(2,1)} %broadcast_in_dim.20), calls=%async_computation.3 | async-start | bytes 1048576 | tf_op jit(solution)/shard_map/all_to_all | solution.py:32
  109.8 16.4 %copy-start = (bf16[1024,512]{1,0:T(8,128)(2,1)S(1)}, bf16[1024,512]{1,0:T(8,128)(2,1)}, u32[]{:S(2)}) copy-start(bf16[1024,512]{1,0:T(8,128)(2,1)} %pad_maximum_fusion.weights) | copy-start | bytes 3145732
  109.8 16.4 %copy-start.1 = (bf16[512,1024]{1,0:T(8,128)(2,1)S(1)}, bf16[512,1024]{1,0:T(8,128)(2,1)}, u32[]{:S(2)}) copy-start(bf16[512,1024]{1,0:T(8,128)(2,1)} %get-tuple-element.55.calib) | copy-start | bytes 3145732
  109.8 16.4 %copy-start.4 = (s32[15]{0:T(128)S(1)}, s32[15]{0:T(128)}, u32[]{:S(2)}) copy-start(s32[15]{0:T(128)} %stack.63.info.refs_0_) | copy-start | bytes 184
  129.3 19.8 %all-to-all-start.4 = ((bf16[32,32,512]{2,1,0:T(8,128)(2,1)}), bf16[32,32,512]{2,1,0:T(8,128)(2,1)S(1)}, u32[]{:S(2)}, u32[]{:S(2)}) async-start(bf16[32,32,512]{2,1,0:T(8,128)(2,1)} %numer.1), calls=%async_computation.4 | async-start | bytes 2097152 | tf_op jit(solution)/shard_map/all_to_all | solution.py:387
  142.1 15.9 %collective-permute-start.10 = (bf16[512,512]{1,0:T(8,128)(2,1)}, bf16[512,512]{1,0:T(8,128)(2,1)S(1)}, u32[]{:S(2)}, u32[]{:S(2)}) collective-permute-start(bf16[512,512]{1,0:T(8,128)(2,1)} %get-tuple-element.72), channel_id=1, source_target_pairs={{0,1},{1,0},{2,3},{3,2},{4,5},{5,4},{6,7},{7,6},{8,9},{9,8},{10,11... | collective-permute-start | bytes 1572872 | tf_op jit(solution)/shard_map/ppermute | solution.py:28
  150.0 17.4 %all-to-all-start.5 = ((bf16[16,32,512]{2,1,0:T(8,128)(2,1)}), bf16[16,32,512]{2,1,0:T(8,128)(2,1)S(1)}, u32[]{:S(2)}, u32[]{:S(2)}) async-start(bf16[16,32,512]{2,1,0:T(8,128)(2,1)} %broadcast_in_dim.23), calls=%async_computation.5 | async-start | bytes 1048576 | tf_op jit(solution)/shard_map/all_to_all | solution.py:389
  (9 other events, 53.7 us)
